TPU v7x, 32 devices: a whole 2x2x4 slice. The times are simulated.
32 devices in a mesh: pix: 4 (over z), mode: 8 (over y, x, core).
Axes of the slice: x: 2, y: 2, z: 4, core: 2. Of those that a mesh axis runs over, the one named last changes fastest.
Arguments:
- frames: float32 [4, 4096, 8192], P(None, 'pix', 'mode'), may hold values from 0 to 500, as said below
- phase_steps: int32 [4], replicated, may hold values from 0 to 3, each once
- pattern_rows: int32 [8192], replicated, may hold values from 0 to 8191, each once
- probes: float32 [2, 32, 8192], replicated, may hold values from -6 to 6
Outputs:
- channels: float32 [2, 32, 8192], replicated
- fields: float32 [2, 32, 4096], P(None, None, ('pix', 'mode'))
- strengths: float32 [32], replicated
Inputs may be any that keep to these rules, and one draw needn't show every extreme that they name: `phase_steps`: each frame has its own phase step. `pattern_rows`: every Hadamard row is displayed exactly once. `frames`: intensities are not negative.
All inputs are finite; a program needn't handle non-finite values.
Results may differ from a plain program's by a relative error of at most 0.0003.
Values sent between devices are 32-bit elements; how exact they have to be, the bound alone decides.
No kernel may reach another device: no remote copies, remote signals or barrier semaphores. Data moves between devices by JAX's collectives and lax.ppermute only.
A program may use at most 128 MiB of HBM per device.

v0:
```python
import math

import jax
import jax.numpy as jnp
from jax import lax
from jax.sharding import PartitionSpec as P

HB = 128
ITERS = 2


precise = lax.Precision.HIGHEST


def demodulate(frames, phase_steps):
    cosine = (phase_steps == 0).astype(jnp.float32) - (phase_steps == 2).astype(jnp.float32)
    sine_part = (phase_steps == 1).astype(jnp.float32) - (phase_steps == 3).astype(jnp.float32)
    real_part = cosine[0] * frames[0]
    imag_part = sine_part[0] * frames[0]
    for frame_index in range(1, frames.shape[0]):
        real_part = real_part + cosine[frame_index] * frames[frame_index]
        imag_part = imag_part + sine_part[frame_index] * frames[frame_index]
    return (0.25 * real_part, 0.25 * imag_part)


def sign_table(table_order):
    positions = jnp.arange(table_order, dtype=jnp.int32)
    common = positions[:, None] & positions[None, :]
    parity = jnp.zeros((table_order, table_order), jnp.int32)
    for bit_place in range(table_order.bit_length() - 1):
        parity = parity + (common >> bit_place & 1)
    return (1 - 2 * (parity & 1)).astype(jnp.float32)


def hadamard_rows(values):
    length = values.shape[-1]
    leading = values.shape[:-1]
    inner_signs = sign_table(HB)
    outer_signs = sign_table(length // HB)
    shaped = values.reshape((-1, length // HB, HB))
    shaped = jnp.matmul(shaped, inner_signs, precision=precise)
    shaped = jnp.einsum("ab,nbc->nac", outer_signs, shaped, precision=precise)
    return shaped.reshape(leading + (length,)) * (1.0 / math.sqrt(length))


def contract_last(first_arg, second_arg):
    return lax.dot_general(first_arg, second_arg, (((1,), (1,)), ((), ())), precision=precise)


def forward(matrix, vectors):
    real_out = contract_last(vectors[0], matrix[0]) - contract_last(vectors[1], matrix[1])
    imag_out = contract_last(vectors[1], matrix[0]) + contract_last(vectors[0], matrix[1])
    return jnp.stack([real_out, imag_out])


def backward(matrix, images):
    real_out = jnp.dot(images[0], matrix[0], precision=precise) + jnp.dot(
        images[1], matrix[1], precision=precise
    )
    imag_out = jnp.dot(images[1], matrix[0], precision=precise) - jnp.dot(
        images[0], matrix[1], precision=precise
    )
    return jnp.stack([real_out, imag_out])


def orthonormal(vectors):
    mode_count = vectors.shape[2]
    stacked = jnp.concatenate([vectors[0], vectors[1]], axis=1)
    gram_matrix = jnp.dot(stacked, stacked.T, precision=precise)
    factor = jnp.linalg.cholesky(gram_matrix)
    solved = lax.linalg.triangular_solve(factor, stacked, left_side=True, lower=True)
    return jnp.stack([solved[:, :mode_count], solved[:, mode_count:]])


def local(frames, phase_steps, pattern_rows, probes):
    columns = frames.shape[2]
    groups = lax.axis_size("mode")
    modes_total = columns * groups
    devices = lax.axis_size("pix") * groups
    real_part, imag_part = demodulate(frames, phase_steps)
    positions = jnp.arange(modes_total, dtype=jnp.int32)
    inverse = jnp.zeros((modes_total,), jnp.int32).at[pattern_rows].set(positions)
    current = orthonormal(probes)
    rows_here = real_part.shape[0] // groups
    demodulated = jnp.stack([real_part, imag_part]).reshape(2, groups, rows_here, columns)
    ordered = jnp.take(
        lax.all_to_all(demodulated, "mode", split_axis=1, concat_axis=3, tiled=True),
        inverse,
        axis=3,
    )
    matrix = hadamard_rows(ordered)
    matrix = matrix.reshape(2, rows_here, modes_total)
    for iteration in range(ITERS):
        images = forward(matrix, current)
        returned = lax.psum(backward(matrix, images), ("pix", "mode"))
        current = orthonormal(returned)
    fields = forward(matrix, current)
    local_power = jnp.sum(fields * fields, axis=(0, 2))
    strengths = lax.psum(local_power, ("pix", "mode")) / (fields.shape[2] * devices)
    channels = math.sqrt(modes_total) * current
    return (channels, fields, strengths)


def solution(mesh):
    in_specs = (P(None, "pix", "mode"), P(), P(), P())
    out_specs = (P(), P(None, None, ("pix", "mode")), P())
    return jax.shard_map(local, mesh=mesh, in_specs=in_specs, out_specs=out_specs, check_vma=False)
```

profile of v0, /device:TPU:0, one launch (start us, length us, event | category | flops | bytes accessed | tf_op | source)
XLA Modules:
  0.0 704.6 jit_solution(8088165573559418275)
XLA Ops:
  8.5 12.0 %add_multiply_fusion.1 = (f32[1,1024,1024]{2,1,0:T(8,128)S(1)}, f32[1,1024,1024]{2,1,0:T(8,128)S(1)}) fusion(f32[4,1024,1024]{2,1,0:T(8,128)} %param.7, f32[]{:T(128)} %bitcast.9, f32[]{:T(128)} %bitcast.8, f32[]{:T(128)} %bitcast.7, f32[]{:T(128)} %bitcast.6, f32[]{:T(128)} %bitcast.14, f32[]{:T(128)} %bitcast.13, f32[]{:T(128)} %bitcast.12, f32[]{:T(128)} %bitcast.11), kind=kLoop, calls=%fused_computation.52 | loop fusion | flops 16777216 | bytes 25165856 | tf_op jit(solution)/shard_map/mul | solution.py:23
  22.2 4.1 copy.21
  26.3 5.3 all-to-all-start
  32.8 1.8 fusion.69
  34.6 2.9 cholesky.59
  38.9 2.4 custom-call.7
  41.4 30.7 %scatter_custom_fusion = s32[8192]{0:T(1024)S(1)} fusion(s32[8192]{0:T(1024)S(1)} %compare_select_fusion.1, s32[8192]{0:T(1024)S(1)} %iota.46, s32[]{:T(128)} %constant.66.clone.1), kind=kCustom, calls=%fused_computation.208 | custom fusion | bytes 32772 | tf_op jit(solution)/shard_map/scatter | solution.py:82
  72.1 3.1 fusion.68
  75.2 50.9 %all-to-all-done = f32[2,8,128,1024]{3,2,0,1:T(8,128)} async-done(((f32[2,8,128,1024]{3,2,0,1:T(8,128)}), f32[2,8,128,1024]{3,2,0,1:T(8,128)}, u32[]{:S(2)}, u32[]{:S(2)}) %all-to-all-start) | async-done | bytes 8388640 | tf_op jit(solution)/shard_map/all_to_all | solution.py:87
  126.1 8.7 %copy.22 = f32[2,8,128,1024]{2,3,1,0:T(8,128)} copy(f32[2,8,128,1024]{3,2,0,1:T(8,128)} %all-to-all-done) | data formatting | bytes 16777216 | tf_op jit(solution)/shard_map/all_to_all | solution.py:87
  134.8 15.4 %copy.23 = f32[2,128,8192]{1,0,2:T(2,128)} copy(f32[2,128,8192]{1,2,0:T(8,128)} %bitcast.173) | data formatting | bytes 16777216 | tf_op jit(solution)/shard_map/all_to_all | solution.py:87
  150.1 59.4 %gather_fusion = f32[8192,2,128]{2,1,0:T(2,128)} fusion(f32[2,128,8192]{1,0,2:T(2,128)} %copy.23, s32[8192]{0:T(1024)S(1)} %fusion.166), kind=kCustom, calls=%fused_computation | custom fusion | bytes 16809984 | tf_op jit(solution)/shard_map/jit(_take)/gather | solution.py:86
  209.5 11.5 %gather.7 = f32[256,64,128]{0,2,1:T(8,128)} reshape(f32[2,128,8192]{1,0,2:T(2,128)} %bitcast.172) | data formatting | bytes 16777216 | tf_op jit(solution)/shard_map/jit(_take)/gather | solution.py:86
  221.0 8.7 %copy.24 = f32[256,64,128]{2,1,0:T(8,128)} copy(f32[256,64,128]{0,2,1:T(8,128)} %gather.7) | data formatting | bytes 16777216 | tf_op jit(solution)/shard_map/jit(_take)/gather | solution.py:86
  229.7 13.0 %fusion.4 = f32[256,64,128]{2,1,0:T(8,128)S(1)} fusion(f32[256,64,128]{2,1,0:T(8,128)} %copy.24, pred[64,128]{1,0:T(8,128)(4,1)S(1)} %and_bitcast_fusion), kind=kOutput, calls=%fused_computation.12 | convolution fusion | flops 3223732224 | bytes 16785408 | tf_op jit(solution)/shard_map/dot_general | solution.py:41
  242.8 8.9 %multiply_bitcast_fusion = f32[256,64,128]{2,1,0:T(8,128)S(1)} fusion(f32[256,64,128]{2,1,0:T(8,128)S(1)} %fusion.4), kind=kOutput, calls=%fused_computation.11 | convolution fusion | flops 1612800000 | bytes 16777216 | tf_op jit(solution)/shard_map/ab,nbc->nac/dot_general | solution.py:42
  253.3 5.8 fusion.20
  259.1 5.6 fusion.18
  264.7 5.6 fusion.70
  270.3 4.8 fusion.38
  275.0 5.6 fusion.73
  280.7 4.9 fusion.34
  285.6 4.6 fusion.3
  290.2 4.6 fusion.2
  296.6 134.7 %all-reduce.3.cloned.1.call-done = f32[2,32,8192]{2,1,0:T(8,128)} async-done(((f32[2,32,8192]{2,1,0:T(8,128)}), f32[2,32,8192]{2,1,0:T(8,128)}) %all-reduce.3.cloned.1.call-update) | async-done | bytes 2097168 | tf_op jit(solution)/shard_map/psum | solution.py:95
  431.3 1.7 slice_bitcast_fusion.3
  433.0 1.8 fusion.67
  434.8 2.9 cholesky.70
  439.1 2.4 custom-call.8
  441.5 1.9 fusion.66
  443.7 5.6 fusion.14
  449.3 5.8 fusion.12
  455.1 5.6 fusion.76
  460.7 4.5 fusion.30
  465.2 6.0 fusion.79
  471.2 4.5 fusion.26
  475.8 4.8 fusion.1
  480.5 4.6 fusion
  486.6 133.7 %all-reduce.5.cloned.1.call-done = f32[2,32,8192]{2,1,0:T(8,128)} async-done(((f32[2,32,8192]{2,1,0:T(8,128)}), f32[2,32,8192]{2,1,0:T(8,128)}) %all-reduce.5.cloned.1.call-update) | async-done | bytes 2097168 | tf_op jit(solution)/shard_map/psum | solution.py:95
  622.0 1.8 fusion.65
  623.8 2.9 cholesky.81
  628.1 2.4 custom-call.9
  630.5 1.9 fusion.64
  632.7 5.8 fusion.8
  638.5 5.6 fusion.6
  644.2 5.8 fusion.85
  650.1 5.6 fusion.91
  656.4 38.9 %psum.23 = f32[32]{0:T(128)S(1)} all-reduce(f32[32]{0:T(128)S(1)} %get-tuple-element.5), channel_id=1, replica_groups=mesh['pix'=4,'mode'=8] {'pix','mode'}, use_global_device_ids=true, to_apply=%region_6.9 | all-reduce | flops 32 | bytes 256 | tf_op jit(solution)/shard_map/psum | solution.py:99
  (53 shorter events, 18.4 us)
Async XLA Ops:
  26.3 5.4 copy-start.7
  26.3 99.8 %all-to-all-start = ((f32[2,8,128,1024]{3,2,0,1:T(8,128)}), f32[2,8,128,1024]{3,2,0,1:T(8,128)}, u32[]{:S(2)}, u32[]{:S(2)}) async-start(f32[2,8,128,1024]{3,2,0,1:T(8,128)} %copy.21), calls=%async_computation | async-start | bytes 16777216 | tf_op jit(solution)/shard_map/all_to_all | solution.py:87
  31.6 9.7 %copy-start.8 = (s32[8192]{0:T(1024)S(1)}, s32[8192]{0:T(1024)}, u32[]{:S(2)}) copy-start(s32[8192]{0:T(1024)} %param.9) | copy-start | bytes 98308
  31.6 399.7 %all-reduce.3.cloned.1.call-start = ((), (), s32[]{:S(2)}) async-start(), calls=%async_computation.1 | async-start | bytes 4194304 | tf_op jit(solution)/shard_map/psum | solution.py:95
  31.8 1.0 copy-start.6
  253.3 27.4 %copy-start = (f32[128,64,128]{2,1,0:T(8,128)}, f32[128,64,128]{2,1,0:T(8,128)S(1)}, u32[]{:S(2)}) copy-start(f32[128,64,128]{2,1,0:T(8,128)S(1)} %get-tuple-element.9) | copy-start | bytes 12582916
  253.3 36.9 %copy-start.3 = (f32[128,64,128]{2,1,0:T(8,128)}, f32[128,64,128]{2,1,0:T(8,128)S(1)}, u32[]{:S(2)}) copy-start(f32[128,64,128]{2,1,0:T(8,128)S(1)} %get-tuple-element.10) | copy-start | bytes 12582916
  296.4 323.9 %all-reduce.5.cloned.1.call-start = ((), (), s32[]{:S(2)}) async-start(), calls=%async_computation.2 | async-start | bytes 4194304 | tf_op jit(solution)/shard_map/psum | solution.py:95
  441.5 2.2 copy-start.4
  443.7 11.4 %copy-start.1 = (f32[128,64,128]{2,1,0:T(8,128)S(1)}, f32[128,64,128]{2,1,0:T(8,128)}, u32[]{:S(2)}) copy-start(f32[128,64,128]{2,1,0:T(8,128)} %copy-done) | copy-start | bytes 12582916
  630.5 2.2 copy-start.5
  638.5 5.7 copy-start.2
Sparse Core Ops, SparseCore 0:
  296.5 134.7 all-reduce.2
  486.7 133.4 all-reduce.4
where the time goes:
time: 711 us; the launch traced here: 705 us
  waiting for transfers between devices  319 us (45%)
  local copies, waits for them, and re-layouts  146 us (21%)
  matrix products  140 us (20%)
  other arithmetic  40.2 us (6%)
  blocking collectives  38.9 us (5%)
  between operations  14.9 us (2%)
    psum x2, waiting for transfers between devices, local(): returned = lax.psum(backward(matrix, images), ('pix', 'mode'))  268 us
    gather x3, local copies, waits for them, and re-layouts, local(): jnp.take(lax.all_to_all(demodulated, 'mode', split_axis=1, concat_axis=3,...  79.6 us
    dot_general x12, matrix products, contract_last(): lax.dot_general(first_arg, second_arg, (((1,), (1,)), ((), ())), precisio...  68.2 us
    all_to_all x1, waiting for transfers between devices, local(): lax.all_to_all(demodulated, 'mode', split_axis=1, concat_axis=3, tiled=True)  50.9 us
    psum x1, blocking collectives, local(): lax.psum(local_power, ('pix', 'mode')) / (fields.shape[2] * devices)  38.9 us
    scatter x1, local copies, waits for them, and re-layouts, local(): jnp.zeros((modes_total,), jnp.int32).at[pattern_rows].set(positions)  30.7 us
    all_to_all x2, local copies, waits for them, and re-layouts, local(): lax.all_to_all(demodulated, 'mode', split_axis=1, concat_axis=3, tiled=True)  24 us
  transfers between devices with their start and end apart: 3, of which 3 were waited for; matrix products, arithmetic and copies ran while one was open for 6% of the time, Pallas kernels for 0%

commit v1 on v0

v1 whole, which is shorter than its diff:
```python
import functools
import math

import jax
import jax.numpy as jnp
from jax import lax
from jax.experimental import pallas as pl
from jax.experimental.pallas import tpu as pltpu
from jax.sharding import PartitionSpec as P

HB = 128
ITERS = 2
BLOCK = 256
F32 = jnp.float32
BF16 = jnp.bfloat16

precise = lax.Precision.HIGHEST
NT = (((1,), (1,)), ((), ()))
NN = (((1,), (0,)), ((), ()))
VMEM = pl.BlockSpec(memory_space=pltpu.VMEM)
SMEM = pl.BlockSpec(memory_space=pltpu.SMEM)


def dot(a, b, dims):
    return lax.dot_general(a, b, dims, preferred_element_type=F32)


def exact(a, b, dims):
    return lax.dot_general(a, b, dims, precision=precise, preferred_element_type=F32)


def split(values):
    high = values.astype(BF16)
    return high, (values - high.astype(F32)).astype(BF16)


def sign_table(order):
    row = lax.broadcasted_iota(jnp.int32, (order, order), 0)
    common = row & lax.broadcasted_iota(jnp.int32, (order, order), 1)
    parity = common
    shift = 16
    while shift:
        parity = parity ^ (parity >> shift)
        shift //= 2
    return (1 - 2 * (parity & 1)).astype(F32)


def butterfly(ref, count, size):
    step = 1
    while step < count:
        radix = 8 if step * 8 <= count else count // step
        groups = count // radix

        def body(g, carry, step=step, radix=radix):
            low = g % step
            base = (g // step) * (step * radix) + low
            for s in range(size // 8):
                at = [pl.multiple_of((base + r * step) * size + s * 8, 8) for r in range(radix)]
                v = [ref[pl.ds(a, 8), :] for a in at]
                half = 1
                while half < radix:
                    v = [
                        v[r] + v[r + half] if not r & half else v[r - half] - v[r]
                        for r in range(radix)
                    ]
                    half *= 2
                for a, x in zip(at, v):
                    ref[pl.ds(a, 8), :] = x
            return carry

        lax.fori_loop(0, groups, body, 0)
        step *= radix


def rows_of(vectors):
    return jnp.concatenate([vectors, jnp.zeros_like(vectors)], axis=0).T


def start_kernel(scale, idx_ref, probes_ref, u_ref, w_ref, g_ref):
    modes = probes_ref.shape[1]
    outer = modes // HB
    count = u_ref.shape[1]
    signs = sign_table(HB).astype(BF16)

    def inner(i, carry):
        at = pl.multiple_of(i * HB, HB)
        high, low = split(rows_of(probes_ref[:, pl.ds(at, HB)]))
        w_ref[pl.ds(at, HB), :] = dot(signs, high, NN) + dot(signs, low, NN)
        return carry

    lax.fori_loop(0, outer, inner, 0)
    butterfly(w_ref, outer, HB)

    def gather(t, carry):
        at = pl.multiple_of(t * 8, 8)
        for q in range(8):
            g_ref[pl.ds(at + q, 1), :] = w_ref[pl.ds(idx_ref[at + q], 1), :]
        return carry

    lax.fori_loop(0, count // 8, gather, 0)
    for b in range(count // HB):
        part = g_ref[b * HB : (b + 1) * HB, :].T
        u_ref[:, b * HB : (b + 1) * HB] = part[: u_ref.shape[0]] * scale


def start_vectors(idx, probes, scale):
    vectors, modes = probes.shape
    count = idx.shape[0]
    return pl.pallas_call(
        functools.partial(start_kernel, scale),
        out_shape=jax.ShapeDtypeStruct((vectors, count), F32),
        in_specs=[SMEM, VMEM],
        out_specs=VMEM,
        scratch_shapes=[pltpu.VMEM((modes, 128), F32), pltpu.VMEM((count, 128), F32)],
        compiler_params=pltpu.CompilerParams(vmem_limit_bytes=16 << 20),
    )(idx, probes)


def end_kernel(idx_ref, x_ref, inv_ref, out_ref, s_ref, w_ref):
    chunks, vectors, count = x_ref.shape
    modes = out_ref.shape[1]
    outer = modes // HB
    half = vectors // 2
    signs = sign_table(HB).astype(BF16)
    per = count // HB

    def turn(i, carry):
        c = i // per
        at = pl.multiple_of((i % per) * HB, HB)
        to = pl.multiple_of(i * HB, HB)
        s_ref[pl.ds(to, HB), :] = rows_of(x_ref[c, :, pl.ds(at, HB)])
        return carry

    lax.fori_loop(0, modes // HB, turn, 0)

    def scatter(t, carry):
        at = pl.multiple_of(t * 8, 8)
        for q in range(8):
            w_ref[pl.ds(idx_ref[at + q], 1), :] = s_ref[pl.ds(at + q, 1), :]
        return carry

    lax.fori_loop(0, modes // 8, scatter, 0)
    butterfly(w_ref, outer, HB)

    def inner(i, carry):
        at = pl.multiple_of(i * HB, HB)
        high, low = split(w_ref[pl.ds(at, HB), :].T[:vectors])
        both = dot(jnp.concatenate([high, low], axis=0), signs, NN)
        total = both[:vectors] + both[vectors:]
        out_ref[:half, pl.ds(at, HB)] = exact(inv_ref[...], total[:half], NN)
        out_ref[half:, pl.ds(at, HB)] = exact(inv_ref[...], total[half:], NN)
        return carry

    lax.fori_loop(0, outer, inner, 0)


def end_vectors(idx, gathered, inv):
    chunks, vectors, count = gathered.shape
    modes = chunks * count
    return pl.pallas_call(
        end_kernel,
        out_shape=jax.ShapeDtypeStruct((vectors, modes), F32),
        in_specs=[SMEM, VMEM, VMEM],
        out_specs=VMEM,
        scratch_shapes=[pltpu.VMEM((modes, 128), F32), pltpu.VMEM((modes, 128), F32)],
        compiler_params=pltpu.CompilerParams(vmem_limit_bytes=24 << 20),
    )(idx, gathered, inv)


def stack_forward(u):
    half = u.shape[0] // 2
    turned = jnp.concatenate([-u[half:], u[:half]], axis=0)
    uh, ul = split(u)
    th, tl = split(turned)
    return jnp.concatenate([uh, ul], axis=0), jnp.concatenate([th, tl], axis=0)


def apply_forward(both, turned, dh, dl):
    n = both.shape[0] // 2
    wide = dot(both, dh[0], NT) + dot(turned, dh[1], NT)
    low = dot(both[:n], dl[0], NT) + dot(turned[:n], dl[1], NT)
    return wide[:n] + wide[n:] + low


def demod_kernel(inv_ref, f0, f1, f2, f3, u_ref, dh_ref, dl_ref, img_ref, b_ref, t_ref):
    @pl.when(pl.program_id(0) == 0)
    def _():
        b_ref[...], t_ref[...] = stack_forward(u_ref[...])

    for part, plus, minus in ((0, f0, f2), (1, f1, f3)):
        high, low = split(0.25 * (plus[0] - minus[0]))
        dh_ref[part] = high
        dl_ref[part] = low
    img_ref[...] = apply_forward(b_ref[...], t_ref[...], dh_ref, dl_ref)


def demodulate(steps_at, frames, u):
    steps, rows, cols = frames.shape
    vectors = u.shape[0]
    block = min(BLOCK, rows)

    def frame(s):
        return pl.BlockSpec((1, block, cols), lambda i, at: (at[s], i, 0))

    planes = pl.BlockSpec((2, block, cols), lambda i, at: (0, i, 0))
    return pl.pallas_call(
        demod_kernel,
        grid_spec=pltpu.PrefetchScalarGridSpec(
            num_scalar_prefetch=1,
            grid=(rows // block,),
            in_specs=[frame(0), frame(1), frame(2), frame(3)]
            + [pl.BlockSpec((vectors, cols), lambda i, at: (0, 0))],
            out_specs=[planes, planes, pl.BlockSpec((vectors, block), lambda i, at: (0, i))],
            scratch_shapes=[pltpu.VMEM((2 * vectors, cols), BF16)] * 2,
        ),
        out_shape=[
            jax.ShapeDtypeStruct((2, rows, cols), BF16),
            jax.ShapeDtypeStruct((2, rows, cols), BF16),
            jax.ShapeDtypeStruct((vectors, rows), F32),
        ],
        compiler_params=pltpu.CompilerParams(vmem_limit_bytes=24 << 20),
    )(steps_at, frames, frames, frames, frames, u)


def forward_kernel(u_ref, dh_ref, dl_ref, img_ref, b_ref, t_ref):
    @pl.when(pl.program_id(0) == 0)
    def _():
        b_ref[...], t_ref[...] = stack_forward(u_ref[...])

    img_ref[...] = apply_forward(b_ref[...], t_ref[...], dh_ref, dl_ref)


def forward(u, dh, dl):
    _, rows, cols = dh.shape
    vectors = u.shape[0]
    block = min(BLOCK, rows)
    planes = pl.BlockSpec((2, block, cols), lambda i: (0, i, 0))
    return pl.pallas_call(
        forward_kernel,
        grid=(rows // block,),
        in_specs=[pl.BlockSpec((vectors, cols), lambda i: (0, 0)), planes, planes],
        out_specs=pl.BlockSpec((vectors, block), lambda i: (0, i)),
        scratch_shapes=[pltpu.VMEM((2 * vectors, cols), BF16)] * 2,
        out_shape=jax.ShapeDtypeStruct((vectors, rows), F32),
        compiler_params=pltpu.CompilerParams(vmem_limit_bytes=16 << 20),
    )(u, dh, dl)


def backward_kernel(inv_ref, img_ref, dh_ref, dl_ref, ret_ref):
    vectors = img_ref.shape[0]
    half = vectors // 2
    real = exact(inv_ref[...], img_ref[:half], NN)
    imag = exact(inv_ref[...], img_ref[half:], NN)
    total = None
    for part, rows in ((0, [real, imag]), (1, [imag, -real])):
        high, low = split(jnp.concatenate(rows, axis=0))
        wide = dot(jnp.concatenate([high, low], axis=0), dh_ref[part], NN)
        here = wide[:vectors] + wide[vectors:] + dot(high, dl_ref[part], NN)
        total = here if total is None else total + here

    @pl.when(pl.program_id(0) == 0)
    def _():
        ret_ref[...] = total

    @pl.when(pl.program_id(0) != 0)
    def _():
        ret_ref[...] += total


def backward(inv, images, dh, dl):
    _, rows, cols = dh.shape
    vectors = images.shape[0]
    block = min(BLOCK, rows)
    planes = pl.BlockSpec((2, block, cols), lambda i: (0, i, 0))
    return pl.pallas_call(
        backward_kernel,
        grid=(rows // block,),
        in_specs=[
            pl.BlockSpec(inv.shape, lambda i: (0, 0)),
            pl.BlockSpec((vectors, block), lambda i: (0, i)),
            planes,
            planes,
        ],
        out_specs=pl.BlockSpec((vectors, cols), lambda i: (0, 0)),
        out_shape=jax.ShapeDtypeStruct((vectors, cols), F32),
        compiler_params=pltpu.CompilerParams(vmem_limit_bytes=16 << 20),
    )(inv, images, dh, dl)


def gram(vectors):
    half = vectors.shape[0] // 2
    return exact(vectors[:half], vectors[:half], NT) + exact(vectors[half:], vectors[half:], NT)


def inverse_factor(gram_matrix):
    factor = jnp.linalg.cholesky(gram_matrix)
    eye = jnp.eye(gram_matrix.shape[0], dtype=F32)
    return lax.linalg.triangular_solve(factor, eye, left_side=True, lower=True)


def normalise(inv, vectors):
    half = inv.shape[0]
    return jnp.concatenate([exact(inv, vectors[:half], NN), exact(inv, vectors[half:], NN)], axis=0)


def flip(n, bit):
    return [(i, i ^ bit) for i in range(n)]


def pick(pieces, here, n):
    bit = 1
    while bit < n:
        odd = (here & bit) != 0
        pieces = [jnp.where(odd, pieces[b ^ bit], pieces[b]) for b in range(n)]
        bit *= 2
    return pieces


def scatter_sum(blocks, axis, step, n):
    size = lax.axis_size(axis)
    here = (lax.axis_index(axis) // step) % n
    mine = pick(blocks, here, n)
    total = mine[0]
    for b in range(1, n):
        total = total + lax.ppermute(mine[b], axis, flip(size, b * step))
    return total


def gather_all(block, axis, step, n):
    size = lax.axis_size(axis)
    here = (lax.axis_index(axis) // step) % n
    pieces = [block] + [lax.ppermute(block, axis, flip(size, b * step)) for b in range(1, n)]
    return pick(pieces, here, n)


def share_sum(block, axis, step, n):
    size = lax.axis_size(axis)
    total = block
    for b in range(1, n):
        total = total + lax.ppermute(block, axis, flip(size, b * step))
    return total


def double_sum(block, axis):
    size = lax.axis_size(axis)
    bit = 1
    while bit < size:
        block = block + lax.ppermute(block, axis, flip(size, bit))
        bit *= 2
    return block


def sum_pix(x):
    n = lax.axis_size("pix")
    if n != 4:
        return double_sum(x, "pix")
    rows = x.shape[0] // n
    mine = scatter_sum([x[i * rows : (i + 1) * rows] for i in range(n)], "pix", 1, n)
    return jnp.concatenate(gather_all(mine, "pix", 1, n), axis=0)


def pack(gram_matrix, width):
    return jnp.pad(gram_matrix.reshape(1, -1), ((0, 7), (0, width - gram_matrix.size)))


def sum_mode(x, extra=None):
    n = lax.axis_size("mode")
    rows, cols = x.shape
    if n != 8:
        total = double_sum(x, "mode")
        return total, (None if extra is None else double_sum(extra, "mode"))
    half = rows // 2
    odd = (lax.axis_index("mode") % 2) != 0
    mine = jnp.where(odd, x[half:], x[:half])
    other = jnp.where(odd, x[:half], x[half:])
    if extra is not None:
        k = extra.shape[0]
        row = pack(extra, cols)
        mine = jnp.concatenate([mine, row], axis=0)
        other = jnp.concatenate([other, row], axis=0)
    chip = mine + lax.ppermute(other, "mode", flip(n, 1))
    chip = share_sum(chip, "mode", 2, 4)
    mine = chip[:half]
    other = lax.ppermute(mine, "mode", flip(n, 1))
    total = jnp.concatenate([jnp.where(odd, other, mine), jnp.where(odd, mine, other)], axis=0)
    if extra is None:
        return total, None
    return total, chip[half, : k * k].reshape(k, k)


def local(frames, phase_steps, pattern_rows, probes):
    columns = frames.shape[2]
    rows = frames.shape[1]
    groups = lax.axis_size("mode")
    pixels = rows * lax.axis_size("pix")
    modes_total = columns * groups
    k = probes.shape[1]
    vectors = 2 * k
    probes = probes.reshape(vectors, modes_total)
    here = lax.axis_index("mode")
    steps_at = jnp.sum(
        jnp.where(phase_steps[None, :] == jnp.arange(4)[:, None], jnp.arange(4)[None, :], 0), axis=1
    ).astype(jnp.int32)
    my_rows = lax.dynamic_slice_in_dim(pattern_rows, here * columns, columns)
    u = start_vectors(my_rows, probes, 1.0 / math.sqrt(modes_total))
    dh, dl, images = demodulate(steps_at, frames, u)
    inv = inverse_factor(gram(probes))
    images, _ = sum_mode(images)
    returned = sum_pix(backward(inv, images, dh, dl))
    for iteration in range(1, ITERS):
        images = forward(returned, dh, dl)
        images, gram_matrix = sum_mode(images, gram(returned))
        inv = inverse_factor(gram_matrix)
        returned = sum_pix(backward(inv, images, dh, dl))
    images = forward(returned, dh, dl)
    images, gram_matrix = sum_mode(images, gram(returned))
    inv = inverse_factor(gram_matrix)
    width = rows // groups
    fields = normalise(inv, lax.dynamic_slice_in_dim(images, here * width, width, 1))
    power = jnp.sum(fields * fields, axis=1)
    power = jnp.broadcast_to((power[:k] + power[k:])[None, :], (8, k))
    power = double_sum(double_sum(power, "mode"), "pix")
    strengths = power[0] / pixels
    third = vectors // 8 * 3 // 8 * 8
    parts = [(0, third), (third, 2 * third), (2 * third, vectors)]
    gathered = jnp.concatenate(
        [lax.all_gather(returned[a:b], "mode", tiled=False) for a, b in parts], axis=1
    )
    channels = end_vectors(pattern_rows, gathered, inv)
    return (channels.reshape(2, k, modes_total), fields.reshape(2, k, width), strengths)


def solution(mesh):
    in_specs = (P(None, "pix", "mode"), P(), P(), P())
    out_specs = (P(), P(None, None, ("pix", "mode")), P())
    return jax.shard_map(local, mesh=mesh, in_specs=in_specs, out_specs=out_specs, check_vma=False)
```

time: 711 us -> 240 us (0.34)
  waiting for transfers between devices: 319 us -> 42.7 us
  matrix products: 140 us -> 3.92 us
  local copies, waits for them, and re-layouts: 146 us -> 21.9 us
  Pallas kernels: 0 us -> 82.8 us
  starting transfers between devices: 5.59 us -> 34.6 us
  other arithmetic: 40.2 us -> 22.9 us
  between operations: 14.9 us -> 1.13 us
  blocking collectives: 38.9 us -> 29.1 us
    psum x2 -> x0, waiting for transfers between devices: 268 us -> none  [local(): returned = lax.psum(backward(matrix, images), ('pix', 'mode'))]
    dot_general x25 -> x8, matrix products: 133 us -> 3.24 us  [exact(): lax.dot_general(a, b, dims, precision=precise, preferred_element_type=F32)]
    pallas_call x0 -> x7, Pallas kernels: none -> 82.8 us  [the longest x1 46.1 us: end_vectors(): pl.pallas_call(end_kernel, out_shape=jax.ShapeDtypeStruct((vectors, modes...]
    gather x3 -> x0, local copies, waits for them, and re-layouts: 79.6 us -> none  [local(): jnp.take(lax.all_to_all(demodulated, 'mode', split_axis=1, concat_axis=3,...]
    all_to_all x1 -> x0, waiting for transfers between devices: 50.9 us -> none  [local(): lax.all_to_all(demodulated, 'mode', split_axis=1, concat_axis=3, tiled=True)]
    ppermute x0 -> x32, waiting for transfers between devices: none -> 42.7 us  [the longest x9 17.8 us: share_sum(): total = total + lax.ppermute(block, axis, flip(size, b * step))]
    psum x1 -> x0, blocking collectives: 38.9 us -> none  [local(): lax.psum(local_power, ('pix', 'mode')) / (fields.shape[2] * devices)]
    ppermute x0 -> x32, starting transfers between devices: none -> 34.6 us  [the longest x9 11.2 us: share_sum(): total = total + lax.ppermute(block, axis, flip(size, b * step))]
  transfers between devices with their start and end apart: 3 -> 32, of which waited for: 3 -> 20; matrix products, arithmetic and copies ran while one was open for 6% -> 10% of each run, Pallas kernels for 0% -> 19%
where the time goes in v1:
time: 240 us; the launch traced here: 239 us
  Pallas kernels  82.8 us (34%)
  waiting for transfers between devices  42.7 us (18%)
  starting transfers between devices  34.6 us (14%)
  blocking collectives  29.1 us (12%)
  other arithmetic  22.9 us (10%)
  local copies, waits for them, and re-layouts  21.9 us (9%)
  matrix products  3.92 us (2%)
    pallas_call x1, Pallas kernels, end_vectors(): pl.pallas_call(end_kernel, out_shape=jax.ShapeDtypeStruct((vectors, modes...  46.1 us
    all_gather x3, blocking collectives, local(): lax.all_gather(returned[a:b], 'mode', tiled=False)  29.1 us
    unnamed x20, local copies, waits for them, and re-layouts  20.6 us
    pallas_call x1, Pallas kernels, start_vectors(): pl.pallas_call(functools.partial(start_kernel, scale), out_shape=jax.Shap...  18.3 us
    ppermute x9, waiting for transfers between devices, share_sum(): total = total + lax.ppermute(block, axis, flip(size, b * step))  17.8 us
    ppermute x9, starting transfers between devices, share_sum(): total = total + lax.ppermute(block, axis, flip(size, b * step))  11.2 us
    another operation x9, other arithmetic, inverse_factor(): factor = jnp.linalg.cholesky(gram_matrix)  10.8 us
    ppermute x6, waiting for transfers between devices, scatter_sum(): total = total + lax.ppermute(mine[b], axis, flip(size, b * step))  10.6 us
  transfers between devices with their start and end apart: 32, of which 20 were waited for; matrix products, arithmetic and copies ran while one was open for 10% of the time, Pallas kernels for 19%

profile of v1, /device:TPU:0, one launch (start us, length us, event | category | flops | bytes accessed | tf_op | source)
XLA Modules:
  0.0 239.1 jit_solution(2416398572075690510)
XLA Ops:
  2.1 1.6 copy-done.7
  3.7 18.3 %shard_map.67.u_ref = f32[64,1024]{1,0:T(8,128)S(1)} custom-call(s32[1024]{0:T(1024)S(1)} %dynamic_slice.6.idx_ref, f32[64,8192]{1,0:T(8,128)S(1)} %bitcast.43), custom_call_target="tpu_custom_call" | custom-call | tf_op jit(solution)/shard_map/pallas_call | solution.py:109
  22.1 5.8 %copy-done = f32[4,1024,1024]{2,1,0:T(8,128)S(1)} copy-done((f32[4,1024,1024]{2,1,0:T(8,128)S(1)}, f32[4,1024,1024]{2,1,0:T(8,128)}, u32[]{:S(2)}) %copy-start) | copy-done | bytes 16777240
  27.8 4.5 %shard_map.68 = (bf16[2,1024,1024]{2,1,0:T(8,128)(2,1)S(1)}, bf16[2,1024,1024]{2,1,0:T(8,128)(2,1)S(1)}, f32[64,1024]{1,0:T(8,128)S(1)}) custom-call(s32[4]{0:T(128)S(1)} %select_reduce_fusion.2.inv_ref, f32[4,1024,1024]{2,1,0:T(8,128)S(1)} %copy-done, f32[4,1024,1024]{2,1,0:T(8,128)S(1)} %copy-done, f32[4,1024,1024]{2,1,0:T(8,128)S(1)} %copy-done, ...), custom_call_target="tpu_custom_call" | custom-call | tf_op jit(solution)/shard_map/pallas_call | solution.py:206
  32.3 1.9 copy-done.1
  34.3 2.0 copy-done.4
  38.9 2.9 %cholesky.59 = f32[32,32]{1,0:T(8,128)S(1)} custom-call(f32[32,32]{1,0:T(8,128)S(1)} %fusion.45), custom_call_target="Cholesky" | custom-call | tf_op jit(solution)/shard_map/jit(cholesky)/cholesky | solution.py:296
  42.5 2.6 %collective-permute-start.1 = (f32[32,1024]{1,0:T(8,128)S(1)}, f32[32,1024]{1,0:T(8,128)S(1)}, u32[]{:S(2)}, u32[]{:S(2)}) collective-permute-start(f32[32,1024]{1,0:T(8,128)S(1)} %select_add_fusion), channel_id=1, source_target_pairs={{0,2},{1,3},{2,0},{3,1},{4,6},{5,7},{6,4},{7,5},{8,10},{9,11},{10,... | collective-permute-start | bytes 393224 | tf_op jit(solution)/shard_map/ppermute | solution.py:340
  45.1 1.5 collective-permute-start.2
  47.3 2.4 %custom-call.7 = f32[1,32,32]{1,2,0:T(8,128)S(1)} custom-call(f32[1,32,32]{2,1,0:T(8,128)S(1)} %fusion.33), custom_call_target="InvertDiagBlocksLowerTriangular" | custom-call | tf_op jit(solution)/shard_map/triangular_solve/custom-call.0 | solution.py:298
  49.7 3.8 %collective-permute-done.2 = f32[32,1024]{1,0:T(8,128)S(1)} collective-permute-done((f32[32,1024]{1,0:T(8,128)S(1)}, f32[32,1024]{1,0:T(8,128)S(1)}, u32[]{:S(2)}, u32[]{:S(2)}) %collective-permute-start.2) | collective-permute-done | bytes 131104 | tf_op jit(solution)/shard_map/ppermute | solution.py:340
  55.0 2.2 copy-done.2
  57.2 2.2 copy-done.5
  59.4 3.2 %shard_map.69 = f32[64,1024]{1,0:T(8,128)S(1)} custom-call(f32[32,32]{1,0:T(8,128)S(1)} %fusion.31.inv_ref, f32[64,1024]{1,0:T(8,128)S(1)} %pad_maximum_fusion.1.img_ref, bf16[2,1024,1024]{2,1,0:T(8,128)(2,1)S(1)} %copy-done.2, bf16[2,1024,1024]{2,1,0:T(8,128)(2,1)S(1)} %copy-done.5), custom_call_target="tpu_custom_call" | custom-call | tf_op jit(solution)/shard_map/pallas_call | solution.py:275
  62.6 1.6 collective-permute-start.5
  64.3 2.6 %collective-permute-start.6 = (f32[16,1024]{1,0:T(8,128)S(1)}, f32[16,1024]{1,0:T(8,128)S(1)}, u32[]{:S(2)}, u32[]{:S(2)}) collective-permute-start(f32[16,1024]{1,0:T(8,128)S(1)} %get-tuple-element.31), channel_id=1, source_target_pairs={{0,16},{8,24},{16,0},{24,8},{1,17},{9,25},{17,1},{25,9},{2,18},{10... | collective-permute-start | bytes 196616 | tf_op jit(solution)/shard_map/ppermute | solution.py:325
  67.1 4.7 %collective-permute-done.6 = f32[16,1024]{1,0:T(8,128)S(1)} collective-permute-done((f32[16,1024]{1,0:T(8,128)S(1)}, f32[16,1024]{1,0:T(8,128)S(1)}, u32[]{:S(2)}, u32[]{:S(2)}) %collective-permute-start.6) | collective-permute-done | bytes 65568 | tf_op jit(solution)/shard_map/ppermute | solution.py:325
  74.0 2.4 %collective-permute-start.8 = (f32[16,1024]{1,0:T(8,128)S(1)}, f32[16,1024]{1,0:T(8,128)S(1)}, u32[]{:S(2)}, u32[]{:S(2)}) collective-permute-start(f32[16,1024]{1,0:T(8,128)S(1)} %add_add_fusion.4), channel_id=1, source_target_pairs={{0,24},{8,16},{16,8},{24,0},{1,25},{9,17},{17,9},{25,1},{2,26},{10... | collective-permute-start | bytes 196616 | tf_op jit(solution)/shard_map/ppermute | solution.py:332
  76.6 1.5 collective-permute-done.10
  78.2 2.0 collective-permute-done.8
  80.1 1.7 collective-permute-done.9
  82.2 3.7 %shard_map.70 = f32[64,1024]{1,0:T(8,128)S(1)} custom-call(f32[64,1024]{1,0:T(8,128)S(1)} %pad_maximum_fusion.2.u_ref, bf16[2,1024,1024]{2,1,0:T(8,128)(2,1)S(1)} %copy-done.2, bf16[2,1024,1024]{2,1,0:T(8,128)(2,1)S(1)} %copy-done.5), custom_call_target="tpu_custom_call" | custom-call | tf_op jit(solution)/shard_map/pallas_call | solution.py:238
  91.4 3.6 %collective-permute-done.12 = f32[40,1024]{1,0:T(8,128)S(1)} collective-permute-done((f32[40,1024]{1,0:T(8,128)S(1)}, f32[40,1024]{1,0:T(8,128)S(1)}, u32[]{:S(2)}, u32[]{:S(2)}) %collective-permute-start.12) | collective-permute-done | bytes 163872 | tf_op jit(solution)/shard_map/ppermute | solution.py:340
  94.9 2.0 collective-permute-done.13
  97.0 1.6 collective-permute-done.14
  98.9 2.9 %cholesky.70 = f32[32,32]{1,0:T(8,128)S(1)} custom-call(f32[32,32]{1,0:T(8,128)S(1)} %fusion.43), custom_call_target="Cholesky" | custom-call | tf_op jit(solution)/shard_map/jit(cholesky)/cholesky | solution.py:296
  103.2 2.4 %custom-call.8 = f32[1,32,32]{1,2,0:T(8,128)S(1)} custom-call(f32[1,32,32]{2,1,0:T(8,128)S(1)} %fusion.34), custom_call_target="InvertDiagBlocksLowerTriangular" | custom-call | tf_op jit(solution)/shard_map/triangular_solve/custom-call.0 | solution.py:298
  105.9 2.2 copy-done.3
  108.1 2.2 copy-done.6
  110.3 3.2 %shard_map.71 = f32[64,1024]{1,0:T(8,128)S(1)} custom-call(f32[32,32]{1,0:T(8,128)S(1)} %fusion.29.inv_ref, f32[64,1024]{1,0:T(8,128)S(1)} %pad_maximum_fusion.3.img_ref, bf16[2,1024,1024]{2,1,0:T(8,128)(2,1)S(1)} %copy-done.3, bf16[2,1024,1024]{2,1,0:T(8,128)(2,1)S(1)} %copy-done.6), custom_call_target="tpu_custom_call" | custom-call | tf_op jit(solution)/shard_map/pallas_call | solution.py:275
  113.6 2.9 %collective-permute-start.17 = (f32[16,1024]{1,0:T(8,128)S(1)}, f32[16,1024]{1,0:T(8,128)S(1)}, u32[]{:S(2)}, u32[]{:S(2)}) collective-permute-start(f32[16,1024]{1,0:T(8,128)S(1)} %get-tuple-element.22), channel_id=1, source_target_pairs={{0,16},{8,24},{16,0},{24,8},{1,17},{9,25},{17,1},{25,9},{2,18},{10... | collective-permute-start | bytes 196616 | tf_op jit(solution)/shard_map/ppermute | solution.py:325
  119.2 1.5 collective-permute-done.17
  120.8 1.8 collective-permute-done.18
  122.6 2.2 collective-permute-start.19
  125.5 1.6 collective-permute-start.21
  127.1 2.4 %collective-permute-done.19 = f32[16,1024]{1,0:T(8,128)S(1)} collective-permute-done((f32[16,1024]{1,0:T(8,128)S(1)}, f32[16,1024]{1,0:T(8,128)S(1)}, u32[]{:S(2)}, u32[]{:S(2)}) %collective-permute-start.19) | collective-permute-done | bytes 65568 | tf_op jit(solution)/shard_map/ppermute | solution.py:332
  129.5 2.0 collective-permute-done.20
  131.8 3.7 %shard_map.72 = f32[64,1024]{1,0:T(8,128)S(1)} custom-call(f32[64,1024]{1,0:T(8,128)S(1)} %pad_maximum_fusion.4.u_ref, bf16[2,1024,1024]{2,1,0:T(8,128)(2,1)S(1)} %copy-done.3, bf16[2,1024,1024]{2,1,0:T(8,128)(2,1)S(1)} %copy-done.6), custom_call_target="tpu_custom_call" | custom-call | tf_op jit(solution)/shard_map/pallas_call | solution.py:238
  138.3 1.5 collective-permute-start.24
  141.0 3.6 %collective-permute-done.23 = f32[40,1024]{1,0:T(8,128)S(1)} collective-permute-done((f32[40,1024]{1,0:T(8,128)S(1)}, f32[40,1024]{1,0:T(8,128)S(1)}, u32[]{:S(2)}, u32[]{:S(2)}) %collective-permute-start.23) | collective-permute-done | bytes 163872 | tf_op jit(solution)/shard_map/ppermute | solution.py:340
  144.6 3.2 %collective-permute-done.24 = f32[40,1024]{1,0:T(8,128)S(1)} collective-permute-done((f32[40,1024]{1,0:T(8,128)S(1)}, f32[40,1024]{1,0:T(8,128)S(1)}, u32[]{:S(2)}, u32[]{:S(2)}) %collective-permute-start.24) | collective-permute-done | bytes 163872 | tf_op jit(solution)/shard_map/ppermute | solution.py:340
  148.1 2.9 %cholesky.81 = f32[32,32]{1,0:T(8,128)S(1)} custom-call(f32[32,32]{1,0:T(8,128)S(1)} %fusion.41), custom_call_target="Cholesky" | custom-call | tf_op jit(solution)/shard_map/jit(cholesky)/cholesky | solution.py:296
  152.3 2.4 %custom-call.9 = f32[1,32,32]{1,2,0:T(8,128)S(1)} custom-call(f32[1,32,32]{2,1,0:T(8,128)S(1)} %fusion.35), custom_call_target="InvertDiagBlocksLowerTriangular" | custom-call | tf_op jit(solution)/shard_map/triangular_solve/custom-call.0 | solution.py:298
  158.8 9.9 %all-gather.1 = f32[192,1024]{1,0:T(8,128)S(1)} all-gather(f32[24,1024]{1,0:T(8,128)S(1)} %get-tuple-element.36), channel_id=3, replica_groups=mesh['pix'=4,'mode'=8] {'mode'}, dimensions={0}, use_global_device_ids=true | all-gather | bytes 884736 | tf_op jit(solution)/shard_map/all_gather | solution.py:427
  170.1 9.4 %all-gather = f32[192,1024]{1,0:T(8,128)S(1)} all-gather(f32[24,1024]{1,0:T(8,128)S(1)} %get-tuple-element.35), channel_id=2, replica_groups=mesh['pix'=4,'mode'=8] {'mode'}, dimensions={0}, use_global_device_ids=true | all-gather | bytes 884736 | tf_op jit(solution)/shard_map/all_gather | solution.py:427
  179.6 9.8 %all-gather.2 = f32[128,1024]{1,0:T(8,128)S(1)} all-gather(f32[16,1024]{1,0:T(8,128)S(1)} %get-tuple-element.20), channel_id=4, replica_groups=mesh['pix'=4,'mode'=8] {'mode'}, dimensions={0}, use_global_device_ids=true | all-gather | bytes 589824 | tf_op jit(solution)/shard_map/all_gather | solution.py:427
  189.4 2.3 collective-permute-start.31
  192.5 46.1 %shard_map.73 = f32[64,8192]{1,0:T(8,128)} custom-call(s32[8192]{0:T(1024)S(1)} %copy-done.9, f32[8,64,1024]{2,1,0:T(8,128)S(1)} %pad_maximum_fusion.x_ref, f32[32,32]{1,0:T(8,128)S(1)} %fusion.27.inv_ref), custom_call_target="tpu_custom_call" | custom-call | tf_op jit(solution)/shard_map/pallas_call | solution.py:160
  (124 shorter events, 33.1 us)
Async XLA Ops:
  2.1 1.6 copy-start.7
  22.0 5.8 %copy-start = (f32[4,1024,1024]{2,1,0:T(8,128)S(1)}, f32[4,1024,1024]{2,1,0:T(8,128)}, u32[]{:S(2)}) copy-start(f32[4,1024,1024]{2,1,0:T(8,128)} %f3.1) | copy-start | bytes 50331652
  27.8 9.0 %copy-start.8 = (f32[2,32,8192]{2,1,0:T(8,128)S(1)}, f32[2,32,8192]{2,1,0:T(8,128)}, u32[]{:S(2)}) copy-start(f32[2,32,8192]{2,1,0:T(8,128)} %param.10) | copy-start | bytes 6291460
  32.3 1.9 copy-start.1
  34.3 2.0 copy-start.4
  36.3 6.2 %collective-permute-start = (f32[32,1024]{1,0:T(8,128)S(1)}, f32[32,1024]{1,0:T(8,128)S(1)}, u32[]{:S(2)}, u32[]{:S(2)}) collective-permute-start(f32[32,1024]{1,0:T(8,128)S(1)} %slice_select_fusion.4), channel_id=1, source_target_pairs={{0,1},{1,0},{2,3},{3,2},{4,5},{5,4},{6,7},{7,6},{8,9},{9,8},{10,11... | collective-permute-start | bytes 393224 | tf_op jit(solution)/shard_map/ppermute | solution.py:381
  42.5 7.2 %collective-permute-start.1 = (f32[32,1024]{1,0:T(8,128)S(1)}, f32[32,1024]{1,0:T(8,128)S(1)}, u32[]{:S(2)}, u32[]{:S(2)}) collective-permute-start(f32[32,1024]{1,0:T(8,128)S(1)} %select_add_fusion), channel_id=1, source_target_pairs={{0,2},{1,3},{2,0},{3,1},{4,6},{5,7},{6,4},{7,5},{8,10},{9,11},{10,... | collective-permute-start | bytes 393224 | tf_op jit(solution)/shard_map/ppermute | solution.py:340
  45.1 8.4 %collective-permute-start.2 = (f32[32,1024]{1,0:T(8,128)S(1)}, f32[32,1024]{1,0:T(8,128)S(1)}, u32[]{:S(2)}, u32[]{:S(2)}) collective-permute-start(f32[32,1024]{1,0:T(8,128)S(1)} %select_add_fusion), channel_id=1, source_target_pairs={{0,4},{1,5},{2,6},{3,7},{4,0},{5,1},{6,2},{7,3},{8,12},{9,13},{10,... | collective-permute-start | bytes 393224 | tf_op jit(solution)/shard_map/ppermute | solution.py:340
  46.6 6.9 %collective-permute-start.3 = (f32[32,1024]{1,0:T(8,128)S(1)}, f32[32,1024]{1,0:T(8,128)S(1)}, u32[]{:S(2)}, u32[]{:S(2)}) collective-permute-start(f32[32,1024]{1,0:T(8,128)S(1)} %select_add_fusion), channel_id=1, source_target_pairs={{0,6},{1,7},{2,4},{3,5},{4,2},{5,3},{6,0},{7,1},{8,14},{9,15},{10,... | collective-permute-start | bytes 393224 | tf_op jit(solution)/shard_map/ppermute | solution.py:340
  53.5 1.4 collective-permute-start.4
  55.0 2.2 copy-start.2
  57.2 2.2 copy-start.5
  62.6 4.5 %collective-permute-start.5 = (f32[16,1024]{1,0:T(8,128)S(1)}, f32[16,1024]{1,0:T(8,128)S(1)}, u32[]{:S(2)}, u32[]{:S(2)}) collective-permute-start(f32[16,1024]{1,0:T(8,128)S(1)} %get-tuple-element.30), channel_id=1, source_target_pairs={{0,8},{8,0},{16,24},{24,16},{1,9},{9,1},{17,25},{25,17},{2,10},{10... | collective-permute-start | bytes 196616 | tf_op jit(solution)/shard_map/ppermute | solution.py:325
  64.3 7.5 %collective-permute-start.6 = (f32[16,1024]{1,0:T(8,128)S(1)}, f32[16,1024]{1,0:T(8,128)S(1)}, u32[]{:S(2)}, u32[]{:S(2)}) collective-permute-start(f32[16,1024]{1,0:T(8,128)S(1)} %get-tuple-element.31), channel_id=1, source_target_pairs={{0,16},{8,24},{16,0},{24,8},{1,17},{9,25},{17,1},{25,9},{2,18},{10... | collective-permute-start | bytes 196616 | tf_op jit(solution)/shard_map/ppermute | solution.py:325
  66.9 6.2 %collective-permute-start.7 = (f32[16,1024]{1,0:T(8,128)S(1)}, f32[16,1024]{1,0:T(8,128)S(1)}, u32[]{:S(2)}, u32[]{:S(2)}) collective-permute-start(f32[16,1024]{1,0:T(8,128)S(1)} %get-tuple-element.32), channel_id=1, source_target_pairs={{0,24},{8,16},{16,8},{24,0},{1,25},{9,17},{17,9},{25,1},{2,26},{10... | collective-permute-start | bytes 196616 | tf_op jit(solution)/shard_map/ppermute | solution.py:325
  73.1 5.1 %collective-permute-start.10 = (f32[16,1024]{1,0:T(8,128)S(1)}, f32[16,1024]{1,0:T(8,128)S(1)}, u32[]{:S(2)}, u32[]{:S(2)}) collective-permute-start(f32[16,1024]{1,0:T(8,128)S(1)} %add_add_fusion.4), channel_id=1, source_target_pairs={{0,8},{8,0},{16,24},{24,16},{1,9},{9,1},{17,25},{25,17},{2,10},{10... | collective-permute-start | bytes 196616 | tf_op jit(solution)/shard_map/ppermute | solution.py:332
  74.0 6.2 %collective-permute-start.8 = (f32[16,1024]{1,0:T(8,128)S(1)}, f32[16,1024]{1,0:T(8,128)S(1)}, u32[]{:S(2)}, u32[]{:S(2)}) collective-permute-start(f32[16,1024]{1,0:T(8,128)S(1)} %add_add_fusion.4), channel_id=1, source_target_pairs={{0,24},{8,16},{16,8},{24,0},{1,25},{9,17},{17,9},{25,1},{2,26},{10... | collective-permute-start | bytes 196616 | tf_op jit(solution)/shard_map/ppermute | solution.py:332
  76.4 5.5 %collective-permute-start.9 = (f32[16,1024]{1,0:T(8,128)S(1)}, f32[16,1024]{1,0:T(8,128)S(1)}, u32[]{:S(2)}, u32[]{:S(2)}) collective-permute-start(f32[16,1024]{1,0:T(8,128)S(1)} %add_add_fusion.4), channel_id=1, source_target_pairs={{0,16},{8,24},{16,0},{24,8},{1,17},{9,25},{17,1},{25,9},{2,18},{10... | collective-permute-start | bytes 196616 | tf_op jit(solution)/shard_map/ppermute | solution.py:332
  86.3 1.5 collective-permute-start.11
  87.8 7.1 %collective-permute-start.12 = (f32[40,1024]{1,0:T(8,128)S(1)}, f32[40,1024]{1,0:T(8,128)S(1)}, u32[]{:S(2)}, u32[]{:S(2)}) collective-permute-start(f32[40,1024]{1,0:T(8,128)S(1)} %fusion.11), channel_id=1, source_target_pairs={{0,2},{1,3},{2,0},{3,1},{4,6},{5,7},{6,4},{7,5},{8,10},{9,11},{10,... | collective-permute-start | bytes 491528 | tf_op jit(solution)/shard_map/ppermute | solution.py:340
  89.1 7.8 %collective-permute-start.13 = (f32[40,1024]{1,0:T(8,128)S(1)}, f32[40,1024]{1,0:T(8,128)S(1)}, u32[]{:S(2)}, u32[]{:S(2)}) collective-permute-start(f32[40,1024]{1,0:T(8,128)S(1)} %fusion.11), channel_id=1, source_target_pairs={{0,4},{1,5},{2,6},{3,7},{4,0},{5,1},{6,2},{7,3},{8,12},{9,13},{10,... | collective-permute-start | bytes 491528 | tf_op jit(solution)/shard_map/ppermute | solution.py:340
  89.9 8.7 %collective-permute-start.14 = (f32[40,1024]{1,0:T(8,128)S(1)}, f32[40,1024]{1,0:T(8,128)S(1)}, u32[]{:S(2)}, u32[]{:S(2)}) collective-permute-start(f32[40,1024]{1,0:T(8,128)S(1)} %fusion.11), channel_id=1, source_target_pairs={{0,6},{1,7},{2,4},{3,5},{4,2},{5,3},{6,0},{7,1},{8,14},{9,15},{10,... | collective-permute-start | bytes 491528 | tf_op jit(solution)/shard_map/ppermute | solution.py:340
  98.7 7.2 %collective-permute-start.15 = (f32[32,1024]{1,0:T(8,128)S(1)}, f32[32,1024]{1,0:T(8,128)S(1)}, u32[]{:S(2)}, u32[]{:S(2)}) collective-permute-start(f32[32,1024]{1,0:T(8,128)S(1)} %slice.151), channel_id=1, source_target_pairs={{0,1},{1,0},{2,3},{3,2},{4,5},{5,4},{6,7},{7,6},{8,9},{9,8},{10,11... | collective-permute-start | bytes 393224 | tf_op jit(solution)/shard_map/ppermute | solution.py:384
  105.9 2.2 copy-start.3
  108.1 2.2 copy-start.6
  113.5 5.7 %collective-permute-start.16 = (f32[16,1024]{1,0:T(8,128)S(1)}, f32[16,1024]{1,0:T(8,128)S(1)}, u32[]{:S(2)}, u32[]{:S(2)}) collective-permute-start(f32[16,1024]{1,0:T(8,128)S(1)} %get-tuple-element.21), channel_id=1, source_target_pairs={{0,8},{8,0},{16,24},{24,16},{1,9},{9,1},{17,25},{25,17},{2,10},{10... | collective-permute-start | bytes 196616 | tf_op jit(solution)/shard_map/ppermute | solution.py:325
  113.6 7.2 %collective-permute-start.17 = (f32[16,1024]{1,0:T(8,128)S(1)}, f32[16,1024]{1,0:T(8,128)S(1)}, u32[]{:S(2)}, u32[]{:S(2)}) collective-permute-start(f32[16,1024]{1,0:T(8,128)S(1)} %get-tuple-element.22), channel_id=1, source_target_pairs={{0,16},{8,24},{16,0},{24,8},{1,17},{9,25},{17,1},{25,9},{2,18},{10... | collective-permute-start | bytes 196616 | tf_op jit(solution)/shard_map/ppermute | solution.py:325
  116.5 6.1 %collective-permute-start.18 = (f32[16,1024]{1,0:T(8,128)S(1)}, f32[16,1024]{1,0:T(8,128)S(1)}, u32[]{:S(2)}, u32[]{:S(2)}) collective-permute-start(f32[16,1024]{1,0:T(8,128)S(1)} %get-tuple-element.23), channel_id=1, source_target_pairs={{0,24},{8,16},{16,8},{24,0},{1,25},{9,17},{17,9},{25,1},{2,26},{10... | collective-permute-start | bytes 196616 | tf_op jit(solution)/shard_map/ppermute | solution.py:325
  122.6 6.9 %collective-permute-start.19 = (f32[16,1024]{1,0:T(8,128)S(1)}, f32[16,1024]{1,0:T(8,128)S(1)}, u32[]{:S(2)}, u32[]{:S(2)}) collective-permute-start(f32[16,1024]{1,0:T(8,128)S(1)} %add_add_fusion.3), channel_id=1, source_target_pairs={{0,24},{8,16},{16,8},{24,0},{1,25},{9,17},{17,9},{25,1},{2,26},{10... | collective-permute-start | bytes 196616 | tf_op jit(solution)/shard_map/ppermute | solution.py:332
  124.8 6.6 %collective-permute-start.20 = (f32[16,1024]{1,0:T(8,128)S(1)}, f32[16,1024]{1,0:T(8,128)S(1)}, u32[]{:S(2)}, u32[]{:S(2)}) collective-permute-start(f32[16,1024]{1,0:T(8,128)S(1)} %add_add_fusion.3), channel_id=1, source_target_pairs={{0,16},{8,24},{16,0},{24,8},{1,17},{9,25},{17,1},{25,9},{2,18},{10... | collective-permute-start | bytes 196616 | tf_op jit(solution)/shard_map/ppermute | solution.py:332
  125.5 6.0 %collective-permute-start.21 = (f32[16,1024]{1,0:T(8,128)S(1)}, f32[16,1024]{1,0:T(8,128)S(1)}, u32[]{:S(2)}, u32[]{:S(2)}) collective-permute-start(f32[16,1024]{1,0:T(8,128)S(1)} %add_add_fusion.3), channel_id=1, source_target_pairs={{0,8},{8,0},{16,24},{24,16},{1,9},{9,1},{17,25},{25,17},{2,10},{10... | collective-permute-start | bytes 196616 | tf_op jit(solution)/shard_map/ppermute | solution.py:332
  135.9 1.5 collective-permute-start.22
  137.4 7.1 %collective-permute-start.23 = (f32[40,1024]{1,0:T(8,128)S(1)}, f32[40,1024]{1,0:T(8,128)S(1)}, u32[]{:S(2)}, u32[]{:S(2)}) collective-permute-start(f32[40,1024]{1,0:T(8,128)S(1)} %fusion.7), channel_id=1, source_target_pairs={{0,2},{1,3},{2,0},{3,1},{4,6},{5,7},{6,4},{7,5},{8,10},{9,11},{10,... | collective-permute-start | bytes 491528 | tf_op jit(solution)/shard_map/ppermute | solution.py:340
  138.3 9.5 %collective-permute-start.24 = (f32[40,1024]{1,0:T(8,128)S(1)}, f32[40,1024]{1,0:T(8,128)S(1)}, u32[]{:S(2)}, u32[]{:S(2)}) collective-permute-start(f32[40,1024]{1,0:T(8,128)S(1)} %fusion.7), channel_id=1, source_target_pairs={{0,4},{1,5},{2,6},{3,7},{4,0},{5,1},{6,2},{7,3},{8,12},{9,13},{10,... | collective-permute-start | bytes 491528 | tf_op jit(solution)/shard_map/ppermute | solution.py:340
  139.8 8.0 %collective-permute-start.25 = (f32[40,1024]{1,0:T(8,128)S(1)}, f32[40,1024]{1,0:T(8,128)S(1)}, u32[]{:S(2)}, u32[]{:S(2)}) collective-permute-start(f32[40,1024]{1,0:T(8,128)S(1)} %fusion.7), channel_id=1, source_target_pairs={{0,6},{1,7},{2,4},{3,5},{4,2},{5,3},{6,0},{7,1},{8,14},{9,15},{10,... | collective-permute-start | bytes 491528 | tf_op jit(solution)/shard_map/ppermute | solution.py:340
  147.9 7.2 %collective-permute-start.26 = (f32[32,1024]{1,0:T(8,128)S(1)}, f32[32,1024]{1,0:T(8,128)S(1)}, u32[]{:S(2)}, u32[]{:S(2)}) collective-permute-start(f32[32,1024]{1,0:T(8,128)S(1)} %slice.159), channel_id=1, source_target_pairs={{0,1},{1,0},{2,3},{3,2},{4,5},{5,4},{6,7},{7,6},{8,9},{9,8},{10,11... | collective-permute-start | bytes 393224 | tf_op jit(solution)/shard_map/ppermute | solution.py:384
  156.2 1.3 collective-permute-start.27
  157.5 11.1 %collective-permute-start.28 = (f32[8,32]{1,0:T(8,128)S(1)}, f32[8,32]{1,0:T(8,128)S(1)}, u32[]{:S(2)}, u32[]{:S(2)}) collective-permute-start(f32[8,32]{1,0:T(8,128)S(1)} %broadcast_add_fusion), channel_id=1, source_target_pairs={{0,2},{1,3},{2,0},{3,1},{4,6},{5,7},{6,4},{7,5},{8,10},{9,11},{10,... | collective-permute-start | bytes 3080 | tf_op jit(solution)/shard_map/ppermute | solution.py:348
  168.6 10.9 %collective-permute-start.29 = (f32[8,32]{1,0:T(8,128)S(1)}, f32[8,32]{1,0:T(8,128)S(1)}, u32[]{:S(2)}, u32[]{:S(2)}) collective-permute-start(f32[8,32]{1,0:T(8,128)S(1)} %fusion.54), channel_id=1, source_target_pairs={{0,4},{1,5},{2,6},{3,7},{4,0},{5,1},{6,2},{7,3},{8,12},{9,13},{10,... | collective-permute-start | bytes 3080 | tf_op jit(solution)/shard_map/ppermute | solution.py:348
  179.5 9.8 %collective-permute-start.30 = (f32[8,32]{1,0:T(8,128)S(1)}, f32[8,32]{1,0:T(8,128)S(1)}, u32[]{:S(2)}, u32[]{:S(2)}) collective-permute-start(f32[8,32]{1,0:T(8,128)S(1)} %add.140), channel_id=1, source_target_pairs={{0,8},{8,0},{16,24},{24,16},{1,9},{9,1},{17,25},{25,17},{2,10},{10... | collective-permute-start | bytes 3080 | tf_op jit(solution)/shard_map/ppermute | solution.py:348
  189.4 49.2 %collective-permute-start.31 = (f32[8,32]{1,0:T(8,128)S(1)}, f32[8,32]{1,0:T(8,128)S(1)}, u32[]{:S(2)}, u32[]{:S(2)}) collective-permute-start(f32[8,32]{1,0:T(8,128)S(1)} %add.141), channel_id=1, source_target_pairs={{0,16},{8,24},{16,0},{24,8},{1,17},{9,25},{17,1},{25,9},{2,18},{10... | collective-permute-start | bytes 3080 | tf_op jit(solution)/shard_map/ppermute | solution.py:348
  191.7 0.8 copy-start.9

commit v2 on v1

v2 whole, which is shorter than its diff:
```python
import functools
import math

import jax
import jax.numpy as jnp
from jax import lax
from jax.experimental import pallas as pl
from jax.experimental.pallas import tpu as pltpu
from jax.sharding import PartitionSpec as P

HB = 128
ITERS = 2
BLOCK = 256
F32 = jnp.float32
BF16 = jnp.bfloat16

precise = lax.Precision.HIGHEST
NT = (((1,), (1,)), ((), ()))
NN = (((1,), (0,)), ((), ()))
VMEM = pl.BlockSpec(memory_space=pltpu.VMEM)
SMEM = pl.BlockSpec(memory_space=pltpu.SMEM)


def dot(a, b, dims):
    return lax.dot_general(a, b, dims, preferred_element_type=F32)


def exact(a, b, dims):
    return lax.dot_general(a, b, dims, precision=precise, preferred_element_type=F32)


def split(values):
    high = values.astype(BF16)
    return high, (values - high.astype(F32)).astype(BF16)


def sign_table(order):
    row = lax.broadcasted_iota(jnp.int32, (order, order), 0)
    common = row & lax.broadcasted_iota(jnp.int32, (order, order), 1)
    parity = common
    shift = 16
    while shift:
        parity = parity ^ (parity >> shift)
        shift //= 2
    return (1 - 2 * (parity & 1)).astype(F32)


def butterfly(ref, count):
    rows = ref.shape[0]
    step = 1
    while step < count:
        radix = min(8, count // step)

        def body(g, carry, step=step, radix=radix):
            base = (g // step) * (step * radix) + g % step
            for s in range(rows // 8):
                at = [pl.multiple_of((base + r * step) * HB, HB) for r in range(radix)]
                v = [ref[s * 8 : s * 8 + 8, pl.ds(a, HB)] for a in at]
                half = 1
                while half < radix:
                    v = [
                        v[r] + v[r + half] if not r & half else v[r - half] - v[r]
                        for r in range(radix)
                    ]
                    half *= 2
                for a, x in zip(at, v):
                    ref[s * 8 : s * 8 + 8, pl.ds(a, HB)] = x
            return carry

        lax.fori_loop(0, count // radix, body, 0)
        step *= radix


def block_loop(count, unroll, body):
    unroll = math.gcd(count, unroll)

    def many(i, carry):
        for q in range(unroll):
            body(i * unroll + q)
        return carry

    lax.fori_loop(0, count // unroll, many, 0)


def start_kernel(
    scale, idx_ref, at_ref, probes_ref, frames_ref, dh_ref, dl_ref, img_ref,
    f_ref, w_ref, n_ref, g_ref, b_ref, t_ref, sems,
):
    vectors, modes = probes_ref.shape
    rows, count = frames_ref.shape[1:]
    outer = modes // HB
    block = min(BLOCK, rows)
    copies = [
        [
            pltpu.make_async_copy(
                frames_ref.at[s, pl.ds(i * block, block)],
                f_ref.at[s, pl.ds(i * block, block)],
                sems.at[s, i],
            )
            for s in range(frames_ref.shape[0])
        ]
        for i in range(rows // block)
    ]
    for row in copies:
        for c in row:
            c.start()
    signs = sign_table(HB).astype(BF16)

    def inner(i):
        at = pl.multiple_of(i * HB, HB)
        both = dot(jnp.concatenate(split(probes_ref[:, pl.ds(at, HB)]), axis=0), signs, NN)
        w_ref[:, pl.ds(at, HB)] = both[:vectors] + both[vectors:]

    block_loop(outer, 8, inner)
    butterfly(w_ref, outer)

    def turn(i):
        at = pl.multiple_of(i * HB, HB)
        here = w_ref[:, pl.ds(at, HB)]
        n_ref[pl.ds(at, HB), :] = jnp.concatenate([here, here], axis=0).T

    block_loop(outer, 8, turn)

    def gather(t, carry):
        at = pl.multiple_of(t * 8, 8)
        for q in range(8):
            g_ref[pl.ds(at + q, 1), :] = n_ref[pl.ds(idx_ref[at + q], 1), :]
        return carry

    lax.fori_loop(0, count // 8, gather, 0)
    parts = [g_ref[b * HB : (b + 1) * HB, :].T[:vectors] for b in range(count // HB)]
    b_ref[...], t_ref[...] = stack_forward(jnp.concatenate(parts, axis=1) * scale)
    for i, row in enumerate(copies):
        for c in row:
            c.wait()
        span = slice(i * block, (i + 1) * block)
        for part in (0, 1):
            high, low = split(0.25 * (f_ref[at_ref[part], span] - f_ref[at_ref[part + 2], span]))
            dh_ref[part, span] = high
            dl_ref[part, span] = low
        img_ref[:, span] = apply_forward(b_ref[...], t_ref[...], dh_ref, dl_ref, span)


def start(idx, steps_at, probes, frames, scale):
    vectors, modes = probes.shape
    steps, rows, count = frames.shape
    planes = jax.ShapeDtypeStruct((2, rows, count), BF16)
    return pl.pallas_call(
        functools.partial(start_kernel, scale),
        out_shape=[planes, planes, jax.ShapeDtypeStruct((vectors, rows), F32)],
        in_specs=[SMEM, SMEM, VMEM, pl.BlockSpec(memory_space=pltpu.HBM)],
        out_specs=[VMEM, VMEM, VMEM],
        scratch_shapes=[
            pltpu.VMEM((steps, rows, count), F32),
            pltpu.VMEM((vectors, modes), F32),
            pltpu.VMEM((modes, HB), F32),
            pltpu.VMEM((count, HB), F32),
            pltpu.VMEM((2 * vectors, count), BF16),
            pltpu.VMEM((2 * vectors, count), BF16),
            pltpu.SemaphoreType.DMA((steps, rows // min(BLOCK, rows))),
        ],
        compiler_params=pltpu.CompilerParams(vmem_limit_bytes=44 << 20),
    )(idx, steps_at, probes, frames)


def scatter_kernel(base_ref, idx_ref, *refs):
    s_ref, w_ref = refs[-1], refs[-2]
    pieces = [r for r in refs[:-2] if len(r.shape) == 2 and r.shape[1] == s_ref.shape[0]]
    count = s_ref.shape[0]
    for p, x_ref in enumerate(pieces):
        for i in range(count // HB):
            high, low = split(x_ref[:, i * HB : (i + 1) * HB])
            both = jnp.concatenate([high.astype(F32), low.astype(F32)], axis=0)
            s_ref[i * HB : (i + 1) * HB, :] = both.T
        base = base_ref[p]

        def move(t, carry, base=base):
            at = pl.multiple_of(t * 16, 16)
            for q in range(16):
                w_ref[pl.ds(idx_ref[base + at + q], 1), :] = s_ref[pl.ds(at + q, 1), :]
            return carry

        lax.fori_loop(0, count // 16, move, 0)


def scatter_rows(bases, idx, pieces, table=None):
    count = pieces[0].shape[1]
    args = [bases, idx, *pieces] + ([] if table is None else [table])
    return pl.pallas_call(
        scatter_kernel,
        out_shape=jax.ShapeDtypeStruct((idx.shape[0], HB), F32),
        in_specs=[SMEM, SMEM] + [VMEM] * (len(args) - 2),
        out_specs=VMEM,
        scratch_shapes=[pltpu.VMEM((count, HB), F32)],
        input_output_aliases={} if table is None else {len(args) - 1: 0},
        compiler_params=pltpu.CompilerParams(vmem_limit_bytes=8 << 20),
    )(*args)


def end_kernel(inv_ref, w_ref, out_ref):
    vectors, modes = out_ref.shape
    half = vectors // 2
    outer = modes // HB
    signs = sign_table(HB).astype(BF16)
    zero = jnp.zeros((half, half), F32)
    wide = jnp.concatenate(
        [jnp.concatenate([inv_ref[...], zero], 1), jnp.concatenate([zero, inv_ref[...]], 1)], 0
    )
    high, low = split(wide)
    mix = jnp.concatenate(
        [jnp.concatenate([high, high], 1), jnp.concatenate([low, jnp.zeros_like(low)], 1)], 0
    )

    def first(i):
        at = pl.multiple_of(i * HB, HB)
        both = dot(mix, w_ref[pl.ds(at, HB), :].astype(BF16), NT)
        out_ref[:, pl.ds(at, HB)] = both[:vectors] + both[vectors:]

    block_loop(outer, 8, first)
    butterfly(out_ref, outer)

    def inner(i):
        at = pl.multiple_of(i * HB, HB)
        both = dot(jnp.concatenate(split(out_ref[:, pl.ds(at, HB)]), axis=0), signs, NN)
        out_ref[:, pl.ds(at, HB)] = both[:vectors] + both[vectors:]

    block_loop(outer, 8, inner)


def end_vectors(inv, table, vectors):
    return pl.pallas_call(
        end_kernel,
        out_shape=jax.ShapeDtypeStruct((vectors, table.shape[0]), F32),
        in_specs=[VMEM, VMEM],
        out_specs=VMEM,
        compiler_params=pltpu.CompilerParams(vmem_limit_bytes=12 << 20),
    )(inv, table)


def factor_kernel(g_ref, out_ref):
    n = g_ref.shape[0]
    row = lax.broadcasted_iota(jnp.int32, (n, n), 0)
    eye = (row == lax.broadcasted_iota(jnp.int32, (n, n), 1)).astype(F32)
    both = jnp.concatenate([g_ref[...], eye], axis=1)
    below = lax.broadcasted_iota(jnp.int32, (n, 1), 0)
    for k in range(n - 1):
        scaled = both[k : k + 1] * (1.0 / both[k : k + 1, k : k + 1])
        both = both - jnp.where(below > k, both[:, k : k + 1], 0.0) * scaled
    pivots = jnp.sum(both[:, :n] * eye, axis=1, keepdims=True)
    out_ref[...] = both[:, n:] * (1.0 / jnp.sqrt(pivots))


def inverse_factor(gram_matrix):
    return pl.pallas_call(
        factor_kernel,
        out_shape=jax.ShapeDtypeStruct(gram_matrix.shape, F32),
        in_specs=[VMEM],
        out_specs=VMEM,
        compiler_params=pltpu.CompilerParams(vmem_limit_bytes=2 << 20),
    )(gram_matrix)


def stack_forward(u):
    half = u.shape[0] // 2
    turned = jnp.concatenate([-u[half:], u[:half]], axis=0)
    uh, ul = split(u)
    th, tl = split(turned)
    return jnp.concatenate([uh, ul], axis=0), jnp.concatenate([th, tl], axis=0)


def apply_forward(both, turned, dh, dl, span):
    n = both.shape[0] // 2
    wide = dot(both, dh[0, span], NT) + dot(turned, dh[1, span], NT)
    low = dot(both[:n], dl[0, span], NT) + dot(turned[:n], dl[1, span], NT)
    return wide[:n] + wide[n:] + low


def forward_kernel(u_ref, dh_ref, dl_ref, img_ref):
    both, turned = stack_forward(u_ref[...])
    rows = dh_ref.shape[1]
    block = min(BLOCK, rows)
    width = img_ref.shape[-1]
    for i in range(rows // block):
        part = apply_forward(both, turned, dh_ref, dl_ref, slice(i * block, (i + 1) * block))
        if len(img_ref.shape) == 2:
            img_ref[:, i * block : (i + 1) * block] = part
        else:
            for j in range(block // width):
                img_ref[i * block // width + j] = part[:, j * width : (j + 1) * width]


def forward(u, dh, dl, places=None):
    rows = dh.shape[1]
    vectors = u.shape[0]
    shape = (vectors, rows) if places is None else (places, vectors, rows // places)
    return pl.pallas_call(
        forward_kernel,
        out_shape=jax.ShapeDtypeStruct(shape, F32),
        in_specs=[VMEM, VMEM, VMEM],
        out_specs=VMEM,
        compiler_params=pltpu.CompilerParams(vmem_limit_bytes=12 << 20),
    )(u, dh, dl)


def backward_kernel(*refs):
    inv_ref = refs[0] if len(refs) == 5 else None
    img_ref, dh_ref, dl_ref, ret_ref = refs[-4:]
    vectors, rows = img_ref.shape
    half = vectors // 2
    real, imag = img_ref[:half], img_ref[half:]
    if inv_ref is not None:
        real = exact(inv_ref[...], real, NN)
        imag = exact(inv_ref[...], imag, NN)
    stacks = []
    for pair in ([real, imag], [imag, -real]):
        high, low = split(jnp.concatenate(pair, axis=0))
        stacks.append((high, jnp.concatenate([high, low], axis=0)))
    cols = dh_ref.shape[2]
    block = min(BLOCK, cols)
    for i in range(cols // block):
        span = slice(i * block, (i + 1) * block)
        wide = dot(stacks[0][1], dh_ref[0, :, span], NN) + dot(stacks[1][1], dh_ref[1, :, span], NN)
        low = dot(stacks[0][0], dl_ref[0, :, span], NN) + dot(stacks[1][0], dl_ref[1, :, span], NN)
        ret_ref[:, span] = wide[:vectors] + wide[vectors:] + low


def backward(inv, images, dh, dl):
    args = ([] if inv is None else [inv]) + [images, dh, dl]
    return pl.pallas_call(
        backward_kernel,
        out_shape=jax.ShapeDtypeStruct((images.shape[0], dh.shape[2]), F32),
        in_specs=[VMEM] * len(args),
        out_specs=VMEM,
        compiler_params=pltpu.CompilerParams(vmem_limit_bytes=12 << 20),
    )(*args)


def gram(vectors):
    half = vectors.shape[0] // 2
    return exact(vectors[:half], vectors[:half], NT) + exact(vectors[half:], vectors[half:], NT)


def normalise(inv, vectors):
    half = inv.shape[0]
    return jnp.concatenate([exact(inv, vectors[:half], NN), exact(inv, vectors[half:], NN)], axis=0)


def flip(n, bit):
    return [(i, i ^ bit) for i in range(n)]


def pick(pieces, here, n):
    bit = 1
    while bit < n:
        odd = (here & bit) != 0
        pieces = [jnp.where(odd, pieces[b ^ bit], pieces[b]) for b in range(n)]
        bit *= 2
    return pieces


def scatter_sum(blocks, axis, step, n):
    size = lax.axis_size(axis)
    here = (lax.axis_index(axis) // step) % n
    mine = pick(blocks, here, n)
    total = mine[0]
    for b in range(1, n):
        total = total + lax.ppermute(mine[b], axis, flip(size, b * step))
    return total


def gather_all(block, axis, step, n):
    size = lax.axis_size(axis)
    here = (lax.axis_index(axis) // step) % n
    pieces = [block] + [lax.ppermute(block, axis, flip(size, b * step)) for b in range(1, n)]
    return pick(pieces, here, n)


def share_sum(block, axis, step, n):
    size = lax.axis_size(axis)
    total = block
    for b in range(1, n):
        total = total + lax.ppermute(block, axis, flip(size, b * step))
    return total


def double_sum(block, axis):
    size = lax.axis_size(axis)
    bit = 1
    while bit < size:
        block = block + lax.ppermute(block, axis, flip(size, bit))
        bit *= 2
    return block


def sum_pix(x):
    n = lax.axis_size("pix")
    if n != 4:
        return double_sum(x, "pix")
    rows = x.shape[0] // n
    mine = scatter_sum([x[i * rows : (i + 1) * rows] for i in range(n)], "pix", 1, n)
    return jnp.concatenate(gather_all(mine, "pix", 1, n), axis=0)


def pack(gram_matrix, width):
    return jnp.pad(gram_matrix.reshape(1, -1), ((0, 7), (0, width - gram_matrix.size)))


def sum_mode(x, extra=None):
    n = lax.axis_size("mode")
    rows, cols = x.shape
    if n != 8:
        total = double_sum(x, "mode")
        return total, (None if extra is None else double_sum(extra, "mode"))
    half = rows // 2
    odd = (lax.axis_index("mode") % 2) != 0
    mine = jnp.where(odd, x[half:], x[:half])
    other = jnp.where(odd, x[:half], x[half:])
    if extra is not None:
        k = extra.shape[0]
        row = pack(extra, cols)
        mine = jnp.concatenate([mine, row], axis=0)
        other = jnp.concatenate([other, row], axis=0)
    chip = mine + lax.ppermute(other, "mode", flip(n, 1))
    chip = share_sum(chip, "mode", 2, 4)
    mine = chip[:half]
    other = lax.ppermute(mine, "mode", flip(n, 1))
    total = jnp.concatenate([jnp.where(odd, other, mine), jnp.where(odd, mine, other)], axis=0)
    if extra is None:
        return total, None
    return total, chip[half, : k * k].reshape(k, k)


def scatter_mode(pieces, extra):
    places, rows, width = pieces.shape
    k = extra.shape[0]
    n = lax.axis_size("mode")
    here = lax.axis_index("mode")
    if n != 8:
        total = double_sum(pieces, "mode")
        return lax.dynamic_index_in_dim(total, here, 0, False), double_sum(extra, "mode")
    chips = pieces.reshape(4, 2, rows, width)
    odd = (here % 2) != 0
    mine = jnp.where(odd, chips[:, 1], chips[:, 0]).reshape(4 * rows, width)
    other = jnp.where(odd, chips[:, 0], chips[:, 1]).reshape(4 * rows, width)
    small = extra.reshape(k * k // width, width)
    got = lax.ppermute(jnp.concatenate([other, small], axis=0), "mode", flip(n, 1))
    mine = mine + got[: 4 * rows]
    small = small + got[4 * rows :]
    blocks = [
        jnp.concatenate([mine[i * rows : (i + 1) * rows], small], axis=0) for i in range(4)
    ]
    total = scatter_sum(blocks, "mode", 2, 4)
    return total[:rows], total[rows:].reshape(k, k)


def gather_rows(block, idx):
    n = lax.axis_size("mode")
    here = lax.axis_index("mode")
    count = block.shape[1]

    def bases(bits):
        return jnp.stack([(here ^ b) * count for b in bits]).astype(jnp.int32)

    if n != 8:
        pieces = [block]
        bit = 1
        while bit < n:
            pieces = pieces + [lax.ppermute(p, "mode", flip(n, bit)) for p in pieces]
            bit *= 2
        return scatter_rows(bases(range(n)), idx, pieces)
    far = {b: lax.ppermute(block, "mode", flip(n, b)) for b in (2, 4, 6)}
    near = lax.ppermute(block, "mode", flip(n, 1))
    table = scatter_rows(bases((0, 1)), idx, [block, near])
    for b in (2, 4, 6):
        other = lax.ppermute(far[b], "mode", flip(n, 1))
        table = scatter_rows(bases((b, b ^ 1)), idx, [far[b], other], table)
    return table


def local(frames, phase_steps, pattern_rows, probes):
    columns = frames.shape[2]
    rows = frames.shape[1]
    groups = lax.axis_size("mode")
    pixels = rows * lax.axis_size("pix")
    modes_total = columns * groups
    k = probes.shape[1]
    vectors = 2 * k
    probes = probes.reshape(vectors, modes_total)
    here = lax.axis_index("mode")
    steps_at = jnp.sum(
        jnp.where(phase_steps[None, :] == jnp.arange(4)[:, None], jnp.arange(4)[None, :], 0), axis=1
    ).astype(jnp.int32)
    my_rows = lax.dynamic_slice_in_dim(pattern_rows, here * columns, columns)
    dh, dl, images = start(my_rows, steps_at, probes, frames, 1.0 / math.sqrt(modes_total))
    inv = inverse_factor(gram(probes))
    images, _ = sum_mode(images)
    returned = sum_pix(backward(inv, images, dh, dl))
    for iteration in range(1, ITERS):
        images, gram_matrix = sum_mode(forward(returned, dh, dl), gram(returned))
        inv = inverse_factor(gram_matrix)
        returned = normalise(inv, sum_pix(backward(None, images, dh, dl)))
    table = gather_rows(returned, pattern_rows)
    fields, gram_matrix = scatter_mode(forward(returned, dh, dl, groups), gram(returned))
    inv = inverse_factor(gram_matrix)
    fields = normalise(inv, fields)
    power = jnp.sum(fields * fields, axis=1)
    power = jnp.broadcast_to((power[:k] + power[k:])[None, :], (8, k))
    power = double_sum(double_sum(power, "mode"), "pix")
    strengths = power[0] / pixels
    channels = end_vectors(inv, table, vectors)
    return (channels.reshape(2, k, modes_total), fields.reshape(2, k, -1), strengths)


def solution(mesh):
    in_specs = (P(None, "pix", "mode"), P(), P(), P())
    out_specs = (P(), P(None, None, ("pix", "mode")), P())
    return jax.shard_map(local, mesh=mesh, in_specs=in_specs, out_specs=out_specs, check_vma=False)
```

time: 240 us -> 179 us (0.75)
  blocking collectives: 29.1 us -> 0 us
  Pallas kernels: 82.8 us -> 59.3 us
  other arithmetic: 22.9 us -> 2.96 us
  waiting for transfers between devices: 42.7 us -> 56.9 us
  local copies, waits for them, and re-layouts: 21.9 us -> 17.8 us
    all_gather x3 -> x0, blocking collectives: 29.1 us -> none  [local(): lax.all_gather(returned[a:b], 'mode', tiled=False)]
    pallas_call x7 -> x13, Pallas kernels: 82.8 us -> 59.3 us  [the longest x1 14.2 us: start(): pl.pallas_call(functools.partial(start_kernel, scale), out_shape=[planes,...]
    another operation x15 -> x4, other arithmetic: 20 us -> 0.3 us  [bases(): return jnp.stack([(here ^ b) * count for b in bits]).astype(jnp.int32)]
    ppermute x5, waiting for transfers between devices: 0.82 us -> 17.7 us  [double_sum(): block = block + lax.ppermute(block, axis, flip(size, bit))]
    ppermute x9 -> x6, waiting for transfers between devices: 17.8 us -> 12.8 us  [share_sum(): total = total + lax.ppermute(block, axis, flip(size, b * step))]
    ppermute x0 -> x8, starting transfers between devices: none -> 4.14 us  [the longest x3 3.49 us: gather_rows(): far = {b: lax.ppermute(block, 'mode', flip(n, b)) for b in (2, 4, 6)}]
    unnamed x20 -> x24, local copies, waits for them, and re-layouts: 20.6 us -> 16.7 us
    ppermute x6 -> x9, starting transfers between devices: 8.9 us -> 12.5 us  [scatter_sum(): total = total + lax.ppermute(mine[b], axis, flip(size, b * step))]
  transfers between devices with their start and end apart: 32 -> 38, of which waited for: 20 -> 26; matrix products, arithmetic and copies ran while one was open for 10% -> 2% of each run, Pallas kernels for 19% -> 9%
where the time goes in v2:
time: 179 us; the launch traced here: 178 us
  Pallas kernels  59.3 us (33%)
  waiting for transfers between devices  56.9 us (32%)
  starting transfers between devices  36.4 us (20%)
  local copies, waits for them, and re-layouts  17.8 us (10%)
  matrix products  3.74 us (2%)
  other arithmetic  2.96 us (2%)
    ppermute x5, waiting for transfers between devices, double_sum(): block = block + lax.ppermute(block, axis, flip(size, bit))  17.7 us
    unnamed x24, local copies, waits for them, and re-layouts  16.7 us
    pallas_call x1, Pallas kernels, start(): pl.pallas_call(functools.partial(start_kernel, scale), out_shape=[planes,...  14.2 us
    pallas_call x4, Pallas kernels, scatter_rows(): pl.pallas_call(scatter_kernel, out_shape=jax.ShapeDtypeStruct((idx.shape[...  14.1 us
    ppermute x9, waiting for transfers between devices, scatter_sum(): total = total + lax.ppermute(mine[b], axis, flip(size, b * step))  14 us
    pallas_call x1, Pallas kernels, end_vectors(): pl.pallas_call(end_kernel, out_shape=jax.ShapeDtypeStruct((vectors, table...  14 us
    ppermute x6, waiting for transfers between devices, share_sum(): total = total + lax.ppermute(block, axis, flip(size, b * step))  12.8 us
    ppermute x9, starting transfers between devices, scatter_sum(): total = total + lax.ppermute(mine[b], axis, flip(size, b * step))  12.5 us
  transfers between devices with their start and end apart: 38, of which 26 were waited for; matrix products, arithmetic and copies ran while one was open for 2% of the time, Pallas kernels for 9%

profile of v2, /device:TPU:0, one launch (start us, length us, event | category | flops | bytes accessed | tf_op | source)
XLA Modules:
  0.0 178.2 jit_solution(2856512407846477550)
XLA Ops:
  2.1 1.6 copy-done.9
  3.7 14.2 %shard_map.68 = (bf16[2,1024,1024]{2,1,0:T(8,128)(2,1)S(1)}, bf16[2,1024,1024]{2,1,0:T(8,128)(2,1)}, f32[64,1024]{1,0:T(8,128)S(1)}) custom-call(s32[1024]{0:T(1024)S(1)} %dynamic_slice.3.idx_ref, s32[4]{0:T(128)S(1)} %select_reduce_fusion.at_ref, f32[64,8192]{1,0:T(8,128)S(1)} %bitcast.31, f32[4,1024,1024]{2,1,0:T(8,128)} %frames_ref.1), custom_call_target="tpu_custom_call" | custom-call | tf_op jit(solution)/shard_map/pallas_call | solution.py:148
  17.9 2.0 %copy-done = bf16[2,1024,1024]{2,1,0:T(8,128)(2,1)} copy-done((bf16[2,1024,1024]{2,1,0:T(8,128)(2,1)}, bf16[2,1024,1024]{2,1,0:T(8,128)(2,1)S(1)}, u32[]{:S(2)}) %copy-start) | copy-done | bytes 4194328
  21.5 2.9 %collective-permute-start.1 = (f32[32,1024]{1,0:T(8,128)S(1)}, f32[32,1024]{1,0:T(8,128)S(1)}, u32[]{:S(2)}, u32[]{:S(2)}) collective-permute-start(f32[32,1024]{1,0:T(8,128)S(1)} %select_add_fusion), channel_id=1, source_target_pairs={{0,2},{1,3},{2,0},{3,1},{4,6},{5,7},{6,4},{7,5},{8,10},{9,11},{10,... | collective-permute-start | bytes 393224 | tf_op jit(solution)/shard_map/ppermute | solution.py:382
  24.4 1.5 collective-permute-start.2
  26.9 1.5 collective-permute-done.1
  28.4 4.1 %collective-permute-done.2 = f32[32,1024]{1,0:T(8,128)S(1)} collective-permute-done((f32[32,1024]{1,0:T(8,128)S(1)}, f32[32,1024]{1,0:T(8,128)S(1)}, u32[]{:S(2)}, u32[]{:S(2)}) %collective-permute-start.2) | collective-permute-done | bytes 131104 | tf_op jit(solution)/shard_map/ppermute | solution.py:382
  33.6 2.8 %shard_map.67.refs_0_ = f32[32,32]{1,0:T(8,128)S(1)} custom-call(f32[32,32]{1,0:T(8,128)S(1)} %convolution_add_fusion.2.g_ref), custom_call_target="tpu_custom_call" | custom-call | tf_op jit(solution)/shard_map/pallas_call | solution.py:254
  36.4 2.2 %copy-done.1 = bf16[2,1024,1024]{2,1,0:T(8,128)(2,1)S(1)} copy-done((bf16[2,1024,1024]{2,1,0:T(8,128)(2,1)S(1)}, bf16[2,1024,1024]{2,1,0:T(8,128)(2,1)}, u32[]{:S(2)}) %copy-start.1) | copy-done | bytes 4194328
  38.6 2.2 %copy-done.5 = bf16[2,1024,1024]{2,1,0:T(8,128)(2,1)S(1)} copy-done((bf16[2,1024,1024]{2,1,0:T(8,128)(2,1)S(1)}, bf16[2,1024,1024]{2,1,0:T(8,128)(2,1)}, u32[]{:S(2)}) %copy-start.5) | copy-done | bytes 4194328
  40.8 1.7 shard_map.69
  42.5 1.6 collective-permute-start.5
  44.2 2.6 %collective-permute-start.6 = (f32[16,1024]{1,0:T(8,128)S(1)}, f32[16,1024]{1,0:T(8,128)S(1)}, u32[]{:S(2)}, u32[]{:S(2)}) collective-permute-start(f32[16,1024]{1,0:T(8,128)S(1)} %get-tuple-element.27), channel_id=1, source_target_pairs={{0,16},{8,24},{16,0},{24,8},{1,17},{9,25},{17,1},{25,9},{2,18},{10... | collective-permute-start | bytes 196616 | tf_op jit(solution)/shard_map/ppermute | solution.py:367
  47.1 4.1 %collective-permute-done.6 = f32[16,1024]{1,0:T(8,128)S(1)} collective-permute-done((f32[16,1024]{1,0:T(8,128)S(1)}, f32[16,1024]{1,0:T(8,128)S(1)}, u32[]{:S(2)}, u32[]{:S(2)}) %collective-permute-start.6) | collective-permute-done | bytes 65568 | tf_op jit(solution)/shard_map/ppermute | solution.py:367
  51.2 1.6 collective-permute-done.7
  54.2 2.4 %collective-permute-start.8 = (f32[16,1024]{1,0:T(8,128)S(1)}, f32[16,1024]{1,0:T(8,128)S(1)}, u32[]{:S(2)}, u32[]{:S(2)}) collective-permute-start(f32[16,1024]{1,0:T(8,128)S(1)} %add_add_fusion.3), channel_id=1, source_target_pairs={{0,24},{8,16},{16,8},{24,0},{1,25},{9,17},{17,9},{25,1},{2,26},{10... | collective-permute-start | bytes 196616 | tf_op jit(solution)/shard_map/ppermute | solution.py:374
  57.2 3.6 %collective-permute-done.8 = f32[16,1024]{1,0:T(8,128)S(1)} collective-permute-done((f32[16,1024]{1,0:T(8,128)S(1)}, f32[16,1024]{1,0:T(8,128)S(1)}, u32[]{:S(2)}, u32[]{:S(2)}) %collective-permute-start.8) | collective-permute-done | bytes 65568 | tf_op jit(solution)/shard_map/ppermute | solution.py:374
  60.8 2.1 %collective-permute-done.9 = f32[16,1024]{1,0:T(8,128)S(1)} collective-permute-done((f32[16,1024]{1,0:T(8,128)S(1)}, f32[16,1024]{1,0:T(8,128)S(1)}, u32[]{:S(2)}, u32[]{:S(2)}) %collective-permute-start.9) | collective-permute-done | bytes 65568 | tf_op jit(solution)/shard_map/ppermute | solution.py:374
  63.2 2.7 %shard_map.70 = f32[64,1024]{1,0:T(8,128)S(1)} custom-call(f32[64,1024]{1,0:T(8,128)S(1)} %pad_maximum_fusion.1.u_ref, bf16[2,1024,1024]{2,1,0:T(8,128)(2,1)S(1)} %copy-done.2, bf16[2,1024,1024]{2,1,0:T(8,128)(2,1)S(1)} %copy-done.6), custom_call_target="tpu_custom_call" | custom-call | tf_op jit(solution)/shard_map/pallas_call | solution.py:296
  69.9 1.4 collective-permute-start.14
  71.4 3.6 %collective-permute-done.12 = f32[40,1024]{1,0:T(8,128)S(1)} collective-permute-done((f32[40,1024]{1,0:T(8,128)S(1)}, f32[40,1024]{1,0:T(8,128)S(1)}, u32[]{:S(2)}, u32[]{:S(2)}) %collective-permute-start.12) | collective-permute-done | bytes 163872 | tf_op jit(solution)/shard_map/ppermute | solution.py:382
  74.9 2.0 %collective-permute-done.13 = f32[40,1024]{1,0:T(8,128)S(1)} collective-permute-done((f32[40,1024]{1,0:T(8,128)S(1)}, f32[40,1024]{1,0:T(8,128)S(1)}, u32[]{:S(2)}, u32[]{:S(2)}) %collective-permute-start.13) | collective-permute-done | bytes 163872 | tf_op jit(solution)/shard_map/ppermute | solution.py:382
  77.0 1.6 collective-permute-done.14
  80.1 2.2 %copy-done.3 = bf16[2,1024,1024]{2,1,0:T(8,128)(2,1)S(1)} copy-done((bf16[2,1024,1024]{2,1,0:T(8,128)(2,1)S(1)}, bf16[2,1024,1024]{2,1,0:T(8,128)(2,1)}, u32[]{:S(2)}) %copy-start.3) | copy-done | bytes 4194328
  82.3 2.2 %copy-done.7 = bf16[2,1024,1024]{2,1,0:T(8,128)(2,1)S(1)} copy-done((bf16[2,1024,1024]{2,1,0:T(8,128)(2,1)S(1)}, bf16[2,1024,1024]{2,1,0:T(8,128)(2,1)}, u32[]{:S(2)}) %copy-start.7) | copy-done | bytes 4194328
  84.5 1.6 shard_map.72
  86.2 2.7 %collective-permute-start.17 = (f32[16,1024]{1,0:T(8,128)S(1)}, f32[16,1024]{1,0:T(8,128)S(1)}, u32[]{:S(2)}, u32[]{:S(2)}) collective-permute-start(f32[16,1024]{1,0:T(8,128)S(1)} %get-tuple-element.18), channel_id=1, source_target_pairs={{0,16},{8,24},{16,0},{24,8},{1,17},{9,25},{17,1},{25,9},{2,18},{10... | collective-permute-start | bytes 196616 | tf_op jit(solution)/shard_map/ppermute | solution.py:367
  88.9 1.7 collective-permute-start.18
  91.4 2.7 %collective-permute-done.17 = f32[16,1024]{1,0:T(8,128)S(1)} collective-permute-done((f32[16,1024]{1,0:T(8,128)S(1)}, f32[16,1024]{1,0:T(8,128)S(1)}, u32[]{:S(2)}, u32[]{:S(2)}) %collective-permute-start.17) | collective-permute-done | bytes 65568 | tf_op jit(solution)/shard_map/ppermute | solution.py:367
  95.1 2.0 %collective-permute-start.19 = (f32[16,1024]{1,0:T(8,128)S(1)}, f32[16,1024]{1,0:T(8,128)S(1)}, u32[]{:S(2)}, u32[]{:S(2)}) collective-permute-start(f32[16,1024]{1,0:T(8,128)S(1)} %add_add_fusion.2), channel_id=1, source_target_pairs={{0,24},{8,16},{16,8},{24,0},{1,25},{9,17},{17,9},{25,1},{2,26},{10... | collective-permute-start | bytes 196616 | tf_op jit(solution)/shard_map/ppermute | solution.py:374
  97.8 1.8 %collective-permute-start.21 = (f32[16,1024]{1,0:T(8,128)S(1)}, f32[16,1024]{1,0:T(8,128)S(1)}, u32[]{:S(2)}, u32[]{:S(2)}) collective-permute-start(f32[16,1024]{1,0:T(8,128)S(1)} %add_add_fusion.2), channel_id=1, source_target_pairs={{0,8},{8,0},{16,24},{24,16},{1,9},{9,1},{17,25},{25,17},{2,10},{10... | collective-permute-start | bytes 196616 | tf_op jit(solution)/shard_map/ppermute | solution.py:374
  99.7 2.8 %shard_map.71 = f32[32,32]{1,0:T(8,128)S(1)} custom-call(f32[32,32]{1,0:T(8,128)S(1)} %reshape_squeeze.3.g_ref), custom_call_target="tpu_custom_call" | custom-call | tf_op jit(solution)/shard_map/pallas_call | solution.py:254
  104.4 2.2 %copy-done.4 = bf16[2,1024,1024]{2,1,0:T(8,128)(2,1)S(1)} copy-done((bf16[2,1024,1024]{2,1,0:T(8,128)(2,1)S(1)}, bf16[2,1024,1024]{2,1,0:T(8,128)(2,1)}, u32[]{:S(2)}) %copy-start.4) | copy-done | bytes 4194328
  106.6 2.2 %copy-done.8 = bf16[2,1024,1024]{2,1,0:T(8,128)(2,1)S(1)} copy-done((bf16[2,1024,1024]{2,1,0:T(8,128)(2,1)S(1)}, bf16[2,1024,1024]{2,1,0:T(8,128)(2,1)}, u32[]{:S(2)}) %copy-start.8) | copy-done | bytes 4194328
  108.8 2.7 %shard_map.73 = f32[8,64,128]{2,1,0:T(8,128)S(1)} custom-call(f32[64,1024]{1,0:T(8,128)S(1)} %pad_maximum_fusion.3.u_ref.refs_0_, bf16[2,1024,1024]{2,1,0:T(8,128)(2,1)S(1)} %copy-done.4, bf16[2,1024,1024]{2,1,0:T(8,128)(2,1)S(1)} %copy-done.8), custom_call_target="tpu_custom_call" | custom-call | tf_op jit(solution)/shard_map/pallas_call | solution.py:296
  114.2 1.5 collective-permute-start.24
  118.2 2.4 %collective-permute-done.25 = f32[72,128]{1,0:T(8,128)S(1)} collective-permute-done((f32[72,128]{1,0:T(8,128)S(1)}, f32[72,128]{1,0:T(8,128)S(1)}, u32[]{:S(2)}, u32[]{:S(2)}) %collective-permute-start.25) | collective-permute-done | bytes 36896 | tf_op jit(solution)/shard_map/ppermute | solution.py:367
  120.7 2.8 %shard_map.74.inv_ref = f32[32,32]{1,0:T(8,128)S(1)} custom-call(f32[32,32]{1,0:T(8,128)S(1)} %reshape.47.g_ref), custom_call_target="tpu_custom_call" | custom-call | tf_op jit(solution)/shard_map/pallas_call | solution.py:254
  126.4 1.5 collective-permute-start.30
  128.4 1.5 collective-permute-start.26
  131.1 10.2 %collective-permute-done.35 = f32[8,32]{1,0:T(8,128)S(1)} collective-permute-done((f32[8,32]{1,0:T(8,128)S(1)}, f32[8,32]{1,0:T(8,128)S(1)}, u32[]{:S(2)}, u32[]{:S(2)}) %collective-permute-start.35) | collective-permute-done | bytes 1056 | tf_op jit(solution)/shard_map/ppermute | solution.py:390
  141.8 3.2 %collective-permute-done.36 = f32[8,32]{1,0:T(8,128)S(1)} collective-permute-done((f32[8,32]{1,0:T(8,128)S(1)}, f32[8,32]{1,0:T(8,128)S(1)}, u32[]{:S(2)}, u32[]{:S(2)}) %collective-permute-start.36) | collective-permute-done | bytes 1056 | tf_op jit(solution)/shard_map/ppermute | solution.py:390
  146.4 3.1 %collective-permute-done.37 = f32[8,32]{1,0:T(8,128)S(1)} collective-permute-done((f32[8,32]{1,0:T(8,128)S(1)}, f32[8,32]{1,0:T(8,128)S(1)}, u32[]{:S(2)}, u32[]{:S(2)}) %collective-permute-start.37) | collective-permute-done | bytes 1056 | tf_op jit(solution)/shard_map/ppermute | solution.py:390
  150.0 3.5 %shard_map.75.refs_2_ = f32[8192,128]{1,0:T(8,128)S(1)} custom-call(s32[2]{0:T(128)S(1)} %pad_add_fusion.3.base_ref, s32[8192]{0:T(1024)S(1)} %copy-done.11, f32[64,1024]{1,0:T(8,128)S(1)} %pad_maximum_fusion.3.u_ref.refs_0_, f32[64,1024]{1,0:T(8,128)S(1)} %collective-permute-done.32.refs_1_), custom_call_target="tpu_custom_call" | custom-call | tf_op jit(solution)/shard_map/pallas_call | solution.py:189
  153.6 3.5 %shard_map.76.refs_2_ = f32[8192,128]{1,0:T(8,128)S(1)} custom-call(s32[2]{0:T(128)S(1)} %pad_add_fusion.2.base_ref, s32[8192]{0:T(1024)S(1)} %copy-done.11, f32[64,1024]{1,0:T(8,128)S(1)} %collective-permute-done.30.refs_0_, f32[64,1024]{1,0:T(8,128)S(1)} %collective-permute-done.31.refs_1_, ...), custom_call_target="tpu_custom_call", output_to_operand_aliasing={{}: (4, {})} | custom-call | tf_op jit(solution)/shard_map/pallas_call | solution.py:189
  157.1 3.5 %shard_map.77.refs_2_ = f32[8192,128]{1,0:T(8,128)S(1)} custom-call(s32[2]{0:T(128)S(1)} %pad_add_fusion.1.base_ref, s32[8192]{0:T(1024)S(1)} %copy-done.11, f32[64,1024]{1,0:T(8,128)S(1)} %collective-permute-done.28.refs_0_, f32[64,1024]{1,0:T(8,128)S(1)} %collective-permute-done.29.refs_1_, ...), custom_call_target="tpu_custom_call", output_to_operand_aliasing={{}: (4, {})} | custom-call | tf_op jit(solution)/shard_map/pallas_call | solution.py:189
  160.7 3.5 %shard_map.78.w_ref = f32[8192,128]{1,0:T(8,128)S(1)} custom-call(s32[2]{0:T(128)S(1)} %pad_add_fusion.base_ref, s32[8192]{0:T(1024)S(1)} %copy-done.11, f32[64,1024]{1,0:T(8,128)S(1)} %collective-permute-done.26.refs_0_, f32[64,1024]{1,0:T(8,128)S(1)} %collective-permute-done.27.refs_1_, ...), custom_call_target="tpu_custom_call", output_to_operand_aliasing={{}: (4, {})} | custom-call | tf_op jit(solution)/shard_map/pallas_call | solution.py:189
  164.2 14.0 %shard_map.79 = f32[64,8192]{1,0:T(8,128)} custom-call(f32[32,32]{1,0:T(8,128)S(1)} %shard_map.74.inv_ref, f32[8192,128]{1,0:T(8,128)S(1)} %shard_map.78.w_ref), custom_call_target="tpu_custom_call" | custom-call | tf_op jit(solution)/shard_map/pallas_call | solution.py:231
  (123 shorter events, 30.0 us)
Async XLA Ops:
  3.7 22.2 %copy-start.10 = (f32[2,32,8192]{2,1,0:T(8,128)S(1)}, f32[2,32,8192]{2,1,0:T(8,128)}, u32[]{:S(2)}) copy-start(f32[2,32,8192]{2,1,0:T(8,128)} %param.7) | copy-start | bytes 6291460
  19.9 1.5 collective-permute-start
  21.5 6.9 %collective-permute-start.1 = (f32[32,1024]{1,0:T(8,128)S(1)}, f32[32,1024]{1,0:T(8,128)S(1)}, u32[]{:S(2)}, u32[]{:S(2)}) collective-permute-start(f32[32,1024]{1,0:T(8,128)S(1)} %select_add_fusion), channel_id=1, source_target_pairs={{0,2},{1,3},{2,0},{3,1},{4,6},{5,7},{6,4},{7,5},{8,10},{9,11},{10,... | collective-permute-start | bytes 393224 | tf_op jit(solution)/shard_map/ppermute | solution.py:382
  24.4 8.1 %collective-permute-start.2 = (f32[32,1024]{1,0:T(8,128)S(1)}, f32[32,1024]{1,0:T(8,128)S(1)}, u32[]{:S(2)}, u32[]{:S(2)}) collective-permute-start(f32[32,1024]{1,0:T(8,128)S(1)} %select_add_fusion), channel_id=1, source_target_pairs={{0,4},{1,5},{2,6},{3,7},{4,0},{5,1},{6,2},{7,3},{8,12},{9,13},{10,... | collective-permute-start | bytes 393224 | tf_op jit(solution)/shard_map/ppermute | solution.py:382
  25.9 6.6 %collective-permute-start.3 = (f32[32,1024]{1,0:T(8,128)S(1)}, f32[32,1024]{1,0:T(8,128)S(1)}, u32[]{:S(2)}, u32[]{:S(2)}) collective-permute-start(f32[32,1024]{1,0:T(8,128)S(1)} %select_add_fusion), channel_id=1, source_target_pairs={{0,6},{1,7},{2,4},{3,5},{4,2},{5,3},{6,0},{7,1},{8,14},{9,15},{10,... | collective-permute-start | bytes 393224 | tf_op jit(solution)/shard_map/ppermute | solution.py:382
  32.5 3.8 %collective-permute-start.4 = (f32[32,1024]{1,0:T(8,128)S(1)}, f32[32,1024]{1,0:T(8,128)S(1)}, u32[]{:S(2)}, u32[]{:S(2)}) collective-permute-start(f32[32,1024]{1,0:T(8,128)S(1)} %add_add_fusion.1), channel_id=1, source_target_pairs={{0,1},{1,0},{2,3},{3,2},{4,5},{5,4},{6,7},{7,6},{8,9},{9,8},{10,11... | collective-permute-start | bytes 393224 | tf_op jit(solution)/shard_map/ppermute | solution.py:426
  36.4 2.2 %copy-start.1 = (bf16[2,1024,1024]{2,1,0:T(8,128)(2,1)S(1)}, bf16[2,1024,1024]{2,1,0:T(8,128)(2,1)}, u32[]{:S(2)}) copy-start(bf16[2,1024,1024]{2,1,0:T(8,128)(2,1)} %copy-done) | copy-start | bytes 12582916
  38.6 2.2 %copy-start.5 = (bf16[2,1024,1024]{2,1,0:T(8,128)(2,1)S(1)}, bf16[2,1024,1024]{2,1,0:T(8,128)(2,1)}, u32[]{:S(2)}) copy-start(bf16[2,1024,1024]{2,1,0:T(8,128)(2,1)} %get-tuple-element.8.refs_3_.dl_ref.refs_2_) | copy-start | bytes 12582916
  40.8 22.4 %copy-start.2 = (bf16[2,1024,1024]{2,1,0:T(8,128)(2,1)S(1)}, bf16[2,1024,1024]{2,1,0:T(8,128)(2,1)}, u32[]{:S(2)}) copy-start(bf16[2,1024,1024]{2,1,0:T(8,128)(2,1)} %copy-done) | copy-start | bytes 12582916
  40.8 22.4 %copy-start.6 = (bf16[2,1024,1024]{2,1,0:T(8,128)(2,1)S(1)}, bf16[2,1024,1024]{2,1,0:T(8,128)(2,1)}, u32[]{:S(2)}) copy-start(bf16[2,1024,1024]{2,1,0:T(8,128)(2,1)} %get-tuple-element.8.refs_3_.dl_ref.refs_2_) | copy-start | bytes 12582916
  42.5 4.6 %collective-permute-start.5 = (f32[16,1024]{1,0:T(8,128)S(1)}, f32[16,1024]{1,0:T(8,128)S(1)}, u32[]{:S(2)}, u32[]{:S(2)}) collective-permute-start(f32[16,1024]{1,0:T(8,128)S(1)} %get-tuple-element.26), channel_id=1, source_target_pairs={{0,8},{8,0},{16,24},{24,16},{1,9},{9,1},{17,25},{25,17},{2,10},{10... | collective-permute-start | bytes 196616 | tf_op jit(solution)/shard_map/ppermute | solution.py:367
  44.2 7.0 %collective-permute-start.6 = (f32[16,1024]{1,0:T(8,128)S(1)}, f32[16,1024]{1,0:T(8,128)S(1)}, u32[]{:S(2)}, u32[]{:S(2)}) collective-permute-start(f32[16,1024]{1,0:T(8,128)S(1)} %get-tuple-element.27), channel_id=1, source_target_pairs={{0,16},{8,24},{16,0},{24,8},{1,17},{9,25},{17,1},{25,9},{2,18},{10... | collective-permute-start | bytes 196616 | tf_op jit(solution)/shard_map/ppermute | solution.py:367
  46.8 6.1 %collective-permute-start.7 = (f32[16,1024]{1,0:T(8,128)S(1)}, f32[16,1024]{1,0:T(8,128)S(1)}, u32[]{:S(2)}, u32[]{:S(2)}) collective-permute-start(f32[16,1024]{1,0:T(8,128)S(1)} %get-tuple-element.28), channel_id=1, source_target_pairs={{0,24},{8,16},{16,8},{24,0},{1,25},{9,17},{17,9},{25,1},{2,26},{10... | collective-permute-start | bytes 196616 | tf_op jit(solution)/shard_map/ppermute | solution.py:367
  52.9 4.3 %collective-permute-start.10 = (f32[16,1024]{1,0:T(8,128)S(1)}, f32[16,1024]{1,0:T(8,128)S(1)}, u32[]{:S(2)}, u32[]{:S(2)}) collective-permute-start(f32[16,1024]{1,0:T(8,128)S(1)} %add_add_fusion.3), channel_id=1, source_target_pairs={{0,8},{8,0},{16,24},{24,16},{1,9},{9,1},{17,25},{25,17},{2,10},{10... | collective-permute-start | bytes 196616 | tf_op jit(solution)/shard_map/ppermute | solution.py:374
  54.2 6.6 %collective-permute-start.8 = (f32[16,1024]{1,0:T(8,128)S(1)}, f32[16,1024]{1,0:T(8,128)S(1)}, u32[]{:S(2)}, u32[]{:S(2)}) collective-permute-start(f32[16,1024]{1,0:T(8,128)S(1)} %add_add_fusion.3), channel_id=1, source_target_pairs={{0,24},{8,16},{16,8},{24,0},{1,25},{9,17},{17,9},{25,1},{2,26},{10... | collective-permute-start | bytes 196616 | tf_op jit(solution)/shard_map/ppermute | solution.py:374
  56.6 6.2 %collective-permute-start.9 = (f32[16,1024]{1,0:T(8,128)S(1)}, f32[16,1024]{1,0:T(8,128)S(1)}, u32[]{:S(2)}, u32[]{:S(2)}) collective-permute-start(f32[16,1024]{1,0:T(8,128)S(1)} %add_add_fusion.3), channel_id=1, source_target_pairs={{0,16},{8,24},{16,0},{24,8},{1,17},{9,25},{17,1},{25,9},{2,18},{10... | collective-permute-start | bytes 196616 | tf_op jit(solution)/shard_map/ppermute | solution.py:374
  66.3 1.5 collective-permute-start.11
  67.8 7.1 %collective-permute-start.12 = (f32[40,1024]{1,0:T(8,128)S(1)}, f32[40,1024]{1,0:T(8,128)S(1)}, u32[]{:S(2)}, u32[]{:S(2)}) collective-permute-start(f32[40,1024]{1,0:T(8,128)S(1)} %fusion.7), channel_id=1, source_target_pairs={{0,2},{1,3},{2,0},{3,1},{4,6},{5,7},{6,4},{7,5},{8,10},{9,11},{10,... | collective-permute-start | bytes 491528 | tf_op jit(solution)/shard_map/ppermute | solution.py:382
  69.1 7.9 %collective-permute-start.13 = (f32[40,1024]{1,0:T(8,128)S(1)}, f32[40,1024]{1,0:T(8,128)S(1)}, u32[]{:S(2)}, u32[]{:S(2)}) collective-permute-start(f32[40,1024]{1,0:T(8,128)S(1)} %fusion.7), channel_id=1, source_target_pairs={{0,4},{1,5},{2,6},{3,7},{4,0},{5,1},{6,2},{7,3},{8,12},{9,13},{10,... | collective-permute-start | bytes 491528 | tf_op jit(solution)/shard_map/ppermute | solution.py:382
  69.9 8.7 %collective-permute-start.14 = (f32[40,1024]{1,0:T(8,128)S(1)}, f32[40,1024]{1,0:T(8,128)S(1)}, u32[]{:S(2)}, u32[]{:S(2)}) collective-permute-start(f32[40,1024]{1,0:T(8,128)S(1)} %fusion.7), channel_id=1, source_target_pairs={{0,6},{1,7},{2,4},{3,5},{4,2},{5,3},{6,0},{7,1},{8,14},{9,15},{10,... | collective-permute-start | bytes 491528 | tf_op jit(solution)/shard_map/ppermute | solution.py:382
  78.6 1.4 collective-permute-start.15
  80.1 2.2 %copy-start.3 = (bf16[2,1024,1024]{2,1,0:T(8,128)(2,1)S(1)}, bf16[2,1024,1024]{2,1,0:T(8,128)(2,1)}, u32[]{:S(2)}) copy-start(bf16[2,1024,1024]{2,1,0:T(8,128)(2,1)} %copy-done) | copy-start | bytes 12582916
  82.3 2.2 %copy-start.7 = (bf16[2,1024,1024]{2,1,0:T(8,128)(2,1)S(1)}, bf16[2,1024,1024]{2,1,0:T(8,128)(2,1)}, u32[]{:S(2)}) copy-start(bf16[2,1024,1024]{2,1,0:T(8,128)(2,1)} %get-tuple-element.8.refs_3_.dl_ref.refs_2_) | copy-start | bytes 12582916
  86.1 5.3 %collective-permute-start.16 = (f32[16,1024]{1,0:T(8,128)S(1)}, f32[16,1024]{1,0:T(8,128)S(1)}, u32[]{:S(2)}, u32[]{:S(2)}) collective-permute-start(f32[16,1024]{1,0:T(8,128)S(1)} %get-tuple-element.17), channel_id=1, source_target_pairs={{0,8},{8,0},{16,24},{24,16},{1,9},{9,1},{17,25},{25,17},{2,10},{10... | collective-permute-start | bytes 196616 | tf_op jit(solution)/shard_map/ppermute | solution.py:367
  86.2 7.9 %collective-permute-start.17 = (f32[16,1024]{1,0:T(8,128)S(1)}, f32[16,1024]{1,0:T(8,128)S(1)}, u32[]{:S(2)}, u32[]{:S(2)}) collective-permute-start(f32[16,1024]{1,0:T(8,128)S(1)} %get-tuple-element.18), channel_id=1, source_target_pairs={{0,16},{8,24},{16,0},{24,8},{1,17},{9,25},{17,1},{25,9},{2,18},{10... | collective-permute-start | bytes 196616 | tf_op jit(solution)/shard_map/ppermute | solution.py:367
  88.9 6.2 %collective-permute-start.18 = (f32[16,1024]{1,0:T(8,128)S(1)}, f32[16,1024]{1,0:T(8,128)S(1)}, u32[]{:S(2)}, u32[]{:S(2)}) collective-permute-start(f32[16,1024]{1,0:T(8,128)S(1)} %get-tuple-element.19), channel_id=1, source_target_pairs={{0,24},{8,16},{16,8},{24,0},{1,25},{9,17},{17,9},{25,1},{2,26},{10... | collective-permute-start | bytes 196616 | tf_op jit(solution)/shard_map/ppermute | solution.py:367
  95.1 7.3 %collective-permute-start.19 = (f32[16,1024]{1,0:T(8,128)S(1)}, f32[16,1024]{1,0:T(8,128)S(1)}, u32[]{:S(2)}, u32[]{:S(2)}) collective-permute-start(f32[16,1024]{1,0:T(8,128)S(1)} %add_add_fusion.2), channel_id=1, source_target_pairs={{0,24},{8,16},{16,8},{24,0},{1,25},{9,17},{17,9},{25,1},{2,26},{10... | collective-permute-start | bytes 196616 | tf_op jit(solution)/shard_map/ppermute | solution.py:374
  97.1 6.4 %collective-permute-start.20 = (f32[16,1024]{1,0:T(8,128)S(1)}, f32[16,1024]{1,0:T(8,128)S(1)}, u32[]{:S(2)}, u32[]{:S(2)}) collective-permute-start(f32[16,1024]{1,0:T(8,128)S(1)} %add_add_fusion.2), channel_id=1, source_target_pairs={{0,16},{8,24},{16,0},{24,8},{1,17},{9,25},{17,1},{25,9},{2,18},{10... | collective-permute-start | bytes 196616 | tf_op jit(solution)/shard_map/ppermute | solution.py:374
  97.8 5.7 %collective-permute-start.21 = (f32[16,1024]{1,0:T(8,128)S(1)}, f32[16,1024]{1,0:T(8,128)S(1)}, u32[]{:S(2)}, u32[]{:S(2)}) collective-permute-start(f32[16,1024]{1,0:T(8,128)S(1)} %add_add_fusion.2), channel_id=1, source_target_pairs={{0,8},{8,0},{16,24},{24,16},{1,9},{9,1},{17,25},{25,17},{2,10},{10... | collective-permute-start | bytes 196616 | tf_op jit(solution)/shard_map/ppermute | solution.py:374
  104.4 2.2 %copy-start.4 = (bf16[2,1024,1024]{2,1,0:T(8,128)(2,1)S(1)}, bf16[2,1024,1024]{2,1,0:T(8,128)(2,1)}, u32[]{:S(2)}) copy-start(bf16[2,1024,1024]{2,1,0:T(8,128)(2,1)} %copy-done) | copy-start | bytes 12582916
  106.6 2.2 %copy-start.8 = (bf16[2,1024,1024]{2,1,0:T(8,128)(2,1)S(1)}, bf16[2,1024,1024]{2,1,0:T(8,128)(2,1)}, u32[]{:S(2)}) copy-start(bf16[2,1024,1024]{2,1,0:T(8,128)(2,1)} %get-tuple-element.8.refs_3_.dl_ref.refs_2_) | copy-start | bytes 12582916
  108.8 41.3 %copy-start.11 = (s32[8192]{0:T(1024)S(1)}, s32[8192]{0:T(1024)}, u32[]{:S(2)}) copy-start(s32[8192]{0:T(1024)} %idx_ref.7) | copy-start | bytes 98308
  111.9 1.4 collective-permute-start.22
  113.4 4.0 %collective-permute-start.23 = (f32[72,128]{1,0:T(8,128)S(1)}, f32[72,128]{1,0:T(8,128)S(1)}, u32[]{:S(2)}, u32[]{:S(2)}) collective-permute-start(f32[72,128]{1,0:T(8,128)S(1)} %get-tuple-element.31), channel_id=1, source_target_pairs={{0,2},{1,3},{2,0},{3,1},{4,6},{5,7},{6,4},{7,5},{8,10},{9,11},{10,... | collective-permute-start | bytes 110600 | tf_op jit(solution)/shard_map/ppermute | solution.py:367
  114.2 4.0 %collective-permute-start.24 = (f32[72,128]{1,0:T(8,128)S(1)}, f32[72,128]{1,0:T(8,128)S(1)}, u32[]{:S(2)}, u32[]{:S(2)}) collective-permute-start(f32[72,128]{1,0:T(8,128)S(1)} %get-tuple-element.32), channel_id=1, source_target_pairs={{0,4},{1,5},{2,6},{3,7},{4,0},{5,1},{6,2},{7,3},{8,12},{9,13},{10,... | collective-permute-start | bytes 110600 | tf_op jit(solution)/shard_map/ppermute | solution.py:367
  115.7 4.9 %collective-permute-start.25 = (f32[72,128]{1,0:T(8,128)S(1)}, f32[72,128]{1,0:T(8,128)S(1)}, u32[]{:S(2)}, u32[]{:S(2)}) collective-permute-start(f32[72,128]{1,0:T(8,128)S(1)} %get-tuple-element.33), channel_id=1, source_target_pairs={{0,6},{1,7},{2,4},{3,5},{4,2},{5,3},{6,0},{7,1},{8,14},{9,15},{10,... | collective-permute-start | bytes 110600 | tf_op jit(solution)/shard_map/ppermute | solution.py:367
  124.6 1.2 collective-permute-start.33
  125.8 4.1 %collective-permute-start.34 = (f32[8,32]{1,0:T(8,128)S(1)}, f32[8,32]{1,0:T(8,128)S(1)}, u32[]{:S(2)}, u32[]{:S(2)}) collective-permute-start(f32[8,32]{1,0:T(8,128)S(1)} %broadcast_add_fusion), channel_id=1, source_target_pairs={{0,2},{1,3},{2,0},{3,1},{4,6},{5,7},{6,4},{7,5},{8,10},{9,11},{10,... | collective-permute-start | bytes 3080 | tf_op jit(solution)/shard_map/ppermute | solution.py:390
  126.4 19.4 %collective-permute-start.30 = (f32[64,1024]{1,0:T(8,128)S(1)}, f32[64,1024]{1,0:T(8,128)S(1)}, u32[]{:S(2)}, u32[]{:S(2)}) collective-permute-start(f32[64,1024]{1,0:T(8,128)S(1)} %pad_maximum_fusion.3.u_ref.refs_0_), channel_id=1, source_target_pairs={{0,2},{1,3},{2,0},{3,1},{4,6},{5,7},{6,4},{7,5},{8,10},{9,11},{10,... | collective-permute-start | bytes 786440 | tf_op jit(solution)/shard_map/ppermute | solution.py:471
  127.9 17.9 %collective-permute-start.28 = (f32[64,1024]{1,0:T(8,128)S(1)}, f32[64,1024]{1,0:T(8,128)S(1)}, u32[]{:S(2)}, u32[]{:S(2)}) collective-permute-start(f32[64,1024]{1,0:T(8,128)S(1)} %pad_maximum_fusion.3.u_ref.refs_0_), channel_id=1, source_target_pairs={{0,4},{1,5},{2,6},{3,7},{4,0},{5,1},{6,2},{7,3},{8,12},{9,13},{10,... | collective-permute-start | bytes 786440 | tf_op jit(solution)/shard_map/ppermute | solution.py:471
  128.4 17.9 %collective-permute-start.26 = (f32[64,1024]{1,0:T(8,128)S(1)}, f32[64,1024]{1,0:T(8,128)S(1)}, u32[]{:S(2)}, u32[]{:S(2)}) collective-permute-start(f32[64,1024]{1,0:T(8,128)S(1)} %pad_maximum_fusion.3.u_ref.refs_0_), channel_id=1, source_target_pairs={{0,6},{1,7},{2,4},{3,5},{4,2},{5,3},{6,0},{7,1},{8,14},{9,15},{10,... | collective-permute-start | bytes 786440 | tf_op jit(solution)/shard_map/ppermute | solution.py:471
  129.9 11.5 %collective-permute-start.35 = (f32[8,32]{1,0:T(8,128)S(1)}, f32[8,32]{1,0:T(8,128)S(1)}, u32[]{:S(2)}, u32[]{:S(2)}) collective-permute-start(f32[8,32]{1,0:T(8,128)S(1)} %fusion.45), channel_id=1, source_target_pairs={{0,4},{1,5},{2,6},{3,7},{4,0},{5,1},{6,2},{7,3},{8,12},{9,13},{10,... | collective-permute-start | bytes 3080 | tf_op jit(solution)/shard_map/ppermute | solution.py:390
  141.4 3.6 %collective-permute-start.36 = (f32[8,32]{1,0:T(8,128)S(1)}, f32[8,32]{1,0:T(8,128)S(1)}, u32[]{:S(2)}, u32[]{:S(2)}) collective-permute-start(f32[8,32]{1,0:T(8,128)S(1)} %add.135), channel_id=1, source_target_pairs={{0,8},{8,0},{16,24},{24,16},{1,9},{9,1},{17,25},{25,17},{2,10},{10... | collective-permute-start | bytes 3080 | tf_op jit(solution)/shard_map/ppermute | solution.py:390
  141.7 8.3 %collective-permute-start.32 = (f32[64,1024]{1,0:T(8,128)S(1)}, f32[64,1024]{1,0:T(8,128)S(1)}, u32[]{:S(2)}, u32[]{:S(2)}) collective-permute-start(f32[64,1024]{1,0:T(8,128)S(1)} %pad_maximum_fusion.3.u_ref.refs_0_), channel_id=1, source_target_pairs={{0,1},{1,0},{2,3},{3,2},{4,5},{5,4},{6,7},{7,6},{8,9},{9,8},{10,11... | collective-permute-start | bytes 786440 | tf_op jit(solution)/shard_map/ppermute | solution.py:472
  145.0 4.5 %collective-permute-start.37 = (f32[8,32]{1,0:T(8,128)S(1)}, f32[8,32]{1,0:T(8,128)S(1)}, u32[]{:S(2)}, u32[]{:S(2)}) collective-permute-start(f32[8,32]{1,0:T(8,128)S(1)} %add.136), channel_id=1, source_target_pairs={{0,16},{8,24},{16,0},{24,8},{1,17},{9,25},{17,1},{25,9},{2,18},{10... | collective-permute-start | bytes 3080 | tf_op jit(solution)/shard_map/ppermute | solution.py:390
  145.7 7.8 %collective-permute-start.31 = (f32[64,1024]{1,0:T(8,128)S(1)}, f32[64,1024]{1,0:T(8,128)S(1)}, u32[]{:S(2)}, u32[]{:S(2)}) collective-permute-start(f32[64,1024]{1,0:T(8,128)S(1)} %collective-permute-done.30.refs_0_), channel_id=1, source_target_pairs={{0,1},{1,0},{2,3},{3,2},{4,5},{5,4},{6,7},{7,6},{8,9},{9,8},{10,11... | collective-permute-start | bytes 786440 | tf_op jit(solution)/shard_map/ppermute | solution.py:475
  145.7 11.4 %collective-permute-start.29 = (f32[64,1024]{1,0:T(8,128)S(1)}, f32[64,1024]{1,0:T(8,128)S(1)}, u32[]{:S(2)}, u32[]{:S(2)}) collective-permute-start(f32[64,1024]{1,0:T(8,128)S(1)} %collective-permute-done.28.refs_0_), channel_id=1, source_target_pairs={{0,1},{1,0},{2,3},{3,2},{4,5},{5,4},{6,7},{7,6},{8,9},{9,8},{10,11... | collective-permute-start | bytes 786440 | tf_op jit(solution)/shard_map/ppermute | solution.py:475
  146.3 14.4 %collective-permute-start.27 = (f32[64,1024]{1,0:T(8,128)S(1)}, f32[64,1024]{1,0:T(8,128)S(1)}, u32[]{:S(2)}, u32[]{:S(2)}) collective-permute-start(f32[64,1024]{1,0:T(8,128)S(1)} %collective-permute-done.26.refs_0_), channel_id=1, source_target_pairs={{0,1},{1,0},{2,3},{3,2},{4,5},{5,4},{6,7},{7,6},{8,9},{9,8},{10,11... | collective-permute-start | bytes 786440 | tf_op jit(solution)/shard_map/ppermute | solution.py:475
  (2 other events, 3.6 us)

commit v3 on v2

--- a/solution.py
+++ b/solution.py
@@ -27,6 +27,10 @@
 
 def exact(a, b, dims):
     return lax.dot_general(a, b, dims, precision=precise, preferred_element_type=F32)
+
+
+def in_vmem(x):
+    return pltpu.with_memory_space_constraint(x, pltpu.VMEM)
 
 
 def split(values):
@@ -83,8 +87,8 @@
 
 
 def start_kernel(
-    scale, idx_ref, at_ref, probes_ref, frames_ref, dh_ref, dl_ref, img_ref,
-    f_ref, w_ref, n_ref, g_ref, b_ref, t_ref, sems,
+    scale, here_ref, idx_ref, at_ref, probes_ref, frames_ref,
+    dh_ref, dl_ref, img_ref, mask_ref, base_ref, f_ref, w_ref, n_ref, g_ref, b_ref, t_ref, sems,
 ):
     vectors, modes = probes_ref.shape
     rows, count = frames_ref.shape[1:]
@@ -104,6 +108,12 @@
     for row in copies:
         for c in row:
             c.start()
+    for b in range(4):
+        for place, axis_row in ((here_ref[0], 0), (here_ref[1], 4)):
+            bit = ((place >> b) & 1).astype(F32)
+            mask_ref[axis_row + b : axis_row + b + 1, :] = jnp.full((1, HB), bit, F32)
+    for b in range(base_ref.shape[0]):
+        base_ref[b] = (here_ref[0] ^ b) * count
     signs = sign_table(HB).astype(BF16)
 
     def inner(i):
@@ -141,15 +151,26 @@
         img_ref[:, span] = apply_forward(b_ref[...], t_ref[...], dh_ref, dl_ref, span)
 
 
-def start(idx, steps_at, probes, frames, scale):
+def cost(us):
+    return pl.CostEstimate(flops=0, transcendentals=0, bytes_accessed=int(us * 3.5e6))
+
+
+def start(here, idx, steps_at, probes, frames, scale):
     vectors, modes = probes.shape
     steps, rows, count = frames.shape
-    planes = jax.ShapeDtypeStruct((2, rows, count), BF16)
+    planes = pltpu.VMEM((2, rows, count), BF16)
     return pl.pallas_call(
         functools.partial(start_kernel, scale),
-        out_shape=[planes, planes, jax.ShapeDtypeStruct((vectors, rows), F32)],
-        in_specs=[SMEM, SMEM, VMEM, pl.BlockSpec(memory_space=pltpu.HBM)],
-        out_specs=[VMEM, VMEM, VMEM],
+        out_shape=[
+            planes,
+            planes,
+            jax.ShapeDtypeStruct((vectors, rows), F32),
+            jax.ShapeDtypeStruct((8, HB), F32),
+            jax.ShapeDtypeStruct((modes // count,), jnp.int32),
+        ],
+        in_specs=[SMEM, SMEM, SMEM, VMEM, pl.BlockSpec(memory_space=pltpu.HBM)],
+        out_specs=[VMEM, VMEM, VMEM, VMEM, SMEM],
+        cost_estimate=cost(12),
         scratch_shapes=[
             pltpu.VMEM((steps, rows, count), F32),
             pltpu.VMEM((vectors, modes), F32),
@@ -160,10 +181,10 @@
             pltpu.SemaphoreType.DMA((steps, rows // min(BLOCK, rows))),
         ],
         compiler_params=pltpu.CompilerParams(vmem_limit_bytes=44 << 20),
-    )(idx, steps_at, probes, frames)
-
-
-def scatter_kernel(base_ref, idx_ref, *refs):
+    )(here, idx, steps_at, probes, frames)
+
+
+def scatter_kernel(places, base_ref, idx_ref, *refs):
     s_ref, w_ref = refs[-1], refs[-2]
     pieces = [r for r in refs[:-2] if len(r.shape) == 2 and r.shape[1] == s_ref.shape[0]]
     count = s_ref.shape[0]
@@ -172,7 +193,7 @@
             high, low = split(x_ref[:, i * HB : (i + 1) * HB])
             both = jnp.concatenate([high.astype(F32), low.astype(F32)], axis=0)
             s_ref[i * HB : (i + 1) * HB, :] = both.T
-        base = base_ref[p]
+        base = base_ref[places[p]]
 
         def move(t, carry, base=base):
             at = pl.multiple_of(t * 16, 16)
@@ -183,11 +204,12 @@
         lax.fori_loop(0, count // 16, move, 0)
 
 
-def scatter_rows(bases, idx, pieces, table=None):
+def scatter_rows(places, bases, idx, pieces, table=None):
     count = pieces[0].shape[1]
     args = [bases, idx, *pieces] + ([] if table is None else [table])
     return pl.pallas_call(
-        scatter_kernel,
+        functools.partial(scatter_kernel, places),
+        cost_estimate=cost(1.7 * len(pieces)),
         out_shape=jax.ShapeDtypeStruct((idx.shape[0], HB), F32),
         in_specs=[SMEM, SMEM] + [VMEM] * (len(args) - 2),
         out_specs=VMEM,
@@ -230,6 +252,7 @@
 def end_vectors(inv, table, vectors):
     return pl.pallas_call(
         end_kernel,
+        cost_estimate=cost(12),
         out_shape=jax.ShapeDtypeStruct((vectors, table.shape[0]), F32),
         in_specs=[VMEM, VMEM],
         out_specs=VMEM,
@@ -238,10 +261,11 @@
 
 
 def factor_kernel(g_ref, out_ref):
-    n = g_ref.shape[0]
+    n = out_ref.shape[0]
+    square = jnp.concatenate([g_ref[:, i * n : (i + 1) * n] for i in range(n // 8)], axis=0)
     row = lax.broadcasted_iota(jnp.int32, (n, n), 0)
     eye = (row == lax.broadcasted_iota(jnp.int32, (n, n), 1)).astype(F32)
-    both = jnp.concatenate([g_ref[...], eye], axis=1)
+    both = jnp.concatenate([square, eye], axis=1)
     below = lax.broadcasted_iota(jnp.int32, (n, 1), 0)
     for k in range(n - 1):
         scaled = both[k : k + 1] * (1.0 / both[k : k + 1, k : k + 1])
@@ -250,14 +274,20 @@
     out_ref[...] = both[:, n:] * (1.0 / jnp.sqrt(pivots))
 
 
-def inverse_factor(gram_matrix):
+def pack(gram_matrix):
+    n = gram_matrix.shape[0]
+    return jnp.concatenate([gram_matrix[i : i + 8] for i in range(0, n, 8)], axis=1)
+
+
+def inverse_factor(packed, n):
     return pl.pallas_call(
         factor_kernel,
-        out_shape=jax.ShapeDtypeStruct(gram_matrix.shape, F32),
+        cost_estimate=cost(2.7),
+        out_shape=jax.ShapeDtypeStruct((n, n), F32),
         in_specs=[VMEM],
         out_specs=VMEM,
         compiler_params=pltpu.CompilerParams(vmem_limit_bytes=2 << 20),
-    )(gram_matrix)
+    )(packed)
 
 
 def stack_forward(u):
@@ -275,7 +305,13 @@
     return wide[:n] + wide[n:] + low
 
 
-def forward_kernel(u_ref, dh_ref, dl_ref, img_ref):
+def gram(vectors):
+    half = vectors.shape[0] // 2
+    return exact(vectors[:half], vectors[:half], NT) + exact(vectors[half:], vectors[half:], NT)
+
+
+def forward_kernel(u_ref, dh_ref, dl_ref, img_ref, gram_ref):
+    gram_ref[...] = pack(gram(u_ref[...]))
     both, turned = stack_forward(u_ref[...])
     rows = dh_ref.shape[1]
     block = min(BLOCK, rows)
@@ -295,11 +331,15 @@
     shape = (vectors, rows) if places is None else (places, vectors, rows // places)
     return pl.pallas_call(
         forward_kernel,
-        out_shape=jax.ShapeDtypeStruct(shape, F32),
+        out_shape=[
+            jax.ShapeDtypeStruct(shape, F32),
+            jax.ShapeDtypeStruct((8, vectors // 2 * vectors // 16), F32),
+        ],
         in_specs=[VMEM, VMEM, VMEM],
-        out_specs=VMEM,
+        out_specs=[VMEM, VMEM],
+        cost_estimate=cost(2.7),
         compiler_params=pltpu.CompilerParams(vmem_limit_bytes=12 << 20),
-    )(u, dh, dl)
+    )(u, in_vmem(dh), in_vmem(dl))
 
 
 def backward_kernel(*refs):
@@ -325,9 +365,10 @@
 
 
 def backward(inv, images, dh, dl):
-    args = ([] if inv is None else [inv]) + [images, dh, dl]
+    args = ([] if inv is None else [inv]) + [images, in_vmem(dh), in_vmem(dl)]
     return pl.pallas_call(
         backward_kernel,
+        cost_estimate=cost(1.6),
         out_shape=jax.ShapeDtypeStruct((images.shape[0], dh.shape[2]), F32),
         in_specs=[VMEM] * len(args),
         out_specs=VMEM,
@@ -335,11 +376,6 @@
     )(*args)
 
 
-def gram(vectors):
-    half = vectors.shape[0] // 2
-    return exact(vectors[:half], vectors[:half], NT) + exact(vectors[half:], vectors[half:], NT)
-
-
 def normalise(inv, vectors):
     half = inv.shape[0]
     return jnp.concatenate([exact(inv, vectors[:half], NN), exact(inv, vectors[half:], NN)], axis=0)
@@ -349,30 +385,25 @@
     return [(i, i ^ bit) for i in range(n)]
 
 
-def pick(pieces, here, n):
-    bit = 1
-    while bit < n:
-        odd = (here & bit) != 0
-        pieces = [jnp.where(odd, pieces[b ^ bit], pieces[b]) for b in range(n)]
-        bit *= 2
+def pick(pieces, odds):
+    for bit, odd in enumerate(odds):
+        pieces = [jnp.where(odd, pieces[b ^ (1 << bit)], pieces[b]) for b in range(len(pieces))]
     return pieces
 
 
-def scatter_sum(blocks, axis, step, n):
+def scatter_sum(blocks, axis, step, odds):
     size = lax.axis_size(axis)
-    here = (lax.axis_index(axis) // step) % n
-    mine = pick(blocks, here, n)
+    mine = pick(blocks, odds)
     total = mine[0]
-    for b in range(1, n):
+    for b in range(1, len(blocks)):
         total = total + lax.ppermute(mine[b], axis, flip(size, b * step))
     return total
 
 
-def gather_all(block, axis, step, n):
+def gather_all(block, axis, step, odds):
     size = lax.axis_size(axis)
-    here = (lax.axis_index(axis) // step) % n
-    pieces = [block] + [lax.ppermute(block, axis, flip(size, b * step)) for b in range(1, n)]
-    return pick(pieces, here, n)
+    far = [lax.ppermute(block, axis, flip(size, b * step)) for b in range(1, 2 ** len(odds))]
+    return pick([block] + far, odds)
 
 
 def share_sum(block, axis, step, n):
@@ -392,32 +423,28 @@
     return block
 
 
-def sum_pix(x):
+def sum_pix(x, odds):
     n = lax.axis_size("pix")
     if n != 4:
         return double_sum(x, "pix")
     rows = x.shape[0] // n
-    mine = scatter_sum([x[i * rows : (i + 1) * rows] for i in range(n)], "pix", 1, n)
-    return jnp.concatenate(gather_all(mine, "pix", 1, n), axis=0)
-
-
-def pack(gram_matrix, width):
-    return jnp.pad(gram_matrix.reshape(1, -1), ((0, 7), (0, width - gram_matrix.size)))
-
-
-def sum_mode(x, extra=None):
+    odds = odds[4:6]
+    mine = scatter_sum([x[i * rows : (i + 1) * rows] for i in range(n)], "pix", 1, odds)
+    return jnp.concatenate(gather_all(mine, "pix", 1, odds), axis=0)
+
+
+def sum_mode(x, odds, extra=None):
     n = lax.axis_size("mode")
     rows, cols = x.shape
     if n != 8:
-        total = double_sum(x, "mode")
-        return total, (None if extra is None else double_sum(extra, "mode"))
+        return double_sum(x, "mode"), (None if extra is None else double_sum(extra, "mode"))
     half = rows // 2
-    odd = (lax.axis_index("mode") % 2) != 0
+    odd = odds[0]
     mine = jnp.where(odd, x[half:], x[:half])
     other = jnp.where(odd, x[:half], x[half:])
     if extra is not None:
-        k = extra.shape[0]
-        row = pack(extra, cols)
+        width = extra.shape[1]
+        row = jnp.pad(extra, ((0, 0), (0, cols - width)))
         mine = jnp.concatenate([mine, row], axis=0)
         other = jnp.concatenate([other, row], axis=0)
     chip = mine + lax.ppermute(other, "mode", flip(n, 1))
@@ -425,55 +452,45 @@
     mine = chip[:half]
     other = lax.ppermute(mine, "mode", flip(n, 1))
     total = jnp.concatenate([jnp.where(odd, other, mine), jnp.where(odd, mine, other)], axis=0)
-    if extra is None:
-        return total, None
-    return total, chip[half, : k * k].reshape(k, k)
-
-
-def scatter_mode(pieces, extra):
+    return total, (None if extra is None else chip[half:, :width])
+
+
+def scatter_mode(pieces, odds, extra):
     places, rows, width = pieces.shape
-    k = extra.shape[0]
     n = lax.axis_size("mode")
     here = lax.axis_index("mode")
     if n != 8:
         total = double_sum(pieces, "mode")
         return lax.dynamic_index_in_dim(total, here, 0, False), double_sum(extra, "mode")
-    chips = pieces.reshape(4, 2, rows, width)
-    odd = (here % 2) != 0
-    mine = jnp.where(odd, chips[:, 1], chips[:, 0]).reshape(4 * rows, width)
-    other = jnp.where(odd, chips[:, 0], chips[:, 1]).reshape(4 * rows, width)
-    small = extra.reshape(k * k // width, width)
-    got = lax.ppermute(jnp.concatenate([other, small], axis=0), "mode", flip(n, 1))
+    odd = odds[0]
+    mine = jnp.concatenate([jnp.where(odd, pieces[2 * i + 1], pieces[2 * i]) for i in range(4)])
+    other = [jnp.where(odd, pieces[2 * i], pieces[2 * i + 1]) for i in range(4)]
+    small = jnp.pad(extra, ((0, 0), (0, width - extra.shape[1])))
+    got = lax.ppermute(jnp.concatenate(other + [small], axis=0), "mode", flip(n, 1))
     mine = mine + got[: 4 * rows]
     small = small + got[4 * rows :]
     blocks = [
         jnp.concatenate([mine[i * rows : (i + 1) * rows], small], axis=0) for i in range(4)
     ]
-    total = scatter_sum(blocks, "mode", 2, 4)
-    return total[:rows], total[rows:].reshape(k, k)
-
-
-def gather_rows(block, idx):
+    total = scatter_sum(blocks, "mode", 2, odds[1:3])
+    return total[:rows], total[rows:, : extra.shape[1]]
+
+
+def gather_rows(block, bases, idx):
     n = lax.axis_size("mode")
-    here = lax.axis_index("mode")
-    count = block.shape[1]
-
-    def bases(bits):
-        return jnp.stack([(here ^ b) * count for b in bits]).astype(jnp.int32)
-
     if n != 8:
         pieces = [block]
         bit = 1
         while bit < n:
             pieces = pieces + [lax.ppermute(p, "mode", flip(n, bit)) for p in pieces]
             bit *= 2
-        return scatter_rows(bases(range(n)), idx, pieces)
+        return scatter_rows(range(n), bases, idx, pieces)
+    near = lax.ppermute(block, "mode", flip(n, 1))
     far = {b: lax.ppermute(block, "mode", flip(n, b)) for b in (2, 4, 6)}
-    near = lax.ppermute(block, "mode", flip(n, 1))
-    table = scatter_rows(bases((0, 1)), idx, [block, near])
+    table = scatter_rows((0, 1), bases, idx, [block, near])
     for b in (2, 4, 6):
         other = lax.ppermute(far[b], "mode", flip(n, 1))
-        table = scatter_rows(bases((b, b ^ 1)), idx, [far[b], other], table)
+        table = scatter_rows((b, b ^ 1), bases, idx, [far[b], other], table)
     return table
 
 
@@ -486,22 +503,26 @@
     k = probes.shape[1]
     vectors = 2 * k
     probes = probes.reshape(vectors, modes_total)
-    here = lax.axis_index("mode")
+    here = jnp.stack([lax.axis_index("mode"), lax.axis_index("pix")]).astype(jnp.int32)
     steps_at = jnp.sum(
         jnp.where(phase_steps[None, :] == jnp.arange(4)[:, None], jnp.arange(4)[None, :], 0), axis=1
     ).astype(jnp.int32)
-    my_rows = lax.dynamic_slice_in_dim(pattern_rows, here * columns, columns)
-    dh, dl, images = start(my_rows, steps_at, probes, frames, 1.0 / math.sqrt(modes_total))
-    inv = inverse_factor(gram(probes))
-    images, _ = sum_mode(images)
-    returned = sum_pix(backward(inv, images, dh, dl))
+    my_rows = lax.dynamic_slice_in_dim(pattern_rows, lax.axis_index("mode") * columns, columns)
+    scale = 1.0 / math.sqrt(modes_total)
+    dh, dl, images, masks, bases = start(here, my_rows, steps_at, probes, frames, scale)
+    odds = [masks[b : b + 1, :1] != 0 for b in range(8)]
+    inv = inverse_factor(pack(gram(probes)), k)
+    images, _ = sum_mode(images, odds)
+    returned = sum_pix(backward(inv, images, dh, dl), odds)
     for iteration in range(1, ITERS):
-        images, gram_matrix = sum_mode(forward(returned, dh, dl), gram(returned))
-        inv = inverse_factor(gram_matrix)
-        returned = normalise(inv, sum_pix(backward(None, images, dh, dl)))
-    table = gather_rows(returned, pattern_rows)
-    fields, gram_matrix = scatter_mode(forward(returned, dh, dl, groups), gram(returned))
-    inv = inverse_factor(gram_matrix)
+        images, packed = forward(returned, dh, dl)
+        images, packed = sum_mode(images, odds, packed)
+        inv = inverse_factor(packed, k)
+        returned = normalise(inv, sum_pix(backward(None, images, dh, dl), odds))
+    table = gather_rows(returned, bases, pattern_rows)
+    images, packed = forward(returned, dh, dl, groups)
+    fields, packed = scatter_mode(images, odds, packed)
+    inv = inverse_factor(packed, k)
     fields = normalise(inv, fields)
     power = jnp.sum(fields * fields, axis=1)
     power = jnp.broadcast_to((power[:k] + power[k:])[None, :], (8, k))

time: 179 us -> 156 us (0.87)
  local copies, waits for them, and re-layouts: 17.8 us -> 1.31 us
  waiting for transfers between devices: 56.9 us -> 48.2 us
  between operations: 1.14 us -> 4.3 us
    unnamed x24 -> x4, local copies, waits for them, and re-layouts: 16.7 us -> 0.01 us
    ppermute x5, waiting for transfers between devices: 17.7 us -> 10.4 us  [double_sum(): block = block + lax.ppermute(block, axis, flip(size, bit))]
    ppermute x3, waiting for transfers between devices: 0.01 us -> 3.85 us  [gather_rows(): far = {b: lax.ppermute(block, 'mode', flip(n, b)) for b in (2, 4, 6)}]
    ppermute x9, waiting for transfers between devices: 14 us -> 10.9 us  [scatter_sum(): total = total + lax.ppermute(mine[b], axis, flip(size, b * step))]
    dot_general x10 -> x6, matrix products: 3.74 us -> 2.74 us  [exact(): lax.dot_general(a, b, dims, precision=precise, preferred_element_type=F32)]
  transfers between devices with their start and end apart: 38 -> 38, of which waited for: 26 -> 23; matrix products, arithmetic and copies ran while one was open for 2% -> 2% of each run, Pallas kernels for 9% -> 12%
where the time goes in v3:
time: 156 us
  Pallas kernels  59.1 us (38%)
  waiting for transfers between devices  48.2 us (31%)
  starting transfers between devices  37.1 us (24%)
  between operations  4.3 us (3%)
  other arithmetic  2.82 us (2%)
  matrix products  2.74 us (2%)
    pallas_call x4, Pallas kernels, scatter_rows(): pl.pallas_call(functools.partial(scatter_kernel, places), cost_estimate=c...  14.1 us
    pallas_call x1, Pallas kernels, end_vectors(): pl.pallas_call(end_kernel, cost_estimate=cost(12), out_shape=jax.ShapeDty...  14 us
    pallas_call x1, Pallas kernels, start(): pl.pallas_call(functools.partial(start_kernel, scale), out_shape=[planes,...  13.6 us
    ppermute x6, waiting for transfers between devices, share_sum(): total = total + lax.ppermute(block, axis, flip(size, b * step))  12.8 us
    ppermute x9, starting transfers between devices, scatter_sum(): total = total + lax.ppermute(mine[b], axis, flip(size, b * step))  12.5 us
    ppermute x9, waiting for transfers between devices, scatter_sum(): total = total + lax.ppermute(mine[b], axis, flip(size, b * step))  10.9 us
    ppermute x5, waiting for transfers between devices, double_sum(): block = block + lax.ppermute(block, axis, flip(size, bit))  10.4 us
    pallas_call x3, Pallas kernels, inverse_factor(): pl.pallas_call(factor_kernel, cost_estimate=cost(2.7), out_shape=jax.Shap...  8.27 us
  transfers between devices with their start and end apart: 38, of which 23 were waited for; matrix products, arithmetic and copies ran while one was open for 2% of the time, Pallas kernels for 12%

profile of v3, /device:TPU:0, one launch (start us, length us, event | category | flops | bytes accessed | tf_op | source)
XLA Modules:
  0.0 155.6 jit_solution(3955859954419543251)
XLA Ops:
  2.2 13.6 %shard_map.67 = (bf16[2,1024,1024]{2,1,0:T(8,128)(2,1)S(1)}, bf16[2,1024,1024]{2,1,0:T(8,128)(2,1)S(1)}, f32[64,1024]{1,0:T(8,128)S(1)}, f32[8,128]{1,0:T(8,128)S(1)}, s32[8]{0:T(128)S(1)}) custom-call(s32[2]{0:T(128)S(1)} %pad_add_fusion.here_ref, s32[1024]{0:T(1024)S(1)} %dynamic_slice.3.idx_ref, s32[4]{0:T(128)S(1)} %select_reduce_fusion.at_ref, ...), custom_call_target="tpu_custom_call" | custom-call | bytes 42000000 | tf_op jit(solution)/shard_map/pallas_call | solution.py:162
  18.5 2.9 %collective-permute-start.1 = (f32[32,1024]{1,0:T(8,128)S(1)}, f32[32,1024]{1,0:T(8,128)S(1)}, u32[]{:S(2)}, u32[]{:S(2)}) collective-permute-start(f32[32,1024]{1,0:T(8,128)S(1)} %select_add_fusion), channel_id=1, source_target_pairs={{0,2},{1,3},{2,0},{3,1},{4,6},{5,7},{6,4},{7,5},{8,10},{9,11},{10,... | collective-permute-start | bytes 393224 | tf_op jit(solution)/shard_map/ppermute | solution.py:413
  21.4 1.5 collective-permute-start.2
  24.0 1.4 collective-permute-done.1
  25.4 4.1 %collective-permute-done.2 = f32[32,1024]{1,0:T(8,128)S(1)} collective-permute-done((f32[32,1024]{1,0:T(8,128)S(1)}, f32[32,1024]{1,0:T(8,128)S(1)}, u32[]{:S(2)}, u32[]{:S(2)}) %collective-permute-start.2) | collective-permute-done | bytes 131104 | tf_op jit(solution)/shard_map/ppermute | solution.py:413
  29.7 2.8 %shard_map.68.refs_0_ = f32[32,32]{1,0:T(8,128)S(1)} custom-call(f32[8,128]{1,0:T(8,128)S(1)} %pad_maximum_fusion.9.g_ref), custom_call_target="tpu_custom_call" | custom-call | bytes 9450000 | tf_op jit(solution)/shard_map/pallas_call | solution.py:283
  33.9 1.7 %shard_map.69 = f32[64,1024]{1,0:T(8,128)S(1)} custom-call(f32[32,32]{1,0:T(8,128)S(1)} %shard_map.68.refs_0_, f32[64,1024]{1,0:T(8,128)S(1)} %pad_maximum_fusion.refs_1_, bf16[2,1024,1024]{2,1,0:T(8,128)(2,1)S(1)} %get-tuple-element.14.refs_2_.dh_ref.refs_1_, bf16[2,1024,1024]{2,1,0:T(8,128)(2,1)S(1)} %get-tuple-element.15.refs_3_.dl_ref.refs_2_), custom_call_target="tpu_custom_call" | custom-call | bytes 5600000 | tf_op jit(solution)/shard_map/pallas_call | solution.py:369
  35.6 1.6 %collective-permute-start.5 = (f32[16,1024]{1,0:T(8,128)S(1)}, f32[16,1024]{1,0:T(8,128)S(1)}, u32[]{:S(2)}, u32[]{:S(2)}) collective-permute-start(f32[16,1024]{1,0:T(8,128)S(1)} %get-tuple-element.40), channel_id=1, source_target_pairs={{0,8},{8,0},{16,24},{24,16},{1,9},{9,1},{17,25},{25,17},{2,10},{10... | collective-permute-start | bytes 196616 | tf_op jit(solution)/shard_map/ppermute | solution.py:399
  37.2 2.6 %collective-permute-start.6 = (f32[16,1024]{1,0:T(8,128)S(1)}, f32[16,1024]{1,0:T(8,128)S(1)}, u32[]{:S(2)}, u32[]{:S(2)}) collective-permute-start(f32[16,1024]{1,0:T(8,128)S(1)} %get-tuple-element.41), channel_id=1, source_target_pairs={{0,16},{8,24},{16,0},{24,8},{1,17},{9,25},{17,1},{25,9},{2,18},{10... | collective-permute-start | bytes 196616 | tf_op jit(solution)/shard_map/ppermute | solution.py:399
  40.2 4.1 %collective-permute-done.6 = f32[16,1024]{1,0:T(8,128)S(1)} collective-permute-done((f32[16,1024]{1,0:T(8,128)S(1)}, f32[16,1024]{1,0:T(8,128)S(1)}, u32[]{:S(2)}, u32[]{:S(2)}) %collective-permute-start.6) | collective-permute-done | bytes 65568 | tf_op jit(solution)/shard_map/ppermute | solution.py:399
  44.3 1.7 %collective-permute-done.7 = f32[16,1024]{1,0:T(8,128)S(1)} collective-permute-done((f32[16,1024]{1,0:T(8,128)S(1)}, f32[16,1024]{1,0:T(8,128)S(1)}, u32[]{:S(2)}, u32[]{:S(2)}) %collective-permute-start.7) | collective-permute-done | bytes 65568 | tf_op jit(solution)/shard_map/ppermute | solution.py:399
  45.9 1.3 collective-permute-start.10
  47.3 2.4 %collective-permute-start.8 = (f32[16,1024]{1,0:T(8,128)S(1)}, f32[16,1024]{1,0:T(8,128)S(1)}, u32[]{:S(2)}, u32[]{:S(2)}) collective-permute-start(f32[16,1024]{1,0:T(8,128)S(1)} %add_add_fusion.3), channel_id=1, source_target_pairs={{0,24},{8,16},{16,8},{24,0},{1,25},{9,17},{17,9},{25,1},{2,26},{10... | collective-permute-start | bytes 196616 | tf_op jit(solution)/shard_map/ppermute | solution.py:405
  50.3 3.6 %collective-permute-done.8 = f32[16,1024]{1,0:T(8,128)S(1)} collective-permute-done((f32[16,1024]{1,0:T(8,128)S(1)}, f32[16,1024]{1,0:T(8,128)S(1)}, u32[]{:S(2)}, u32[]{:S(2)}) %collective-permute-start.8) | collective-permute-done | bytes 65568 | tf_op jit(solution)/shard_map/ppermute | solution.py:405
  53.9 2.1 %collective-permute-done.9 = f32[16,1024]{1,0:T(8,128)S(1)} collective-permute-done((f32[16,1024]{1,0:T(8,128)S(1)}, f32[16,1024]{1,0:T(8,128)S(1)}, u32[]{:S(2)}, u32[]{:S(2)}) %collective-permute-start.9) | collective-permute-done | bytes 65568 | tf_op jit(solution)/shard_map/ppermute | solution.py:405
  56.0 2.9 %shard_map.70 = (f32[64,1024]{1,0:T(8,128)S(1)}, f32[8,128]{1,0:T(8,128)S(1)}) custom-call(f32[64,1024]{1,0:T(8,128)S(1)} %pad_maximum_fusion.1.u_ref, bf16[2,1024,1024]{2,1,0:T(8,128)(2,1)S(1)} %get-tuple-element.14.refs_2_.dh_ref.refs_1_, bf16[2,1024,1024]{2,1,0:T(8,128)(2,1)S(1)} %get-tuple-element.15.refs_3_.dl_ref.refs_2_), custom_call_target="tpu_custom_call" | custom-call | bytes 9450000 | tf_op jit(solution)/shard_map/pallas_call | solution.py:332
  59.0 1.4 collective-permute-done.11
  60.4 1.3 collective-permute-start.12
  62.6 1.4 collective-permute-start.14
  64.0 3.6 %collective-permute-done.12 = f32[40,1024]{1,0:T(8,128)S(1)} collective-permute-done((f32[40,1024]{1,0:T(8,128)S(1)}, f32[40,1024]{1,0:T(8,128)S(1)}, u32[]{:S(2)}, u32[]{:S(2)}) %collective-permute-start.12) | collective-permute-done | bytes 163872 | tf_op jit(solution)/shard_map/ppermute | solution.py:413
  67.6 2.0 %collective-permute-done.13 = f32[40,1024]{1,0:T(8,128)S(1)} collective-permute-done((f32[40,1024]{1,0:T(8,128)S(1)}, f32[40,1024]{1,0:T(8,128)S(1)}, u32[]{:S(2)}, u32[]{:S(2)}) %collective-permute-start.13) | collective-permute-done | bytes 163872 | tf_op jit(solution)/shard_map/ppermute | solution.py:413
  69.6 1.6 %collective-permute-done.14 = f32[40,1024]{1,0:T(8,128)S(1)} collective-permute-done((f32[40,1024]{1,0:T(8,128)S(1)}, f32[40,1024]{1,0:T(8,128)S(1)}, u32[]{:S(2)}, u32[]{:S(2)}) %collective-permute-start.14) | collective-permute-done | bytes 163872 | tf_op jit(solution)/shard_map/ppermute | solution.py:413
  71.4 1.3 collective-permute-done.15
  72.8 1.6 %shard_map.72 = f32[64,1024]{1,0:T(8,128)S(1)} custom-call(f32[64,1024]{1,0:T(8,128)S(1)} %pad_maximum_fusion.2.refs_0_, bf16[2,1024,1024]{2,1,0:T(8,128)(2,1)S(1)} %get-tuple-element.14.refs_2_.dh_ref.refs_1_, bf16[2,1024,1024]{2,1,0:T(8,128)(2,1)S(1)} %get-tuple-element.15.refs_3_.dl_ref.refs_2_), custom_call_target="tpu_custom_call" | custom-call | bytes 5600000 | tf_op jit(solution)/shard_map/pallas_call | solution.py:369
  74.5 2.7 %collective-permute-start.17 = (f32[16,1024]{1,0:T(8,128)S(1)}, f32[16,1024]{1,0:T(8,128)S(1)}, u32[]{:S(2)}, u32[]{:S(2)}) collective-permute-start(f32[16,1024]{1,0:T(8,128)S(1)} %get-tuple-element.32), channel_id=1, source_target_pairs={{0,16},{8,24},{16,0},{24,8},{1,17},{9,25},{17,1},{25,9},{2,18},{10... | collective-permute-start | bytes 196616 | tf_op jit(solution)/shard_map/ppermute | solution.py:399
  77.2 1.7 %collective-permute-start.18 = (f32[16,1024]{1,0:T(8,128)S(1)}, f32[16,1024]{1,0:T(8,128)S(1)}, u32[]{:S(2)}, u32[]{:S(2)}) collective-permute-start(f32[16,1024]{1,0:T(8,128)S(1)} %get-tuple-element.33), channel_id=1, source_target_pairs={{0,24},{8,16},{16,8},{24,0},{1,25},{9,17},{17,9},{25,1},{2,26},{10... | collective-permute-start | bytes 196616 | tf_op jit(solution)/shard_map/ppermute | solution.py:399
  79.7 2.7 %collective-permute-done.17 = f32[16,1024]{1,0:T(8,128)S(1)} collective-permute-done((f32[16,1024]{1,0:T(8,128)S(1)}, f32[16,1024]{1,0:T(8,128)S(1)}, u32[]{:S(2)}, u32[]{:S(2)}) %collective-permute-start.17) | collective-permute-done | bytes 65568 | tf_op jit(solution)/shard_map/ppermute | solution.py:399
  83.4 2.0 %collective-permute-start.19 = (f32[16,1024]{1,0:T(8,128)S(1)}, f32[16,1024]{1,0:T(8,128)S(1)}, u32[]{:S(2)}, u32[]{:S(2)}) collective-permute-start(f32[16,1024]{1,0:T(8,128)S(1)} %add_add_fusion.2), channel_id=1, source_target_pairs={{0,24},{8,16},{16,8},{24,0},{1,25},{9,17},{17,9},{25,1},{2,26},{10... | collective-permute-start | bytes 196616 | tf_op jit(solution)/shard_map/ppermute | solution.py:405
  86.1 1.8 %collective-permute-start.21 = (f32[16,1024]{1,0:T(8,128)S(1)}, f32[16,1024]{1,0:T(8,128)S(1)}, u32[]{:S(2)}, u32[]{:S(2)}) collective-permute-start(f32[16,1024]{1,0:T(8,128)S(1)} %add_add_fusion.2), channel_id=1, source_target_pairs={{0,8},{8,0},{16,24},{24,16},{1,9},{9,1},{17,25},{25,17},{2,10},{10... | collective-permute-start | bytes 196616 | tf_op jit(solution)/shard_map/ppermute | solution.py:405
  89.2 2.8 %shard_map.71 = f32[32,32]{1,0:T(8,128)S(1)} custom-call(f32[8,128]{1,0:T(8,128)S(1)} %slice.217.g_ref), custom_call_target="tpu_custom_call" | custom-call | bytes 9450000 | tf_op jit(solution)/shard_map/pallas_call | solution.py:283
  92.5 2.9 %shard_map.73 = (f32[8,64,128]{2,1,0:T(8,128)S(1)}, f32[8,128]{1,0:T(8,128)S(1)}) custom-call(f32[64,1024]{1,0:T(8,128)S(1)} %pad_maximum_fusion.3.u_ref.refs_0_, bf16[2,1024,1024]{2,1,0:T(8,128)(2,1)S(1)} %get-tuple-element.14.refs_2_.dh_ref.refs_1_, bf16[2,1024,1024]{2,1,0:T(8,128)(2,1)S(1)} %get-tuple-element.15.refs_3_.dl_ref.refs_2_), custom_call_target="tpu_custom_call" | custom-call | bytes 9450000 | tf_op jit(solution)/shard_map/pallas_call | solution.py:332
  95.6 1.3 collective-permute-done.22
  97.9 1.5 collective-permute-start.24
  99.4 1.2 collective-permute-start.25
  101.4 1.5 collective-permute-start.28
  102.9 1.2 collective-permute-start.26
  104.7 2.8 %shard_map.74.inv_ref = f32[32,32]{1,0:T(8,128)S(1)} custom-call(f32[8,128]{1,0:T(8,128)S(1)} %slice.229.g_ref), custom_call_target="tpu_custom_call" | custom-call | bytes 9450000 | tf_op jit(solution)/shard_map/pallas_call | solution.py:283
  108.6 1.2 collective-permute-done.33
  110.8 3.8 %collective-permute-done.28.refs_0_ = f32[64,1024]{1,0:T(8,128)S(1)} collective-permute-done((f32[64,1024]{1,0:T(8,128)S(1)}, f32[64,1024]{1,0:T(8,128)S(1)}, u32[]{:S(2)}, u32[]{:S(2)}) %collective-permute-start.28) | collective-permute-done | bytes 262176 | tf_op jit(solution)/shard_map/ppermute | solution.py:489
  115.1 1.4 collective-permute-start.35
  116.6 2.2 %collective-permute-done.35 = f32[8,32]{1,0:T(8,128)S(1)} collective-permute-done((f32[8,32]{1,0:T(8,128)S(1)}, f32[8,32]{1,0:T(8,128)S(1)}, u32[]{:S(2)}, u32[]{:S(2)}) %collective-permute-start.35) | collective-permute-done | bytes 1056 | tf_op jit(solution)/shard_map/ppermute | solution.py:421
  119.0 3.4 %collective-permute-done.36 = f32[8,32]{1,0:T(8,128)S(1)} collective-permute-done((f32[8,32]{1,0:T(8,128)S(1)}, f32[8,32]{1,0:T(8,128)S(1)}, u32[]{:S(2)}, u32[]{:S(2)}) %collective-permute-start.36) | collective-permute-done | bytes 1056 | tf_op jit(solution)/shard_map/ppermute | solution.py:421
  123.2 3.7 %collective-permute-done.37 = f32[8,32]{1,0:T(8,128)S(1)} collective-permute-done((f32[8,32]{1,0:T(8,128)S(1)}, f32[8,32]{1,0:T(8,128)S(1)}, u32[]{:S(2)}, u32[]{:S(2)}) %collective-permute-start.37) | collective-permute-done | bytes 1056 | tf_op jit(solution)/shard_map/ppermute | solution.py:421
  127.4 3.5 %shard_map.75.refs_2_ = f32[8192,128]{1,0:T(8,128)S(1)} custom-call(s32[8]{0:T(128)S(1)} %get-tuple-element.20.base_ref, s32[8192]{0:T(1024)S(1)} %copy-done, f32[64,1024]{1,0:T(8,128)S(1)} %pad_maximum_fusion.3.u_ref.refs_0_, f32[64,1024]{1,0:T(8,128)S(1)} %collective-permute-done.32.refs_1_), custom_call_target="tpu_custom_call" | custom-call | bytes 11900000 | tf_op jit(solution)/shard_map/pallas_call | solution.py:210
  130.9 3.5 %shard_map.76.refs_2_ = f32[8192,128]{1,0:T(8,128)S(1)} custom-call(s32[8]{0:T(128)S(1)} %get-tuple-element.20.base_ref, s32[8192]{0:T(1024)S(1)} %copy-done, f32[64,1024]{1,0:T(8,128)S(1)} %collective-permute-done.30.refs_0_, f32[64,1024]{1,0:T(8,128)S(1)} %collective-permute-done.31.refs_1_, ...), custom_call_target="tpu_custom_call", output_to_operand_aliasing={{}: (4, {})} | custom-call | bytes 11900000 | tf_op jit(solution)/shard_map/pallas_call | solution.py:210
  134.5 3.5 %shard_map.77.refs_2_ = f32[8192,128]{1,0:T(8,128)S(1)} custom-call(s32[8]{0:T(128)S(1)} %get-tuple-element.20.base_ref, s32[8192]{0:T(1024)S(1)} %copy-done, f32[64,1024]{1,0:T(8,128)S(1)} %collective-permute-done.28.refs_0_, f32[64,1024]{1,0:T(8,128)S(1)} %collective-permute-done.29.refs_1_, ...), custom_call_target="tpu_custom_call", output_to_operand_aliasing={{}: (4, {})} | custom-call | bytes 11900000 | tf_op jit(solution)/shard_map/pallas_call | solution.py:210
  138.0 3.5 %shard_map.78.w_ref = f32[8192,128]{1,0:T(8,128)S(1)} custom-call(s32[8]{0:T(128)S(1)} %get-tuple-element.20.base_ref, s32[8192]{0:T(1024)S(1)} %copy-done, f32[64,1024]{1,0:T(8,128)S(1)} %collective-permute-done.26.refs_0_, f32[64,1024]{1,0:T(8,128)S(1)} %collective-permute-done.27.refs_1_, ...), custom_call_target="tpu_custom_call", output_to_operand_aliasing={{}: (4, {})} | custom-call | bytes 11900000 | tf_op jit(solution)/shard_map/pallas_call | solution.py:210
  141.6 14.0 %shard_map.79 = f32[64,8192]{1,0:T(8,128)} custom-call(f32[32,32]{1,0:T(8,128)S(1)} %shard_map.74.inv_ref, f32[8192,128]{1,0:T(8,128)S(1)} %shard_map.78.w_ref), custom_call_target="tpu_custom_call" | custom-call | bytes 42000000 | tf_op jit(solution)/shard_map/pallas_call | solution.py:253
  (99 shorter events, 16.9 us)
Async XLA Ops:
  2.2 15.4 %copy-start.1 = (f32[2,32,8192]{2,1,0:T(8,128)S(1)}, f32[2,32,8192]{2,1,0:T(8,128)}, u32[]{:S(2)}) copy-start(f32[2,32,8192]{2,1,0:T(8,128)} %param.7) | copy-start | bytes 6291460
  17.0 1.5 collective-permute-start
  18.5 6.9 %collective-permute-start.1 = (f32[32,1024]{1,0:T(8,128)S(1)}, f32[32,1024]{1,0:T(8,128)S(1)}, u32[]{:S(2)}, u32[]{:S(2)}) collective-permute-start(f32[32,1024]{1,0:T(8,128)S(1)} %select_add_fusion), channel_id=1, source_target_pairs={{0,2},{1,3},{2,0},{3,1},{4,6},{5,7},{6,4},{7,5},{8,10},{9,11},{10,... | collective-permute-start | bytes 393224 | tf_op jit(solution)/shard_map/ppermute | solution.py:413
  21.4 8.1 %collective-permute-start.2 = (f32[32,1024]{1,0:T(8,128)S(1)}, f32[32,1024]{1,0:T(8,128)S(1)}, u32[]{:S(2)}, u32[]{:S(2)}) collective-permute-start(f32[32,1024]{1,0:T(8,128)S(1)} %select_add_fusion), channel_id=1, source_target_pairs={{0,4},{1,5},{2,6},{3,7},{4,0},{5,1},{6,2},{7,3},{8,12},{9,13},{10,... | collective-permute-start | bytes 393224 | tf_op jit(solution)/shard_map/ppermute | solution.py:413
  23.0 6.6 %collective-permute-start.3 = (f32[32,1024]{1,0:T(8,128)S(1)}, f32[32,1024]{1,0:T(8,128)S(1)}, u32[]{:S(2)}, u32[]{:S(2)}) collective-permute-start(f32[32,1024]{1,0:T(8,128)S(1)} %select_add_fusion), channel_id=1, source_target_pairs={{0,6},{1,7},{2,4},{3,5},{4,2},{5,3},{6,0},{7,1},{8,14},{9,15},{10,... | collective-permute-start | bytes 393224 | tf_op jit(solution)/shard_map/ppermute | solution.py:413
  29.6 4.2 %collective-permute-start.4 = (f32[32,1024]{1,0:T(8,128)S(1)}, f32[32,1024]{1,0:T(8,128)S(1)}, u32[]{:S(2)}, u32[]{:S(2)}) collective-permute-start(f32[32,1024]{1,0:T(8,128)S(1)} %add_add_fusion.1), channel_id=1, source_target_pairs={{0,1},{1,0},{2,3},{3,2},{4,5},{5,4},{6,7},{7,6},{8,9},{9,8},{10,11... | collective-permute-start | bytes 393224 | tf_op jit(solution)/shard_map/ppermute | solution.py:453
  35.6 4.6 %collective-permute-start.5 = (f32[16,1024]{1,0:T(8,128)S(1)}, f32[16,1024]{1,0:T(8,128)S(1)}, u32[]{:S(2)}, u32[]{:S(2)}) collective-permute-start(f32[16,1024]{1,0:T(8,128)S(1)} %get-tuple-element.40), channel_id=1, source_target_pairs={{0,8},{8,0},{16,24},{24,16},{1,9},{9,1},{17,25},{25,17},{2,10},{10... | collective-permute-start | bytes 196616 | tf_op jit(solution)/shard_map/ppermute | solution.py:399
  37.2 7.0 %collective-permute-start.6 = (f32[16,1024]{1,0:T(8,128)S(1)}, f32[16,1024]{1,0:T(8,128)S(1)}, u32[]{:S(2)}, u32[]{:S(2)}) collective-permute-start(f32[16,1024]{1,0:T(8,128)S(1)} %get-tuple-element.41), channel_id=1, source_target_pairs={{0,16},{8,24},{16,0},{24,8},{1,17},{9,25},{17,1},{25,9},{2,18},{10... | collective-permute-start | bytes 196616 | tf_op jit(solution)/shard_map/ppermute | solution.py:399
  39.8 6.1 %collective-permute-start.7 = (f32[16,1024]{1,0:T(8,128)S(1)}, f32[16,1024]{1,0:T(8,128)S(1)}, u32[]{:S(2)}, u32[]{:S(2)}) collective-permute-start(f32[16,1024]{1,0:T(8,128)S(1)} %get-tuple-element.42), channel_id=1, source_target_pairs={{0,24},{8,16},{16,8},{24,0},{1,25},{9,17},{17,9},{25,1},{2,26},{10... | collective-permute-start | bytes 196616 | tf_op jit(solution)/shard_map/ppermute | solution.py:399
  45.9 4.3 %collective-permute-start.10 = (f32[16,1024]{1,0:T(8,128)S(1)}, f32[16,1024]{1,0:T(8,128)S(1)}, u32[]{:S(2)}, u32[]{:S(2)}) collective-permute-start(f32[16,1024]{1,0:T(8,128)S(1)} %add_add_fusion.3), channel_id=1, source_target_pairs={{0,8},{8,0},{16,24},{24,16},{1,9},{9,1},{17,25},{25,17},{2,10},{10... | collective-permute-start | bytes 196616 | tf_op jit(solution)/shard_map/ppermute | solution.py:405
  47.3 6.6 %collective-permute-start.8 = (f32[16,1024]{1,0:T(8,128)S(1)}, f32[16,1024]{1,0:T(8,128)S(1)}, u32[]{:S(2)}, u32[]{:S(2)}) collective-permute-start(f32[16,1024]{1,0:T(8,128)S(1)} %add_add_fusion.3), channel_id=1, source_target_pairs={{0,24},{8,16},{16,8},{24,0},{1,25},{9,17},{17,9},{25,1},{2,26},{10... | collective-permute-start | bytes 196616 | tf_op jit(solution)/shard_map/ppermute | solution.py:405
  49.7 6.2 %collective-permute-start.9 = (f32[16,1024]{1,0:T(8,128)S(1)}, f32[16,1024]{1,0:T(8,128)S(1)}, u32[]{:S(2)}, u32[]{:S(2)}) collective-permute-start(f32[16,1024]{1,0:T(8,128)S(1)} %add_add_fusion.3), channel_id=1, source_target_pairs={{0,16},{8,24},{16,0},{24,8},{1,17},{9,25},{17,1},{25,9},{2,18},{10... | collective-permute-start | bytes 196616 | tf_op jit(solution)/shard_map/ppermute | solution.py:405
  59.0 1.5 collective-permute-start.11
  60.4 7.1 %collective-permute-start.12 = (f32[40,1024]{1,0:T(8,128)S(1)}, f32[40,1024]{1,0:T(8,128)S(1)}, u32[]{:S(2)}, u32[]{:S(2)}) collective-permute-start(f32[40,1024]{1,0:T(8,128)S(1)} %fusion.7), channel_id=1, source_target_pairs={{0,2},{1,3},{2,0},{3,1},{4,6},{5,7},{6,4},{7,5},{8,10},{9,11},{10,... | collective-permute-start | bytes 491528 | tf_op jit(solution)/shard_map/ppermute | solution.py:413
  61.7 7.8 %collective-permute-start.13 = (f32[40,1024]{1,0:T(8,128)S(1)}, f32[40,1024]{1,0:T(8,128)S(1)}, u32[]{:S(2)}, u32[]{:S(2)}) collective-permute-start(f32[40,1024]{1,0:T(8,128)S(1)} %fusion.7), channel_id=1, source_target_pairs={{0,4},{1,5},{2,6},{3,7},{4,0},{5,1},{6,2},{7,3},{8,12},{9,13},{10,... | collective-permute-start | bytes 491528 | tf_op jit(solution)/shard_map/ppermute | solution.py:413
  62.6 8.7 %collective-permute-start.14 = (f32[40,1024]{1,0:T(8,128)S(1)}, f32[40,1024]{1,0:T(8,128)S(1)}, u32[]{:S(2)}, u32[]{:S(2)}) collective-permute-start(f32[40,1024]{1,0:T(8,128)S(1)} %fusion.7), channel_id=1, source_target_pairs={{0,6},{1,7},{2,4},{3,5},{4,2},{5,3},{6,0},{7,1},{8,14},{9,15},{10,... | collective-permute-start | bytes 491528 | tf_op jit(solution)/shard_map/ppermute | solution.py:413
  71.3 1.4 collective-permute-start.15
  74.4 5.3 %collective-permute-start.16 = (f32[16,1024]{1,0:T(8,128)S(1)}, f32[16,1024]{1,0:T(8,128)S(1)}, u32[]{:S(2)}, u32[]{:S(2)}) collective-permute-start(f32[16,1024]{1,0:T(8,128)S(1)} %get-tuple-element.31), channel_id=1, source_target_pairs={{0,8},{8,0},{16,24},{24,16},{1,9},{9,1},{17,25},{25,17},{2,10},{10... | collective-permute-start | bytes 196616 | tf_op jit(solution)/shard_map/ppermute | solution.py:399
  74.5 7.9 %collective-permute-start.17 = (f32[16,1024]{1,0:T(8,128)S(1)}, f32[16,1024]{1,0:T(8,128)S(1)}, u32[]{:S(2)}, u32[]{:S(2)}) collective-permute-start(f32[16,1024]{1,0:T(8,128)S(1)} %get-tuple-element.32), channel_id=1, source_target_pairs={{0,16},{8,24},{16,0},{24,8},{1,17},{9,25},{17,1},{25,9},{2,18},{10... | collective-permute-start | bytes 196616 | tf_op jit(solution)/shard_map/ppermute | solution.py:399
  77.2 6.2 %collective-permute-start.18 = (f32[16,1024]{1,0:T(8,128)S(1)}, f32[16,1024]{1,0:T(8,128)S(1)}, u32[]{:S(2)}, u32[]{:S(2)}) collective-permute-start(f32[16,1024]{1,0:T(8,128)S(1)} %get-tuple-element.33), channel_id=1, source_target_pairs={{0,24},{8,16},{16,8},{24,0},{1,25},{9,17},{17,9},{25,1},{2,26},{10... | collective-permute-start | bytes 196616 | tf_op jit(solution)/shard_map/ppermute | solution.py:399
  83.4 8.5 %collective-permute-start.19 = (f32[16,1024]{1,0:T(8,128)S(1)}, f32[16,1024]{1,0:T(8,128)S(1)}, u32[]{:S(2)}, u32[]{:S(2)}) collective-permute-start(f32[16,1024]{1,0:T(8,128)S(1)} %add_add_fusion.2), channel_id=1, source_target_pairs={{0,24},{8,16},{16,8},{24,0},{1,25},{9,17},{17,9},{25,1},{2,26},{10... | collective-permute-start | bytes 196616 | tf_op jit(solution)/shard_map/ppermute | solution.py:405
  85.4 6.5 %collective-permute-start.20 = (f32[16,1024]{1,0:T(8,128)S(1)}, f32[16,1024]{1,0:T(8,128)S(1)}, u32[]{:S(2)}, u32[]{:S(2)}) collective-permute-start(f32[16,1024]{1,0:T(8,128)S(1)} %add_add_fusion.2), channel_id=1, source_target_pairs={{0,16},{8,24},{16,0},{24,8},{1,17},{9,25},{17,1},{25,9},{2,18},{10... | collective-permute-start | bytes 196616 | tf_op jit(solution)/shard_map/ppermute | solution.py:405
  86.1 5.8 %collective-permute-start.21 = (f32[16,1024]{1,0:T(8,128)S(1)}, f32[16,1024]{1,0:T(8,128)S(1)}, u32[]{:S(2)}, u32[]{:S(2)}) collective-permute-start(f32[16,1024]{1,0:T(8,128)S(1)} %add_add_fusion.2), channel_id=1, source_target_pairs={{0,8},{8,0},{16,24},{24,16},{1,9},{9,1},{17,25},{25,17},{2,10},{10... | collective-permute-start | bytes 196616 | tf_op jit(solution)/shard_map/ppermute | solution.py:405
  92.5 34.9 %copy-start = (s32[8192]{0:T(1024)S(1)}, s32[8192]{0:T(1024)}, u32[]{:S(2)}) copy-start(s32[8192]{0:T(1024)} %idx_ref.7) | copy-start | bytes 98308
  95.5 1.4 collective-permute-start.22
  97.0 5.9 %collective-permute-start.23 = (f32[72,128]{1,0:T(8,128)S(1)}, f32[72,128]{1,0:T(8,128)S(1)}, u32[]{:S(2)}, u32[]{:S(2)}) collective-permute-start(f32[72,128]{1,0:T(8,128)S(1)} %get-tuple-element.45), channel_id=1, source_target_pairs={{0,2},{1,3},{2,0},{3,1},{4,6},{5,7},{6,4},{7,5},{8,10},{9,11},{10,... | collective-permute-start | bytes 110600 | tf_op jit(solution)/shard_map/ppermute | solution.py:399
  97.9 6.2 %collective-permute-start.24 = (f32[72,128]{1,0:T(8,128)S(1)}, f32[72,128]{1,0:T(8,128)S(1)}, u32[]{:S(2)}, u32[]{:S(2)}) collective-permute-start(f32[72,128]{1,0:T(8,128)S(1)} %get-tuple-element.46), channel_id=1, source_target_pairs={{0,4},{1,5},{2,6},{3,7},{4,0},{5,1},{6,2},{7,3},{8,12},{9,13},{10,... | collective-permute-start | bytes 110600 | tf_op jit(solution)/shard_map/ppermute | solution.py:399
  99.4 5.3 %collective-permute-start.25 = (f32[72,128]{1,0:T(8,128)S(1)}, f32[72,128]{1,0:T(8,128)S(1)}, u32[]{:S(2)}, u32[]{:S(2)}) collective-permute-start(f32[72,128]{1,0:T(8,128)S(1)} %get-tuple-element.47), channel_id=1, source_target_pairs={{0,6},{1,7},{2,4},{3,5},{4,2},{5,3},{6,0},{7,1},{8,14},{9,15},{10,... | collective-permute-start | bytes 110600 | tf_op jit(solution)/shard_map/ppermute | solution.py:399
  100.6 9.7 %collective-permute-start.30 = (f32[64,1024]{1,0:T(8,128)S(1)}, f32[64,1024]{1,0:T(8,128)S(1)}, u32[]{:S(2)}, u32[]{:S(2)}) collective-permute-start(f32[64,1024]{1,0:T(8,128)S(1)} %pad_maximum_fusion.3.u_ref.refs_0_), channel_id=1, source_target_pairs={{0,2},{1,3},{2,0},{3,1},{4,6},{5,7},{6,4},{7,5},{8,10},{9,11},{10,... | collective-permute-start | bytes 786440 | tf_op jit(solution)/shard_map/ppermute | solution.py:489
  101.4 13.3 %collective-permute-start.28 = (f32[64,1024]{1,0:T(8,128)S(1)}, f32[64,1024]{1,0:T(8,128)S(1)}, u32[]{:S(2)}, u32[]{:S(2)}) collective-permute-start(f32[64,1024]{1,0:T(8,128)S(1)} %pad_maximum_fusion.3.u_ref.refs_0_), channel_id=1, source_target_pairs={{0,4},{1,5},{2,6},{3,7},{4,0},{5,1},{6,2},{7,3},{8,12},{9,13},{10,... | collective-permute-start | bytes 786440 | tf_op jit(solution)/shard_map/ppermute | solution.py:489
  102.9 11.7 %collective-permute-start.26 = (f32[64,1024]{1,0:T(8,128)S(1)}, f32[64,1024]{1,0:T(8,128)S(1)}, u32[]{:S(2)}, u32[]{:S(2)}) collective-permute-start(f32[64,1024]{1,0:T(8,128)S(1)} %pad_maximum_fusion.3.u_ref.refs_0_), channel_id=1, source_target_pairs={{0,6},{1,7},{2,4},{3,5},{4,2},{5,3},{6,0},{7,1},{8,14},{9,15},{10,... | collective-permute-start | bytes 786440 | tf_op jit(solution)/shard_map/ppermute | solution.py:489
  108.5 1.2 collective-permute-start.33
  109.7 5.4 %collective-permute-start.34 = (f32[8,32]{1,0:T(8,128)S(1)}, f32[8,32]{1,0:T(8,128)S(1)}, u32[]{:S(2)}, u32[]{:S(2)}) collective-permute-start(f32[8,32]{1,0:T(8,128)S(1)} %broadcast_add_fusion), channel_id=1, source_target_pairs={{0,2},{1,3},{2,0},{3,1},{4,6},{5,7},{6,4},{7,5},{8,10},{9,11},{10,... | collective-permute-start | bytes 3080 | tf_op jit(solution)/shard_map/ppermute | solution.py:421
  110.2 17.1 %collective-permute-start.32 = (f32[64,1024]{1,0:T(8,128)S(1)}, f32[64,1024]{1,0:T(8,128)S(1)}, u32[]{:S(2)}, u32[]{:S(2)}) collective-permute-start(f32[64,1024]{1,0:T(8,128)S(1)} %pad_maximum_fusion.3.u_ref.refs_0_), channel_id=1, source_target_pairs={{0,1},{1,0},{2,3},{3,2},{4,5},{5,4},{6,7},{7,6},{8,9},{9,8},{10,11... | collective-permute-start | bytes 786440 | tf_op jit(solution)/shard_map/ppermute | solution.py:488
  110.3 20.7 %collective-permute-start.31 = (f32[64,1024]{1,0:T(8,128)S(1)}, f32[64,1024]{1,0:T(8,128)S(1)}, u32[]{:S(2)}, u32[]{:S(2)}) collective-permute-start(f32[64,1024]{1,0:T(8,128)S(1)} %collective-permute-done.30.refs_0_), channel_id=1, source_target_pairs={{0,1},{1,0},{2,3},{3,2},{4,5},{5,4},{6,7},{7,6},{8,9},{9,8},{10,11... | collective-permute-start | bytes 786440 | tf_op jit(solution)/shard_map/ppermute | solution.py:492
  114.6 19.9 %collective-permute-start.29 = (f32[64,1024]{1,0:T(8,128)S(1)}, f32[64,1024]{1,0:T(8,128)S(1)}, u32[]{:S(2)}, u32[]{:S(2)}) collective-permute-start(f32[64,1024]{1,0:T(8,128)S(1)} %collective-permute-done.28.refs_0_), channel_id=1, source_target_pairs={{0,1},{1,0},{2,3},{3,2},{4,5},{5,4},{6,7},{7,6},{8,9},{9,8},{10,11... | collective-permute-start | bytes 786440 | tf_op jit(solution)/shard_map/ppermute | solution.py:492
  114.6 23.4 %collective-permute-start.27 = (f32[64,1024]{1,0:T(8,128)S(1)}, f32[64,1024]{1,0:T(8,128)S(1)}, u32[]{:S(2)}, u32[]{:S(2)}) collective-permute-start(f32[64,1024]{1,0:T(8,128)S(1)} %collective-permute-done.26.refs_0_), channel_id=1, source_target_pairs={{0,1},{1,0},{2,3},{3,2},{4,5},{5,4},{6,7},{7,6},{8,9},{9,8},{10,11... | collective-permute-start | bytes 786440 | tf_op jit(solution)/shard_map/ppermute | solution.py:492
  115.1 3.6 %collective-permute-start.35 = (f32[8,32]{1,0:T(8,128)S(1)}, f32[8,32]{1,0:T(8,128)S(1)}, u32[]{:S(2)}, u32[]{:S(2)}) collective-permute-start(f32[8,32]{1,0:T(8,128)S(1)} %fusion.33), channel_id=1, source_target_pairs={{0,4},{1,5},{2,6},{3,7},{4,0},{5,1},{6,2},{7,3},{8,12},{9,13},{10,... | collective-permute-start | bytes 3080 | tf_op jit(solution)/shard_map/ppermute | solution.py:421
  118.7 3.6 %collective-permute-start.36 = (f32[8,32]{1,0:T(8,128)S(1)}, f32[8,32]{1,0:T(8,128)S(1)}, u32[]{:S(2)}, u32[]{:S(2)}) collective-permute-start(f32[8,32]{1,0:T(8,128)S(1)} %add.107), channel_id=1, source_target_pairs={{0,8},{8,0},{16,24},{24,16},{1,9},{9,1},{17,25},{25,17},{2,10},{10... | collective-permute-start | bytes 3080 | tf_op jit(solution)/shard_map/ppermute | solution.py:421
  122.4 4.5 %collective-permute-start.37 = (f32[8,32]{1,0:T(8,128)S(1)}, f32[8,32]{1,0:T(8,128)S(1)}, u32[]{:S(2)}, u32[]{:S(2)}) collective-permute-start(f32[8,32]{1,0:T(8,128)S(1)} %add.108), channel_id=1, source_target_pairs={{0,16},{8,24},{16,0},{24,8},{1,17},{9,25},{17,1},{25,9},{2,18},{10... | collective-permute-start | bytes 3080 | tf_op jit(solution)/shard_map/ppermute | solution.py:421

commit v4 on v3

--- a/solution.py
+++ b/solution.py
@@ -11,6 +11,7 @@
 HB = 128
 ITERS = 2
 BLOCK = 256
+HW = 256
 F32 = jnp.float32
 BF16 = jnp.bfloat16
 
@@ -49,7 +50,7 @@
     return (1 - 2 * (parity & 1)).astype(F32)
 
 
-def butterfly(ref, count):
+def butterfly(ref, count, width):
     rows = ref.shape[0]
     step = 1
     while step < count:
@@ -58,17 +59,20 @@
         def body(g, carry, step=step, radix=radix):
             base = (g // step) * (step * radix) + g % step
             for s in range(rows // 8):
-                at = [pl.multiple_of((base + r * step) * HB, HB) for r in range(radix)]
-                v = [ref[s * 8 : s * 8 + 8, pl.ds(a, HB)] for a in at]
-                half = 1
-                while half < radix:
-                    v = [
-                        v[r] + v[r + half] if not r & half else v[r - half] - v[r]
-                        for r in range(radix)
+                for lane in range(0, width, HB):
+                    at = [
+                        pl.multiple_of((base + r * step) * width + lane, HB) for r in range(radix)
                     ]
-                    half *= 2
-                for a, x in zip(at, v):
-                    ref[s * 8 : s * 8 + 8, pl.ds(a, HB)] = x
+                    v = [ref[s * 8 : s * 8 + 8, pl.ds(a, HB)] for a in at]
+                    half = 1
+                    while half < radix:
+                        v = [
+                            v[r] + v[r + half] if not r & half else v[r - half] - v[r]
+                            for r in range(radix)
+                        ]
+                        half *= 2
+                    for a, x in zip(at, v):
+                        ref[s * 8 : s * 8 + 8, pl.ds(a, HB)] = x
             return carry
 
         lax.fori_loop(0, count // radix, body, 0)
@@ -87,13 +91,15 @@
 
 
 def start_kernel(
-    scale, here_ref, idx_ref, at_ref, probes_ref, frames_ref,
-    dh_ref, dl_ref, img_ref, mask_ref, base_ref, f_ref, w_ref, n_ref, g_ref, b_ref, t_ref, sems,
+    scale, steps_ref, idx_ref, probes_ref, frames_ref,
+    dh_ref, dl_ref, img_ref, mask_ref, base_ref, f_ref, w_ref, n_ref, g_ref, b_ref, t_ref, sems, sem,
 ):
     vectors, modes = probes_ref.shape
-    rows, count = frames_ref.shape[1:]
-    outer = modes // HB
+    steps, rows, count = frames_ref.shape
+    outer = modes // HW
     block = min(BLOCK, rows)
+    first = pltpu.make_async_copy(probes_ref, w_ref, sem)
+    first.start()
     copies = [
         [
             pltpu.make_async_copy(
@@ -101,51 +107,51 @@
                 f_ref.at[s, pl.ds(i * block, block)],
                 sems.at[s, i],
             )
-            for s in range(frames_ref.shape[0])
+            for s in range(steps)
         ]
         for i in range(rows // block)
     ]
     for row in copies:
         for c in row:
             c.start()
+    here = (lax.axis_index("mode"), lax.axis_index("pix"))
     for b in range(4):
-        for place, axis_row in ((here_ref[0], 0), (here_ref[1], 4)):
+        for place, axis_row in ((here[0], 0), (here[1], 4)):
             bit = ((place >> b) & 1).astype(F32)
             mask_ref[axis_row + b : axis_row + b + 1, :] = jnp.full((1, HB), bit, F32)
     for b in range(base_ref.shape[0]):
-        base_ref[b] = (here_ref[0] ^ b) * count
-    signs = sign_table(HB).astype(BF16)
+        base_ref[b] = (here[0] ^ b) * count
+    signs = sign_table(HW).astype(BF16)
+    first.wait()
+    butterfly(w_ref, outer, HW)
 
     def inner(i):
-        at = pl.multiple_of(i * HB, HB)
-        both = dot(jnp.concatenate(split(probes_ref[:, pl.ds(at, HB)]), axis=0), signs, NN)
-        w_ref[:, pl.ds(at, HB)] = both[:vectors] + both[vectors:]
+        at = pl.multiple_of(i * HW, HW)
+        both = jnp.concatenate(split(w_ref[:, pl.ds(at, HW)]), axis=0)
+        n_ref[pl.ds(at, HW), :] = dot(signs, both, NT)
 
     block_loop(outer, 8, inner)
-    butterfly(w_ref, outer)
-
-    def turn(i):
-        at = pl.multiple_of(i * HB, HB)
-        here = w_ref[:, pl.ds(at, HB)]
-        n_ref[pl.ds(at, HB), :] = jnp.concatenate([here, here], axis=0).T
-
-    block_loop(outer, 8, turn)
+    start_at = here[0] * count
 
     def gather(t, carry):
-        at = pl.multiple_of(t * 8, 8)
-        for q in range(8):
-            g_ref[pl.ds(at + q, 1), :] = n_ref[pl.ds(idx_ref[at + q], 1), :]
+        at = pl.multiple_of(t * 32, 32)
+        for q in range(32):
+            g_ref[pl.ds(at + q, 1), :] = n_ref[pl.ds(idx_ref[start_at + at + q], 1), :]
         return carry
 
-    lax.fori_loop(0, count // 8, gather, 0)
-    parts = [g_ref[b * HB : (b + 1) * HB, :].T[:vectors] for b in range(count // HB)]
+    lax.fori_loop(0, count // 32, gather, 0)
+    parts = [g_ref[b * HB : (b + 1) * HB, :].T for b in range(count // HB)]
+    parts = [p[:vectors] + p[vectors:] for p in parts]
     b_ref[...], t_ref[...] = stack_forward(jnp.concatenate(parts, axis=1) * scale)
+    frame = [
+        sum(jnp.where(steps_ref[f] == s, f, 0) for f in range(1, steps)) for s in range(steps)
+    ]
     for i, row in enumerate(copies):
         for c in row:
             c.wait()
         span = slice(i * block, (i + 1) * block)
         for part in (0, 1):
-            high, low = split(0.25 * (f_ref[at_ref[part], span] - f_ref[at_ref[part + 2], span]))
+            high, low = split(0.25 * (f_ref[frame[part], span] - f_ref[frame[part + 2], span]))
             dh_ref[part, span] = high
             dl_ref[part, span] = low
         img_ref[:, span] = apply_forward(b_ref[...], t_ref[...], dh_ref, dl_ref, span)
@@ -155,10 +161,11 @@
     return pl.CostEstimate(flops=0, transcendentals=0, bytes_accessed=int(us * 3.5e6))
 
 
-def start(here, idx, steps_at, probes, frames, scale):
+def start(phase_steps, idx, probes, frames, scale):
     vectors, modes = probes.shape
     steps, rows, count = frames.shape
     planes = pltpu.VMEM((2, rows, count), BF16)
+    hbm = pl.BlockSpec(memory_space=pltpu.HBM)
     return pl.pallas_call(
         functools.partial(start_kernel, scale),
         out_shape=[
@@ -168,7 +175,7 @@
             jax.ShapeDtypeStruct((8, HB), F32),
             jax.ShapeDtypeStruct((modes // count,), jnp.int32),
         ],
-        in_specs=[SMEM, SMEM, SMEM, VMEM, pl.BlockSpec(memory_space=pltpu.HBM)],
+        in_specs=[SMEM, SMEM, hbm, hbm],
         out_specs=[VMEM, VMEM, VMEM, VMEM, SMEM],
         cost_estimate=cost(12),
         scratch_shapes=[
@@ -179,9 +186,10 @@
             pltpu.VMEM((2 * vectors, count), BF16),
             pltpu.VMEM((2 * vectors, count), BF16),
             pltpu.SemaphoreType.DMA((steps, rows // min(BLOCK, rows))),
+            pltpu.SemaphoreType.DMA,
         ],
         compiler_params=pltpu.CompilerParams(vmem_limit_bytes=44 << 20),
-    )(here, idx, steps_at, probes, frames)
+    )(phase_steps, idx, probes, frames)
 
 
 def scatter_kernel(places, base_ref, idx_ref, *refs):
@@ -196,12 +204,12 @@
         base = base_ref[places[p]]
 
         def move(t, carry, base=base):
-            at = pl.multiple_of(t * 16, 16)
-            for q in range(16):
+            at = pl.multiple_of(t * 32, 32)
+            for q in range(32):
                 w_ref[pl.ds(idx_ref[base + at + q], 1), :] = s_ref[pl.ds(at + q, 1), :]
             return carry
 
-        lax.fori_loop(0, count // 16, move, 0)
+        lax.fori_loop(0, count // 32, move, 0)
 
 
 def scatter_rows(places, bases, idx, pieces, table=None):
@@ -222,8 +230,8 @@
 def end_kernel(inv_ref, w_ref, out_ref):
     vectors, modes = out_ref.shape
     half = vectors // 2
-    outer = modes // HB
-    signs = sign_table(HB).astype(BF16)
+    outer = modes // HW
+    signs = sign_table(HW).astype(BF16)
     zero = jnp.zeros((half, half), F32)
     wide = jnp.concatenate(
         [jnp.concatenate([inv_ref[...], zero], 1), jnp.concatenate([zero, inv_ref[...]], 1)], 0
@@ -234,17 +242,17 @@
     )
 
     def first(i):
-        at = pl.multiple_of(i * HB, HB)
-        both = dot(mix, w_ref[pl.ds(at, HB), :].astype(BF16), NT)
-        out_ref[:, pl.ds(at, HB)] = both[:vectors] + both[vectors:]
+        at = pl.multiple_of(i * HW, HW)
+        both = dot(mix, w_ref[pl.ds(at, HW), :].astype(BF16), NT)
+        out_ref[:, pl.ds(at, HW)] = both[:vectors] + both[vectors:]
 
     block_loop(outer, 8, first)
-    butterfly(out_ref, outer)
+    butterfly(out_ref, outer, HW)
 
     def inner(i):
-        at = pl.multiple_of(i * HB, HB)
-        both = dot(jnp.concatenate(split(out_ref[:, pl.ds(at, HB)]), axis=0), signs, NN)
-        out_ref[:, pl.ds(at, HB)] = both[:vectors] + both[vectors:]
+        at = pl.multiple_of(i * HW, HW)
+        both = dot(jnp.concatenate(split(out_ref[:, pl.ds(at, HW)]), axis=0), signs, NN)
+        out_ref[:, pl.ds(at, HW)] = both[:vectors] + both[vectors:]
 
     block_loop(outer, 8, inner)
 
@@ -345,7 +353,7 @@
 def backward_kernel(*refs):
     inv_ref = refs[0] if len(refs) == 5 else None
     img_ref, dh_ref, dl_ref, ret_ref = refs[-4:]
-    vectors, rows = img_ref.shape
+    vectors, _ = img_ref.shape
     half = vectors // 2
     real, imag = img_ref[:half], img_ref[half:]
     if inv_ref is not None:
@@ -395,21 +403,23 @@
     size = lax.axis_size(axis)
     mine = pick(blocks, odds)
     total = mine[0]
-    for b in range(1, len(blocks)):
+    for b in range(len(blocks) - 1, 0, -1):
         total = total + lax.ppermute(mine[b], axis, flip(size, b * step))
     return total
 
 
 def gather_all(block, axis, step, odds):
     size = lax.axis_size(axis)
-    far = [lax.ppermute(block, axis, flip(size, b * step)) for b in range(1, 2 ** len(odds))]
-    return pick([block] + far, odds)
+    far = [block]
+    for b in range(1, 2 ** len(odds)):
+        far.append(lax.ppermute(block, axis, flip(size, b * step)))
+    return pick(far, odds)
 
 
 def share_sum(block, axis, step, n):
     size = lax.axis_size(axis)
     total = block
-    for b in range(1, n):
+    for b in range(n - 1, 0, -1):
         total = total + lax.ppermute(block, axis, flip(size, b * step))
     return total
 
@@ -429,7 +439,8 @@
         return double_sum(x, "pix")
     rows = x.shape[0] // n
     odds = odds[4:6]
-    mine = scatter_sum([x[i * rows : (i + 1) * rows] for i in range(n)], "pix", 1, odds)
+    blocks = [x[i * rows : (i + 1) * rows] for i in range(n)]
+    mine = scatter_sum(blocks, "pix", 1, odds)
     return jnp.concatenate(gather_all(mine, "pix", 1, odds), axis=0)
 
 
@@ -437,7 +448,8 @@
     n = lax.axis_size("mode")
     rows, cols = x.shape
     if n != 8:
-        return double_sum(x, "mode"), (None if extra is None else double_sum(extra, "mode"))
+        small = None if extra is None else double_sum(extra, "mode")
+        return double_sum(x, "mode"), small
     half = rows // 2
     odd = odds[0]
     mine = jnp.where(odd, x[half:], x[:half])
@@ -456,7 +468,7 @@
 
 
 def scatter_mode(pieces, odds, extra):
-    places, rows, width = pieces.shape
+    _, rows, width = pieces.shape
     n = lax.axis_size("mode")
     here = lax.axis_index("mode")
     if n != 8:
@@ -485,16 +497,17 @@
             pieces = pieces + [lax.ppermute(p, "mode", flip(n, bit)) for p in pieces]
             bit *= 2
         return scatter_rows(range(n), bases, idx, pieces)
-    near = lax.ppermute(block, "mode", flip(n, 1))
-    far = {b: lax.ppermute(block, "mode", flip(n, b)) for b in (2, 4, 6)}
-    table = scatter_rows((0, 1), bases, idx, [block, near])
+    got = {}
+    for b in (6, 4, 2, 1):
+        got[b] = lax.ppermute(block, "mode", flip(n, b))
+    table = scatter_rows((0, 1), bases, idx, [block, got[1]])
     for b in (2, 4, 6):
-        other = lax.ppermute(far[b], "mode", flip(n, 1))
-        table = scatter_rows((b, b ^ 1), bases, idx, [far[b], other], table)
+        other = lax.ppermute(got[b], "mode", flip(n, 1))
+        table = scatter_rows((b, b ^ 1), bases, idx, [got[b], other], table)
     return table
 
 
-def local(frames, phase_steps, pattern_rows, probes):
+def measure(frames, phase_steps, pattern_rows, probes):
     columns = frames.shape[2]
     rows = frames.shape[1]
     groups = lax.axis_size("mode")
@@ -503,22 +516,19 @@
     k = probes.shape[1]
     vectors = 2 * k
     probes = probes.reshape(vectors, modes_total)
-    here = jnp.stack([lax.axis_index("mode"), lax.axis_index("pix")]).astype(jnp.int32)
-    steps_at = jnp.sum(
-        jnp.where(phase_steps[None, :] == jnp.arange(4)[:, None], jnp.arange(4)[None, :], 0), axis=1
-    ).astype(jnp.int32)
-    my_rows = lax.dynamic_slice_in_dim(pattern_rows, lax.axis_index("mode") * columns, columns)
     scale = 1.0 / math.sqrt(modes_total)
-    dh, dl, images, masks, bases = start(here, my_rows, steps_at, probes, frames, scale)
+    dh, dl, images, masks, bases = start(phase_steps, pattern_rows, probes, frames, scale)
     odds = [masks[b : b + 1, :1] != 0 for b in range(8)]
     inv = inverse_factor(pack(gram(probes)), k)
     images, _ = sum_mode(images, odds)
-    returned = sum_pix(backward(inv, images, dh, dl), odds)
-    for iteration in range(1, ITERS):
+    partial = backward(inv, images, dh, dl)
+    returned = sum_pix(partial, odds)
+    for _ in range(1, ITERS):
         images, packed = forward(returned, dh, dl)
         images, packed = sum_mode(images, odds, packed)
         inv = inverse_factor(packed, k)
-        returned = normalise(inv, sum_pix(backward(None, images, dh, dl), odds))
+        partial = backward(None, images, dh, dl)
+        returned = normalise(inv, sum_pix(partial, odds))
     table = gather_rows(returned, bases, pattern_rows)
     images, packed = forward(returned, dh, dl, groups)
     fields, packed = scatter_mode(images, odds, packed)
@@ -535,4 +545,6 @@
 def solution(mesh):
     in_specs = (P(None, "pix", "mode"), P(), P(), P())
     out_specs = (P(), P(None, None, ("pix", "mode")), P())
-    return jax.shard_map(local, mesh=mesh, in_specs=in_specs, out_specs=out_specs, check_vma=False)
+    return jax.shard_map(
+        measure, mesh=mesh, in_specs=in_specs, out_specs=out_specs, check_vma=False
+    )

time: 156 us -> 153 us (0.981)
  Pallas kernels: 59.1 us -> 56.8 us
    pallas_call x1, Pallas kernels: 14 us -> 9.33 us  [end_vectors(): pl.pallas_call(end_kernel, cost_estimate=cost(12), out_shape=jax.ShapeDty...]
    pallas_call x1, Pallas kernels: 13.6 us -> 17.2 us  [start(): pl.pallas_call(functools.partial(start_kernel, scale), out_shape=[planes,...]
  transfers between devices with their start and end apart: 38 -> 38, of which waited for: 23 -> 22; matrix products, arithmetic and copies ran while one was open for 2% -> 2% of each run, Pallas kernels for 12% -> 12%
where the time goes in v4:
time: 153 us; the launch traced here: 152 us
  Pallas kernels  56.8 us (37%)
  waiting for transfers between devices  48 us (31%)
  starting transfers between devices  36.5 us (24%)
  between operations  4.29 us (3%)
  matrix products  2.74 us (2%)
  local copies, waits for them, and re-layouts  2.03 us (1%)
  other arithmetic  1.96 us (1%)
    pallas_call x1, Pallas kernels, start(): pl.pallas_call(functools.partial(start_kernel, scale), out_shape=[planes,...  17.2 us
    pallas_call x4, Pallas kernels, scatter_rows(): pl.pallas_call(functools.partial(scatter_kernel, places), cost_estimate=c...  12.8 us
    ppermute x9, starting transfers between devices, scatter_sum(): total = total + lax.ppermute(mine[b], axis, flip(size, b * step))  12.5 us
    ppermute x6, waiting for transfers between devices, share_sum(): total = total + lax.ppermute(block, axis, flip(size, b * step))  12.4 us
    ppermute x5, waiting for transfers between devices, double_sum(): block = block + lax.ppermute(block, axis, flip(size, bit))  11.1 us
    ppermute x9, waiting for transfers between devices, scatter_sum(): total = total + lax.ppermute(mine[b], axis, flip(size, b * step))  10 us
    pallas_call x1, Pallas kernels, end_vectors(): pl.pallas_call(end_kernel, cost_estimate=cost(12), out_shape=jax.ShapeDty...  9.33 us
    pallas_call x3, Pallas kernels, inverse_factor(): pl.pallas_call(factor_kernel, cost_estimate=cost(2.7), out_shape=jax.Shap...  8.27 us
  transfers between devices with their start and end apart: 38, of which 22 were waited for; matrix products, arithmetic and copies ran while one was open for 2% of the time, Pallas kernels for 12%

profile of v4, /device:TPU:0, one launch (start us, length us, event | category | flops | bytes accessed | tf_op | source)
XLA Modules:
  0.0 152.3 jit_solution(214593228610597094)
XLA Ops:
  2.0 17.2 %shard_map.67 = (bf16[2,1024,1024]{2,1,0:T(8,128)(2,1)S(1)}, bf16[2,1024,1024]{2,1,0:T(8,128)(2,1)S(1)}, f32[64,1024]{1,0:T(8,128)S(1)}, f32[8,128]{1,0:T(8,128)S(1)}, s32[8]{0:T(128)S(1)}) custom-call(s32[4]{0:T(128)S(1)} %copy-done.1, s32[8192]{0:T(1024)S(1)} %copy-done, f32[64,8192]{1,0:T(8,128)} %bitcast.36, f32[4,1024,1024]{2,1,0:T(8,128)} %frames_ref.1), custom_call_target="tpu_custom_call" | custom-call | bytes 42000000 | tf_op jit(solution)/shard_map/pallas_call | solution.py:169
  21.1 1.0 fusion.1
  22.1 3.9 %collective-permute-start.1 = (f32[32,1024]{1,0:T(8,128)S(1)}, f32[32,1024]{1,0:T(8,128)S(1)}, u32[]{:S(2)}, u32[]{:S(2)}) collective-permute-start(f32[32,1024]{1,0:T(8,128)S(1)} %select_add_fusion), channel_id=1, source_target_pairs={{0,6},{1,7},{2,4},{3,5},{4,2},{5,3},{6,0},{7,1},{8,14},{9,15},{10,... | collective-permute-start | bytes 393224 | tf_op jit(solution)/shard_map/ppermute | solution.py:423
  26.6 1.0 convolution_add_fusion
  27.6 2.3 %collective-permute-done.1 = f32[32,1024]{1,0:T(8,128)S(1)} collective-permute-done((f32[32,1024]{1,0:T(8,128)S(1)}, f32[32,1024]{1,0:T(8,128)S(1)}, u32[]{:S(2)}, u32[]{:S(2)}) %collective-permute-start.1) | collective-permute-done | bytes 131104 | tf_op jit(solution)/shard_map/ppermute | solution.py:423
  30.0 2.6 %collective-permute-done.2 = f32[32,1024]{1,0:T(8,128)S(1)} collective-permute-done((f32[32,1024]{1,0:T(8,128)S(1)}, f32[32,1024]{1,0:T(8,128)S(1)}, u32[]{:S(2)}, u32[]{:S(2)}) %collective-permute-start.2) | collective-permute-done | bytes 131104 | tf_op jit(solution)/shard_map/ppermute | solution.py:423
  33.1 2.8 %shard_map.68.refs_0_ = f32[32,32]{1,0:T(8,128)S(1)} custom-call(f32[8,128]{1,0:T(8,128)S(1)} %pad_maximum_fusion.9.g_ref), custom_call_target="tpu_custom_call" | custom-call | bytes 9450000 | tf_op jit(solution)/shard_map/pallas_call | solution.py:291
  37.2 1.7 %shard_map.69 = f32[64,1024]{1,0:T(8,128)S(1)} custom-call(f32[32,32]{1,0:T(8,128)S(1)} %shard_map.68.refs_0_, f32[64,1024]{1,0:T(8,128)S(1)} %pad_maximum_fusion.refs_1_, bf16[2,1024,1024]{2,1,0:T(8,128)(2,1)S(1)} %get-tuple-element.14.refs_2_.dh_ref.refs_1_, bf16[2,1024,1024]{2,1,0:T(8,128)(2,1)S(1)} %get-tuple-element.15.refs_3_.dl_ref.refs_2_), custom_call_target="tpu_custom_call" | custom-call | bytes 5600000 | tf_op jit(solution)/shard_map/pallas_call | solution.py:377
  39.0 3.7 %collective-permute-start.5 = (f32[16,1024]{1,0:T(8,128)S(1)}, f32[16,1024]{1,0:T(8,128)S(1)}, u32[]{:S(2)}, u32[]{:S(2)}) collective-permute-start(f32[16,1024]{1,0:T(8,128)S(1)} %get-tuple-element.40), channel_id=1, source_target_pairs={{0,24},{8,16},{16,8},{24,0},{1,25},{9,17},{17,9},{25,1},{2,26},{10... | collective-permute-start | bytes 196616 | tf_op jit(solution)/shard_map/ppermute | solution.py:407
  43.4 2.2 %collective-permute-done.5 = f32[16,1024]{1,0:T(8,128)S(1)} collective-permute-done((f32[16,1024]{1,0:T(8,128)S(1)}, f32[16,1024]{1,0:T(8,128)S(1)}, u32[]{:S(2)}, u32[]{:S(2)}) %collective-permute-start.5) | collective-permute-done | bytes 65568 | tf_op jit(solution)/shard_map/ppermute | solution.py:407
  45.6 3.1 %collective-permute-done.6 = f32[16,1024]{1,0:T(8,128)S(1)} collective-permute-done((f32[16,1024]{1,0:T(8,128)S(1)}, f32[16,1024]{1,0:T(8,128)S(1)}, u32[]{:S(2)}, u32[]{:S(2)}) %collective-permute-start.6) | collective-permute-done | bytes 65568 | tf_op jit(solution)/shard_map/ppermute | solution.py:407
  48.8 1.3 collective-permute-start.10
  50.1 1.4 collective-permute-start.8
  53.1 3.0 %collective-permute-done.8 = f32[16,1024]{1,0:T(8,128)S(1)} collective-permute-done((f32[16,1024]{1,0:T(8,128)S(1)}, f32[16,1024]{1,0:T(8,128)S(1)}, u32[]{:S(2)}, u32[]{:S(2)}) %collective-permute-start.8) | collective-permute-done | bytes 65568 | tf_op jit(solution)/shard_map/ppermute | solution.py:415
  56.2 2.6 %collective-permute-done.9 = f32[16,1024]{1,0:T(8,128)S(1)} collective-permute-done((f32[16,1024]{1,0:T(8,128)S(1)}, f32[16,1024]{1,0:T(8,128)S(1)}, u32[]{:S(2)}, u32[]{:S(2)}) %collective-permute-start.9) | collective-permute-done | bytes 65568 | tf_op jit(solution)/shard_map/ppermute | solution.py:415
  58.8 2.9 %shard_map.70 = (f32[64,1024]{1,0:T(8,128)S(1)}, f32[8,128]{1,0:T(8,128)S(1)}) custom-call(f32[64,1024]{1,0:T(8,128)S(1)} %pad_maximum_fusion.1.u_ref, bf16[2,1024,1024]{2,1,0:T(8,128)(2,1)S(1)} %get-tuple-element.14.refs_2_.dh_ref.refs_1_, bf16[2,1024,1024]{2,1,0:T(8,128)(2,1)S(1)} %get-tuple-element.15.refs_3_.dl_ref.refs_2_), custom_call_target="tpu_custom_call" | custom-call | bytes 9450000 | tf_op jit(solution)/shard_map/pallas_call | solution.py:340
  61.9 1.4 collective-permute-done.11
  63.3 1.7 %collective-permute-start.12 = (f32[40,1024]{1,0:T(8,128)S(1)}, f32[40,1024]{1,0:T(8,128)S(1)}, u32[]{:S(2)}, u32[]{:S(2)}) collective-permute-start(f32[40,1024]{1,0:T(8,128)S(1)} %fusion.7), channel_id=1, source_target_pairs={{0,6},{1,7},{2,4},{3,5},{4,2},{5,3},{6,0},{7,1},{8,14},{9,15},{10,... | collective-permute-start | bytes 491528 | tf_op jit(solution)/shard_map/ppermute | solution.py:423
  65.0 1.3 collective-permute-start.13
  66.8 4.5 %collective-permute-done.12 = f32[40,1024]{1,0:T(8,128)S(1)} collective-permute-done((f32[40,1024]{1,0:T(8,128)S(1)}, f32[40,1024]{1,0:T(8,128)S(1)}, u32[]{:S(2)}, u32[]{:S(2)}) %collective-permute-start.12) | collective-permute-done | bytes 163872 | tf_op jit(solution)/shard_map/ppermute | solution.py:423
  71.3 2.6 %collective-permute-done.13 = f32[40,1024]{1,0:T(8,128)S(1)} collective-permute-done((f32[40,1024]{1,0:T(8,128)S(1)}, f32[40,1024]{1,0:T(8,128)S(1)}, u32[]{:S(2)}, u32[]{:S(2)}) %collective-permute-start.13) | collective-permute-done | bytes 163872 | tf_op jit(solution)/shard_map/ppermute | solution.py:423
  74.1 1.3 collective-permute-done.15
  75.5 1.6 %shard_map.72 = f32[64,1024]{1,0:T(8,128)S(1)} custom-call(f32[64,1024]{1,0:T(8,128)S(1)} %pad_maximum_fusion.2.refs_0_, bf16[2,1024,1024]{2,1,0:T(8,128)(2,1)S(1)} %get-tuple-element.14.refs_2_.dh_ref.refs_1_, bf16[2,1024,1024]{2,1,0:T(8,128)(2,1)S(1)} %get-tuple-element.15.refs_3_.dl_ref.refs_2_), custom_call_target="tpu_custom_call" | custom-call | bytes 5600000 | tf_op jit(solution)/shard_map/pallas_call | solution.py:377
  77.2 2.2 %collective-permute-start.16 = (f32[16,1024]{1,0:T(8,128)S(1)}, f32[16,1024]{1,0:T(8,128)S(1)}, u32[]{:S(2)}, u32[]{:S(2)}) collective-permute-start(f32[16,1024]{1,0:T(8,128)S(1)} %get-tuple-element.31), channel_id=1, source_target_pairs={{0,24},{8,16},{16,8},{24,0},{1,25},{9,17},{17,9},{25,1},{2,26},{10... | collective-permute-start | bytes 196616 | tf_op jit(solution)/shard_map/ppermute | solution.py:407
  79.4 2.2 %collective-permute-start.18 = (f32[16,1024]{1,0:T(8,128)S(1)}, f32[16,1024]{1,0:T(8,128)S(1)}, u32[]{:S(2)}, u32[]{:S(2)}) collective-permute-start(f32[16,1024]{1,0:T(8,128)S(1)} %get-tuple-element.33), channel_id=1, source_target_pairs={{0,8},{8,0},{16,24},{24,16},{1,9},{9,1},{17,25},{25,17},{2,10},{10... | collective-permute-start | bytes 196616 | tf_op jit(solution)/shard_map/ppermute | solution.py:407
  81.7 2.4 %collective-permute-done.16 = f32[16,1024]{1,0:T(8,128)S(1)} collective-permute-done((f32[16,1024]{1,0:T(8,128)S(1)}, f32[16,1024]{1,0:T(8,128)S(1)}, u32[]{:S(2)}, u32[]{:S(2)}) %collective-permute-start.16) | collective-permute-done | bytes 65568 | tf_op jit(solution)/shard_map/ppermute | solution.py:407
  84.0 2.0 %collective-permute-done.17 = f32[16,1024]{1,0:T(8,128)S(1)} collective-permute-done((f32[16,1024]{1,0:T(8,128)S(1)}, f32[16,1024]{1,0:T(8,128)S(1)}, u32[]{:S(2)}, u32[]{:S(2)}) %collective-permute-start.17) | collective-permute-done | bytes 65568 | tf_op jit(solution)/shard_map/ppermute | solution.py:407
  86.1 2.2 %collective-permute-start.19 = (f32[16,1024]{1,0:T(8,128)S(1)}, f32[16,1024]{1,0:T(8,128)S(1)}, u32[]{:S(2)}, u32[]{:S(2)}) collective-permute-start(f32[16,1024]{1,0:T(8,128)S(1)} %add_add_fusion.2), channel_id=1, source_target_pairs={{0,24},{8,16},{16,8},{24,0},{1,25},{9,17},{17,9},{25,1},{2,26},{10... | collective-permute-start | bytes 196616 | tf_op jit(solution)/shard_map/ppermute | solution.py:415
  88.3 2.2 %collective-permute-start.21 = (f32[16,1024]{1,0:T(8,128)S(1)}, f32[16,1024]{1,0:T(8,128)S(1)}, u32[]{:S(2)}, u32[]{:S(2)}) collective-permute-start(f32[16,1024]{1,0:T(8,128)S(1)} %add_add_fusion.2), channel_id=1, source_target_pairs={{0,8},{8,0},{16,24},{24,16},{1,9},{9,1},{17,25},{25,17},{2,10},{10... | collective-permute-start | bytes 196616 | tf_op jit(solution)/shard_map/ppermute | solution.py:415
  91.8 2.8 %shard_map.71 = f32[32,32]{1,0:T(8,128)S(1)} custom-call(f32[8,128]{1,0:T(8,128)S(1)} %slice.217.g_ref), custom_call_target="tpu_custom_call" | custom-call | bytes 9450000 | tf_op jit(solution)/shard_map/pallas_call | solution.py:291
  95.3 2.9 %shard_map.73 = (f32[8,64,128]{2,1,0:T(8,128)S(1)}, f32[8,128]{1,0:T(8,128)S(1)}) custom-call(f32[64,1024]{1,0:T(8,128)S(1)} %pad_maximum_fusion.3.u_ref.refs_0_, bf16[2,1024,1024]{2,1,0:T(8,128)(2,1)S(1)} %get-tuple-element.14.refs_2_.dh_ref.refs_1_, bf16[2,1024,1024]{2,1,0:T(8,128)(2,1)S(1)} %get-tuple-element.15.refs_3_.dl_ref.refs_2_), custom_call_target="tpu_custom_call" | custom-call | bytes 9450000 | tf_op jit(solution)/shard_map/pallas_call | solution.py:340
  98.4 1.3 collective-permute-done.22
  99.8 1.7 %collective-permute-start.23 = (f32[72,128]{1,0:T(8,128)S(1)}, f32[72,128]{1,0:T(8,128)S(1)}, u32[]{:S(2)}, u32[]{:S(2)}) collective-permute-start(f32[72,128]{1,0:T(8,128)S(1)} %get-tuple-element.45), channel_id=1, source_target_pairs={{0,6},{1,7},{2,4},{3,5},{4,2},{5,3},{6,0},{7,1},{8,14},{9,15},{10,... | collective-permute-start | bytes 110600 | tf_op jit(solution)/shard_map/ppermute | solution.py:407
  101.5 1.3 collective-permute-start.24
  103.3 1.5 collective-permute-start.30
  105.6 1.3 collective-permute-start.26
  107.2 2.8 %shard_map.74.inv_ref = f32[32,32]{1,0:T(8,128)S(1)} custom-call(f32[8,128]{1,0:T(8,128)S(1)} %slice.229.g_ref), custom_call_target="tpu_custom_call" | custom-call | bytes 9450000 | tf_op jit(solution)/shard_map/pallas_call | solution.py:291
  111.1 1.2 collective-permute-done.33
  112.3 1.2 collective-permute-start.34
  114.0 3.8 %collective-permute-done.26.refs_0_ = f32[64,1024]{1,0:T(8,128)S(1)} collective-permute-done((f32[64,1024]{1,0:T(8,128)S(1)}, f32[64,1024]{1,0:T(8,128)S(1)}, u32[]{:S(2)}, u32[]{:S(2)}) %collective-permute-start.26) | collective-permute-done | bytes 262176 | tf_op jit(solution)/shard_map/ppermute | solution.py:502
  118.6 2.9 %collective-permute-done.35 = f32[8,32]{1,0:T(8,128)S(1)} collective-permute-done((f32[8,32]{1,0:T(8,128)S(1)}, f32[8,32]{1,0:T(8,128)S(1)}, u32[]{:S(2)}, u32[]{:S(2)}) %collective-permute-start.35) | collective-permute-done | bytes 1056 | tf_op jit(solution)/shard_map/ppermute | solution.py:431
  121.9 3.2 %collective-permute-done.36 = f32[8,32]{1,0:T(8,128)S(1)} collective-permute-done((f32[8,32]{1,0:T(8,128)S(1)}, f32[8,32]{1,0:T(8,128)S(1)}, u32[]{:S(2)}, u32[]{:S(2)}) %collective-permute-start.36) | collective-permute-done | bytes 1056 | tf_op jit(solution)/shard_map/ppermute | solution.py:431
  125.8 3.8 %collective-permute-done.37 = f32[8,32]{1,0:T(8,128)S(1)} collective-permute-done((f32[8,32]{1,0:T(8,128)S(1)}, f32[8,32]{1,0:T(8,128)S(1)}, u32[]{:S(2)}, u32[]{:S(2)}) %collective-permute-start.37) | collective-permute-done | bytes 1056 | tf_op jit(solution)/shard_map/ppermute | solution.py:431
  130.1 3.2 %shard_map.75.refs_2_ = f32[8192,128]{1,0:T(8,128)S(1)} custom-call(s32[8]{0:T(128)S(1)} %get-tuple-element.20.base_ref, s32[8192]{0:T(1024)S(1)} %copy-done, f32[64,1024]{1,0:T(8,128)S(1)} %pad_maximum_fusion.3.u_ref.refs_0_, f32[64,1024]{1,0:T(8,128)S(1)} %collective-permute-done.32.refs_1_), custom_call_target="tpu_custom_call" | custom-call | bytes 11900000 | tf_op jit(solution)/shard_map/pallas_call | solution.py:218
  133.3 3.2 %shard_map.76.refs_2_ = f32[8192,128]{1,0:T(8,128)S(1)} custom-call(s32[8]{0:T(128)S(1)} %get-tuple-element.20.base_ref, s32[8192]{0:T(1024)S(1)} %copy-done, f32[64,1024]{1,0:T(8,128)S(1)} %collective-permute-done.30.refs_0_, f32[64,1024]{1,0:T(8,128)S(1)} %collective-permute-done.31.refs_1_, ...), custom_call_target="tpu_custom_call", output_to_operand_aliasing={{}: (4, {})} | custom-call | bytes 11900000 | tf_op jit(solution)/shard_map/pallas_call | solution.py:218
  136.6 3.2 %shard_map.77.refs_2_ = f32[8192,128]{1,0:T(8,128)S(1)} custom-call(s32[8]{0:T(128)S(1)} %get-tuple-element.20.base_ref, s32[8192]{0:T(1024)S(1)} %copy-done, f32[64,1024]{1,0:T(8,128)S(1)} %collective-permute-done.28.refs_0_, f32[64,1024]{1,0:T(8,128)S(1)} %collective-permute-done.29.refs_1_, ...), custom_call_target="tpu_custom_call", output_to_operand_aliasing={{}: (4, {})} | custom-call | bytes 11900000 | tf_op jit(solution)/shard_map/pallas_call | solution.py:218
  139.8 3.2 %shard_map.78.w_ref = f32[8192,128]{1,0:T(8,128)S(1)} custom-call(s32[8]{0:T(128)S(1)} %get-tuple-element.20.base_ref, s32[8192]{0:T(1024)S(1)} %copy-done, f32[64,1024]{1,0:T(8,128)S(1)} %collective-permute-done.26.refs_0_, f32[64,1024]{1,0:T(8,128)S(1)} %collective-permute-done.27.refs_1_, ...), custom_call_target="tpu_custom_call", output_to_operand_aliasing={{}: (4, {})} | custom-call | bytes 11900000 | tf_op jit(solution)/shard_map/pallas_call | solution.py:218
  143.0 9.3 %shard_map.79 = f32[64,8192]{1,0:T(8,128)} custom-call(f32[32,32]{1,0:T(8,128)S(1)} %shard_map.74.inv_ref, f32[8192,128]{1,0:T(8,128)S(1)} %shard_map.78.w_ref), custom_call_target="tpu_custom_call" | custom-call | bytes 42000000 | tf_op jit(solution)/shard_map/pallas_call | solution.py:261
  (98 shorter events, 13.8 us)
Async XLA Ops:
  0.6 0.8 copy-start
  1.4 0.7 copy-start.1
  2.0 19.1 %copy-start.2 = (f32[2,32,8192]{2,1,0:T(8,128)S(1)}, f32[2,32,8192]{2,1,0:T(8,128)}, u32[]{:S(2)}) copy-start(f32[2,32,8192]{2,1,0:T(8,128)} %param.7) | copy-start | bytes 6291460
  20.6 1.5 %collective-permute-start = (f32[32,1024]{1,0:T(8,128)S(1)}, f32[32,1024]{1,0:T(8,128)S(1)}, u32[]{:S(2)}, u32[]{:S(2)}) collective-permute-start(f32[32,1024]{1,0:T(8,128)S(1)} %slice_select_fusion.2), channel_id=1, source_target_pairs={{0,1},{1,0},{2,3},{3,2},{4,5},{5,4},{6,7},{7,6},{8,9},{9,8},{10,11... | collective-permute-start | bytes 393224 | tf_op jit(solution)/shard_map/ppermute | solution.py:462
  22.1 7.8 %collective-permute-start.1 = (f32[32,1024]{1,0:T(8,128)S(1)}, f32[32,1024]{1,0:T(8,128)S(1)}, u32[]{:S(2)}, u32[]{:S(2)}) collective-permute-start(f32[32,1024]{1,0:T(8,128)S(1)} %select_add_fusion), channel_id=1, source_target_pairs={{0,6},{1,7},{2,4},{3,5},{4,2},{5,3},{6,0},{7,1},{8,14},{9,15},{10,... | collective-permute-start | bytes 393224 | tf_op jit(solution)/shard_map/ppermute | solution.py:423
  26.0 6.6 %collective-permute-start.2 = (f32[32,1024]{1,0:T(8,128)S(1)}, f32[32,1024]{1,0:T(8,128)S(1)}, u32[]{:S(2)}, u32[]{:S(2)}) collective-permute-start(f32[32,1024]{1,0:T(8,128)S(1)} %select_add_fusion), channel_id=1, source_target_pairs={{0,4},{1,5},{2,6},{3,7},{4,0},{5,1},{6,2},{7,3},{8,12},{9,13},{10,... | collective-permute-start | bytes 393224 | tf_op jit(solution)/shard_map/ppermute | solution.py:423
  26.5 6.4 %collective-permute-start.3 = (f32[32,1024]{1,0:T(8,128)S(1)}, f32[32,1024]{1,0:T(8,128)S(1)}, u32[]{:S(2)}, u32[]{:S(2)}) collective-permute-start(f32[32,1024]{1,0:T(8,128)S(1)} %select_add_fusion), channel_id=1, source_target_pairs={{0,2},{1,3},{2,0},{3,1},{4,6},{5,7},{6,4},{7,5},{8,10},{9,11},{10,... | collective-permute-start | bytes 393224 | tf_op jit(solution)/shard_map/ppermute | solution.py:423
  32.9 4.2 %collective-permute-start.4 = (f32[32,1024]{1,0:T(8,128)S(1)}, f32[32,1024]{1,0:T(8,128)S(1)}, u32[]{:S(2)}, u32[]{:S(2)}) collective-permute-start(f32[32,1024]{1,0:T(8,128)S(1)} %add_add_fusion.1), channel_id=1, source_target_pairs={{0,1},{1,0},{2,3},{3,2},{4,5},{5,4},{6,7},{7,6},{8,9},{9,8},{10,11... | collective-permute-start | bytes 393224 | tf_op jit(solution)/shard_map/ppermute | solution.py:465
  39.0 6.6 %collective-permute-start.5 = (f32[16,1024]{1,0:T(8,128)S(1)}, f32[16,1024]{1,0:T(8,128)S(1)}, u32[]{:S(2)}, u32[]{:S(2)}) collective-permute-start(f32[16,1024]{1,0:T(8,128)S(1)} %get-tuple-element.40), channel_id=1, source_target_pairs={{0,24},{8,16},{16,8},{24,0},{1,25},{9,17},{17,9},{25,1},{2,26},{10... | collective-permute-start | bytes 196616 | tf_op jit(solution)/shard_map/ppermute | solution.py:407
  42.6 6.1 %collective-permute-start.6 = (f32[16,1024]{1,0:T(8,128)S(1)}, f32[16,1024]{1,0:T(8,128)S(1)}, u32[]{:S(2)}, u32[]{:S(2)}) collective-permute-start(f32[16,1024]{1,0:T(8,128)S(1)} %get-tuple-element.41), channel_id=1, source_target_pairs={{0,16},{8,24},{16,0},{24,8},{1,17},{9,25},{17,1},{25,9},{2,18},{10... | collective-permute-start | bytes 196616 | tf_op jit(solution)/shard_map/ppermute | solution.py:407
  42.6 6.1 %collective-permute-start.7 = (f32[16,1024]{1,0:T(8,128)S(1)}, f32[16,1024]{1,0:T(8,128)S(1)}, u32[]{:S(2)}, u32[]{:S(2)}) collective-permute-start(f32[16,1024]{1,0:T(8,128)S(1)} %get-tuple-element.42), channel_id=1, source_target_pairs={{0,8},{8,0},{16,24},{24,16},{1,9},{9,1},{17,25},{25,17},{2,10},{10... | collective-permute-start | bytes 196616 | tf_op jit(solution)/shard_map/ppermute | solution.py:407
  48.8 4.3 %collective-permute-start.10 = (f32[16,1024]{1,0:T(8,128)S(1)}, f32[16,1024]{1,0:T(8,128)S(1)}, u32[]{:S(2)}, u32[]{:S(2)}) collective-permute-start(f32[16,1024]{1,0:T(8,128)S(1)} %add_add_fusion.3), channel_id=1, source_target_pairs={{0,8},{8,0},{16,24},{24,16},{1,9},{9,1},{17,25},{25,17},{2,10},{10... | collective-permute-start | bytes 196616 | tf_op jit(solution)/shard_map/ppermute | solution.py:415
  50.1 6.1 %collective-permute-start.8 = (f32[16,1024]{1,0:T(8,128)S(1)}, f32[16,1024]{1,0:T(8,128)S(1)}, u32[]{:S(2)}, u32[]{:S(2)}) collective-permute-start(f32[16,1024]{1,0:T(8,128)S(1)} %add_add_fusion.3), channel_id=1, source_target_pairs={{0,24},{8,16},{16,8},{24,0},{1,25},{9,17},{17,9},{25,1},{2,26},{10... | collective-permute-start | bytes 196616 | tf_op jit(solution)/shard_map/ppermute | solution.py:415
  51.5 7.2 %collective-permute-start.9 = (f32[16,1024]{1,0:T(8,128)S(1)}, f32[16,1024]{1,0:T(8,128)S(1)}, u32[]{:S(2)}, u32[]{:S(2)}) collective-permute-start(f32[16,1024]{1,0:T(8,128)S(1)} %add_add_fusion.3), channel_id=1, source_target_pairs={{0,16},{8,24},{16,0},{24,8},{1,17},{9,25},{17,1},{25,9},{2,18},{10... | collective-permute-start | bytes 196616 | tf_op jit(solution)/shard_map/ppermute | solution.py:415
  61.8 1.5 collective-permute-start.11
  63.3 8.1 %collective-permute-start.12 = (f32[40,1024]{1,0:T(8,128)S(1)}, f32[40,1024]{1,0:T(8,128)S(1)}, u32[]{:S(2)}, u32[]{:S(2)}) collective-permute-start(f32[40,1024]{1,0:T(8,128)S(1)} %fusion.7), channel_id=1, source_target_pairs={{0,6},{1,7},{2,4},{3,5},{4,2},{5,3},{6,0},{7,1},{8,14},{9,15},{10,... | collective-permute-start | bytes 491528 | tf_op jit(solution)/shard_map/ppermute | solution.py:423
  65.0 9.0 %collective-permute-start.13 = (f32[40,1024]{1,0:T(8,128)S(1)}, f32[40,1024]{1,0:T(8,128)S(1)}, u32[]{:S(2)}, u32[]{:S(2)}) collective-permute-start(f32[40,1024]{1,0:T(8,128)S(1)} %fusion.7), channel_id=1, source_target_pairs={{0,4},{1,5},{2,6},{3,7},{4,0},{5,1},{6,2},{7,3},{8,12},{9,13},{10,... | collective-permute-start | bytes 491528 | tf_op jit(solution)/shard_map/ppermute | solution.py:423
  66.3 7.7 %collective-permute-start.14 = (f32[40,1024]{1,0:T(8,128)S(1)}, f32[40,1024]{1,0:T(8,128)S(1)}, u32[]{:S(2)}, u32[]{:S(2)}) collective-permute-start(f32[40,1024]{1,0:T(8,128)S(1)} %fusion.7), channel_id=1, source_target_pairs={{0,2},{1,3},{2,0},{3,1},{4,6},{5,7},{6,4},{7,5},{8,10},{9,11},{10,... | collective-permute-start | bytes 491528 | tf_op jit(solution)/shard_map/ppermute | solution.py:423
  74.1 1.4 collective-permute-start.15
  77.2 6.8 %collective-permute-start.16 = (f32[16,1024]{1,0:T(8,128)S(1)}, f32[16,1024]{1,0:T(8,128)S(1)}, u32[]{:S(2)}, u32[]{:S(2)}) collective-permute-start(f32[16,1024]{1,0:T(8,128)S(1)} %get-tuple-element.31), channel_id=1, source_target_pairs={{0,24},{8,16},{16,8},{24,0},{1,25},{9,17},{17,9},{25,1},{2,26},{10... | collective-permute-start | bytes 196616 | tf_op jit(solution)/shard_map/ppermute | solution.py:407
  79.4 6.6 %collective-permute-start.17 = (f32[16,1024]{1,0:T(8,128)S(1)}, f32[16,1024]{1,0:T(8,128)S(1)}, u32[]{:S(2)}, u32[]{:S(2)}) collective-permute-start(f32[16,1024]{1,0:T(8,128)S(1)} %get-tuple-element.32), channel_id=1, source_target_pairs={{0,16},{8,24},{16,0},{24,8},{1,17},{9,25},{17,1},{25,9},{2,18},{10... | collective-permute-start | bytes 196616 | tf_op jit(solution)/shard_map/ppermute | solution.py:407
  79.4 6.6 %collective-permute-start.18 = (f32[16,1024]{1,0:T(8,128)S(1)}, f32[16,1024]{1,0:T(8,128)S(1)}, u32[]{:S(2)}, u32[]{:S(2)}) collective-permute-start(f32[16,1024]{1,0:T(8,128)S(1)} %get-tuple-element.33), channel_id=1, source_target_pairs={{0,8},{8,0},{16,24},{24,16},{1,9},{9,1},{17,25},{25,17},{2,10},{10... | collective-permute-start | bytes 196616 | tf_op jit(solution)/shard_map/ppermute | solution.py:407
  86.1 8.5 %collective-permute-start.19 = (f32[16,1024]{1,0:T(8,128)S(1)}, f32[16,1024]{1,0:T(8,128)S(1)}, u32[]{:S(2)}, u32[]{:S(2)}) collective-permute-start(f32[16,1024]{1,0:T(8,128)S(1)} %add_add_fusion.2), channel_id=1, source_target_pairs={{0,24},{8,16},{16,8},{24,0},{1,25},{9,17},{17,9},{25,1},{2,26},{10... | collective-permute-start | bytes 196616 | tf_op jit(solution)/shard_map/ppermute | solution.py:415
  88.3 6.4 %collective-permute-start.20 = (f32[16,1024]{1,0:T(8,128)S(1)}, f32[16,1024]{1,0:T(8,128)S(1)}, u32[]{:S(2)}, u32[]{:S(2)}) collective-permute-start(f32[16,1024]{1,0:T(8,128)S(1)} %add_add_fusion.2), channel_id=1, source_target_pairs={{0,16},{8,24},{16,0},{24,8},{1,17},{9,25},{17,1},{25,9},{2,18},{10... | collective-permute-start | bytes 196616 | tf_op jit(solution)/shard_map/ppermute | solution.py:415
  88.3 6.4 %collective-permute-start.21 = (f32[16,1024]{1,0:T(8,128)S(1)}, f32[16,1024]{1,0:T(8,128)S(1)}, u32[]{:S(2)}, u32[]{:S(2)}) collective-permute-start(f32[16,1024]{1,0:T(8,128)S(1)} %add_add_fusion.2), channel_id=1, source_target_pairs={{0,8},{8,0},{16,24},{24,16},{1,9},{9,1},{17,25},{25,17},{2,10},{10... | collective-permute-start | bytes 196616 | tf_op jit(solution)/shard_map/ppermute | solution.py:415
  98.3 1.4 collective-permute-start.22
  99.8 5.8 %collective-permute-start.23 = (f32[72,128]{1,0:T(8,128)S(1)}, f32[72,128]{1,0:T(8,128)S(1)}, u32[]{:S(2)}, u32[]{:S(2)}) collective-permute-start(f32[72,128]{1,0:T(8,128)S(1)} %get-tuple-element.45), channel_id=1, source_target_pairs={{0,6},{1,7},{2,4},{3,5},{4,2},{5,3},{6,0},{7,1},{8,14},{9,15},{10,... | collective-permute-start | bytes 110600 | tf_op jit(solution)/shard_map/ppermute | solution.py:407
  101.5 5.3 %collective-permute-start.24 = (f32[72,128]{1,0:T(8,128)S(1)}, f32[72,128]{1,0:T(8,128)S(1)}, u32[]{:S(2)}, u32[]{:S(2)}) collective-permute-start(f32[72,128]{1,0:T(8,128)S(1)} %get-tuple-element.46), channel_id=1, source_target_pairs={{0,4},{1,5},{2,6},{3,7},{4,0},{5,1},{6,2},{7,3},{8,12},{9,13},{10,... | collective-permute-start | bytes 110600 | tf_op jit(solution)/shard_map/ppermute | solution.py:407
  102.8 4.4 %collective-permute-start.25 = (f32[72,128]{1,0:T(8,128)S(1)}, f32[72,128]{1,0:T(8,128)S(1)}, u32[]{:S(2)}, u32[]{:S(2)}) collective-permute-start(f32[72,128]{1,0:T(8,128)S(1)} %get-tuple-element.47), channel_id=1, source_target_pairs={{0,2},{1,3},{2,0},{3,1},{4,6},{5,7},{6,4},{7,5},{8,10},{9,11},{10,... | collective-permute-start | bytes 110600 | tf_op jit(solution)/shard_map/ppermute | solution.py:407
  103.3 10.1 %collective-permute-start.30 = (f32[64,1024]{1,0:T(8,128)S(1)}, f32[64,1024]{1,0:T(8,128)S(1)}, u32[]{:S(2)}, u32[]{:S(2)}) collective-permute-start(f32[64,1024]{1,0:T(8,128)S(1)} %pad_maximum_fusion.3.u_ref.refs_0_), channel_id=1, source_target_pairs={{0,2},{1,3},{2,0},{3,1},{4,6},{5,7},{6,4},{7,5},{8,10},{9,11},{10,... | collective-permute-start | bytes 786440 | tf_op jit(solution)/shard_map/ppermute | solution.py:502
  104.8 9.1 %collective-permute-start.28 = (f32[64,1024]{1,0:T(8,128)S(1)}, f32[64,1024]{1,0:T(8,128)S(1)}, u32[]{:S(2)}, u32[]{:S(2)}) collective-permute-start(f32[64,1024]{1,0:T(8,128)S(1)} %pad_maximum_fusion.3.u_ref.refs_0_), channel_id=1, source_target_pairs={{0,4},{1,5},{2,6},{3,7},{4,0},{5,1},{6,2},{7,3},{8,12},{9,13},{10,... | collective-permute-start | bytes 786440 | tf_op jit(solution)/shard_map/ppermute | solution.py:502
  105.6 12.2 %collective-permute-start.26 = (f32[64,1024]{1,0:T(8,128)S(1)}, f32[64,1024]{1,0:T(8,128)S(1)}, u32[]{:S(2)}, u32[]{:S(2)}) collective-permute-start(f32[64,1024]{1,0:T(8,128)S(1)} %pad_maximum_fusion.3.u_ref.refs_0_), channel_id=1, source_target_pairs={{0,6},{1,7},{2,4},{3,5},{4,2},{5,3},{6,0},{7,1},{8,14},{9,15},{10,... | collective-permute-start | bytes 786440 | tf_op jit(solution)/shard_map/ppermute | solution.py:502
  111.1 1.2 collective-permute-start.33
  112.3 5.5 %collective-permute-start.34 = (f32[8,32]{1,0:T(8,128)S(1)}, f32[8,32]{1,0:T(8,128)S(1)}, u32[]{:S(2)}, u32[]{:S(2)}) collective-permute-start(f32[8,32]{1,0:T(8,128)S(1)} %broadcast_add_fusion), channel_id=1, source_target_pairs={{0,2},{1,3},{2,0},{3,1},{4,6},{5,7},{6,4},{7,5},{8,10},{9,11},{10,... | collective-permute-start | bytes 3080 | tf_op jit(solution)/shard_map/ppermute | solution.py:431
  113.4 16.7 %collective-permute-start.32 = (f32[64,1024]{1,0:T(8,128)S(1)}, f32[64,1024]{1,0:T(8,128)S(1)}, u32[]{:S(2)}, u32[]{:S(2)}) collective-permute-start(f32[64,1024]{1,0:T(8,128)S(1)} %pad_maximum_fusion.3.u_ref.refs_0_), channel_id=1, source_target_pairs={{0,1},{1,0},{2,3},{3,2},{4,5},{5,4},{6,7},{7,6},{8,9},{9,8},{10,11... | collective-permute-start | bytes 786440 | tf_op jit(solution)/shard_map/ppermute | solution.py:502
  113.4 19.9 %collective-permute-start.31 = (f32[64,1024]{1,0:T(8,128)S(1)}, f32[64,1024]{1,0:T(8,128)S(1)}, u32[]{:S(2)}, u32[]{:S(2)}) collective-permute-start(f32[64,1024]{1,0:T(8,128)S(1)} %collective-permute-done.30.refs_0_), channel_id=1, source_target_pairs={{0,1},{1,0},{2,3},{3,2},{4,5},{5,4},{6,7},{7,6},{8,9},{9,8},{10,11... | collective-permute-start | bytes 786440 | tf_op jit(solution)/shard_map/ppermute | solution.py:505
  113.9 22.6 %collective-permute-start.29 = (f32[64,1024]{1,0:T(8,128)S(1)}, f32[64,1024]{1,0:T(8,128)S(1)}, u32[]{:S(2)}, u32[]{:S(2)}) collective-permute-start(f32[64,1024]{1,0:T(8,128)S(1)} %collective-permute-done.28.refs_0_), channel_id=1, source_target_pairs={{0,1},{1,0},{2,3},{3,2},{4,5},{5,4},{6,7},{7,6},{8,9},{9,8},{10,11... | collective-permute-start | bytes 786440 | tf_op jit(solution)/shard_map/ppermute | solution.py:505
  117.8 22.0 %collective-permute-start.27 = (f32[64,1024]{1,0:T(8,128)S(1)}, f32[64,1024]{1,0:T(8,128)S(1)}, u32[]{:S(2)}, u32[]{:S(2)}) collective-permute-start(f32[64,1024]{1,0:T(8,128)S(1)} %collective-permute-done.26.refs_0_), channel_id=1, source_target_pairs={{0,1},{1,0},{2,3},{3,2},{4,5},{5,4},{6,7},{7,6},{8,9},{9,8},{10,11... | collective-permute-start | bytes 786440 | tf_op jit(solution)/shard_map/ppermute | solution.py:505
  117.8 3.7 %collective-permute-start.35 = (f32[8,32]{1,0:T(8,128)S(1)}, f32[8,32]{1,0:T(8,128)S(1)}, u32[]{:S(2)}, u32[]{:S(2)}) collective-permute-start(f32[8,32]{1,0:T(8,128)S(1)} %fusion.33), channel_id=1, source_target_pairs={{0,4},{1,5},{2,6},{3,7},{4,0},{5,1},{6,2},{7,3},{8,12},{9,13},{10,... | collective-permute-start | bytes 3080 | tf_op jit(solution)/shard_map/ppermute | solution.py:431
  121.5 3.6 %collective-permute-start.36 = (f32[8,32]{1,0:T(8,128)S(1)}, f32[8,32]{1,0:T(8,128)S(1)}, u32[]{:S(2)}, u32[]{:S(2)}) collective-permute-start(f32[8,32]{1,0:T(8,128)S(1)} %add.103), channel_id=1, source_target_pairs={{0,8},{8,0},{16,24},{24,16},{1,9},{9,1},{17,25},{25,17},{2,10},{10... | collective-permute-start | bytes 3080 | tf_op jit(solution)/shard_map/ppermute | solution.py:431
  125.1 4.5 %collective-permute-start.37 = (f32[8,32]{1,0:T(8,128)S(1)}, f32[8,32]{1,0:T(8,128)S(1)}, u32[]{:S(2)}, u32[]{:S(2)}) collective-permute-start(f32[8,32]{1,0:T(8,128)S(1)} %add.104), channel_id=1, source_target_pairs={{0,16},{8,24},{16,0},{24,8},{1,17},{9,25},{17,1},{25,9},{2,18},{10... | collective-permute-start | bytes 3080 | tf_op jit(solution)/shard_map/ppermute | solution.py:431

commit v5 on v4

--- a/solution.py
+++ b/solution.py
@@ -12,6 +12,7 @@
 ITERS = 2
 BLOCK = 256
 HW = 256
+COPY = 512
 F32 = jnp.float32
 BF16 = jnp.bfloat16
 
@@ -50,20 +51,17 @@
     return (1 - 2 * (parity & 1)).astype(F32)
 
 
-def butterfly(ref, count, width):
-    rows = ref.shape[0]
+def butterfly(src, dst, count, width):
+    rows = src.shape[0]
     step = 1
     while step < count:
-        radix = min(8, count // step)
-
-        def body(g, carry, step=step, radix=radix):
+        radix = min(32, count // step)
+        for g in range(count // radix):
             base = (g // step) * (step * radix) + g % step
-            for s in range(rows // 8):
+            for s in range(0, rows, 8):
                 for lane in range(0, width, HB):
-                    at = [
-                        pl.multiple_of((base + r * step) * width + lane, HB) for r in range(radix)
-                    ]
-                    v = [ref[s * 8 : s * 8 + 8, pl.ds(a, HB)] for a in at]
+                    at = [(base + r * step) * width + lane for r in range(radix)]
+                    v = [src[s : s + 8, a : a + HB] for a in at]
                     half = 1
                     while half < radix:
                         v = [
@@ -72,11 +70,9 @@
                         ]
                         half *= 2
                     for a, x in zip(at, v):
-                        ref[s * 8 : s * 8 + 8, pl.ds(a, HB)] = x
-            return carry
-
-        lax.fori_loop(0, count // radix, body, 0)
+                        dst[s : s + 8, a : a + HB] = x
         step *= radix
+        src = dst
 
 
 def block_loop(count, unroll, body):
@@ -91,14 +87,21 @@
 
 
 def start_kernel(
-    scale, steps_ref, idx_ref, probes_ref, frames_ref,
-    dh_ref, dl_ref, img_ref, mask_ref, base_ref, f_ref, w_ref, n_ref, g_ref, b_ref, t_ref, sems, sem,
+    scale, phase_ref, rows_ref, probes_ref, frames_ref,
+    dh_ref, dl_ref, img_ref, mask_ref, base_ref, f_ref, p_ref, w_ref, n_ref, g_ref, b_ref, t_ref, idx_ref, steps_ref,
+    sems, sem, tiny,
 ):
     vectors, modes = probes_ref.shape
     steps, rows, count = frames_ref.shape
     outer = modes // HW
-    block = min(BLOCK, rows)
-    first = pltpu.make_async_copy(probes_ref, w_ref, sem)
+    block = min(COPY, rows)
+    small = [
+        pltpu.make_async_copy(rows_ref, idx_ref, tiny.at[0]),
+        pltpu.make_async_copy(phase_ref, steps_ref, tiny.at[1]),
+    ]
+    for c in small:
+        c.start()
+    first = pltpu.make_async_copy(probes_ref, p_ref, sem)
     first.start()
     copies = [
         [
@@ -111,9 +114,6 @@
         ]
         for i in range(rows // block)
     ]
-    for row in copies:
-        for c in row:
-            c.start()
     here = (lax.axis_index("mode"), lax.axis_index("pix"))
     for b in range(4):
         for place, axis_row in ((here[0], 0), (here[1], 4)):
@@ -123,7 +123,11 @@
         base_ref[b] = (here[0] ^ b) * count
     signs = sign_table(HW).astype(BF16)
     first.wait()
-    butterfly(w_ref, outer, HW)
+    half = (len(copies) + 1) // 2
+    for row in copies[:half]:
+        for c in row:
+            c.start()
+    butterfly(p_ref, w_ref, outer, HW)
 
     def inner(i):
         at = pl.multiple_of(i * HW, HW)
@@ -131,7 +135,11 @@
         n_ref[pl.ds(at, HW), :] = dot(signs, both, NT)
 
     block_loop(outer, 8, inner)
+    for row in copies[half:]:
+        for c in row:
+            c.start()
     start_at = here[0] * count
+    small[0].wait()
 
     def gather(t, carry):
         at = pl.multiple_of(t * 32, 32)
@@ -143,6 +151,7 @@
     parts = [g_ref[b * HB : (b + 1) * HB, :].T for b in range(count // HB)]
     parts = [p[:vectors] + p[vectors:] for p in parts]
     b_ref[...], t_ref[...] = stack_forward(jnp.concatenate(parts, axis=1) * scale)
+    small[1].wait()
     frame = [
         sum(jnp.where(steps_ref[f] == s, f, 0) for f in range(1, steps)) for s in range(steps)
     ]
@@ -175,21 +184,25 @@
             jax.ShapeDtypeStruct((8, HB), F32),
             jax.ShapeDtypeStruct((modes // count,), jnp.int32),
         ],
-        in_specs=[SMEM, SMEM, hbm, hbm],
+        in_specs=[hbm, hbm, hbm, hbm],
         out_specs=[VMEM, VMEM, VMEM, VMEM, SMEM],
         cost_estimate=cost(12),
         scratch_shapes=[
             pltpu.VMEM((steps, rows, count), F32),
             pltpu.VMEM((vectors, modes), F32),
+            pltpu.VMEM((vectors, modes), F32),
             pltpu.VMEM((modes, HB), F32),
             pltpu.VMEM((count, HB), F32),
             pltpu.VMEM((2 * vectors, count), BF16),
             pltpu.VMEM((2 * vectors, count), BF16),
-            pltpu.SemaphoreType.DMA((steps, rows // min(BLOCK, rows))),
+            pltpu.SMEM((modes,), jnp.int32),
+            pltpu.SMEM((steps,), jnp.int32),
+            pltpu.SemaphoreType.DMA((steps, rows // min(COPY, rows))),
             pltpu.SemaphoreType.DMA,
+            pltpu.SemaphoreType.DMA((2,)),
         ],
         compiler_params=pltpu.CompilerParams(vmem_limit_bytes=44 << 20),
-    )(phase_steps, idx, probes, frames)
+    )(*[pltpu.with_memory_space_constraint(x, pltpu.HBM) for x in (phase_steps, idx, probes, frames)])
 
 
 def scatter_kernel(places, base_ref, idx_ref, *refs):
@@ -227,7 +240,7 @@
     )(*args)
 
 
-def end_kernel(inv_ref, w_ref, out_ref):
+def end_kernel(inv_ref, w_ref, out_ref, y_ref, z_ref, o_ref, sems):
     vectors, modes = out_ref.shape
     half = vectors // 2
     outer = modes // HW
@@ -244,27 +257,36 @@
     def first(i):
         at = pl.multiple_of(i * HW, HW)
         both = dot(mix, w_ref[pl.ds(at, HW), :].astype(BF16), NT)
-        out_ref[:, pl.ds(at, HW)] = both[:vectors] + both[vectors:]
+        y_ref[:, pl.ds(at, HW)] = both[:vectors] + both[vectors:]
 
     block_loop(outer, 8, first)
-    butterfly(out_ref, outer, HW)
-
-    def inner(i):
-        at = pl.multiple_of(i * HW, HW)
-        both = dot(jnp.concatenate(split(out_ref[:, pl.ds(at, HW)]), axis=0), signs, NN)
-        out_ref[:, pl.ds(at, HW)] = both[:vectors] + both[vectors:]
-
-    block_loop(outer, 8, inner)
+    butterfly(y_ref, z_ref, outer, HW)
+    per = modes // sems.shape[0]
+    copies = [
+        pltpu.make_async_copy(
+            o_ref.at[:, pl.ds(c * per, per)], out_ref.at[:, pl.ds(c * per, per)], sems.at[c]
+        )
+        for c in range(sems.shape[0])
+    ]
+    for c, copy in enumerate(copies):
+        for i in range(c * per, (c + 1) * per, HW):
+            both = dot(jnp.concatenate(split(z_ref[:, i : i + HW]), axis=0), signs, NN)
+            o_ref[:, i : i + HW] = both[:vectors] + both[vectors:]
+        copy.start()
+    for copy in copies:
+        copy.wait()
 
 
 def end_vectors(inv, table, vectors):
     return pl.pallas_call(
         end_kernel,
-        cost_estimate=cost(12),
+        cost_estimate=cost(6),
         out_shape=jax.ShapeDtypeStruct((vectors, table.shape[0]), F32),
         in_specs=[VMEM, VMEM],
-        out_specs=VMEM,
-        compiler_params=pltpu.CompilerParams(vmem_limit_bytes=12 << 20),
+        out_specs=pl.BlockSpec(memory_space=pltpu.HBM),
+        scratch_shapes=[pltpu.VMEM((vectors, table.shape[0]), F32)] * 3
+        + [pltpu.SemaphoreType.DMA((4,))],
+        compiler_params=pltpu.CompilerParams(vmem_limit_bytes=14 << 20),
     )(inv, table)
 
 

time: 153 us -> 138 us (0.902)
  Pallas kernels: 56.8 us -> 43.3 us
    pallas_call x1, Pallas kernels: 17.2 us -> 9.64 us  [start(): pl.pallas_call(functools.partial(start_kernel, scale), out_shape=[planes,...]
    pallas_call x1, Pallas kernels: 9.33 us -> 3.52 us  [end_vectors(): pl.pallas_call(end_kernel, cost_estimate=cost(6), out_shape=jax.ShapeDtyp...]
  transfers between devices with their start and end apart: 38 -> 38, of which waited for: 22 -> 21; matrix products, arithmetic and copies ran while one was open for 2% -> 3% of each run, Pallas kernels for 12% -> 13%
where the time goes in v5:
time: 138 us; the launch traced here: 137 us
  waiting for transfers between devices  47.8 us (35%)
  Pallas kernels  43.3 us (31%)
  starting transfers between devices  36.5 us (26%)
  between operations  4.45 us (3%)
  matrix products  2.73 us (2%)
  other arithmetic  1.98 us (1%)
    pallas_call x4, Pallas kernels, scatter_rows(): pl.pallas_call(functools.partial(scatter_kernel, places), cost_estimate=c...  12.8 us
    ppermute x9, starting transfers between devices, scatter_sum(): total = total + lax.ppermute(mine[b], axis, flip(size, b * step))  12.5 us
    ppermute x6, waiting for transfers between devices, share_sum(): total = total + lax.ppermute(block, axis, flip(size, b * step))  12.4 us
    ppermute x5, waiting for transfers between devices, double_sum(): block = block + lax.ppermute(block, axis, flip(size, bit))  11 us
    ppermute x9, waiting for transfers between devices, scatter_sum(): total = total + lax.ppermute(mine[b], axis, flip(size, b * step))  10 us
    pallas_call x1, Pallas kernels, start(): pl.pallas_call(functools.partial(start_kernel, scale), out_shape=[planes,...  9.64 us
    pallas_call x3, Pallas kernels, inverse_factor(): pl.pallas_call(factor_kernel, cost_estimate=cost(2.7), out_shape=jax.Shap...  8.38 us
    ppermute x6, starting transfers between devices, share_sum(): total = total + lax.ppermute(block, axis, flip(size, b * step))  8.05 us
  transfers between devices with their start and end apart: 38, of which 21 were waited for; matrix products, arithmetic and copies ran while one was open for 3% of the time, Pallas kernels for 13%

profile of v5, /device:TPU:0, one launch (start us, length us, event | category | flops | bytes accessed | tf_op | source)
XLA Modules:
  0.0 137.4 jit_solution(16676435956064306880)
XLA Ops:
  0.6 9.6 %shard_map.67 = (bf16[2,1024,1024]{2,1,0:T(8,128)(2,1)S(1)}, bf16[2,1024,1024]{2,1,0:T(8,128)(2,1)S(1)}, f32[64,1024]{1,0:T(8,128)S(1)}, f32[8,128]{1,0:T(8,128)S(1)}, s32[8]{0:T(128)S(1)}) custom-call(s32[4]{0:T(128)} %phase_ref.1, s32[8192]{0:T(1024)} %idx_ref.7, f32[64,8192]{1,0:T(8,128)} %bitcast.36, f32[4,1024,1024]{2,1,0:T(8,128)} %frames_ref.1), custom_call_target="tpu_custom_call" | custom-call | bytes 42000000 | tf_op jit(solution)/shard_map/pallas_call | solution.py:178
  12.1 1.0 fusion.1
  13.1 3.9 %collective-permute-start.1 = (f32[32,1024]{1,0:T(8,128)S(1)}, f32[32,1024]{1,0:T(8,128)S(1)}, u32[]{:S(2)}, u32[]{:S(2)}) collective-permute-start(f32[32,1024]{1,0:T(8,128)S(1)} %select_add_fusion), channel_id=1, source_target_pairs={{0,6},{1,7},{2,4},{3,5},{4,2},{5,3},{6,0},{7,1},{8,14},{9,15},{10,... | collective-permute-start | bytes 393224 | tf_op jit(solution)/shard_map/ppermute | solution.py:445
  17.6 1.0 convolution_add_fusion
  18.6 2.3 %collective-permute-done.1 = f32[32,1024]{1,0:T(8,128)S(1)} collective-permute-done((f32[32,1024]{1,0:T(8,128)S(1)}, f32[32,1024]{1,0:T(8,128)S(1)}, u32[]{:S(2)}, u32[]{:S(2)}) %collective-permute-start.1) | collective-permute-done | bytes 131104 | tf_op jit(solution)/shard_map/ppermute | solution.py:445
  20.9 2.6 %collective-permute-done.2 = f32[32,1024]{1,0:T(8,128)S(1)} collective-permute-done((f32[32,1024]{1,0:T(8,128)S(1)}, f32[32,1024]{1,0:T(8,128)S(1)}, u32[]{:S(2)}, u32[]{:S(2)}) %collective-permute-start.2) | collective-permute-done | bytes 131104 | tf_op jit(solution)/shard_map/ppermute | solution.py:445
  24.0 2.8 %shard_map.68.refs_0_ = f32[32,32]{1,0:T(8,128)S(1)} custom-call(f32[8,128]{1,0:T(8,128)S(1)} %pad_maximum_fusion.9.g_ref), custom_call_target="tpu_custom_call" | custom-call | bytes 9450000 | tf_op jit(solution)/shard_map/pallas_call | solution.py:313
  28.2 1.7 %shard_map.69 = f32[64,1024]{1,0:T(8,128)S(1)} custom-call(f32[32,32]{1,0:T(8,128)S(1)} %shard_map.68.refs_0_, f32[64,1024]{1,0:T(8,128)S(1)} %pad_maximum_fusion.refs_1_, bf16[2,1024,1024]{2,1,0:T(8,128)(2,1)S(1)} %get-tuple-element.14.refs_2_.dh_ref.refs_1_, bf16[2,1024,1024]{2,1,0:T(8,128)(2,1)S(1)} %get-tuple-element.15.refs_3_.dl_ref.refs_2_), custom_call_target="tpu_custom_call" | custom-call | bytes 5600000 | tf_op jit(solution)/shard_map/pallas_call | solution.py:399
  29.9 3.7 %collective-permute-start.5 = (f32[16,1024]{1,0:T(8,128)S(1)}, f32[16,1024]{1,0:T(8,128)S(1)}, u32[]{:S(2)}, u32[]{:S(2)}) collective-permute-start(f32[16,1024]{1,0:T(8,128)S(1)} %get-tuple-element.40), channel_id=1, source_target_pairs={{0,24},{8,16},{16,8},{24,0},{1,25},{9,17},{17,9},{25,1},{2,26},{10... | collective-permute-start | bytes 196616 | tf_op jit(solution)/shard_map/ppermute | solution.py:429
  34.4 2.2 %collective-permute-done.5 = f32[16,1024]{1,0:T(8,128)S(1)} collective-permute-done((f32[16,1024]{1,0:T(8,128)S(1)}, f32[16,1024]{1,0:T(8,128)S(1)}, u32[]{:S(2)}, u32[]{:S(2)}) %collective-permute-start.5) | collective-permute-done | bytes 65568 | tf_op jit(solution)/shard_map/ppermute | solution.py:429
  36.5 3.1 %collective-permute-done.6 = f32[16,1024]{1,0:T(8,128)S(1)} collective-permute-done((f32[16,1024]{1,0:T(8,128)S(1)}, f32[16,1024]{1,0:T(8,128)S(1)}, u32[]{:S(2)}, u32[]{:S(2)}) %collective-permute-start.6) | collective-permute-done | bytes 65568 | tf_op jit(solution)/shard_map/ppermute | solution.py:429
  39.7 1.3 collective-permute-start.10
  41.0 1.4 %collective-permute-start.8 = (f32[16,1024]{1,0:T(8,128)S(1)}, f32[16,1024]{1,0:T(8,128)S(1)}, u32[]{:S(2)}, u32[]{:S(2)}) collective-permute-start(f32[16,1024]{1,0:T(8,128)S(1)} %add_add_fusion.3), channel_id=1, source_target_pairs={{0,24},{8,16},{16,8},{24,0},{1,25},{9,17},{17,9},{25,1},{2,26},{10... | collective-permute-start | bytes 196616 | tf_op jit(solution)/shard_map/ppermute | solution.py:437
  44.1 3.0 %collective-permute-done.8 = f32[16,1024]{1,0:T(8,128)S(1)} collective-permute-done((f32[16,1024]{1,0:T(8,128)S(1)}, f32[16,1024]{1,0:T(8,128)S(1)}, u32[]{:S(2)}, u32[]{:S(2)}) %collective-permute-start.8) | collective-permute-done | bytes 65568 | tf_op jit(solution)/shard_map/ppermute | solution.py:437
  47.1 2.6 %collective-permute-done.9 = f32[16,1024]{1,0:T(8,128)S(1)} collective-permute-done((f32[16,1024]{1,0:T(8,128)S(1)}, f32[16,1024]{1,0:T(8,128)S(1)}, u32[]{:S(2)}, u32[]{:S(2)}) %collective-permute-start.9) | collective-permute-done | bytes 65568 | tf_op jit(solution)/shard_map/ppermute | solution.py:437
  49.7 2.9 %shard_map.70 = (f32[64,1024]{1,0:T(8,128)S(1)}, f32[8,128]{1,0:T(8,128)S(1)}) custom-call(f32[64,1024]{1,0:T(8,128)S(1)} %pad_maximum_fusion.1.u_ref, bf16[2,1024,1024]{2,1,0:T(8,128)(2,1)S(1)} %get-tuple-element.14.refs_2_.dh_ref.refs_1_, bf16[2,1024,1024]{2,1,0:T(8,128)(2,1)S(1)} %get-tuple-element.15.refs_3_.dl_ref.refs_2_), custom_call_target="tpu_custom_call" | custom-call | bytes 9450000 | tf_op jit(solution)/shard_map/pallas_call | solution.py:362
  52.8 1.4 %collective-permute-done.11 = f32[40,1024]{1,0:T(8,128)S(1)} collective-permute-done((f32[40,1024]{1,0:T(8,128)S(1)}, f32[40,1024]{1,0:T(8,128)S(1)}, u32[]{:S(2)}, u32[]{:S(2)}) %collective-permute-start.11) | collective-permute-done | bytes 163872 | tf_op jit(solution)/shard_map/ppermute | solution.py:484
  54.2 1.7 %collective-permute-start.12 = (f32[40,1024]{1,0:T(8,128)S(1)}, f32[40,1024]{1,0:T(8,128)S(1)}, u32[]{:S(2)}, u32[]{:S(2)}) collective-permute-start(f32[40,1024]{1,0:T(8,128)S(1)} %fusion.7), channel_id=1, source_target_pairs={{0,6},{1,7},{2,4},{3,5},{4,2},{5,3},{6,0},{7,1},{8,14},{9,15},{10,... | collective-permute-start | bytes 491528 | tf_op jit(solution)/shard_map/ppermute | solution.py:445
  55.9 1.3 collective-permute-start.13
  57.7 4.5 %collective-permute-done.12 = f32[40,1024]{1,0:T(8,128)S(1)} collective-permute-done((f32[40,1024]{1,0:T(8,128)S(1)}, f32[40,1024]{1,0:T(8,128)S(1)}, u32[]{:S(2)}, u32[]{:S(2)}) %collective-permute-start.12) | collective-permute-done | bytes 163872 | tf_op jit(solution)/shard_map/ppermute | solution.py:445
  62.3 2.6 %collective-permute-done.13 = f32[40,1024]{1,0:T(8,128)S(1)} collective-permute-done((f32[40,1024]{1,0:T(8,128)S(1)}, f32[40,1024]{1,0:T(8,128)S(1)}, u32[]{:S(2)}, u32[]{:S(2)}) %collective-permute-start.13) | collective-permute-done | bytes 163872 | tf_op jit(solution)/shard_map/ppermute | solution.py:445
  65.1 1.3 collective-permute-done.15
  66.4 1.4 %shard_map.72 = f32[64,1024]{1,0:T(8,128)S(1)} custom-call(f32[64,1024]{1,0:T(8,128)S(1)} %pad_maximum_fusion.2.refs_0_, bf16[2,1024,1024]{2,1,0:T(8,128)(2,1)S(1)} %get-tuple-element.14.refs_2_.dh_ref.refs_1_, bf16[2,1024,1024]{2,1,0:T(8,128)(2,1)S(1)} %get-tuple-element.15.refs_3_.dl_ref.refs_2_), custom_call_target="tpu_custom_call" | custom-call | bytes 5600000 | tf_op jit(solution)/shard_map/pallas_call | solution.py:399
  67.9 2.2 %collective-permute-start.16 = (f32[16,1024]{1,0:T(8,128)S(1)}, f32[16,1024]{1,0:T(8,128)S(1)}, u32[]{:S(2)}, u32[]{:S(2)}) collective-permute-start(f32[16,1024]{1,0:T(8,128)S(1)} %get-tuple-element.31), channel_id=1, source_target_pairs={{0,24},{8,16},{16,8},{24,0},{1,25},{9,17},{17,9},{25,1},{2,26},{10... | collective-permute-start | bytes 196616 | tf_op jit(solution)/shard_map/ppermute | solution.py:429
  70.1 2.2 %collective-permute-start.18 = (f32[16,1024]{1,0:T(8,128)S(1)}, f32[16,1024]{1,0:T(8,128)S(1)}, u32[]{:S(2)}, u32[]{:S(2)}) collective-permute-start(f32[16,1024]{1,0:T(8,128)S(1)} %get-tuple-element.33), channel_id=1, source_target_pairs={{0,8},{8,0},{16,24},{24,16},{1,9},{9,1},{17,25},{25,17},{2,10},{10... | collective-permute-start | bytes 196616 | tf_op jit(solution)/shard_map/ppermute | solution.py:429
  72.4 2.4 %collective-permute-done.16 = f32[16,1024]{1,0:T(8,128)S(1)} collective-permute-done((f32[16,1024]{1,0:T(8,128)S(1)}, f32[16,1024]{1,0:T(8,128)S(1)}, u32[]{:S(2)}, u32[]{:S(2)}) %collective-permute-start.16) | collective-permute-done | bytes 65568 | tf_op jit(solution)/shard_map/ppermute | solution.py:429
  74.7 2.0 %collective-permute-done.17 = f32[16,1024]{1,0:T(8,128)S(1)} collective-permute-done((f32[16,1024]{1,0:T(8,128)S(1)}, f32[16,1024]{1,0:T(8,128)S(1)}, u32[]{:S(2)}, u32[]{:S(2)}) %collective-permute-start.17) | collective-permute-done | bytes 65568 | tf_op jit(solution)/shard_map/ppermute | solution.py:429
  76.8 2.2 %collective-permute-start.19 = (f32[16,1024]{1,0:T(8,128)S(1)}, f32[16,1024]{1,0:T(8,128)S(1)}, u32[]{:S(2)}, u32[]{:S(2)}) collective-permute-start(f32[16,1024]{1,0:T(8,128)S(1)} %add_add_fusion.2), channel_id=1, source_target_pairs={{0,24},{8,16},{16,8},{24,0},{1,25},{9,17},{17,9},{25,1},{2,26},{10... | collective-permute-start | bytes 196616 | tf_op jit(solution)/shard_map/ppermute | solution.py:437
  79.0 2.2 %collective-permute-start.21 = (f32[16,1024]{1,0:T(8,128)S(1)}, f32[16,1024]{1,0:T(8,128)S(1)}, u32[]{:S(2)}, u32[]{:S(2)}) collective-permute-start(f32[16,1024]{1,0:T(8,128)S(1)} %add_add_fusion.2), channel_id=1, source_target_pairs={{0,8},{8,0},{16,24},{24,16},{1,9},{9,1},{17,25},{25,17},{2,10},{10... | collective-permute-start | bytes 196616 | tf_op jit(solution)/shard_map/ppermute | solution.py:437
  82.6 2.9 %shard_map.71 = f32[32,32]{1,0:T(8,128)S(1)} custom-call(f32[8,128]{1,0:T(8,128)S(1)} %slice.217.g_ref), custom_call_target="tpu_custom_call" | custom-call | bytes 9450000 | tf_op jit(solution)/shard_map/pallas_call | solution.py:313
  86.1 2.9 %shard_map.73 = (f32[8,64,128]{2,1,0:T(8,128)S(1)}, f32[8,128]{1,0:T(8,128)S(1)}) custom-call(f32[64,1024]{1,0:T(8,128)S(1)} %pad_maximum_fusion.3.u_ref.refs_0_, bf16[2,1024,1024]{2,1,0:T(8,128)(2,1)S(1)} %get-tuple-element.14.refs_2_.dh_ref.refs_1_, bf16[2,1024,1024]{2,1,0:T(8,128)(2,1)S(1)} %get-tuple-element.15.refs_3_.dl_ref.refs_2_), custom_call_target="tpu_custom_call" | custom-call | bytes 9450000 | tf_op jit(solution)/shard_map/pallas_call | solution.py:362
  89.1 1.3 collective-permute-done.22
  90.5 1.7 %collective-permute-start.23 = (f32[72,128]{1,0:T(8,128)S(1)}, f32[72,128]{1,0:T(8,128)S(1)}, u32[]{:S(2)}, u32[]{:S(2)}) collective-permute-start(f32[72,128]{1,0:T(8,128)S(1)} %get-tuple-element.45), channel_id=1, source_target_pairs={{0,6},{1,7},{2,4},{3,5},{4,2},{5,3},{6,0},{7,1},{8,14},{9,15},{10,... | collective-permute-start | bytes 110600 | tf_op jit(solution)/shard_map/ppermute | solution.py:429
  92.2 1.3 collective-permute-start.24
  94.1 1.5 %collective-permute-start.30 = (f32[64,1024]{1,0:T(8,128)S(1)}, f32[64,1024]{1,0:T(8,128)S(1)}, u32[]{:S(2)}, u32[]{:S(2)}) collective-permute-start(f32[64,1024]{1,0:T(8,128)S(1)} %pad_maximum_fusion.3.u_ref.refs_0_), channel_id=1, source_target_pairs={{0,2},{1,3},{2,0},{3,1},{4,6},{5,7},{6,4},{7,5},{8,10},{9,11},{10,... | collective-permute-start | bytes 786440 | tf_op jit(solution)/shard_map/ppermute | solution.py:524
  96.3 1.3 collective-permute-start.26
  97.9 2.8 %shard_map.74.inv_ref = f32[32,32]{1,0:T(8,128)S(1)} custom-call(f32[8,128]{1,0:T(8,128)S(1)} %slice.229.g_ref), custom_call_target="tpu_custom_call" | custom-call | bytes 9450000 | tf_op jit(solution)/shard_map/pallas_call | solution.py:313
  101.8 1.2 collective-permute-done.33
  103.0 1.2 collective-permute-start.34
  104.7 3.8 %collective-permute-done.26.refs_0_ = f32[64,1024]{1,0:T(8,128)S(1)} collective-permute-done((f32[64,1024]{1,0:T(8,128)S(1)}, f32[64,1024]{1,0:T(8,128)S(1)}, u32[]{:S(2)}, u32[]{:S(2)}) %collective-permute-start.26) | collective-permute-done | bytes 262176 | tf_op jit(solution)/shard_map/ppermute | solution.py:524
  109.3 2.9 %collective-permute-done.35 = f32[8,32]{1,0:T(8,128)S(1)} collective-permute-done((f32[8,32]{1,0:T(8,128)S(1)}, f32[8,32]{1,0:T(8,128)S(1)}, u32[]{:S(2)}, u32[]{:S(2)}) %collective-permute-start.35) | collective-permute-done | bytes 1056 | tf_op jit(solution)/shard_map/ppermute | solution.py:453
  112.6 3.2 %collective-permute-done.36 = f32[8,32]{1,0:T(8,128)S(1)} collective-permute-done((f32[8,32]{1,0:T(8,128)S(1)}, f32[8,32]{1,0:T(8,128)S(1)}, u32[]{:S(2)}, u32[]{:S(2)}) %collective-permute-start.36) | collective-permute-done | bytes 1056 | tf_op jit(solution)/shard_map/ppermute | solution.py:453
  116.5 3.8 %collective-permute-done.37 = f32[8,32]{1,0:T(8,128)S(1)} collective-permute-done((f32[8,32]{1,0:T(8,128)S(1)}, f32[8,32]{1,0:T(8,128)S(1)}, u32[]{:S(2)}, u32[]{:S(2)}) %collective-permute-start.37) | collective-permute-done | bytes 1056 | tf_op jit(solution)/shard_map/ppermute | solution.py:453
  120.8 3.2 %shard_map.75.refs_2_ = f32[8192,128]{1,0:T(8,128)S(1)} custom-call(s32[8]{0:T(128)S(1)} %get-tuple-element.20.base_ref, s32[8192]{0:T(1024)S(1)} %copy-done, f32[64,1024]{1,0:T(8,128)S(1)} %pad_maximum_fusion.3.u_ref.refs_0_, f32[64,1024]{1,0:T(8,128)S(1)} %collective-permute-done.32.refs_1_), custom_call_target="tpu_custom_call" | custom-call | bytes 11900000 | tf_op jit(solution)/shard_map/pallas_call | solution.py:231
  124.0 3.2 %shard_map.76.refs_2_ = f32[8192,128]{1,0:T(8,128)S(1)} custom-call(s32[8]{0:T(128)S(1)} %get-tuple-element.20.base_ref, s32[8192]{0:T(1024)S(1)} %copy-done, f32[64,1024]{1,0:T(8,128)S(1)} %collective-permute-done.30.refs_0_, f32[64,1024]{1,0:T(8,128)S(1)} %collective-permute-done.31.refs_1_, ...), custom_call_target="tpu_custom_call", output_to_operand_aliasing={{}: (4, {})} | custom-call | bytes 11900000 | tf_op jit(solution)/shard_map/pallas_call | solution.py:231
  127.3 3.2 %shard_map.77.refs_2_ = f32[8192,128]{1,0:T(8,128)S(1)} custom-call(s32[8]{0:T(128)S(1)} %get-tuple-element.20.base_ref, s32[8192]{0:T(1024)S(1)} %copy-done, f32[64,1024]{1,0:T(8,128)S(1)} %collective-permute-done.28.refs_0_, f32[64,1024]{1,0:T(8,128)S(1)} %collective-permute-done.29.refs_1_, ...), custom_call_target="tpu_custom_call", output_to_operand_aliasing={{}: (4, {})} | custom-call | bytes 11900000 | tf_op jit(solution)/shard_map/pallas_call | solution.py:231
  130.5 3.2 %shard_map.78.w_ref = f32[8192,128]{1,0:T(8,128)S(1)} custom-call(s32[8]{0:T(128)S(1)} %get-tuple-element.20.base_ref, s32[8192]{0:T(1024)S(1)} %copy-done, f32[64,1024]{1,0:T(8,128)S(1)} %collective-permute-done.26.refs_0_, f32[64,1024]{1,0:T(8,128)S(1)} %collective-permute-done.27.refs_1_, ...), custom_call_target="tpu_custom_call", output_to_operand_aliasing={{}: (4, {})} | custom-call | bytes 11900000 | tf_op jit(solution)/shard_map/pallas_call | solution.py:231
  133.7 3.5 %shard_map.79 = f32[64,8192]{1,0:T(8,128)} custom-call(f32[32,32]{1,0:T(8,128)S(1)} %shard_map.74.inv_ref, f32[8192,128]{1,0:T(8,128)S(1)} %shard_map.78.w_ref), custom_call_target="tpu_custom_call" | custom-call | bytes 21000000 | tf_op jit(solution)/shard_map/pallas_call | solution.py:281
  (96 shorter events, 12.3 us)
Async XLA Ops:
  0.6 11.5 %copy-start.1 = (f32[2,32,8192]{2,1,0:T(8,128)S(1)}, f32[2,32,8192]{2,1,0:T(8,128)}, u32[]{:S(2)}) copy-start(f32[2,32,8192]{2,1,0:T(8,128)} %param.7) | copy-start | bytes 6291460
  11.5 1.5 %collective-permute-start = (f32[32,1024]{1,0:T(8,128)S(1)}, f32[32,1024]{1,0:T(8,128)S(1)}, u32[]{:S(2)}, u32[]{:S(2)}) collective-permute-start(f32[32,1024]{1,0:T(8,128)S(1)} %slice_select_fusion.2), channel_id=1, source_target_pairs={{0,1},{1,0},{2,3},{3,2},{4,5},{5,4},{6,7},{7,6},{8,9},{9,8},{10,11... | collective-permute-start | bytes 393224 | tf_op jit(solution)/shard_map/ppermute | solution.py:484
  13.1 7.8 %collective-permute-start.1 = (f32[32,1024]{1,0:T(8,128)S(1)}, f32[32,1024]{1,0:T(8,128)S(1)}, u32[]{:S(2)}, u32[]{:S(2)}) collective-permute-start(f32[32,1024]{1,0:T(8,128)S(1)} %select_add_fusion), channel_id=1, source_target_pairs={{0,6},{1,7},{2,4},{3,5},{4,2},{5,3},{6,0},{7,1},{8,14},{9,15},{10,... | collective-permute-start | bytes 393224 | tf_op jit(solution)/shard_map/ppermute | solution.py:445
  17.0 6.6 %collective-permute-start.2 = (f32[32,1024]{1,0:T(8,128)S(1)}, f32[32,1024]{1,0:T(8,128)S(1)}, u32[]{:S(2)}, u32[]{:S(2)}) collective-permute-start(f32[32,1024]{1,0:T(8,128)S(1)} %select_add_fusion), channel_id=1, source_target_pairs={{0,4},{1,5},{2,6},{3,7},{4,0},{5,1},{6,2},{7,3},{8,12},{9,13},{10,... | collective-permute-start | bytes 393224 | tf_op jit(solution)/shard_map/ppermute | solution.py:445
  17.5 6.4 %collective-permute-start.3 = (f32[32,1024]{1,0:T(8,128)S(1)}, f32[32,1024]{1,0:T(8,128)S(1)}, u32[]{:S(2)}, u32[]{:S(2)}) collective-permute-start(f32[32,1024]{1,0:T(8,128)S(1)} %select_add_fusion), channel_id=1, source_target_pairs={{0,2},{1,3},{2,0},{3,1},{4,6},{5,7},{6,4},{7,5},{8,10},{9,11},{10,... | collective-permute-start | bytes 393224 | tf_op jit(solution)/shard_map/ppermute | solution.py:445
  23.9 4.2 %collective-permute-start.4 = (f32[32,1024]{1,0:T(8,128)S(1)}, f32[32,1024]{1,0:T(8,128)S(1)}, u32[]{:S(2)}, u32[]{:S(2)}) collective-permute-start(f32[32,1024]{1,0:T(8,128)S(1)} %add_add_fusion.1), channel_id=1, source_target_pairs={{0,1},{1,0},{2,3},{3,2},{4,5},{5,4},{6,7},{7,6},{8,9},{9,8},{10,11... | collective-permute-start | bytes 393224 | tf_op jit(solution)/shard_map/ppermute | solution.py:487
  29.9 6.6 %collective-permute-start.5 = (f32[16,1024]{1,0:T(8,128)S(1)}, f32[16,1024]{1,0:T(8,128)S(1)}, u32[]{:S(2)}, u32[]{:S(2)}) collective-permute-start(f32[16,1024]{1,0:T(8,128)S(1)} %get-tuple-element.40), channel_id=1, source_target_pairs={{0,24},{8,16},{16,8},{24,0},{1,25},{9,17},{17,9},{25,1},{2,26},{10... | collective-permute-start | bytes 196616 | tf_op jit(solution)/shard_map/ppermute | solution.py:429
  33.6 6.1 %collective-permute-start.6 = (f32[16,1024]{1,0:T(8,128)S(1)}, f32[16,1024]{1,0:T(8,128)S(1)}, u32[]{:S(2)}, u32[]{:S(2)}) collective-permute-start(f32[16,1024]{1,0:T(8,128)S(1)} %get-tuple-element.41), channel_id=1, source_target_pairs={{0,16},{8,24},{16,0},{24,8},{1,17},{9,25},{17,1},{25,9},{2,18},{10... | collective-permute-start | bytes 196616 | tf_op jit(solution)/shard_map/ppermute | solution.py:429
  33.6 6.1 %collective-permute-start.7 = (f32[16,1024]{1,0:T(8,128)S(1)}, f32[16,1024]{1,0:T(8,128)S(1)}, u32[]{:S(2)}, u32[]{:S(2)}) collective-permute-start(f32[16,1024]{1,0:T(8,128)S(1)} %get-tuple-element.42), channel_id=1, source_target_pairs={{0,8},{8,0},{16,24},{24,16},{1,9},{9,1},{17,25},{25,17},{2,10},{10... | collective-permute-start | bytes 196616 | tf_op jit(solution)/shard_map/ppermute | solution.py:429
  39.7 4.3 %collective-permute-start.10 = (f32[16,1024]{1,0:T(8,128)S(1)}, f32[16,1024]{1,0:T(8,128)S(1)}, u32[]{:S(2)}, u32[]{:S(2)}) collective-permute-start(f32[16,1024]{1,0:T(8,128)S(1)} %add_add_fusion.3), channel_id=1, source_target_pairs={{0,8},{8,0},{16,24},{24,16},{1,9},{9,1},{17,25},{25,17},{2,10},{10... | collective-permute-start | bytes 196616 | tf_op jit(solution)/shard_map/ppermute | solution.py:437
  41.0 6.1 %collective-permute-start.8 = (f32[16,1024]{1,0:T(8,128)S(1)}, f32[16,1024]{1,0:T(8,128)S(1)}, u32[]{:S(2)}, u32[]{:S(2)}) collective-permute-start(f32[16,1024]{1,0:T(8,128)S(1)} %add_add_fusion.3), channel_id=1, source_target_pairs={{0,24},{8,16},{16,8},{24,0},{1,25},{9,17},{17,9},{25,1},{2,26},{10... | collective-permute-start | bytes 196616 | tf_op jit(solution)/shard_map/ppermute | solution.py:437
  42.5 7.2 %collective-permute-start.9 = (f32[16,1024]{1,0:T(8,128)S(1)}, f32[16,1024]{1,0:T(8,128)S(1)}, u32[]{:S(2)}, u32[]{:S(2)}) collective-permute-start(f32[16,1024]{1,0:T(8,128)S(1)} %add_add_fusion.3), channel_id=1, source_target_pairs={{0,16},{8,24},{16,0},{24,8},{1,17},{9,25},{17,1},{25,9},{2,18},{10... | collective-permute-start | bytes 196616 | tf_op jit(solution)/shard_map/ppermute | solution.py:437
  52.7 1.5 %collective-permute-start.11 = (f32[40,1024]{1,0:T(8,128)S(1)}, f32[40,1024]{1,0:T(8,128)S(1)}, u32[]{:S(2)}, u32[]{:S(2)}) collective-permute-start(f32[40,1024]{1,0:T(8,128)S(1)} %fusion.6), channel_id=1, source_target_pairs={{0,1},{1,0},{2,3},{3,2},{4,5},{5,4},{6,7},{7,6},{8,9},{9,8},{10,11... | collective-permute-start | bytes 491528 | tf_op jit(solution)/shard_map/ppermute | solution.py:484
  54.2 8.1 %collective-permute-start.12 = (f32[40,1024]{1,0:T(8,128)S(1)}, f32[40,1024]{1,0:T(8,128)S(1)}, u32[]{:S(2)}, u32[]{:S(2)}) collective-permute-start(f32[40,1024]{1,0:T(8,128)S(1)} %fusion.7), channel_id=1, source_target_pairs={{0,6},{1,7},{2,4},{3,5},{4,2},{5,3},{6,0},{7,1},{8,14},{9,15},{10,... | collective-permute-start | bytes 491528 | tf_op jit(solution)/shard_map/ppermute | solution.py:445
  55.9 9.0 %collective-permute-start.13 = (f32[40,1024]{1,0:T(8,128)S(1)}, f32[40,1024]{1,0:T(8,128)S(1)}, u32[]{:S(2)}, u32[]{:S(2)}) collective-permute-start(f32[40,1024]{1,0:T(8,128)S(1)} %fusion.7), channel_id=1, source_target_pairs={{0,4},{1,5},{2,6},{3,7},{4,0},{5,1},{6,2},{7,3},{8,12},{9,13},{10,... | collective-permute-start | bytes 491528 | tf_op jit(solution)/shard_map/ppermute | solution.py:445
  57.2 7.7 %collective-permute-start.14 = (f32[40,1024]{1,0:T(8,128)S(1)}, f32[40,1024]{1,0:T(8,128)S(1)}, u32[]{:S(2)}, u32[]{:S(2)}) collective-permute-start(f32[40,1024]{1,0:T(8,128)S(1)} %fusion.7), channel_id=1, source_target_pairs={{0,2},{1,3},{2,0},{3,1},{4,6},{5,7},{6,4},{7,5},{8,10},{9,11},{10,... | collective-permute-start | bytes 491528 | tf_op jit(solution)/shard_map/ppermute | solution.py:445
  65.0 1.4 %collective-permute-start.15 = (f32[32,1024]{1,0:T(8,128)S(1)}, f32[32,1024]{1,0:T(8,128)S(1)}, u32[]{:S(2)}, u32[]{:S(2)}) collective-permute-start(f32[32,1024]{1,0:T(8,128)S(1)} %slice.218), channel_id=1, source_target_pairs={{0,1},{1,0},{2,3},{3,2},{4,5},{5,4},{6,7},{7,6},{8,9},{9,8},{10,11... | collective-permute-start | bytes 393224 | tf_op jit(solution)/shard_map/ppermute | solution.py:487
  67.9 6.8 %collective-permute-start.16 = (f32[16,1024]{1,0:T(8,128)S(1)}, f32[16,1024]{1,0:T(8,128)S(1)}, u32[]{:S(2)}, u32[]{:S(2)}) collective-permute-start(f32[16,1024]{1,0:T(8,128)S(1)} %get-tuple-element.31), channel_id=1, source_target_pairs={{0,24},{8,16},{16,8},{24,0},{1,25},{9,17},{17,9},{25,1},{2,26},{10... | collective-permute-start | bytes 196616 | tf_op jit(solution)/shard_map/ppermute | solution.py:429
  70.1 6.6 %collective-permute-start.17 = (f32[16,1024]{1,0:T(8,128)S(1)}, f32[16,1024]{1,0:T(8,128)S(1)}, u32[]{:S(2)}, u32[]{:S(2)}) collective-permute-start(f32[16,1024]{1,0:T(8,128)S(1)} %get-tuple-element.32), channel_id=1, source_target_pairs={{0,16},{8,24},{16,0},{24,8},{1,17},{9,25},{17,1},{25,9},{2,18},{10... | collective-permute-start | bytes 196616 | tf_op jit(solution)/shard_map/ppermute | solution.py:429
  70.1 6.6 %collective-permute-start.18 = (f32[16,1024]{1,0:T(8,128)S(1)}, f32[16,1024]{1,0:T(8,128)S(1)}, u32[]{:S(2)}, u32[]{:S(2)}) collective-permute-start(f32[16,1024]{1,0:T(8,128)S(1)} %get-tuple-element.33), channel_id=1, source_target_pairs={{0,8},{8,0},{16,24},{24,16},{1,9},{9,1},{17,25},{25,17},{2,10},{10... | collective-permute-start | bytes 196616 | tf_op jit(solution)/shard_map/ppermute | solution.py:429
  76.8 8.7 %collective-permute-start.19 = (f32[16,1024]{1,0:T(8,128)S(1)}, f32[16,1024]{1,0:T(8,128)S(1)}, u32[]{:S(2)}, u32[]{:S(2)}) collective-permute-start(f32[16,1024]{1,0:T(8,128)S(1)} %add_add_fusion.2), channel_id=1, source_target_pairs={{0,24},{8,16},{16,8},{24,0},{1,25},{9,17},{17,9},{25,1},{2,26},{10... | collective-permute-start | bytes 196616 | tf_op jit(solution)/shard_map/ppermute | solution.py:437
  79.0 6.5 %collective-permute-start.20 = (f32[16,1024]{1,0:T(8,128)S(1)}, f32[16,1024]{1,0:T(8,128)S(1)}, u32[]{:S(2)}, u32[]{:S(2)}) collective-permute-start(f32[16,1024]{1,0:T(8,128)S(1)} %add_add_fusion.2), channel_id=1, source_target_pairs={{0,16},{8,24},{16,0},{24,8},{1,17},{9,25},{17,1},{25,9},{2,18},{10... | collective-permute-start | bytes 196616 | tf_op jit(solution)/shard_map/ppermute | solution.py:437
  79.0 6.5 %collective-permute-start.21 = (f32[16,1024]{1,0:T(8,128)S(1)}, f32[16,1024]{1,0:T(8,128)S(1)}, u32[]{:S(2)}, u32[]{:S(2)}) collective-permute-start(f32[16,1024]{1,0:T(8,128)S(1)} %add_add_fusion.2), channel_id=1, source_target_pairs={{0,8},{8,0},{16,24},{24,16},{1,9},{9,1},{17,25},{25,17},{2,10},{10... | collective-permute-start | bytes 196616 | tf_op jit(solution)/shard_map/ppermute | solution.py:437
  86.0 34.8 %copy-start = (s32[8192]{0:T(1024)S(1)}, s32[8192]{0:T(1024)}, u32[]{:S(2)}) copy-start(s32[8192]{0:T(1024)} %idx_ref.7) | copy-start | bytes 98308
  89.0 1.4 %collective-permute-start.22 = (f32[264,128]{1,0:T(8,128)S(1)}, f32[264,128]{1,0:T(8,128)S(1)}, u32[]{:S(2)}, u32[]{:S(2)}) collective-permute-start(f32[264,128]{1,0:T(8,128)S(1)} %constant_dynamic-update-slice_fusion), channel_id=1, source_target_pairs={{0,1},{1,0},{2,3},{3,2},{4,5},{5,4},{6,7},{7,6},{8,9},{9,8},{10,11... | collective-permute-start | bytes 405512 | tf_op jit(solution)/shard_map/ppermute | solution.py:503
  90.5 5.8 %collective-permute-start.23 = (f32[72,128]{1,0:T(8,128)S(1)}, f32[72,128]{1,0:T(8,128)S(1)}, u32[]{:S(2)}, u32[]{:S(2)}) collective-permute-start(f32[72,128]{1,0:T(8,128)S(1)} %get-tuple-element.45), channel_id=1, source_target_pairs={{0,6},{1,7},{2,4},{3,5},{4,2},{5,3},{6,0},{7,1},{8,14},{9,15},{10,... | collective-permute-start | bytes 110600 | tf_op jit(solution)/shard_map/ppermute | solution.py:429
  92.2 5.3 %collective-permute-start.24 = (f32[72,128]{1,0:T(8,128)S(1)}, f32[72,128]{1,0:T(8,128)S(1)}, u32[]{:S(2)}, u32[]{:S(2)}) collective-permute-start(f32[72,128]{1,0:T(8,128)S(1)} %get-tuple-element.46), channel_id=1, source_target_pairs={{0,4},{1,5},{2,6},{3,7},{4,0},{5,1},{6,2},{7,3},{8,12},{9,13},{10,... | collective-permute-start | bytes 110600 | tf_op jit(solution)/shard_map/ppermute | solution.py:429
  93.5 4.4 %collective-permute-start.25 = (f32[72,128]{1,0:T(8,128)S(1)}, f32[72,128]{1,0:T(8,128)S(1)}, u32[]{:S(2)}, u32[]{:S(2)}) collective-permute-start(f32[72,128]{1,0:T(8,128)S(1)} %get-tuple-element.47), channel_id=1, source_target_pairs={{0,2},{1,3},{2,0},{3,1},{4,6},{5,7},{6,4},{7,5},{8,10},{9,11},{10,... | collective-permute-start | bytes 110600 | tf_op jit(solution)/shard_map/ppermute | solution.py:429
  94.1 10.1 %collective-permute-start.30 = (f32[64,1024]{1,0:T(8,128)S(1)}, f32[64,1024]{1,0:T(8,128)S(1)}, u32[]{:S(2)}, u32[]{:S(2)}) collective-permute-start(f32[64,1024]{1,0:T(8,128)S(1)} %pad_maximum_fusion.3.u_ref.refs_0_), channel_id=1, source_target_pairs={{0,2},{1,3},{2,0},{3,1},{4,6},{5,7},{6,4},{7,5},{8,10},{9,11},{10,... | collective-permute-start | bytes 786440 | tf_op jit(solution)/shard_map/ppermute | solution.py:524
  95.6 9.1 %collective-permute-start.28 = (f32[64,1024]{1,0:T(8,128)S(1)}, f32[64,1024]{1,0:T(8,128)S(1)}, u32[]{:S(2)}, u32[]{:S(2)}) collective-permute-start(f32[64,1024]{1,0:T(8,128)S(1)} %pad_maximum_fusion.3.u_ref.refs_0_), channel_id=1, source_target_pairs={{0,4},{1,5},{2,6},{3,7},{4,0},{5,1},{6,2},{7,3},{8,12},{9,13},{10,... | collective-permute-start | bytes 786440 | tf_op jit(solution)/shard_map/ppermute | solution.py:524
  96.3 12.2 %collective-permute-start.26 = (f32[64,1024]{1,0:T(8,128)S(1)}, f32[64,1024]{1,0:T(8,128)S(1)}, u32[]{:S(2)}, u32[]{:S(2)}) collective-permute-start(f32[64,1024]{1,0:T(8,128)S(1)} %pad_maximum_fusion.3.u_ref.refs_0_), channel_id=1, source_target_pairs={{0,6},{1,7},{2,4},{3,5},{4,2},{5,3},{6,0},{7,1},{8,14},{9,15},{10,... | collective-permute-start | bytes 786440 | tf_op jit(solution)/shard_map/ppermute | solution.py:524
  101.8 1.2 collective-permute-start.33
  103.0 5.5 %collective-permute-start.34 = (f32[8,32]{1,0:T(8,128)S(1)}, f32[8,32]{1,0:T(8,128)S(1)}, u32[]{:S(2)}, u32[]{:S(2)}) collective-permute-start(f32[8,32]{1,0:T(8,128)S(1)} %broadcast_add_fusion), channel_id=1, source_target_pairs={{0,2},{1,3},{2,0},{3,1},{4,6},{5,7},{6,4},{7,5},{8,10},{9,11},{10,... | collective-permute-start | bytes 3080 | tf_op jit(solution)/shard_map/ppermute | solution.py:453
  104.1 16.7 %collective-permute-start.32 = (f32[64,1024]{1,0:T(8,128)S(1)}, f32[64,1024]{1,0:T(8,128)S(1)}, u32[]{:S(2)}, u32[]{:S(2)}) collective-permute-start(f32[64,1024]{1,0:T(8,128)S(1)} %pad_maximum_fusion.3.u_ref.refs_0_), channel_id=1, source_target_pairs={{0,1},{1,0},{2,3},{3,2},{4,5},{5,4},{6,7},{7,6},{8,9},{9,8},{10,11... | collective-permute-start | bytes 786440 | tf_op jit(solution)/shard_map/ppermute | solution.py:524
  104.2 19.9 %collective-permute-start.31 = (f32[64,1024]{1,0:T(8,128)S(1)}, f32[64,1024]{1,0:T(8,128)S(1)}, u32[]{:S(2)}, u32[]{:S(2)}) collective-permute-start(f32[64,1024]{1,0:T(8,128)S(1)} %collective-permute-done.30.refs_0_), channel_id=1, source_target_pairs={{0,1},{1,0},{2,3},{3,2},{4,5},{5,4},{6,7},{7,6},{8,9},{9,8},{10,11... | collective-permute-start | bytes 786440 | tf_op jit(solution)/shard_map/ppermute | solution.py:527
  104.7 22.6 %collective-permute-start.29 = (f32[64,1024]{1,0:T(8,128)S(1)}, f32[64,1024]{1,0:T(8,128)S(1)}, u32[]{:S(2)}, u32[]{:S(2)}) collective-permute-start(f32[64,1024]{1,0:T(8,128)S(1)} %collective-permute-done.28.refs_0_), channel_id=1, source_target_pairs={{0,1},{1,0},{2,3},{3,2},{4,5},{5,4},{6,7},{7,6},{8,9},{9,8},{10,11... | collective-permute-start | bytes 786440 | tf_op jit(solution)/shard_map/ppermute | solution.py:527
  108.5 22.0 %collective-permute-start.27 = (f32[64,1024]{1,0:T(8,128)S(1)}, f32[64,1024]{1,0:T(8,128)S(1)}, u32[]{:S(2)}, u32[]{:S(2)}) collective-permute-start(f32[64,1024]{1,0:T(8,128)S(1)} %collective-permute-done.26.refs_0_), channel_id=1, source_target_pairs={{0,1},{1,0},{2,3},{3,2},{4,5},{5,4},{6,7},{7,6},{8,9},{9,8},{10,11... | collective-permute-start | bytes 786440 | tf_op jit(solution)/shard_map/ppermute | solution.py:527
  108.5 3.7 %collective-permute-start.35 = (f32[8,32]{1,0:T(8,128)S(1)}, f32[8,32]{1,0:T(8,128)S(1)}, u32[]{:S(2)}, u32[]{:S(2)}) collective-permute-start(f32[8,32]{1,0:T(8,128)S(1)} %fusion.33), channel_id=1, source_target_pairs={{0,4},{1,5},{2,6},{3,7},{4,0},{5,1},{6,2},{7,3},{8,12},{9,13},{10,... | collective-permute-start | bytes 3080 | tf_op jit(solution)/shard_map/ppermute | solution.py:453
  112.2 3.6 %collective-permute-start.36 = (f32[8,32]{1,0:T(8,128)S(1)}, f32[8,32]{1,0:T(8,128)S(1)}, u32[]{:S(2)}, u32[]{:S(2)}) collective-permute-start(f32[8,32]{1,0:T(8,128)S(1)} %add.103), channel_id=1, source_target_pairs={{0,8},{8,0},{16,24},{24,16},{1,9},{9,1},{17,25},{25,17},{2,10},{10... | collective-permute-start | bytes 3080 | tf_op jit(solution)/shard_map/ppermute | solution.py:453
  115.8 4.5 %collective-permute-start.37 = (f32[8,32]{1,0:T(8,128)S(1)}, f32[8,32]{1,0:T(8,128)S(1)}, u32[]{:S(2)}, u32[]{:S(2)}) collective-permute-start(f32[8,32]{1,0:T(8,128)S(1)} %add.104), channel_id=1, source_target_pairs={{0,16},{8,24},{16,0},{24,8},{1,17},{9,25},{17,1},{25,9},{2,18},{10... | collective-permute-start | bytes 3080 | tf_op jit(solution)/shard_map/ppermute | solution.py:453

commit v6 on v5

--- a/solution.py
+++ b/solution.py
@@ -87,8 +87,9 @@
 
 
 def start_kernel(
-    scale, phase_ref, rows_ref, probes_ref, frames_ref,
-    dh_ref, dl_ref, img_ref, mask_ref, base_ref, f_ref, p_ref, w_ref, n_ref, g_ref, b_ref, t_ref, idx_ref, steps_ref,
+    scale, cut, phase_ref, rows_ref, probes_ref, frames_ref,
+    dh_ref, dl_ref, img_ref, mask_ref, base_ref, b_ref, t_ref, f_ref, p_ref, w_ref, n_ref, g_ref,
+    idx_ref, steps_ref,
     sems, sem, tiny,
 ):
     vectors, modes = probes_ref.shape
@@ -163,29 +164,173 @@
             high, low = split(0.25 * (f_ref[frame[part], span] - f_ref[frame[part + 2], span]))
             dh_ref[part, span] = high
             dl_ref[part, span] = low
-        img_ref[:, span] = apply_forward(b_ref[...], t_ref[...], dh_ref, dl_ref, span)
+        if not cut:
+            img_ref[:, span] = apply_forward(b_ref[...], t_ref[...], dh_ref, dl_ref, span)
+    if cut:
+        from_rows(img_ref, "other", b_ref[...], t_ref[...], dh_ref, dl_ref)
+
+
+def side_start(side, rows):
+    core = lax.axis_index("mode") & 1
+    return pl.multiple_of((core if side == "own" else 1 - core) * (rows // 2), rows // 2)
+
+
+def from_rows(img_ref, side, both, turned, dh_ref, dl_ref):
+    rows = dh_ref.shape[1]
+    base = side_start(side, rows)
+    for i in range(0, rows // 2, BLOCK):
+        span = pl.ds(base + i, BLOCK)
+        img_ref[:, i : i + BLOCK] = apply_forward(both, turned, dh_ref, dl_ref, span)
+
+
+def own_kernel(b_ref, t_ref, dh_ref, dl_ref, img_ref):
+    from_rows(img_ref, "own", b_ref[...], t_ref[...], dh_ref, dl_ref)
+
+
+def own_half(both, turned, dh, dl):
+    return pl.pallas_call(
+        own_kernel,
+        out_shape=jax.ShapeDtypeStruct((both.shape[0] // 2, dh.shape[1] // 2), F32),
+        in_specs=[VMEM] * 4,
+        out_specs=VMEM,
+        cost_estimate=cost(1.3),
+        compiler_params=pltpu.CompilerParams(vmem_limit_bytes=8 << 20),
+    )(both, turned, in_vmem(dh), in_vmem(dl))
+
+
+def ahead_kernel(bits, side, has_inv, has_acc, places, *refs):
+    refs = list(refs)
+    inv = refs.pop(0)[...] if has_inv else None
+    acc_ref, acc_gram = (refs.pop(0), refs.pop(0)) if has_acc else (None, None)
+    pieces = [refs.pop(0)[...] for _ in bits]
+    dh_ref, dl_ref, img_ref = refs[:3]
+    here = lax.axis_index("pix")
+    width = pieces[0].shape[1]
+    half = pieces[0].shape[0] // 2
+    if has_inv:
+        pieces = [
+            jnp.concatenate([exact(inv, p[:half], NN), exact(inv, p[half:], NN)], axis=0)
+            for p in pieces
+        ]
+    if len(refs) > 3:
+        total = pack(sum(gram(p) for p in pieces))
+        refs[3][...] = total if acc_gram is None else total + acc_gram[...]
+    stacks = [stack_forward(p) for p in pieces]
+    cols = [pl.ds(pl.multiple_of((here ^ b) * width, width), width) for b in bits]
+    rows = dh_ref.shape[1]
+    base = 0 if side is None else side_start(side, rows)
+    for i in range(0, rows if side is None else rows // 2, BLOCK):
+        span = pl.ds(base + i, BLOCK)
+        part = sum(apply_ahead(*st, dh_ref, dl_ref, span, col) for st, col in zip(stacks, cols))
+        if acc_ref is not None:
+            part = part + acc_ref[:, span]
+        if places is None:
+            img_ref[:, i : i + BLOCK] = part
+        else:
+            w = rows // places
+            for j in range(BLOCK // w):
+                img_ref[i // w + j] = part[:, j * w : (j + 1) * w]
+
+
+def apply_ahead(both, turned, dh, dl, span, col):
+    n = both.shape[0] // 2
+    wide = dot(both, dh[0, span, col], NT) + dot(turned, dh[1, span, col], NT)
+    low = dot(both[:n], dl[0, span, col], NT) + dot(turned[:n], dl[1, span, col], NT)
+    return wide[:n] + wide[n:] + low
+
+
+def ahead(pieces, bits, dh, dl, side=None, inv=None, acc=None, places=None, with_gram=True):
+    rows = dh.shape[1]
+    vectors = pieces[0].shape[0]
+    shape = (vectors, rows if side is None else rows // 2)
+    if places is not None:
+        shape = (places, vectors, rows // places)
+    out = [jax.ShapeDtypeStruct(shape, F32)]
+    if with_gram:
+        out.append(jax.ShapeDtypeStruct((8, vectors // 2 * vectors // 16), F32))
+    args = ([] if inv is None else [inv]) + (list(acc) if acc else []) + list(pieces)
+    args += [in_vmem(dh), in_vmem(dl)]
+    kernel = functools.partial(
+        ahead_kernel, tuple(bits), side, inv is not None, acc is not None, places
+    )
+    return pl.pallas_call(
+        kernel,
+        out_shape=out,
+        in_specs=[VMEM] * len(args),
+        out_specs=[VMEM] * len(out),
+        cost_estimate=cost(0.7 * len(bits) * (1 if side is None else 0.5)),
+        compiler_params=pltpu.CompilerParams(vmem_limit_bytes=8 << 20),
+    )(*args)
+
+
+def behind_kernel(bits, side, has_inv, has_acc, *refs):
+    refs = list(refs)
+    inv = refs.pop(0)[...] if has_inv else None
+    img_ref = refs.pop(0)
+    accs = [refs.pop(0) for _ in bits] if has_acc else [None] * len(bits)
+    dh_ref, dl_ref = refs[:2]
+    outs = refs[2:]
+    vectors, _ = img_ref.shape
+    half = vectors // 2
+    real, imag = img_ref[:half], img_ref[half:]
+    if has_inv:
+        real, imag = exact(inv, real, NN), exact(inv, imag, NN)
+    stacks = []
+    for pair in ([real, imag], [imag, -real]):
+        high, low = split(jnp.concatenate(pair, axis=0))
+        stacks.append((high, jnp.concatenate([high, low], axis=0)))
+    here = lax.axis_index("pix")
+    rows = dh_ref.shape[1]
+    span = pl.ds(side_start(side, rows), rows // 2)
+    for b, acc, out in zip(bits, accs, outs):
+        width = out.shape[1]
+        col = pl.ds(pl.multiple_of((here ^ b) * width, width), width)
+        wide = dot(stacks[0][1], dh_ref[0, span, col], NN) + dot(stacks[1][1], dh_ref[1, span, col], NN)
+        low = dot(stacks[0][0], dl_ref[0, span, col], NN) + dot(stacks[1][0], dl_ref[1, span, col], NN)
+        total = wide[:vectors] + wide[vectors:] + low
+        out[...] = total if acc is None else total + acc[...]
+
+
+def behind(images, bits, dh, dl, side, inv=None, accs=None):
+    vectors = images.shape[0]
+    width = dh.shape[2] // lax.axis_size("pix")
+    args = ([] if inv is None else [inv]) + [images] + (list(accs) if accs else [])
+    args += [in_vmem(dh), in_vmem(dl)]
+    kernel = functools.partial(
+        behind_kernel, tuple(bits), side, inv is not None, accs is not None
+    )
+    return pl.pallas_call(
+        kernel,
+        out_shape=[jax.ShapeDtypeStruct((vectors, width), F32) for _ in bits],
+        in_specs=[VMEM] * len(args),
+        out_specs=[VMEM] * len(bits),
+        cost_estimate=cost(0.2 * len(bits)),
+        compiler_params=pltpu.CompilerParams(vmem_limit_bytes=8 << 20),
+    )(*args)
 
 
 def cost(us):
     return pl.CostEstimate(flops=0, transcendentals=0, bytes_accessed=int(us * 3.5e6))
 
 
-def start(phase_steps, idx, probes, frames, scale):
+def start(phase_steps, idx, probes, frames, scale, cut):
     vectors, modes = probes.shape
     steps, rows, count = frames.shape
     planes = pltpu.VMEM((2, rows, count), BF16)
     hbm = pl.BlockSpec(memory_space=pltpu.HBM)
     return pl.pallas_call(
-        functools.partial(start_kernel, scale),
+        functools.partial(start_kernel, scale, cut),
         out_shape=[
             planes,
             planes,
-            jax.ShapeDtypeStruct((vectors, rows), F32),
+            jax.ShapeDtypeStruct((vectors, rows // 2 if cut else rows), F32),
             jax.ShapeDtypeStruct((8, HB), F32),
             jax.ShapeDtypeStruct((modes // count,), jnp.int32),
+            jax.ShapeDtypeStruct((2 * vectors, count), BF16),
+            jax.ShapeDtypeStruct((2 * vectors, count), BF16),
         ],
         in_specs=[hbm, hbm, hbm, hbm],
-        out_specs=[VMEM, VMEM, VMEM, VMEM, SMEM],
+        out_specs=[VMEM, VMEM, VMEM, VMEM, SMEM, VMEM, VMEM],
         cost_estimate=cost(12),
         scratch_shapes=[
             pltpu.VMEM((steps, rows, count), F32),
@@ -193,8 +338,6 @@
             pltpu.VMEM((vectors, modes), F32),
             pltpu.VMEM((modes, HB), F32),
             pltpu.VMEM((count, HB), F32),
-            pltpu.VMEM((2 * vectors, count), BF16),
-            pltpu.VMEM((2 * vectors, count), BF16),
             pltpu.SMEM((modes,), jnp.int32),
             pltpu.SMEM((steps,), jnp.int32),
             pltpu.SemaphoreType.DMA((steps, rows // min(COPY, rows))),
@@ -292,7 +435,13 @@
 
 def factor_kernel(g_ref, out_ref):
     n = out_ref.shape[0]
-    square = jnp.concatenate([g_ref[:, i * n : (i + 1) * n] for i in range(n // 8)], axis=0)
+    eliminate(
+        jnp.concatenate([g_ref[:, i * n : (i + 1) * n] for i in range(n // 8)], axis=0), out_ref
+    )
+
+
+def eliminate(square, out_ref):
+    n = square.shape[0]
     row = lax.broadcasted_iota(jnp.int32, (n, n), 0)
     eye = (row == lax.broadcasted_iota(jnp.int32, (n, n), 1)).astype(F32)
     both = jnp.concatenate([square, eye], axis=1)
@@ -307,6 +456,22 @@
 def pack(gram_matrix):
     n = gram_matrix.shape[0]
     return jnp.concatenate([gram_matrix[i : i + 8] for i in range(0, n, 8)], axis=1)
+
+
+def probe_factor_kernel(p_ref, out_ref):
+    eliminate(gram(p_ref[...]), out_ref)
+
+
+def probe_factor(probes):
+    n = probes.shape[0] // 2
+    return pl.pallas_call(
+        probe_factor_kernel,
+        out_shape=jax.ShapeDtypeStruct((n, n), F32),
+        in_specs=[VMEM],
+        out_specs=VMEM,
+        cost_estimate=cost(4.5),
+        compiler_params=pltpu.CompilerParams(vmem_limit_bytes=8 << 20),
+    )(probes)
 
 
 def inverse_factor(packed, n):
@@ -529,30 +694,83 @@
     return table
 
 
+def sum_chips(other, own, packed=None):
+    n = lax.axis_size("mode")
+    rows = other.shape[0]
+    if packed is not None:
+        row = jnp.pad(packed, ((0, 0), (0, other.shape[1] - packed.shape[1])))
+        other = jnp.concatenate([other, row], axis=0)
+    got = lax.ppermute(other, "mode", flip(n, 1))
+    own = own()
+    if packed is not None:
+        own = jnp.concatenate([own, row], axis=0)
+    chip = share_sum(own + got, "mode", 2, 4)
+    far = lax.ppermute(chip[:rows], "mode", flip(n, 1))
+    return chip[:rows], far, (None if packed is None else chip[rows:, : packed.shape[1]])
+
+
+def return_pieces(mine, far, dh, dl, inv=None):
+    n = lax.axis_size("pix")
+    near = behind(mine, range(n), dh, dl, "own", inv)
+    third, second = behind(far, (3, 2), dh, dl, "other", inv, (near[3], near[2]))
+    first, total = behind(far, (1, 0), dh, dl, "other", inv, (near[1], near[0]))
+    for b, piece in ((3, third), (2, second), (1, first)):
+        total = total + lax.ppermute(piece, "pix", flip(n, b))
+    out = [total]
+    for b in (1, 2, 3):
+        out.append(lax.ppermute(total, "pix", flip(n, b)))
+    return out
+
+
 def measure(frames, phase_steps, pattern_rows, probes):
     columns = frames.shape[2]
     rows = frames.shape[1]
     groups = lax.axis_size("mode")
-    pixels = rows * lax.axis_size("pix")
+    places = lax.axis_size("pix")
+    pixels = rows * places
     modes_total = columns * groups
     k = probes.shape[1]
     vectors = 2 * k
     probes = probes.reshape(vectors, modes_total)
     scale = 1.0 / math.sqrt(modes_total)
-    dh, dl, images, masks, bases = start(phase_steps, pattern_rows, probes, frames, scale)
+    cut = groups == 8 and places == 4
+    dh, dl, images, masks, bases, both, turned = start(
+        phase_steps, pattern_rows, probes, frames, scale, cut
+    )
     odds = [masks[b : b + 1, :1] != 0 for b in range(8)]
-    inv = inverse_factor(pack(gram(probes)), k)
-    images, _ = sum_mode(images, odds)
-    partial = backward(inv, images, dh, dl)
-    returned = sum_pix(partial, odds)
-    for _ in range(1, ITERS):
-        images, packed = forward(returned, dh, dl)
-        images, packed = sum_mode(images, odds, packed)
-        inv = inverse_factor(packed, k)
-        partial = backward(None, images, dh, dl)
-        returned = normalise(inv, sum_pix(partial, odds))
-    table = gather_rows(returned, bases, pattern_rows)
-    images, packed = forward(returned, dh, dl, groups)
+    inv = probe_factor(probes)
+    if cut:
+        mine, far, _ = sum_chips(images, lambda: own_half(both, turned, dh, dl))
+        pieces = return_pieces(mine, far, dh, dl, inv)
+        inv = None
+        for iteration in range(1, ITERS + 1):
+            early = ahead(pieces[:2], (0, 1), dh, dl, inv=inv)
+            if iteration == ITERS:
+                break
+            other, packed = ahead(pieces[2:], (2, 3), dh, dl, "other", inv, early)
+
+            def own(pieces=pieces, inv=inv, early=early):
+                return ahead(pieces[2:], (2, 3), dh, dl, "own", inv, early, None, False)[0]
+
+            mine, far, packed = sum_chips(other, own, packed)
+            last_inv = inverse_factor(packed, k)
+            pieces = return_pieces(mine, far, dh, dl, inv)
+            inv = last_inv
+        by_place = jnp.concatenate(pick(pieces, odds[4:6]), axis=1)
+        returned = by_place if inv is None else normalise(inv, by_place)
+        table = gather_rows(returned, bases, pattern_rows)
+        images, packed = ahead(pieces[2:], (2, 3), dh, dl, None, inv, early, groups)
+    else:
+        images, _ = sum_mode(images, odds)
+        returned = sum_pix(backward(inv, images, dh, dl), odds)
+        for _ in range(1, ITERS):
+            images, packed = forward(returned, dh, dl)
+            images, packed = sum_mode(images, odds, packed)
+            inv = inverse_factor(packed, k)
+            partial = backward(None, images, dh, dl)
+            returned = normalise(inv, sum_pix(partial, odds))
+        table = gather_rows(returned, bases, pattern_rows)
+        images, packed = forward(returned, dh, dl, groups)
     fields, packed = scatter_mode(images, odds, packed)
     inv = inverse_factor(packed, k)
     fields = normalise(inv, fields)

time: 138 us -> 138 us (level)
  Pallas kernels: 43.3 us -> 49.2 us
  waiting for transfers between devices: 47.8 us -> 44.7 us
  matrix products: 2.73 us -> 0.79 us
    ppermute x9 -> x3, waiting for transfers between devices: 10 us -> 0.25 us  [scatter_sum(): total = total + lax.ppermute(mine[b], axis, flip(size, b * step))]
    ppermute x10 -> x16, starting transfers between devices: 8.78 us -> 17.8 us  [the longest x6 9.04 us: return_pieces(): total = total + lax.ppermute(piece, 'pix', flip(n, b))]
    ppermute x9 -> x3, starting transfers between devices: 12.5 us -> 3.55 us  [scatter_sum(): total = total + lax.ppermute(mine[b], axis, flip(size, b * step))]
    pallas_call x5 -> x14, Pallas kernels: 18.6 us -> 27.4 us  [the longest x1 10.6 us: start(): pl.pallas_call(functools.partial(start_kernel, scale, cut), out_shape=[pl...]
    ppermute x10 -> x16, waiting for transfers between devices: 9.17 us -> 14.7 us  [the longest x6 8.82 us: return_pieces(): total = total + lax.ppermute(piece, 'pix', flip(n, b))]
    pallas_call x3 -> x2, Pallas kernels: 8.38 us -> 5.51 us  [inverse_factor(): pl.pallas_call(factor_kernel, cost_estimate=cost(2.7), out_shape=jax.Shap...]
    dot_general x6 -> x4, matrix products: 2.73 us -> 0.79 us  [exact(): lax.dot_general(a, b, dims, precision=precise, preferred_element_type=F32)]
  transfers between devices with their start and end apart: 38 -> 38, of which waited for: 21 -> 22; matrix products, arithmetic and copies ran while one was open for 3% -> 2% of each run, Pallas kernels for 13% -> 19%
where the time goes in v6:
time: 138 us; the launch traced here: 137 us
  Pallas kernels  49.2 us (36%)
  waiting for transfers between devices  44.7 us (32%)
  starting transfers between devices  35.9 us (26%)
  between operations  4.44 us (3%)
  other arithmetic  1.68 us (1%)
    ppermute x6, waiting for transfers between devices, share_sum(): total = total + lax.ppermute(block, axis, flip(size, b * step))  13.1 us
    pallas_call x4, Pallas kernels, scatter_rows(): pl.pallas_call(functools.partial(scatter_kernel, places), cost_estimate=c...  12.8 us
    ppermute x5, waiting for transfers between devices, double_sum(): block = block + lax.ppermute(block, axis, flip(size, bit))  11.7 us
    pallas_call x1, Pallas kernels, start(): pl.pallas_call(functools.partial(start_kernel, scale, cut), out_shape=[pl...  10.6 us
    ppermute x6, starting transfers between devices, return_pieces(): total = total + lax.ppermute(piece, 'pix', flip(n, b))  9.04 us
    ppermute x6, waiting for transfers between devices, return_pieces(): total = total + lax.ppermute(piece, 'pix', flip(n, b))  8.82 us
    ppermute x6, starting transfers between devices, return_pieces(): out.append(lax.ppermute(total, 'pix', flip(n, b)))  8.01 us
    ppermute x6, starting transfers between devices, share_sum(): total = total + lax.ppermute(block, axis, flip(size, b * step))  7.72 us
  transfers between devices with their start and end apart: 38, of which 22 were waited for; matrix products, arithmetic and copies ran while one was open for 2% of the time, Pallas kernels for 19%

profile of v6, /device:TPU:0, one launch (start us, length us, event | category | flops | bytes accessed | tf_op | source)
XLA Modules:
  0.0 137.3 jit_solution(18114956764387848750)
XLA Ops:
  0.6 10.6 %shard_map.67 = (bf16[2,1024,1024]{2,1,0:T(8,128)(2,1)S(1)}, bf16[2,1024,1024]{2,1,0:T(8,128)(2,1)S(1)}, f32[64,512]{1,0:T(8,128)S(1)}, f32[8,128]{1,0:T(8,128)S...) custom-call(s32[4]{0:T(128)} %phase_ref.1, s32[8192]{0:T(1024)} %idx_ref.7, ...), custom_call_target="tpu_custom_call" | custom-call | bytes 42000000 | tf_op jit(solution)/shard_map/pallas_call | solution.py:321
  11.8 1.4 %shard_map.69 = f32[64,512]{1,0:T(8,128)S(1)} custom-call(bf16[128,1024]{1,0:T(8,128)(2,1)S(1)} %get-tuple-element.35.b_ref, bf16[128,1024]{1,0:T(8,128)(2,1)S(1)} %get-tuple-element.36.t_ref, bf16[2,1024,1024]{2,1,0:T(8,128)(2,1)S(1)} %get-tuple-element.37.dh_ref.refs_2_.refs_4_.refs_1_.refs_3_.refs_5_, ...), custom_call_target="tpu_custom_call" | custom-call | bytes 4550000 | tf_op jit(solution)/shard_map/pallas_call | solution.py:191
  13.3 3.5 %collective-permute-start.1 = (f32[64,512]{1,0:T(8,128)S(1)}, f32[64,512]{1,0:T(8,128)S(1)}, u32[]{:S(2)}, u32[]{:S(2)}) collective-permute-start(f32[64,512]{1,0:T(8,128)S(1)} %add.77), channel_id=1, source_target_pairs={{0,6},{1,7},{2,4},{3,5},{4,2},{5,3},{6,0},{7,1},{8,14},{9,15},{10,... | collective-permute-start | bytes 393224 | tf_op jit(solution)/shard_map/ppermute | solution.py:610
  17.4 3.7 %collective-permute-done.1 = f32[64,512]{1,0:T(8,128)S(1)} collective-permute-done((f32[64,512]{1,0:T(8,128)S(1)}, f32[64,512]{1,0:T(8,128)S(1)}, u32[]{:S(2)}, u32[]{:S(2)}) %collective-permute-start.1) | collective-permute-done | bytes 131104 | tf_op jit(solution)/shard_map/ppermute | solution.py:610
  21.1 2.6 %collective-permute-done.2 = f32[64,512]{1,0:T(8,128)S(1)} collective-permute-done((f32[64,512]{1,0:T(8,128)S(1)}, f32[64,512]{1,0:T(8,128)S(1)}, u32[]{:S(2)}, u32[]{:S(2)}) %collective-permute-start.2) | collective-permute-done | bytes 131104 | tf_op jit(solution)/shard_map/ppermute | solution.py:610
  24.2 4.5 %shard_map.68.refs_0_ = f32[32,32]{1,0:T(8,128)S(1)} custom-call(f32[64,8192]{1,0:T(8,128)S(1)} %bitcast.31), custom_call_target="tpu_custom_call" | custom-call | bytes 15750000 | tf_op jit(solution)/shard_map/pallas_call | solution.py:467
  28.6 1.0 shard_map.70
  30.3 3.7 %collective-permute-start.5 = (f32[64,256]{1,0:T(8,128)S(1)}, f32[64,256]{1,0:T(8,128)S(1)}, u32[]{:S(2)}, u32[]{:S(2)}) collective-permute-start(f32[64,256]{1,0:T(8,128)S(1)} %get-tuple-element.45), channel_id=1, source_target_pairs={{0,24},{8,16},{16,8},{24,0},{1,25},{9,17},{17,9},{25,1},{2,26},{10... | collective-permute-start | bytes 196616 | tf_op jit(solution)/shard_map/ppermute | solution.py:718
  34.7 0.8 collective-permute-start.7
  35.5 1.4 %collective-permute-done.5 = f32[64,256]{1,0:T(8,128)S(1)} collective-permute-done((f32[64,256]{1,0:T(8,128)S(1)}, f32[64,256]{1,0:T(8,128)S(1)}, u32[]{:S(2)}, u32[]{:S(2)}) %collective-permute-start.5) | collective-permute-done | bytes 65568 | tf_op jit(solution)/shard_map/ppermute | solution.py:718
  37.0 3.3 %collective-permute-done.6 = f32[64,256]{1,0:T(8,128)S(1)} collective-permute-done((f32[64,256]{1,0:T(8,128)S(1)}, f32[64,256]{1,0:T(8,128)S(1)}, u32[]{:S(2)}, u32[]{:S(2)}) %collective-permute-start.6) | collective-permute-done | bytes 65568 | tf_op jit(solution)/shard_map/ppermute | solution.py:718
  40.4 1.0 collective-permute-start.8
  41.4 2.1 %collective-permute-start.10 = (f32[64,256]{1,0:T(8,128)S(1)}, f32[64,256]{1,0:T(8,128)S(1)}, u32[]{:S(2)}, u32[]{:S(2)}) collective-permute-start(f32[64,256]{1,0:T(8,128)S(1)} %add_add_fusion.3.refs_0_), channel_id=1, source_target_pairs={{0,24},{8,16},{16,8},{24,0},{1,25},{9,17},{17,9},{25,1},{2,26},{10... | collective-permute-start | bytes 196616 | tf_op jit(solution)/shard_map/ppermute | solution.py:721
  44.8 1.5 %shard_map.73 = (f32[64,1024]{1,0:T(8,128)S(1)}, f32[8,128]{1,0:T(8,128)S(1)}) custom-call(f32[64,256]{1,0:T(8,128)S(1)} %add_add_fusion.3.refs_0_, f32[64,256]{1,0:T(8,128)S(1)} %collective-permute-done.8.refs_1_, bf16[2,1024,1024]{2,1,0:T(8,128)(2,1)S(1)} %get-tuple-element.37.dh_ref.refs_2_.refs_4_.refs_1_.refs_3_.refs_5_, ...), custom_call_target="tpu_custom_call" | custom-call | bytes 4900000 | tf_op jit(solution)/shard_map/pallas_call | solution.py:256
  46.3 1.7 %collective-permute-done.10.refs_3_ = f32[64,256]{1,0:T(8,128)S(1)} collective-permute-done((f32[64,256]{1,0:T(8,128)S(1)}, f32[64,256]{1,0:T(8,128)S(1)}, u32[]{:S(2)}, u32[]{:S(2)}) %collective-permute-start.10) | collective-permute-done | bytes 65568 | tf_op jit(solution)/shard_map/ppermute | solution.py:721
  47.9 2.3 %collective-permute-done.9.refs_2_ = f32[64,256]{1,0:T(8,128)S(1)} collective-permute-done((f32[64,256]{1,0:T(8,128)S(1)}, f32[64,256]{1,0:T(8,128)S(1)}, u32[]{:S(2)}, u32[]{:S(2)}) %collective-permute-start.9) | collective-permute-done | bytes 65568 | tf_op jit(solution)/shard_map/ppermute | solution.py:721
  50.3 0.8 shard_map.75
  52.6 1.7 %collective-permute-start.12 = (f32[72,512]{1,0:T(8,128)S(1)}, f32[72,512]{1,0:T(8,128)S(1)}, u32[]{:S(2)}, u32[]{:S(2)}) collective-permute-start(f32[72,512]{1,0:T(8,128)S(1)} %fusion.2), channel_id=1, source_target_pairs={{0,6},{1,7},{2,4},{3,5},{4,2},{5,3},{6,0},{7,1},{8,14},{9,15},{10,... | collective-permute-start | bytes 442376 | tf_op jit(solution)/shard_map/ppermute | solution.py:610
  54.3 1.3 collective-permute-start.13
  56.1 4.2 %collective-permute-done.12 = f32[72,512]{1,0:T(8,128)S(1)} collective-permute-done((f32[72,512]{1,0:T(8,128)S(1)}, f32[72,512]{1,0:T(8,128)S(1)}, u32[]{:S(2)}, u32[]{:S(2)}) %collective-permute-start.12) | collective-permute-done | bytes 147488 | tf_op jit(solution)/shard_map/ppermute | solution.py:610
  60.3 2.3 %collective-permute-done.13 = f32[72,512]{1,0:T(8,128)S(1)} collective-permute-done((f32[72,512]{1,0:T(8,128)S(1)}, f32[72,512]{1,0:T(8,128)S(1)}, u32[]{:S(2)}, u32[]{:S(2)}) %collective-permute-start.13) | collective-permute-done | bytes 147488 | tf_op jit(solution)/shard_map/ppermute | solution.py:610
  62.8 0.8 shard_map.77
  64.8 2.1 %collective-permute-start.16 = (f32[64,256]{1,0:T(8,128)S(1)}, f32[64,256]{1,0:T(8,128)S(1)}, u32[]{:S(2)}, u32[]{:S(2)}) collective-permute-start(f32[64,256]{1,0:T(8,128)S(1)} %get-tuple-element.57), channel_id=1, source_target_pairs={{0,24},{8,16},{16,8},{24,0},{1,25},{9,17},{17,9},{25,1},{2,26},{10... | collective-permute-start | bytes 196616 | tf_op jit(solution)/shard_map/ppermute | solution.py:718
  67.3 2.5 %collective-permute-start.18 = (f32[64,256]{1,0:T(8,128)S(1)}, f32[64,256]{1,0:T(8,128)S(1)}, u32[]{:S(2)}, u32[]{:S(2)}) collective-permute-start(f32[64,256]{1,0:T(8,128)S(1)} %get-tuple-element.59), channel_id=1, source_target_pairs={{0,8},{8,0},{16,24},{24,16},{1,9},{9,1},{17,25},{25,17},{2,10},{10... | collective-permute-start | bytes 196616 | tf_op jit(solution)/shard_map/ppermute | solution.py:718
  69.8 1.8 %collective-permute-done.16 = f32[64,256]{1,0:T(8,128)S(1)} collective-permute-done((f32[64,256]{1,0:T(8,128)S(1)}, f32[64,256]{1,0:T(8,128)S(1)}, u32[]{:S(2)}, u32[]{:S(2)}) %collective-permute-start.16) | collective-permute-done | bytes 65568 | tf_op jit(solution)/shard_map/ppermute | solution.py:718
  71.6 2.1 %collective-permute-done.17 = f32[64,256]{1,0:T(8,128)S(1)} collective-permute-done((f32[64,256]{1,0:T(8,128)S(1)}, f32[64,256]{1,0:T(8,128)S(1)}, u32[]{:S(2)}, u32[]{:S(2)}) %collective-permute-start.17) | collective-permute-done | bytes 65568 | tf_op jit(solution)/shard_map/ppermute | solution.py:718
  74.1 2.2 %collective-permute-start.20 = (f32[64,256]{1,0:T(8,128)S(1)}, f32[64,256]{1,0:T(8,128)S(1)}, u32[]{:S(2)}, u32[]{:S(2)}) collective-permute-start(f32[64,256]{1,0:T(8,128)S(1)} %add_add_fusion.2.refs_1_), channel_id=1, source_target_pairs={{0,16},{8,24},{16,0},{24,8},{1,17},{9,25},{17,1},{25,9},{2,18},{10... | collective-permute-start | bytes 196616 | tf_op jit(solution)/shard_map/ppermute | solution.py:721
  76.3 1.8 %collective-permute-start.21 = (f32[64,256]{1,0:T(8,128)S(1)}, f32[64,256]{1,0:T(8,128)S(1)}, u32[]{:S(2)}, u32[]{:S(2)}) collective-permute-start(f32[64,256]{1,0:T(8,128)S(1)} %add_add_fusion.2.refs_1_), channel_id=1, source_target_pairs={{0,24},{8,16},{16,8},{24,0},{1,25},{9,17},{17,9},{25,1},{2,26},{10... | collective-permute-start | bytes 196616 | tf_op jit(solution)/shard_map/ppermute | solution.py:721
  82.0 2.8 %shard_map.76.refs_0_ = f32[32,32]{1,0:T(8,128)S(1)} custom-call(f32[8,128]{1,0:T(8,128)S(1)} %slice.128.g_ref), custom_call_target="tpu_custom_call" | custom-call | bytes 9450000 | tf_op jit(solution)/shard_map/pallas_call | solution.py:478
  85.4 1.7 %shard_map.80 = (f32[64,1024]{1,0:T(8,128)S(1)}, f32[8,128]{1,0:T(8,128)S(1)}) custom-call(f32[32,32]{1,0:T(8,128)S(1)} %shard_map.76.refs_0_, f32[64,256]{1,0:T(8,128)S(1)} %add_add_fusion.2.refs_1_, f32[64,256]{1,0:T(8,128)S(1)} %collective-permute-done.19.refs_2_, ...), custom_call_target="tpu_custom_call" | custom-call | bytes 4900000 | tf_op jit(solution)/shard_map/pallas_call | solution.py:256
  87.1 1.7 %shard_map.81 = (f32[8,64,128]{2,1,0:T(8,128)S(1)}, f32[8,128]{1,0:T(8,128)S(1)}) custom-call(f32[32,32]{1,0:T(8,128)S(1)} %shard_map.76.refs_0_, f32[64,1024]{1,0:T(8,128)S(1)} %get-tuple-element.60.refs_1_, f32[8,128]{1,0:T(8,128)S(1)} %get-tuple-element.61.refs_2_, f32[64,256]{1,0:T(8,128)S(1)} %collective-permute-done.20.refs_3_, ...), custom_call_target="tpu_custom_call" | custom-call | bytes 4900000 | tf_op jit(solution)/shard_map/pallas_call | solution.py:256
  89.0 1.3 collective-permute-done.22
  90.4 1.7 %collective-permute-start.23 = (f32[72,128]{1,0:T(8,128)S(1)}, f32[72,128]{1,0:T(8,128)S(1)}, u32[]{:S(2)}, u32[]{:S(2)}) collective-permute-start(f32[72,128]{1,0:T(8,128)S(1)} %get-tuple-element.73), channel_id=1, source_target_pairs={{0,6},{1,7},{2,4},{3,5},{4,2},{5,3},{6,0},{7,1},{8,14},{9,15},{10,... | collective-permute-start | bytes 110600 | tf_op jit(solution)/shard_map/ppermute | solution.py:594
  92.1 1.3 collective-permute-start.24
  94.0 1.6 %collective-permute-start.30 = (f32[64,1024]{1,0:T(8,128)S(1)}, f32[64,1024]{1,0:T(8,128)S(1)}, u32[]{:S(2)}, u32[]{:S(2)}) collective-permute-start(f32[64,1024]{1,0:T(8,128)S(1)} %pad_maximum_fusion.1.refs_0_), channel_id=1, source_target_pairs={{0,2},{1,3},{2,0},{3,1},{4,6},{5,7},{6,4},{7,5},{8,10},{9,11},{10,... | collective-permute-start | bytes 786440 | tf_op jit(solution)/shard_map/ppermute | solution.py:689
  96.3 1.3 collective-permute-start.26
  97.8 2.8 %shard_map.82.inv_ref = f32[32,32]{1,0:T(8,128)S(1)} custom-call(f32[8,128]{1,0:T(8,128)S(1)} %slice.136.g_ref), custom_call_target="tpu_custom_call" | custom-call | bytes 9450000 | tf_op jit(solution)/shard_map/pallas_call | solution.py:478
  101.7 1.2 collective-permute-done.33
  102.9 1.3 collective-permute-start.34
  104.7 3.8 %collective-permute-done.26.refs_0_ = f32[64,1024]{1,0:T(8,128)S(1)} collective-permute-done((f32[64,1024]{1,0:T(8,128)S(1)}, f32[64,1024]{1,0:T(8,128)S(1)}, u32[]{:S(2)}, u32[]{:S(2)}) %collective-permute-start.26) | collective-permute-done | bytes 262176 | tf_op jit(solution)/shard_map/ppermute | solution.py:689
  109.2 2.9 %collective-permute-done.35 = f32[8,32]{1,0:T(8,128)S(1)} collective-permute-done((f32[8,32]{1,0:T(8,128)S(1)}, f32[8,32]{1,0:T(8,128)S(1)}, u32[]{:S(2)}, u32[]{:S(2)}) %collective-permute-start.35) | collective-permute-done | bytes 1056 | tf_op jit(solution)/shard_map/ppermute | solution.py:618
  112.2 3.6 %collective-permute-done.36 = f32[8,32]{1,0:T(8,128)S(1)} collective-permute-done((f32[8,32]{1,0:T(8,128)S(1)}, f32[8,32]{1,0:T(8,128)S(1)}, u32[]{:S(2)}, u32[]{:S(2)}) %collective-permute-start.36) | collective-permute-done | bytes 1056 | tf_op jit(solution)/shard_map/ppermute | solution.py:618
  116.3 4.0 %collective-permute-done.37 = f32[8,32]{1,0:T(8,128)S(1)} collective-permute-done((f32[8,32]{1,0:T(8,128)S(1)}, f32[8,32]{1,0:T(8,128)S(1)}, u32[]{:S(2)}, u32[]{:S(2)}) %collective-permute-start.37) | collective-permute-done | bytes 1056 | tf_op jit(solution)/shard_map/ppermute | solution.py:618
  120.8 3.2 %shard_map.83.refs_2_ = f32[8192,128]{1,0:T(8,128)S(1)} custom-call(s32[8]{0:T(128)S(1)} %get-tuple-element.64.base_ref, s32[8192]{0:T(1024)S(1)} %copy-done.1, f32[64,1024]{1,0:T(8,128)S(1)} %pad_maximum_fusion.1.refs_0_, f32[64,1024]{1,0:T(8,128)S(1)} %collective-permute-done.32.refs_1_), custom_call_target="tpu_custom_call" | custom-call | bytes 11900000 | tf_op jit(solution)/shard_map/pallas_call | solution.py:374
  124.0 3.2 %shard_map.84.refs_2_ = f32[8192,128]{1,0:T(8,128)S(1)} custom-call(s32[8]{0:T(128)S(1)} %get-tuple-element.64.base_ref, s32[8192]{0:T(1024)S(1)} %copy-done.1, f32[64,1024]{1,0:T(8,128)S(1)} %collective-permute-done.30.refs_0_, f32[64,1024]{1,0:T(8,128)S(1)} %collective-permute-done.31.refs_1_, ...), custom_call_target="tpu_custom_call", output_to_operand_aliasing={{}: (4, {})} | custom-call | bytes 11900000 | tf_op jit(solution)/shard_map/pallas_call | solution.py:374
  127.2 3.2 %shard_map.85.refs_2_ = f32[8192,128]{1,0:T(8,128)S(1)} custom-call(s32[8]{0:T(128)S(1)} %get-tuple-element.64.base_ref, s32[8192]{0:T(1024)S(1)} %copy-done.1, f32[64,1024]{1,0:T(8,128)S(1)} %collective-permute-done.28.refs_0_, f32[64,1024]{1,0:T(8,128)S(1)} %collective-permute-done.29.refs_1_, ...), custom_call_target="tpu_custom_call", output_to_operand_aliasing={{}: (4, {})} | custom-call | bytes 11900000 | tf_op jit(solution)/shard_map/pallas_call | solution.py:374
  130.5 3.2 %shard_map.86.w_ref = f32[8192,128]{1,0:T(8,128)S(1)} custom-call(s32[8]{0:T(128)S(1)} %get-tuple-element.64.base_ref, s32[8192]{0:T(1024)S(1)} %copy-done.1, f32[64,1024]{1,0:T(8,128)S(1)} %collective-permute-done.26.refs_0_, f32[64,1024]{1,0:T(8,128)S(1)} %collective-permute-done.27.refs_1_, ...), custom_call_target="tpu_custom_call", output_to_operand_aliasing={{}: (4, {})} | custom-call | bytes 11900000 | tf_op jit(solution)/shard_map/pallas_call | solution.py:374
  133.7 3.5 %shard_map.87 = f32[64,8192]{1,0:T(8,128)} custom-call(f32[32,32]{1,0:T(8,128)S(1)} %shard_map.82.inv_ref, f32[8192,128]{1,0:T(8,128)S(1)} %shard_map.86.w_ref), custom_call_target="tpu_custom_call" | custom-call | bytes 21000000 | tf_op jit(solution)/shard_map/pallas_call | solution.py:424
  (91 shorter events, 15.0 us)
Async XLA Ops:
  11.2 2.0 %collective-permute-start = (f32[64,512]{1,0:T(8,128)S(1)}, f32[64,512]{1,0:T(8,128)S(1)}, u32[]{:S(2)}, u32[]{:S(2)}) collective-permute-start(f32[64,512]{1,0:T(8,128)S(1)} %get-tuple-element.39), channel_id=1, source_target_pairs={{0,1},{1,0},{2,3},{3,2},{4,5},{5,4},{6,7},{7,6},{8,9},{9,8},{10,11... | collective-permute-start | bytes 393224 | tf_op jit(solution)/shard_map/ppermute | solution.py:703
  11.8 12.4 %copy-start = (f32[2,32,8192]{2,1,0:T(8,128)S(1)}, f32[2,32,8192]{2,1,0:T(8,128)}, u32[]{:S(2)}) copy-start(f32[2,32,8192]{2,1,0:T(8,128)} %param.7) | copy-start | bytes 6291460
  13.3 7.8 %collective-permute-start.1 = (f32[64,512]{1,0:T(8,128)S(1)}, f32[64,512]{1,0:T(8,128)S(1)}, u32[]{:S(2)}, u32[]{:S(2)}) collective-permute-start(f32[64,512]{1,0:T(8,128)S(1)} %add.77), channel_id=1, source_target_pairs={{0,6},{1,7},{2,4},{3,5},{4,2},{5,3},{6,0},{7,1},{8,14},{9,15},{10,... | collective-permute-start | bytes 393224 | tf_op jit(solution)/shard_map/ppermute | solution.py:610
  16.8 6.9 %collective-permute-start.2 = (f32[64,512]{1,0:T(8,128)S(1)}, f32[64,512]{1,0:T(8,128)S(1)}, u32[]{:S(2)}, u32[]{:S(2)}) collective-permute-start(f32[64,512]{1,0:T(8,128)S(1)} %add.77), channel_id=1, source_target_pairs={{0,4},{1,5},{2,6},{3,7},{4,0},{5,1},{6,2},{7,3},{8,12},{9,13},{10,... | collective-permute-start | bytes 393224 | tf_op jit(solution)/shard_map/ppermute | solution.py:610
  17.3 6.7 %collective-permute-start.3 = (f32[64,512]{1,0:T(8,128)S(1)}, f32[64,512]{1,0:T(8,128)S(1)}, u32[]{:S(2)}, u32[]{:S(2)}) collective-permute-start(f32[64,512]{1,0:T(8,128)S(1)} %add.77), channel_id=1, source_target_pairs={{0,2},{1,3},{2,0},{3,1},{4,6},{5,7},{6,4},{7,5},{8,10},{9,11},{10,... | collective-permute-start | bytes 393224 | tf_op jit(solution)/shard_map/ppermute | solution.py:610
  24.1 5.6 %collective-permute-start.4 = (f32[64,512]{1,0:T(8,128)S(1)}, f32[64,512]{1,0:T(8,128)S(1)}, u32[]{:S(2)}, u32[]{:S(2)}) collective-permute-start(f32[64,512]{1,0:T(8,128)S(1)} %add_add_fusion.1.refs_1_), channel_id=1, source_target_pairs={{0,1},{1,0},{2,3},{3,2},{4,5},{5,4},{6,7},{7,6},{8,9},{9,8},{10,11... | collective-permute-start | bytes 393224 | tf_op jit(solution)/shard_map/ppermute | solution.py:708
  30.3 6.6 %collective-permute-start.5 = (f32[64,256]{1,0:T(8,128)S(1)}, f32[64,256]{1,0:T(8,128)S(1)}, u32[]{:S(2)}, u32[]{:S(2)}) collective-permute-start(f32[64,256]{1,0:T(8,128)S(1)} %get-tuple-element.45), channel_id=1, source_target_pairs={{0,24},{8,16},{16,8},{24,0},{1,25},{9,17},{17,9},{25,1},{2,26},{10... | collective-permute-start | bytes 196616 | tf_op jit(solution)/shard_map/ppermute | solution.py:718
  34.0 6.2 %collective-permute-start.6 = (f32[64,256]{1,0:T(8,128)S(1)}, f32[64,256]{1,0:T(8,128)S(1)}, u32[]{:S(2)}, u32[]{:S(2)}) collective-permute-start(f32[64,256]{1,0:T(8,128)S(1)} %get-tuple-element.46), channel_id=1, source_target_pairs={{0,16},{8,24},{16,0},{24,8},{1,17},{9,25},{17,1},{25,9},{2,18},{10... | collective-permute-start | bytes 196616 | tf_op jit(solution)/shard_map/ppermute | solution.py:718
  34.7 5.7 %collective-permute-start.7 = (f32[64,256]{1,0:T(8,128)S(1)}, f32[64,256]{1,0:T(8,128)S(1)}, u32[]{:S(2)}, u32[]{:S(2)}) collective-permute-start(f32[64,256]{1,0:T(8,128)S(1)} %get-tuple-element.47), channel_id=1, source_target_pairs={{0,8},{8,0},{16,24},{24,16},{1,9},{9,1},{17,25},{25,17},{2,10},{10... | collective-permute-start | bytes 196616 | tf_op jit(solution)/shard_map/ppermute | solution.py:718
  40.4 4.3 %collective-permute-start.8 = (f32[64,256]{1,0:T(8,128)S(1)}, f32[64,256]{1,0:T(8,128)S(1)}, u32[]{:S(2)}, u32[]{:S(2)}) collective-permute-start(f32[64,256]{1,0:T(8,128)S(1)} %add_add_fusion.3.refs_0_), channel_id=1, source_target_pairs={{0,8},{8,0},{16,24},{24,16},{1,9},{9,1},{17,25},{25,17},{2,10},{10... | collective-permute-start | bytes 196616 | tf_op jit(solution)/shard_map/ppermute | solution.py:721
  41.4 6.5 %collective-permute-start.10 = (f32[64,256]{1,0:T(8,128)S(1)}, f32[64,256]{1,0:T(8,128)S(1)}, u32[]{:S(2)}, u32[]{:S(2)}) collective-permute-start(f32[64,256]{1,0:T(8,128)S(1)} %add_add_fusion.3.refs_0_), channel_id=1, source_target_pairs={{0,24},{8,16},{16,8},{24,0},{1,25},{9,17},{17,9},{25,1},{2,26},{10... | collective-permute-start | bytes 196616 | tf_op jit(solution)/shard_map/ppermute | solution.py:721
  43.5 6.8 %collective-permute-start.9 = (f32[64,256]{1,0:T(8,128)S(1)}, f32[64,256]{1,0:T(8,128)S(1)}, u32[]{:S(2)}, u32[]{:S(2)}) collective-permute-start(f32[64,256]{1,0:T(8,128)S(1)} %add_add_fusion.3.refs_0_), channel_id=1, source_target_pairs={{0,16},{8,24},{16,0},{24,8},{1,17},{9,25},{17,1},{25,9},{2,18},{10... | collective-permute-start | bytes 196616 | tf_op jit(solution)/shard_map/ppermute | solution.py:721
  51.1 1.4 %collective-permute-start.11 = (f32[72,512]{1,0:T(8,128)S(1)}, f32[72,512]{1,0:T(8,128)S(1)}, u32[]{:S(2)}, u32[]{:S(2)}) collective-permute-start(f32[72,512]{1,0:T(8,128)S(1)} %fusion.1), channel_id=1, source_target_pairs={{0,1},{1,0},{2,3},{3,2},{4,5},{5,4},{6,7},{7,6},{8,9},{9,8},{10,11... | collective-permute-start | bytes 442376 | tf_op jit(solution)/shard_map/ppermute | solution.py:703
  52.6 7.7 %collective-permute-start.12 = (f32[72,512]{1,0:T(8,128)S(1)}, f32[72,512]{1,0:T(8,128)S(1)}, u32[]{:S(2)}, u32[]{:S(2)}) collective-permute-start(f32[72,512]{1,0:T(8,128)S(1)} %fusion.2), channel_id=1, source_target_pairs={{0,6},{1,7},{2,4},{3,5},{4,2},{5,3},{6,0},{7,1},{8,14},{9,15},{10,... | collective-permute-start | bytes 442376 | tf_op jit(solution)/shard_map/ppermute | solution.py:610
  54.3 8.3 %collective-permute-start.13 = (f32[72,512]{1,0:T(8,128)S(1)}, f32[72,512]{1,0:T(8,128)S(1)}, u32[]{:S(2)}, u32[]{:S(2)}) collective-permute-start(f32[72,512]{1,0:T(8,128)S(1)} %fusion.2), channel_id=1, source_target_pairs={{0,4},{1,5},{2,6},{3,7},{4,0},{5,1},{6,2},{7,3},{8,12},{9,13},{10,... | collective-permute-start | bytes 442376 | tf_op jit(solution)/shard_map/ppermute | solution.py:610
  55.6 7.0 %collective-permute-start.14 = (f32[72,512]{1,0:T(8,128)S(1)}, f32[72,512]{1,0:T(8,128)S(1)}, u32[]{:S(2)}, u32[]{:S(2)}) collective-permute-start(f32[72,512]{1,0:T(8,128)S(1)} %fusion.2), channel_id=1, source_target_pairs={{0,2},{1,3},{2,0},{3,1},{4,6},{5,7},{6,4},{7,5},{8,10},{9,11},{10,... | collective-permute-start | bytes 442376 | tf_op jit(solution)/shard_map/ppermute | solution.py:610
  62.7 1.4 %collective-permute-start.15 = (f32[64,512]{1,0:T(8,128)S(1)}, f32[64,512]{1,0:T(8,128)S(1)}, u32[]{:S(2)}, u32[]{:S(2)}) collective-permute-start(f32[64,512]{1,0:T(8,128)S(1)} %slice.129.refs_0_), channel_id=1, source_target_pairs={{0,1},{1,0},{2,3},{3,2},{4,5},{5,4},{6,7},{7,6},{8,9},{9,8},{10,11... | collective-permute-start | bytes 393224 | tf_op jit(solution)/shard_map/ppermute | solution.py:708
  64.8 6.8 %collective-permute-start.16 = (f32[64,256]{1,0:T(8,128)S(1)}, f32[64,256]{1,0:T(8,128)S(1)}, u32[]{:S(2)}, u32[]{:S(2)}) collective-permute-start(f32[64,256]{1,0:T(8,128)S(1)} %get-tuple-element.57), channel_id=1, source_target_pairs={{0,24},{8,16},{16,8},{24,0},{1,25},{9,17},{17,9},{25,1},{2,26},{10... | collective-permute-start | bytes 196616 | tf_op jit(solution)/shard_map/ppermute | solution.py:718
  66.8 6.9 %collective-permute-start.17 = (f32[64,256]{1,0:T(8,128)S(1)}, f32[64,256]{1,0:T(8,128)S(1)}, u32[]{:S(2)}, u32[]{:S(2)}) collective-permute-start(f32[64,256]{1,0:T(8,128)S(1)} %get-tuple-element.58), channel_id=1, source_target_pairs={{0,16},{8,24},{16,0},{24,8},{1,17},{9,25},{17,1},{25,9},{2,18},{10... | collective-permute-start | bytes 196616 | tf_op jit(solution)/shard_map/ppermute | solution.py:718
  67.3 6.4 %collective-permute-start.18 = (f32[64,256]{1,0:T(8,128)S(1)}, f32[64,256]{1,0:T(8,128)S(1)}, u32[]{:S(2)}, u32[]{:S(2)}) collective-permute-start(f32[64,256]{1,0:T(8,128)S(1)} %get-tuple-element.59), channel_id=1, source_target_pairs={{0,8},{8,0},{16,24},{24,16},{1,9},{9,1},{17,25},{25,17},{2,10},{10... | collective-permute-start | bytes 196616 | tf_op jit(solution)/shard_map/ppermute | solution.py:718
  73.7 11.0 %collective-permute-start.19 = (f32[64,256]{1,0:T(8,128)S(1)}, f32[64,256]{1,0:T(8,128)S(1)}, u32[]{:S(2)}, u32[]{:S(2)}) collective-permute-start(f32[64,256]{1,0:T(8,128)S(1)} %add_add_fusion.2.refs_1_), channel_id=1, source_target_pairs={{0,8},{8,0},{16,24},{24,16},{1,9},{9,1},{17,25},{25,17},{2,10},{10... | collective-permute-start | bytes 196616 | tf_op jit(solution)/shard_map/ppermute | solution.py:721
  74.1 10.7 %collective-permute-start.20 = (f32[64,256]{1,0:T(8,128)S(1)}, f32[64,256]{1,0:T(8,128)S(1)}, u32[]{:S(2)}, u32[]{:S(2)}) collective-permute-start(f32[64,256]{1,0:T(8,128)S(1)} %add_add_fusion.2.refs_1_), channel_id=1, source_target_pairs={{0,16},{8,24},{16,0},{24,8},{1,17},{9,25},{17,1},{25,9},{2,18},{10... | collective-permute-start | bytes 196616 | tf_op jit(solution)/shard_map/ppermute | solution.py:721
  76.3 8.4 %collective-permute-start.21 = (f32[64,256]{1,0:T(8,128)S(1)}, f32[64,256]{1,0:T(8,128)S(1)}, u32[]{:S(2)}, u32[]{:S(2)}) collective-permute-start(f32[64,256]{1,0:T(8,128)S(1)} %add_add_fusion.2.refs_1_), channel_id=1, source_target_pairs={{0,24},{8,16},{16,8},{24,0},{1,25},{9,17},{17,9},{25,1},{2,26},{10... | collective-permute-start | bytes 196616 | tf_op jit(solution)/shard_map/ppermute | solution.py:721
  87.1 33.7 %copy-start.1 = (s32[8192]{0:T(1024)S(1)}, s32[8192]{0:T(1024)}, u32[]{:S(2)}) copy-start(s32[8192]{0:T(1024)} %idx_ref.7) | copy-start | bytes 98308
  88.9 1.4 %collective-permute-start.22 = (f32[264,128]{1,0:T(8,128)S(1)}, f32[264,128]{1,0:T(8,128)S(1)}, u32[]{:S(2)}, u32[]{:S(2)}) collective-permute-start(f32[264,128]{1,0:T(8,128)S(1)} %constant_dynamic-update-slice_fusion), channel_id=1, source_target_pairs={{0,1},{1,0},{2,3},{3,2},{4,5},{5,4},{6,7},{7,6},{8,9},{9,8},{10,11... | collective-permute-start | bytes 405512 | tf_op jit(solution)/shard_map/ppermute | solution.py:668
  90.4 5.9 %collective-permute-start.23 = (f32[72,128]{1,0:T(8,128)S(1)}, f32[72,128]{1,0:T(8,128)S(1)}, u32[]{:S(2)}, u32[]{:S(2)}) collective-permute-start(f32[72,128]{1,0:T(8,128)S(1)} %get-tuple-element.73), channel_id=1, source_target_pairs={{0,6},{1,7},{2,4},{3,5},{4,2},{5,3},{6,0},{7,1},{8,14},{9,15},{10,... | collective-permute-start | bytes 110600 | tf_op jit(solution)/shard_map/ppermute | solution.py:594
  92.1 5.4 %collective-permute-start.24 = (f32[72,128]{1,0:T(8,128)S(1)}, f32[72,128]{1,0:T(8,128)S(1)}, u32[]{:S(2)}, u32[]{:S(2)}) collective-permute-start(f32[72,128]{1,0:T(8,128)S(1)} %get-tuple-element.74), channel_id=1, source_target_pairs={{0,4},{1,5},{2,6},{3,7},{4,0},{5,1},{6,2},{7,3},{8,12},{9,13},{10,... | collective-permute-start | bytes 110600 | tf_op jit(solution)/shard_map/ppermute | solution.py:594
  93.4 4.4 %collective-permute-start.25 = (f32[72,128]{1,0:T(8,128)S(1)}, f32[72,128]{1,0:T(8,128)S(1)}, u32[]{:S(2)}, u32[]{:S(2)}) collective-permute-start(f32[72,128]{1,0:T(8,128)S(1)} %get-tuple-element.75), channel_id=1, source_target_pairs={{0,2},{1,3},{2,0},{3,1},{4,6},{5,7},{6,4},{7,5},{8,10},{9,11},{10,... | collective-permute-start | bytes 110600 | tf_op jit(solution)/shard_map/ppermute | solution.py:594
  94.0 10.2 %collective-permute-start.30 = (f32[64,1024]{1,0:T(8,128)S(1)}, f32[64,1024]{1,0:T(8,128)S(1)}, u32[]{:S(2)}, u32[]{:S(2)}) collective-permute-start(f32[64,1024]{1,0:T(8,128)S(1)} %pad_maximum_fusion.1.refs_0_), channel_id=1, source_target_pairs={{0,2},{1,3},{2,0},{3,1},{4,6},{5,7},{6,4},{7,5},{8,10},{9,11},{10,... | collective-permute-start | bytes 786440 | tf_op jit(solution)/shard_map/ppermute | solution.py:689
  95.6 9.1 %collective-permute-start.28 = (f32[64,1024]{1,0:T(8,128)S(1)}, f32[64,1024]{1,0:T(8,128)S(1)}, u32[]{:S(2)}, u32[]{:S(2)}) collective-permute-start(f32[64,1024]{1,0:T(8,128)S(1)} %pad_maximum_fusion.1.refs_0_), channel_id=1, source_target_pairs={{0,4},{1,5},{2,6},{3,7},{4,0},{5,1},{6,2},{7,3},{8,12},{9,13},{10,... | collective-permute-start | bytes 786440 | tf_op jit(solution)/shard_map/ppermute | solution.py:689
  96.3 12.2 %collective-permute-start.26 = (f32[64,1024]{1,0:T(8,128)S(1)}, f32[64,1024]{1,0:T(8,128)S(1)}, u32[]{:S(2)}, u32[]{:S(2)}) collective-permute-start(f32[64,1024]{1,0:T(8,128)S(1)} %pad_maximum_fusion.1.refs_0_), channel_id=1, source_target_pairs={{0,6},{1,7},{2,4},{3,5},{4,2},{5,3},{6,0},{7,1},{8,14},{9,15},{10,... | collective-permute-start | bytes 786440 | tf_op jit(solution)/shard_map/ppermute | solution.py:689
  101.7 1.2 collective-permute-start.33
  102.9 5.6 %collective-permute-start.34 = (f32[8,32]{1,0:T(8,128)S(1)}, f32[8,32]{1,0:T(8,128)S(1)}, u32[]{:S(2)}, u32[]{:S(2)}) collective-permute-start(f32[8,32]{1,0:T(8,128)S(1)} %broadcast_add_fusion), channel_id=1, source_target_pairs={{0,2},{1,3},{2,0},{3,1},{4,6},{5,7},{6,4},{7,5},{8,10},{9,11},{10,... | collective-permute-start | bytes 3080 | tf_op jit(solution)/shard_map/ppermute | solution.py:618
  104.1 16.7 %collective-permute-start.32 = (f32[64,1024]{1,0:T(8,128)S(1)}, f32[64,1024]{1,0:T(8,128)S(1)}, u32[]{:S(2)}, u32[]{:S(2)}) collective-permute-start(f32[64,1024]{1,0:T(8,128)S(1)} %pad_maximum_fusion.1.refs_0_), channel_id=1, source_target_pairs={{0,1},{1,0},{2,3},{3,2},{4,5},{5,4},{6,7},{7,6},{8,9},{9,8},{10,11... | collective-permute-start | bytes 786440 | tf_op jit(solution)/shard_map/ppermute | solution.py:689
  104.1 19.9 %collective-permute-start.31 = (f32[64,1024]{1,0:T(8,128)S(1)}, f32[64,1024]{1,0:T(8,128)S(1)}, u32[]{:S(2)}, u32[]{:S(2)}) collective-permute-start(f32[64,1024]{1,0:T(8,128)S(1)} %collective-permute-done.30.refs_0_), channel_id=1, source_target_pairs={{0,1},{1,0},{2,3},{3,2},{4,5},{5,4},{6,7},{7,6},{8,9},{9,8},{10,11... | collective-permute-start | bytes 786440 | tf_op jit(solution)/shard_map/ppermute | solution.py:692
  104.7 22.6 %collective-permute-start.29 = (f32[64,1024]{1,0:T(8,128)S(1)}, f32[64,1024]{1,0:T(8,128)S(1)}, u32[]{:S(2)}, u32[]{:S(2)}) collective-permute-start(f32[64,1024]{1,0:T(8,128)S(1)} %collective-permute-done.28.refs_0_), channel_id=1, source_target_pairs={{0,1},{1,0},{2,3},{3,2},{4,5},{5,4},{6,7},{7,6},{8,9},{9,8},{10,11... | collective-permute-start | bytes 786440 | tf_op jit(solution)/shard_map/ppermute | solution.py:692
  108.5 22.0 %collective-permute-start.27 = (f32[64,1024]{1,0:T(8,128)S(1)}, f32[64,1024]{1,0:T(8,128)S(1)}, u32[]{:S(2)}, u32[]{:S(2)}) collective-permute-start(f32[64,1024]{1,0:T(8,128)S(1)} %collective-permute-done.26.refs_0_), channel_id=1, source_target_pairs={{0,1},{1,0},{2,3},{3,2},{4,5},{5,4},{6,7},{7,6},{8,9},{9,8},{10,11... | collective-permute-start | bytes 786440 | tf_op jit(solution)/shard_map/ppermute | solution.py:692
  108.5 3.7 %collective-permute-start.35 = (f32[8,32]{1,0:T(8,128)S(1)}, f32[8,32]{1,0:T(8,128)S(1)}, u32[]{:S(2)}, u32[]{:S(2)}) collective-permute-start(f32[8,32]{1,0:T(8,128)S(1)} %fusion.21), channel_id=1, source_target_pairs={{0,4},{1,5},{2,6},{3,7},{4,0},{5,1},{6,2},{7,3},{8,12},{9,13},{10,... | collective-permute-start | bytes 3080 | tf_op jit(solution)/shard_map/ppermute | solution.py:618
  112.2 3.6 %collective-permute-start.36 = (f32[8,32]{1,0:T(8,128)S(1)}, f32[8,32]{1,0:T(8,128)S(1)}, u32[]{:S(2)}, u32[]{:S(2)}) collective-permute-start(f32[8,32]{1,0:T(8,128)S(1)} %add.99), channel_id=1, source_target_pairs={{0,8},{8,0},{16,24},{24,16},{1,9},{9,1},{17,25},{25,17},{2,10},{10... | collective-permute-start | bytes 3080 | tf_op jit(solution)/shard_map/ppermute | solution.py:618
  115.8 4.5 %collective-permute-start.37 = (f32[8,32]{1,0:T(8,128)S(1)}, f32[8,32]{1,0:T(8,128)S(1)}, u32[]{:S(2)}, u32[]{:S(2)}) collective-permute-start(f32[8,32]{1,0:T(8,128)S(1)} %add.100), channel_id=1, source_target_pairs={{0,16},{8,24},{16,0},{24,8},{1,17},{9,25},{17,1},{25,9},{2,18},{10... | collective-permute-start | bytes 3080 | tf_op jit(solution)/shard_map/ppermute | solution.py:618

commit v7 on v6

--- a/solution.py
+++ b/solution.py
@@ -228,8 +228,12 @@
             img_ref[:, i : i + BLOCK] = part
         else:
             w = rows // places
+            chip = lax.axis_index("mode") >> 1
+            core = lax.axis_index("mode") & 1
             for j in range(BLOCK // w):
-                img_ref[i // w + j] = part[:, j * w : (j + 1) * w]
+                p = i // w + j
+                slot = ((p & 1) ^ core) * (places // 2) + ((p >> 1) ^ chip)
+                img_ref[slot] = part[:, j * w : (j + 1) * w]
 
 
 def apply_ahead(both, turned, dh, dl, span, col):
@@ -261,6 +265,29 @@
         cost_estimate=cost(0.7 * len(bits) * (1 if side is None else 0.5)),
         compiler_params=pltpu.CompilerParams(vmem_limit_bytes=8 << 20),
     )(*args)
+
+
+def join_kernel(inv_ref, *refs):
+    out_ref = refs[-1]
+    here = lax.axis_index("pix")
+    half = out_ref.shape[0] // 2
+    for b, ref in enumerate(refs[:-1]):
+        width = ref.shape[1]
+        col = pl.ds(pl.multiple_of((here ^ b) * width, width), width)
+        out_ref[:half, col] = exact(inv_ref[...], ref[:half], NN)
+        out_ref[half:, col] = exact(inv_ref[...], ref[half:], NN)
+
+
+def join(inv, pieces):
+    vectors, width = pieces[0].shape
+    return pl.pallas_call(
+        join_kernel,
+        out_shape=jax.ShapeDtypeStruct((vectors, width * len(pieces)), F32),
+        in_specs=[VMEM] * (1 + len(pieces)),
+        out_specs=VMEM,
+        cost_estimate=cost(0.5),
+        compiler_params=pltpu.CompilerParams(vmem_limit_bytes=4 << 20),
+    )(inv, *pieces)
 
 
 def behind_kernel(bits, side, has_inv, has_acc, *refs):
@@ -654,24 +681,25 @@
     return total, (None if extra is None else chip[half:, :width])
 
 
-def scatter_mode(pieces, odds, extra):
-    _, rows, width = pieces.shape
+def scatter_mode(pieces, extra):
+    places, rows, width = pieces.shape
     n = lax.axis_size("mode")
     here = lax.axis_index("mode")
     if n != 8:
         total = double_sum(pieces, "mode")
         return lax.dynamic_index_in_dim(total, here, 0, False), double_sum(extra, "mode")
-    odd = odds[0]
-    mine = jnp.concatenate([jnp.where(odd, pieces[2 * i + 1], pieces[2 * i]) for i in range(4)])
-    other = [jnp.where(odd, pieces[2 * i], pieces[2 * i + 1]) for i in range(4)]
     small = jnp.pad(extra, ((0, 0), (0, width - extra.shape[1])))
-    got = lax.ppermute(jnp.concatenate(other + [small], axis=0), "mode", flip(n, 1))
-    mine = mine + got[: 4 * rows]
-    small = small + got[4 * rows :]
-    blocks = [
-        jnp.concatenate([mine[i * rows : (i + 1) * rows], small], axis=0) for i in range(4)
-    ]
-    total = scatter_sum(blocks, "mode", 2, odds[1:3])
+    flat = pieces.reshape(places * rows, width)
+    cut = 4 * rows
+    got = lax.ppermute(
+        jnp.concatenate([flat[cut:], small], axis=0), "mode", flip(n, 1)
+    )
+    mine = flat[:cut] + got[:cut]
+    small = small + got[cut:]
+    total = jnp.concatenate([mine[:rows], small], axis=0)
+    for b in (3, 2, 1):
+        block = jnp.concatenate([mine[b * rows : (b + 1) * rows], small], axis=0)
+        total = total + lax.ppermute(block, "mode", flip(n, 2 * b))
     return total[:rows], total[rows:, : extra.shape[1]]
 
 
@@ -737,7 +765,6 @@
     dh, dl, images, masks, bases, both, turned = start(
         phase_steps, pattern_rows, probes, frames, scale, cut
     )
-    odds = [masks[b : b + 1, :1] != 0 for b in range(8)]
     inv = probe_factor(probes)
     if cut:
         mine, far, _ = sum_chips(images, lambda: own_half(both, turned, dh, dl))
@@ -756,11 +783,11 @@
             last_inv = inverse_factor(packed, k)
             pieces = return_pieces(mine, far, dh, dl, inv)
             inv = last_inv
-        by_place = jnp.concatenate(pick(pieces, odds[4:6]), axis=1)
-        returned = by_place if inv is None else normalise(inv, by_place)
+        returned = join(inv, pieces)
         table = gather_rows(returned, bases, pattern_rows)
         images, packed = ahead(pieces[2:], (2, 3), dh, dl, None, inv, early, groups)
     else:
+        odds = [masks[b : b + 1, :1] != 0 for b in range(8)]
         images, _ = sum_mode(images, odds)
         returned = sum_pix(backward(inv, images, dh, dl), odds)
         for _ in range(1, ITERS):
@@ -771,7 +798,7 @@
             returned = normalise(inv, sum_pix(partial, odds))
         table = gather_rows(returned, bases, pattern_rows)
         images, packed = forward(returned, dh, dl, groups)
-    fields, packed = scatter_mode(images, odds, packed)
+    fields, packed = scatter_mode(images, packed)
     inv = inverse_factor(packed, k)
     fields = normalise(inv, fields)
     power = jnp.sum(fields * fields, axis=1)

time: 138 us -> 133 us (0.964)
  between operations: 4.44 us -> 1.14 us
  starting transfers between devices: 35.9 us -> 37.5 us
  waiting for transfers between devices: 44.7 us -> 43.1 us
    ppermute x5, starting transfers between devices: 2.55 us -> 4.27 us  [double_sum(): block = block + lax.ppermute(block, axis, flip(size, bit))]
    ppermute x5, waiting for transfers between devices: 11.7 us -> 10.2 us  [double_sum(): block = block + lax.ppermute(block, axis, flip(size, bit))]
  transfers between devices with their start and end apart: 38 -> 38, of which waited for: 22 -> 21; matrix products, arithmetic and copies ran while one was open for 2% -> 1% of each run, Pallas kernels for 19% -> 21%
where the time goes in v7:
time: 133 us
  Pallas kernels  49.6 us (37%)
  waiting for transfers between devices  43.1 us (32%)
  starting transfers between devices  37.5 us (28%)
  other arithmetic  1.57 us (1%)
    ppermute x6, waiting for transfers between devices, share_sum(): total = total + lax.ppermute(block, axis, flip(size, b * step))  13.1 us
    pallas_call x4, Pallas kernels, scatter_rows(): pl.pallas_call(functools.partial(scatter_kernel, places), cost_estimate=c...  12.8 us
    pallas_call x1, Pallas kernels, start(): pl.pallas_call(functools.partial(start_kernel, scale, cut), out_shape=[pl...  10.6 us
    ppermute x5, waiting for transfers between devices, double_sum(): block = block + lax.ppermute(block, axis, flip(size, bit))  10.2 us
    ppermute x6, starting transfers between devices, return_pieces(): total = total + lax.ppermute(piece, 'pix', flip(n, b))  9.03 us
    ppermute x6, waiting for transfers between devices, return_pieces(): total = total + lax.ppermute(piece, 'pix', flip(n, b))  8.82 us
    ppermute x6, starting transfers between devices, return_pieces(): out.append(lax.ppermute(total, 'pix', flip(n, b)))  8.01 us
    ppermute x6, starting transfers between devices, share_sum(): total = total + lax.ppermute(block, axis, flip(size, b * step))  7.72 us
  transfers between devices with their start and end apart: 38, of which 21 were waited for; matrix products, arithmetic and copies ran while one was open for 1% of the time, Pallas kernels for 21%

profile of v7, /device:TPU:0, one launch (start us, length us, event | category | flops | bytes accessed | tf_op | source)
XLA Modules:
  0.0 133.2 jit_solution(1443778671734786332)
XLA Ops:
  0.6 10.6 %shard_map.68 = (bf16[2,1024,1024]{2,1,0:T(8,128)(2,1)S(1)}, bf16[2,1024,1024]{2,1,0:T(8,128)(2,1)S(1)}, f32[64,512]{1,0:T(8,128)S(1)}, f32[8,128]{1,0:T(8,128)}...) custom-call(s32[4]{0:T(128)} %phase_ref.1, s32[8192]{0:T(1024)} %idx_ref.7, ...), custom_call_target="tpu_custom_call" | custom-call | bytes 42000000 | tf_op jit(solution)/shard_map/pallas_call | solution.py:348
  11.8 1.4 %shard_map.69 = f32[64,512]{1,0:T(8,128)S(1)} custom-call(bf16[128,1024]{1,0:T(8,128)(2,1)S(1)} %get-tuple-element.33.b_ref, bf16[128,1024]{1,0:T(8,128)(2,1)S(1)} %get-tuple-element.34.t_ref, bf16[2,1024,1024]{2,1,0:T(8,128)(2,1)S(1)} %get-tuple-element.35.dh_ref.refs_2_.refs_4_.refs_1_.refs_3_.refs_5_, ...), custom_call_target="tpu_custom_call" | custom-call | bytes 4550000 | tf_op jit(solution)/shard_map/pallas_call | solution.py:191
  13.3 3.5 %collective-permute-start.1 = (f32[64,512]{1,0:T(8,128)S(1)}, f32[64,512]{1,0:T(8,128)S(1)}, u32[]{:S(2)}, u32[]{:S(2)}) collective-permute-start(f32[64,512]{1,0:T(8,128)S(1)} %add.77), channel_id=1, source_target_pairs={{0,6},{1,7},{2,4},{3,5},{4,2},{5,3},{6,0},{7,1},{8,14},{9,15},{10,... | collective-permute-start | bytes 393224 | tf_op jit(solution)/shard_map/ppermute | solution.py:637
  17.4 3.7 %collective-permute-done.1 = f32[64,512]{1,0:T(8,128)S(1)} collective-permute-done((f32[64,512]{1,0:T(8,128)S(1)}, f32[64,512]{1,0:T(8,128)S(1)}, u32[]{:S(2)}, u32[]{:S(2)}) %collective-permute-start.1) | collective-permute-done | bytes 131104 | tf_op jit(solution)/shard_map/ppermute | solution.py:637
  21.1 2.6 %collective-permute-done.2 = f32[64,512]{1,0:T(8,128)S(1)} collective-permute-done((f32[64,512]{1,0:T(8,128)S(1)}, f32[64,512]{1,0:T(8,128)S(1)}, u32[]{:S(2)}, u32[]{:S(2)}) %collective-permute-start.2) | collective-permute-done | bytes 131104 | tf_op jit(solution)/shard_map/ppermute | solution.py:637
  24.2 4.5 %shard_map.67.refs_0_ = f32[32,32]{1,0:T(8,128)S(1)} custom-call(f32[64,8192]{1,0:T(8,128)S(1)} %bitcast.11), custom_call_target="tpu_custom_call" | custom-call | bytes 15750000 | tf_op jit(solution)/shard_map/pallas_call | solution.py:494
  28.6 1.0 shard_map.70
  30.3 3.7 %collective-permute-start.5 = (f32[64,256]{1,0:T(8,128)S(1)}, f32[64,256]{1,0:T(8,128)S(1)}, u32[]{:S(2)}, u32[]{:S(2)}) collective-permute-start(f32[64,256]{1,0:T(8,128)S(1)} %get-tuple-element.43), channel_id=1, source_target_pairs={{0,24},{8,16},{16,8},{24,0},{1,25},{9,17},{17,9},{25,1},{2,26},{10... | collective-permute-start | bytes 196616 | tf_op jit(solution)/shard_map/ppermute | solution.py:746
  34.7 0.8 collective-permute-start.7
  35.5 1.5 %collective-permute-done.5 = f32[64,256]{1,0:T(8,128)S(1)} collective-permute-done((f32[64,256]{1,0:T(8,128)S(1)}, f32[64,256]{1,0:T(8,128)S(1)}, u32[]{:S(2)}, u32[]{:S(2)}) %collective-permute-start.5) | collective-permute-done | bytes 65568 | tf_op jit(solution)/shard_map/ppermute | solution.py:746
  37.0 3.3 %collective-permute-done.6 = f32[64,256]{1,0:T(8,128)S(1)} collective-permute-done((f32[64,256]{1,0:T(8,128)S(1)}, f32[64,256]{1,0:T(8,128)S(1)}, u32[]{:S(2)}, u32[]{:S(2)}) %collective-permute-start.6) | collective-permute-done | bytes 65568 | tf_op jit(solution)/shard_map/ppermute | solution.py:746
  40.4 1.0 collective-permute-start.8
  41.5 2.0 %collective-permute-start.10 = (f32[64,256]{1,0:T(8,128)S(1)}, f32[64,256]{1,0:T(8,128)S(1)}, u32[]{:S(2)}, u32[]{:S(2)}) collective-permute-start(f32[64,256]{1,0:T(8,128)S(1)} %add_add_fusion.3.refs_0_), channel_id=1, source_target_pairs={{0,24},{8,16},{16,8},{24,0},{1,25},{9,17},{17,9},{25,1},{2,26},{10... | collective-permute-start | bytes 196616 | tf_op jit(solution)/shard_map/ppermute | solution.py:749
  44.8 1.5 %shard_map.73 = (f32[64,1024]{1,0:T(8,128)S(1)}, f32[8,128]{1,0:T(8,128)S(1)}) custom-call(f32[64,256]{1,0:T(8,128)S(1)} %add_add_fusion.3.refs_0_, f32[64,256]{1,0:T(8,128)S(1)} %collective-permute-done.8.refs_1_, bf16[2,1024,1024]{2,1,0:T(8,128)(2,1)S(1)} %get-tuple-element.35.dh_ref.refs_2_.refs_4_.refs_1_.refs_3_.refs_5_, ...), custom_call_target="tpu_custom_call" | custom-call | bytes 4900000 | tf_op jit(solution)/shard_map/pallas_call | solution.py:260
  46.3 1.7 %collective-permute-done.10.refs_3_ = f32[64,256]{1,0:T(8,128)S(1)} collective-permute-done((f32[64,256]{1,0:T(8,128)S(1)}, f32[64,256]{1,0:T(8,128)S(1)}, u32[]{:S(2)}, u32[]{:S(2)}) %collective-permute-start.10) | collective-permute-done | bytes 65568 | tf_op jit(solution)/shard_map/ppermute | solution.py:749
  47.9 2.3 %collective-permute-done.9.refs_2_ = f32[64,256]{1,0:T(8,128)S(1)} collective-permute-done((f32[64,256]{1,0:T(8,128)S(1)}, f32[64,256]{1,0:T(8,128)S(1)}, u32[]{:S(2)}, u32[]{:S(2)}) %collective-permute-start.9) | collective-permute-done | bytes 65568 | tf_op jit(solution)/shard_map/ppermute | solution.py:749
  50.3 0.8 shard_map.75
  52.6 1.7 %collective-permute-start.12 = (f32[72,512]{1,0:T(8,128)S(1)}, f32[72,512]{1,0:T(8,128)S(1)}, u32[]{:S(2)}, u32[]{:S(2)}) collective-permute-start(f32[72,512]{1,0:T(8,128)S(1)} %fusion.2), channel_id=1, source_target_pairs={{0,6},{1,7},{2,4},{3,5},{4,2},{5,3},{6,0},{7,1},{8,14},{9,15},{10,... | collective-permute-start | bytes 442376 | tf_op jit(solution)/shard_map/ppermute | solution.py:637
  54.3 1.3 collective-permute-start.13
  56.2 4.2 %collective-permute-done.12 = f32[72,512]{1,0:T(8,128)S(1)} collective-permute-done((f32[72,512]{1,0:T(8,128)S(1)}, f32[72,512]{1,0:T(8,128)S(1)}, u32[]{:S(2)}, u32[]{:S(2)}) %collective-permute-start.12) | collective-permute-done | bytes 147488 | tf_op jit(solution)/shard_map/ppermute | solution.py:637
  60.3 2.3 %collective-permute-done.13 = f32[72,512]{1,0:T(8,128)S(1)} collective-permute-done((f32[72,512]{1,0:T(8,128)S(1)}, f32[72,512]{1,0:T(8,128)S(1)}, u32[]{:S(2)}, u32[]{:S(2)}) %collective-permute-start.13) | collective-permute-done | bytes 147488 | tf_op jit(solution)/shard_map/ppermute | solution.py:637
  64.8 2.0 %collective-permute-start.16 = (f32[64,256]{1,0:T(8,128)S(1)}, f32[64,256]{1,0:T(8,128)S(1)}, u32[]{:S(2)}, u32[]{:S(2)}) collective-permute-start(f32[64,256]{1,0:T(8,128)S(1)} %get-tuple-element.55), channel_id=1, source_target_pairs={{0,24},{8,16},{16,8},{24,0},{1,25},{9,17},{17,9},{25,1},{2,26},{10... | collective-permute-start | bytes 196616 | tf_op jit(solution)/shard_map/ppermute | solution.py:746
  67.3 2.5 %collective-permute-start.18 = (f32[64,256]{1,0:T(8,128)S(1)}, f32[64,256]{1,0:T(8,128)S(1)}, u32[]{:S(2)}, u32[]{:S(2)}) collective-permute-start(f32[64,256]{1,0:T(8,128)S(1)} %get-tuple-element.57), channel_id=1, source_target_pairs={{0,8},{8,0},{16,24},{24,16},{1,9},{9,1},{17,25},{25,17},{2,10},{10... | collective-permute-start | bytes 196616 | tf_op jit(solution)/shard_map/ppermute | solution.py:746
  69.8 1.8 %collective-permute-done.16 = f32[64,256]{1,0:T(8,128)S(1)} collective-permute-done((f32[64,256]{1,0:T(8,128)S(1)}, f32[64,256]{1,0:T(8,128)S(1)}, u32[]{:S(2)}, u32[]{:S(2)}) %collective-permute-start.16) | collective-permute-done | bytes 65568 | tf_op jit(solution)/shard_map/ppermute | solution.py:746
  71.6 2.1 %collective-permute-done.17 = f32[64,256]{1,0:T(8,128)S(1)} collective-permute-done((f32[64,256]{1,0:T(8,128)S(1)}, f32[64,256]{1,0:T(8,128)S(1)}, u32[]{:S(2)}, u32[]{:S(2)}) %collective-permute-start.17) | collective-permute-done | bytes 65568 | tf_op jit(solution)/shard_map/ppermute | solution.py:746
  74.1 2.2 %collective-permute-start.20 = (f32[64,256]{1,0:T(8,128)S(1)}, f32[64,256]{1,0:T(8,128)S(1)}, u32[]{:S(2)}, u32[]{:S(2)}) collective-permute-start(f32[64,256]{1,0:T(8,128)S(1)} %add_add_fusion.2.refs_1_.refs_0_), channel_id=1, source_target_pairs={{0,16},{8,24},{16,0},{24,8},{1,17},{9,25},{17,1},{25,9},{2,18},{10... | collective-permute-start | bytes 196616 | tf_op jit(solution)/shard_map/ppermute | solution.py:749
  76.3 1.9 %collective-permute-start.21 = (f32[64,256]{1,0:T(8,128)S(1)}, f32[64,256]{1,0:T(8,128)S(1)}, u32[]{:S(2)}, u32[]{:S(2)}) collective-permute-start(f32[64,256]{1,0:T(8,128)S(1)} %add_add_fusion.2.refs_1_.refs_0_), channel_id=1, source_target_pairs={{0,24},{8,16},{16,8},{24,0},{1,25},{9,17},{17,9},{25,1},{2,26},{10... | collective-permute-start | bytes 196616 | tf_op jit(solution)/shard_map/ppermute | solution.py:749
  78.2 2.8 %shard_map.76.refs_0_.inv_ref = f32[32,32]{1,0:T(8,128)S(1)} custom-call(f32[8,128]{1,0:T(8,128)S(1)} %slice.76.g_ref), custom_call_target="tpu_custom_call" | custom-call | bytes 9450000 | tf_op jit(solution)/shard_map/pallas_call | solution.py:505
  80.9 1.7 %shard_map.80 = (f32[64,1024]{1,0:T(8,128)S(1)}, f32[8,128]{1,0:T(8,128)S(1)}) custom-call(f32[32,32]{1,0:T(8,128)S(1)} %shard_map.76.refs_0_.inv_ref, f32[64,256]{1,0:T(8,128)S(1)} %add_add_fusion.2.refs_1_.refs_0_, f32[64,256]{1,0:T(8,128)S(1)} %collective-permute-done.19.refs_2_.refs_1_, ...), custom_call_target="tpu_custom_call" | custom-call | bytes 4900000 | tf_op jit(solution)/shard_map/pallas_call | solution.py:260
  82.7 1.7 %shard_map.81 = (f32[8,64,128]{2,1,0:T(8,128)S(1)}, f32[8,128]{1,0:T(8,128)S(1)}) custom-call(f32[32,32]{1,0:T(8,128)S(1)} %shard_map.76.refs_0_.inv_ref, f32[64,1024]{1,0:T(8,128)S(1)} %get-tuple-element.58.refs_1_, f32[8,128]{1,0:T(8,128)S(1)} %get-tuple-element.59.refs_2_, f32[64,256]{1,0:T(8,128)S(1)} %collective-permute-done.20.refs_3_.refs_2_, ...), custom_call_target="tpu_custom_call" | custom-call | bytes 4900000 | tf_op jit(solution)/shard_map/pallas_call | solution.py:260
  84.6 1.3 %collective-permute-done.22 = f32[264,128]{1,0:T(8,128)S(1)} collective-permute-done((f32[264,128]{1,0:T(8,128)S(1)}, f32[264,128]{1,0:T(8,128)S(1)}, u32[]{:S(2)}, u32[]{:S(2)}) %collective-permute-start.22) | collective-permute-done | bytes 135200 | tf_op jit(solution)/shard_map/ppermute | solution.py:694
  86.0 1.7 %collective-permute-start.23 = (f32[72,128]{1,0:T(8,128)S(1)}, f32[72,128]{1,0:T(8,128)S(1)}, u32[]{:S(2)}, u32[]{:S(2)}) collective-permute-start(f32[72,128]{1,0:T(8,128)S(1)} %get-tuple-element.71), channel_id=1, source_target_pairs={{0,6},{1,7},{2,4},{3,5},{4,2},{5,3},{6,0},{7,1},{8,14},{9,15},{10,... | collective-permute-start | bytes 110600 | tf_op jit(solution)/shard_map/ppermute | solution.py:702
  87.7 1.3 collective-permute-start.24
  89.9 1.5 %collective-permute-start.30 = (f32[64,1024]{1,0:T(8,128)S(1)}, f32[64,1024]{1,0:T(8,128)S(1)}, u32[]{:S(2)}, u32[]{:S(2)}) collective-permute-start(f32[64,1024]{1,0:T(8,128)S(1)} %shard_map.83.refs_0_), channel_id=1, source_target_pairs={{0,2},{1,3},{2,0},{3,1},{4,6},{5,7},{6,4},{7,5},{8,10},{9,11},{10,... | collective-permute-start | bytes 786440 | tf_op jit(solution)/shard_map/ppermute | solution.py:717
  92.2 1.3 collective-permute-start.26
  93.5 2.8 %shard_map.82.inv_ref = f32[32,32]{1,0:T(8,128)S(1)} custom-call(f32[8,128]{1,0:T(8,128)S(1)} %slice.84.g_ref), custom_call_target="tpu_custom_call" | custom-call | bytes 9450000 | tf_op jit(solution)/shard_map/pallas_call | solution.py:505
  97.4 1.2 collective-permute-done.33
  98.5 1.5 %collective-permute-start.34 = (f32[8,32]{1,0:T(8,128)S(1)}, f32[8,32]{1,0:T(8,128)S(1)}, u32[]{:S(2)}, u32[]{:S(2)}) collective-permute-start(f32[8,32]{1,0:T(8,128)S(1)} %broadcast_add_fusion), channel_id=1, source_target_pairs={{0,2},{1,3},{2,0},{3,1},{4,6},{5,7},{6,4},{7,5},{8,10},{9,11},{10,... | collective-permute-start | bytes 3080 | tf_op jit(solution)/shard_map/ppermute | solution.py:645
  100.6 3.8 %collective-permute-done.26.refs_0_ = f32[64,1024]{1,0:T(8,128)S(1)} collective-permute-done((f32[64,1024]{1,0:T(8,128)S(1)}, f32[64,1024]{1,0:T(8,128)S(1)}, u32[]{:S(2)}, u32[]{:S(2)}) %collective-permute-start.26) | collective-permute-done | bytes 262176 | tf_op jit(solution)/shard_map/ppermute | solution.py:717
  105.1 3.0 %collective-permute-done.35 = f32[8,32]{1,0:T(8,128)S(1)} collective-permute-done((f32[8,32]{1,0:T(8,128)S(1)}, f32[8,32]{1,0:T(8,128)S(1)}, u32[]{:S(2)}, u32[]{:S(2)}) %collective-permute-start.35) | collective-permute-done | bytes 1056 | tf_op jit(solution)/shard_map/ppermute | solution.py:645
  108.9 2.8 %collective-permute-done.36 = f32[8,32]{1,0:T(8,128)S(1)} collective-permute-done((f32[8,32]{1,0:T(8,128)S(1)}, f32[8,32]{1,0:T(8,128)S(1)}, u32[]{:S(2)}, u32[]{:S(2)}) %collective-permute-start.36) | collective-permute-done | bytes 1056 | tf_op jit(solution)/shard_map/ppermute | solution.py:645
  111.7 1.2 collective-permute-start.37
  112.9 3.3 %collective-permute-done.37 = f32[8,32]{1,0:T(8,128)S(1)} collective-permute-done((f32[8,32]{1,0:T(8,128)S(1)}, f32[8,32]{1,0:T(8,128)S(1)}, u32[]{:S(2)}, u32[]{:S(2)}) %collective-permute-start.37) | collective-permute-done | bytes 1056 | tf_op jit(solution)/shard_map/ppermute | solution.py:645
  116.7 3.2 %shard_map.84.refs_2_ = f32[8192,128]{1,0:T(8,128)S(1)} custom-call(s32[8]{0:T(128)S(1)} %get-tuple-element.62.base_ref, s32[8192]{0:T(1024)S(1)} %copy-done.1, f32[64,1024]{1,0:T(8,128)S(1)} %shard_map.83.refs_0_, f32[64,1024]{1,0:T(8,128)S(1)} %collective-permute-done.32.refs_1_), custom_call_target="tpu_custom_call" | custom-call | bytes 11900000 | tf_op jit(solution)/shard_map/pallas_call | solution.py:401
  119.9 3.2 %shard_map.85.refs_2_ = f32[8192,128]{1,0:T(8,128)S(1)} custom-call(s32[8]{0:T(128)S(1)} %get-tuple-element.62.base_ref, s32[8192]{0:T(1024)S(1)} %copy-done.1, f32[64,1024]{1,0:T(8,128)S(1)} %collective-permute-done.30.refs_0_, f32[64,1024]{1,0:T(8,128)S(1)} %collective-permute-done.31.refs_1_, ...), custom_call_target="tpu_custom_call", output_to_operand_aliasing={{}: (4, {})} | custom-call | bytes 11900000 | tf_op jit(solution)/shard_map/pallas_call | solution.py:401
  123.1 3.2 %shard_map.86.refs_2_ = f32[8192,128]{1,0:T(8,128)S(1)} custom-call(s32[8]{0:T(128)S(1)} %get-tuple-element.62.base_ref, s32[8192]{0:T(1024)S(1)} %copy-done.1, f32[64,1024]{1,0:T(8,128)S(1)} %collective-permute-done.28.refs_0_, f32[64,1024]{1,0:T(8,128)S(1)} %collective-permute-done.29.refs_1_, ...), custom_call_target="tpu_custom_call", output_to_operand_aliasing={{}: (4, {})} | custom-call | bytes 11900000 | tf_op jit(solution)/shard_map/pallas_call | solution.py:401
  126.4 3.2 %shard_map.87.w_ref = f32[8192,128]{1,0:T(8,128)S(1)} custom-call(s32[8]{0:T(128)S(1)} %get-tuple-element.62.base_ref, s32[8192]{0:T(1024)S(1)} %copy-done.1, f32[64,1024]{1,0:T(8,128)S(1)} %collective-permute-done.26.refs_0_, f32[64,1024]{1,0:T(8,128)S(1)} %collective-permute-done.27.refs_1_, ...), custom_call_target="tpu_custom_call", output_to_operand_aliasing={{}: (4, {})} | custom-call | bytes 11900000 | tf_op jit(solution)/shard_map/pallas_call | solution.py:401
  129.6 3.5 %shard_map.88 = f32[64,8192]{1,0:T(8,128)} custom-call(f32[32,32]{1,0:T(8,128)S(1)} %shard_map.82.inv_ref, f32[8192,128]{1,0:T(8,128)S(1)} %shard_map.87.w_ref), custom_call_target="tpu_custom_call" | custom-call | bytes 21000000 | tf_op jit(solution)/shard_map/pallas_call | solution.py:451
  (82 shorter events, 15.0 us)
Async XLA Ops:
  11.2 2.0 %collective-permute-start = (f32[64,512]{1,0:T(8,128)S(1)}, f32[64,512]{1,0:T(8,128)S(1)}, u32[]{:S(2)}, u32[]{:S(2)}) collective-permute-start(f32[64,512]{1,0:T(8,128)S(1)} %get-tuple-element.37), channel_id=1, source_target_pairs={{0,1},{1,0},{2,3},{3,2},{4,5},{5,4},{6,7},{7,6},{8,9},{9,8},{10,11... | collective-permute-start | bytes 393224 | tf_op jit(solution)/shard_map/ppermute | solution.py:731
  11.8 12.4 %copy-start = (f32[2,32,8192]{2,1,0:T(8,128)S(1)}, f32[2,32,8192]{2,1,0:T(8,128)}, u32[]{:S(2)}) copy-start(f32[2,32,8192]{2,1,0:T(8,128)} %param.7) | copy-start | bytes 6291460
  13.3 7.8 %collective-permute-start.1 = (f32[64,512]{1,0:T(8,128)S(1)}, f32[64,512]{1,0:T(8,128)S(1)}, u32[]{:S(2)}, u32[]{:S(2)}) collective-permute-start(f32[64,512]{1,0:T(8,128)S(1)} %add.77), channel_id=1, source_target_pairs={{0,6},{1,7},{2,4},{3,5},{4,2},{5,3},{6,0},{7,1},{8,14},{9,15},{10,... | collective-permute-start | bytes 393224 | tf_op jit(solution)/shard_map/ppermute | solution.py:637
  16.8 7.0 %collective-permute-start.2 = (f32[64,512]{1,0:T(8,128)S(1)}, f32[64,512]{1,0:T(8,128)S(1)}, u32[]{:S(2)}, u32[]{:S(2)}) collective-permute-start(f32[64,512]{1,0:T(8,128)S(1)} %add.77), channel_id=1, source_target_pairs={{0,4},{1,5},{2,6},{3,7},{4,0},{5,1},{6,2},{7,3},{8,12},{9,13},{10,... | collective-permute-start | bytes 393224 | tf_op jit(solution)/shard_map/ppermute | solution.py:637
  17.3 6.7 %collective-permute-start.3 = (f32[64,512]{1,0:T(8,128)S(1)}, f32[64,512]{1,0:T(8,128)S(1)}, u32[]{:S(2)}, u32[]{:S(2)}) collective-permute-start(f32[64,512]{1,0:T(8,128)S(1)} %add.77), channel_id=1, source_target_pairs={{0,2},{1,3},{2,0},{3,1},{4,6},{5,7},{6,4},{7,5},{8,10},{9,11},{10,... | collective-permute-start | bytes 393224 | tf_op jit(solution)/shard_map/ppermute | solution.py:637
  24.1 5.6 %collective-permute-start.4 = (f32[64,512]{1,0:T(8,128)S(1)}, f32[64,512]{1,0:T(8,128)S(1)}, u32[]{:S(2)}, u32[]{:S(2)}) collective-permute-start(f32[64,512]{1,0:T(8,128)S(1)} %add_add_fusion.1.refs_1_), channel_id=1, source_target_pairs={{0,1},{1,0},{2,3},{3,2},{4,5},{5,4},{6,7},{7,6},{8,9},{9,8},{10,11... | collective-permute-start | bytes 393224 | tf_op jit(solution)/shard_map/ppermute | solution.py:736
  30.3 6.6 %collective-permute-start.5 = (f32[64,256]{1,0:T(8,128)S(1)}, f32[64,256]{1,0:T(8,128)S(1)}, u32[]{:S(2)}, u32[]{:S(2)}) collective-permute-start(f32[64,256]{1,0:T(8,128)S(1)} %get-tuple-element.43), channel_id=1, source_target_pairs={{0,24},{8,16},{16,8},{24,0},{1,25},{9,17},{17,9},{25,1},{2,26},{10... | collective-permute-start | bytes 196616 | tf_op jit(solution)/shard_map/ppermute | solution.py:746
  34.0 6.2 %collective-permute-start.6 = (f32[64,256]{1,0:T(8,128)S(1)}, f32[64,256]{1,0:T(8,128)S(1)}, u32[]{:S(2)}, u32[]{:S(2)}) collective-permute-start(f32[64,256]{1,0:T(8,128)S(1)} %get-tuple-element.44), channel_id=1, source_target_pairs={{0,16},{8,24},{16,0},{24,8},{1,17},{9,25},{17,1},{25,9},{2,18},{10... | collective-permute-start | bytes 196616 | tf_op jit(solution)/shard_map/ppermute | solution.py:746
  34.7 5.7 %collective-permute-start.7 = (f32[64,256]{1,0:T(8,128)S(1)}, f32[64,256]{1,0:T(8,128)S(1)}, u32[]{:S(2)}, u32[]{:S(2)}) collective-permute-start(f32[64,256]{1,0:T(8,128)S(1)} %get-tuple-element.45), channel_id=1, source_target_pairs={{0,8},{8,0},{16,24},{24,16},{1,9},{9,1},{17,25},{25,17},{2,10},{10... | collective-permute-start | bytes 196616 | tf_op jit(solution)/shard_map/ppermute | solution.py:746
  40.4 4.3 %collective-permute-start.8 = (f32[64,256]{1,0:T(8,128)S(1)}, f32[64,256]{1,0:T(8,128)S(1)}, u32[]{:S(2)}, u32[]{:S(2)}) collective-permute-start(f32[64,256]{1,0:T(8,128)S(1)} %add_add_fusion.3.refs_0_), channel_id=1, source_target_pairs={{0,8},{8,0},{16,24},{24,16},{1,9},{9,1},{17,25},{25,17},{2,10},{10... | collective-permute-start | bytes 196616 | tf_op jit(solution)/shard_map/ppermute | solution.py:749
  41.5 6.5 %collective-permute-start.10 = (f32[64,256]{1,0:T(8,128)S(1)}, f32[64,256]{1,0:T(8,128)S(1)}, u32[]{:S(2)}, u32[]{:S(2)}) collective-permute-start(f32[64,256]{1,0:T(8,128)S(1)} %add_add_fusion.3.refs_0_), channel_id=1, source_target_pairs={{0,24},{8,16},{16,8},{24,0},{1,25},{9,17},{17,9},{25,1},{2,26},{10... | collective-permute-start | bytes 196616 | tf_op jit(solution)/shard_map/ppermute | solution.py:749
  43.5 6.8 %collective-permute-start.9 = (f32[64,256]{1,0:T(8,128)S(1)}, f32[64,256]{1,0:T(8,128)S(1)}, u32[]{:S(2)}, u32[]{:S(2)}) collective-permute-start(f32[64,256]{1,0:T(8,128)S(1)} %add_add_fusion.3.refs_0_), channel_id=1, source_target_pairs={{0,16},{8,24},{16,0},{24,8},{1,17},{9,25},{17,1},{25,9},{2,18},{10... | collective-permute-start | bytes 196616 | tf_op jit(solution)/shard_map/ppermute | solution.py:749
  51.1 1.4 %collective-permute-start.11 = (f32[72,512]{1,0:T(8,128)S(1)}, f32[72,512]{1,0:T(8,128)S(1)}, u32[]{:S(2)}, u32[]{:S(2)}) collective-permute-start(f32[72,512]{1,0:T(8,128)S(1)} %fusion.1), channel_id=1, source_target_pairs={{0,1},{1,0},{2,3},{3,2},{4,5},{5,4},{6,7},{7,6},{8,9},{9,8},{10,11... | collective-permute-start | bytes 442376 | tf_op jit(solution)/shard_map/ppermute | solution.py:731
  52.6 7.7 %collective-permute-start.12 = (f32[72,512]{1,0:T(8,128)S(1)}, f32[72,512]{1,0:T(8,128)S(1)}, u32[]{:S(2)}, u32[]{:S(2)}) collective-permute-start(f32[72,512]{1,0:T(8,128)S(1)} %fusion.2), channel_id=1, source_target_pairs={{0,6},{1,7},{2,4},{3,5},{4,2},{5,3},{6,0},{7,1},{8,14},{9,15},{10,... | collective-permute-start | bytes 442376 | tf_op jit(solution)/shard_map/ppermute | solution.py:637
  54.3 8.3 %collective-permute-start.13 = (f32[72,512]{1,0:T(8,128)S(1)}, f32[72,512]{1,0:T(8,128)S(1)}, u32[]{:S(2)}, u32[]{:S(2)}) collective-permute-start(f32[72,512]{1,0:T(8,128)S(1)} %fusion.2), channel_id=1, source_target_pairs={{0,4},{1,5},{2,6},{3,7},{4,0},{5,1},{6,2},{7,3},{8,12},{9,13},{10,... | collective-permute-start | bytes 442376 | tf_op jit(solution)/shard_map/ppermute | solution.py:637
  55.6 7.0 %collective-permute-start.14 = (f32[72,512]{1,0:T(8,128)S(1)}, f32[72,512]{1,0:T(8,128)S(1)}, u32[]{:S(2)}, u32[]{:S(2)}) collective-permute-start(f32[72,512]{1,0:T(8,128)S(1)} %fusion.2), channel_id=1, source_target_pairs={{0,2},{1,3},{2,0},{3,1},{4,6},{5,7},{6,4},{7,5},{8,10},{9,11},{10,... | collective-permute-start | bytes 442376 | tf_op jit(solution)/shard_map/ppermute | solution.py:637
  62.7 1.4 %collective-permute-start.15 = (f32[64,512]{1,0:T(8,128)S(1)}, f32[64,512]{1,0:T(8,128)S(1)}, u32[]{:S(2)}, u32[]{:S(2)}) collective-permute-start(f32[64,512]{1,0:T(8,128)S(1)} %slice.77.refs_0_), channel_id=1, source_target_pairs={{0,1},{1,0},{2,3},{3,2},{4,5},{5,4},{6,7},{7,6},{8,9},{9,8},{10,11... | collective-permute-start | bytes 393224 | tf_op jit(solution)/shard_map/ppermute | solution.py:736
  64.8 6.8 %collective-permute-start.16 = (f32[64,256]{1,0:T(8,128)S(1)}, f32[64,256]{1,0:T(8,128)S(1)}, u32[]{:S(2)}, u32[]{:S(2)}) collective-permute-start(f32[64,256]{1,0:T(8,128)S(1)} %get-tuple-element.55), channel_id=1, source_target_pairs={{0,24},{8,16},{16,8},{24,0},{1,25},{9,17},{17,9},{25,1},{2,26},{10... | collective-permute-start | bytes 196616 | tf_op jit(solution)/shard_map/ppermute | solution.py:746
  66.8 6.9 %collective-permute-start.17 = (f32[64,256]{1,0:T(8,128)S(1)}, f32[64,256]{1,0:T(8,128)S(1)}, u32[]{:S(2)}, u32[]{:S(2)}) collective-permute-start(f32[64,256]{1,0:T(8,128)S(1)} %get-tuple-element.56), channel_id=1, source_target_pairs={{0,16},{8,24},{16,0},{24,8},{1,17},{9,25},{17,1},{25,9},{2,18},{10... | collective-permute-start | bytes 196616 | tf_op jit(solution)/shard_map/ppermute | solution.py:746
  67.3 6.4 %collective-permute-start.18 = (f32[64,256]{1,0:T(8,128)S(1)}, f32[64,256]{1,0:T(8,128)S(1)}, u32[]{:S(2)}, u32[]{:S(2)}) collective-permute-start(f32[64,256]{1,0:T(8,128)S(1)} %get-tuple-element.57), channel_id=1, source_target_pairs={{0,8},{8,0},{16,24},{24,16},{1,9},{9,1},{17,25},{25,17},{2,10},{10... | collective-permute-start | bytes 196616 | tf_op jit(solution)/shard_map/ppermute | solution.py:746
  73.7 7.2 %collective-permute-start.19 = (f32[64,256]{1,0:T(8,128)S(1)}, f32[64,256]{1,0:T(8,128)S(1)}, u32[]{:S(2)}, u32[]{:S(2)}) collective-permute-start(f32[64,256]{1,0:T(8,128)S(1)} %add_add_fusion.2.refs_1_.refs_0_), channel_id=1, source_target_pairs={{0,8},{8,0},{16,24},{24,16},{1,9},{9,1},{17,25},{25,17},{2,10},{10... | collective-permute-start | bytes 196616 | tf_op jit(solution)/shard_map/ppermute | solution.py:749
  74.1 8.6 %collective-permute-start.20 = (f32[64,256]{1,0:T(8,128)S(1)}, f32[64,256]{1,0:T(8,128)S(1)}, u32[]{:S(2)}, u32[]{:S(2)}) collective-permute-start(f32[64,256]{1,0:T(8,128)S(1)} %add_add_fusion.2.refs_1_.refs_0_), channel_id=1, source_target_pairs={{0,16},{8,24},{16,0},{24,8},{1,17},{9,25},{17,1},{25,9},{2,18},{10... | collective-permute-start | bytes 196616 | tf_op jit(solution)/shard_map/ppermute | solution.py:749
  76.3 6.4 %collective-permute-start.21 = (f32[64,256]{1,0:T(8,128)S(1)}, f32[64,256]{1,0:T(8,128)S(1)}, u32[]{:S(2)}, u32[]{:S(2)}) collective-permute-start(f32[64,256]{1,0:T(8,128)S(1)} %add_add_fusion.2.refs_1_.refs_0_), channel_id=1, source_target_pairs={{0,24},{8,16},{16,8},{24,0},{1,25},{9,17},{17,9},{25,1},{2,26},{10... | collective-permute-start | bytes 196616 | tf_op jit(solution)/shard_map/ppermute | solution.py:749
  82.7 34.0 %copy-start.1 = (s32[8192]{0:T(1024)S(1)}, s32[8192]{0:T(1024)}, u32[]{:S(2)}) copy-start(s32[8192]{0:T(1024)} %idx_ref.7) | copy-start | bytes 98308
  84.5 1.4 %collective-permute-start.22 = (f32[264,128]{1,0:T(8,128)S(1)}, f32[264,128]{1,0:T(8,128)S(1)}, u32[]{:S(2)}, u32[]{:S(2)}) collective-permute-start(f32[264,128]{1,0:T(8,128)S(1)} %pad_maximum_fusion), channel_id=1, source_target_pairs={{0,1},{1,0},{2,3},{3,2},{4,5},{5,4},{6,7},{7,6},{8,9},{9,8},{10,11... | collective-permute-start | bytes 405512 | tf_op jit(solution)/shard_map/ppermute | solution.py:694
  86.0 6.1 %collective-permute-start.23 = (f32[72,128]{1,0:T(8,128)S(1)}, f32[72,128]{1,0:T(8,128)S(1)}, u32[]{:S(2)}, u32[]{:S(2)}) collective-permute-start(f32[72,128]{1,0:T(8,128)S(1)} %get-tuple-element.71), channel_id=1, source_target_pairs={{0,6},{1,7},{2,4},{3,5},{4,2},{5,3},{6,0},{7,1},{8,14},{9,15},{10,... | collective-permute-start | bytes 110600 | tf_op jit(solution)/shard_map/ppermute | solution.py:702
  87.7 5.7 %collective-permute-start.24 = (f32[72,128]{1,0:T(8,128)S(1)}, f32[72,128]{1,0:T(8,128)S(1)}, u32[]{:S(2)}, u32[]{:S(2)}) collective-permute-start(f32[72,128]{1,0:T(8,128)S(1)} %get-tuple-element.72), channel_id=1, source_target_pairs={{0,4},{1,5},{2,6},{3,7},{4,0},{5,1},{6,2},{7,3},{8,12},{9,13},{10,... | collective-permute-start | bytes 110600 | tf_op jit(solution)/shard_map/ppermute | solution.py:702
  89.0 4.4 %collective-permute-start.25 = (f32[72,128]{1,0:T(8,128)S(1)}, f32[72,128]{1,0:T(8,128)S(1)}, u32[]{:S(2)}, u32[]{:S(2)}) collective-permute-start(f32[72,128]{1,0:T(8,128)S(1)} %get-tuple-element.73), channel_id=1, source_target_pairs={{0,2},{1,3},{2,0},{3,1},{4,6},{5,7},{6,4},{7,5},{8,10},{9,11},{10,... | collective-permute-start | bytes 110600 | tf_op jit(solution)/shard_map/ppermute | solution.py:702
  89.9 10.1 %collective-permute-start.30 = (f32[64,1024]{1,0:T(8,128)S(1)}, f32[64,1024]{1,0:T(8,128)S(1)}, u32[]{:S(2)}, u32[]{:S(2)}) collective-permute-start(f32[64,1024]{1,0:T(8,128)S(1)} %shard_map.83.refs_0_), channel_id=1, source_target_pairs={{0,2},{1,3},{2,0},{3,1},{4,6},{5,7},{6,4},{7,5},{8,10},{9,11},{10,... | collective-permute-start | bytes 786440 | tf_op jit(solution)/shard_map/ppermute | solution.py:717
  91.4 9.1 %collective-permute-start.28 = (f32[64,1024]{1,0:T(8,128)S(1)}, f32[64,1024]{1,0:T(8,128)S(1)}, u32[]{:S(2)}, u32[]{:S(2)}) collective-permute-start(f32[64,1024]{1,0:T(8,128)S(1)} %shard_map.83.refs_0_), channel_id=1, source_target_pairs={{0,4},{1,5},{2,6},{3,7},{4,0},{5,1},{6,2},{7,3},{8,12},{9,13},{10,... | collective-permute-start | bytes 786440 | tf_op jit(solution)/shard_map/ppermute | solution.py:717
  92.2 12.2 %collective-permute-start.26 = (f32[64,1024]{1,0:T(8,128)S(1)}, f32[64,1024]{1,0:T(8,128)S(1)}, u32[]{:S(2)}, u32[]{:S(2)}) collective-permute-start(f32[64,1024]{1,0:T(8,128)S(1)} %shard_map.83.refs_0_), channel_id=1, source_target_pairs={{0,6},{1,7},{2,4},{3,5},{4,2},{5,3},{6,0},{7,1},{8,14},{9,15},{10,... | collective-permute-start | bytes 786440 | tf_op jit(solution)/shard_map/ppermute | solution.py:717
  97.3 1.2 collective-permute-start.33
  98.5 5.9 %collective-permute-start.34 = (f32[8,32]{1,0:T(8,128)S(1)}, f32[8,32]{1,0:T(8,128)S(1)}, u32[]{:S(2)}, u32[]{:S(2)}) collective-permute-start(f32[8,32]{1,0:T(8,128)S(1)} %broadcast_add_fusion), channel_id=1, source_target_pairs={{0,2},{1,3},{2,0},{3,1},{4,6},{5,7},{6,4},{7,5},{8,10},{9,11},{10,... | collective-permute-start | bytes 3080 | tf_op jit(solution)/shard_map/ppermute | solution.py:645
  100.0 16.7 %collective-permute-start.32 = (f32[64,1024]{1,0:T(8,128)S(1)}, f32[64,1024]{1,0:T(8,128)S(1)}, u32[]{:S(2)}, u32[]{:S(2)}) collective-permute-start(f32[64,1024]{1,0:T(8,128)S(1)} %shard_map.83.refs_0_), channel_id=1, source_target_pairs={{0,1},{1,0},{2,3},{3,2},{4,5},{5,4},{6,7},{7,6},{8,9},{9,8},{10,11... | collective-permute-start | bytes 786440 | tf_op jit(solution)/shard_map/ppermute | solution.py:717
  100.0 19.9 %collective-permute-start.31 = (f32[64,1024]{1,0:T(8,128)S(1)}, f32[64,1024]{1,0:T(8,128)S(1)}, u32[]{:S(2)}, u32[]{:S(2)}) collective-permute-start(f32[64,1024]{1,0:T(8,128)S(1)} %collective-permute-done.30.refs_0_), channel_id=1, source_target_pairs={{0,1},{1,0},{2,3},{3,2},{4,5},{5,4},{6,7},{7,6},{8,9},{9,8},{10,11... | collective-permute-start | bytes 786440 | tf_op jit(solution)/shard_map/ppermute | solution.py:720
  100.5 22.6 %collective-permute-start.29 = (f32[64,1024]{1,0:T(8,128)S(1)}, f32[64,1024]{1,0:T(8,128)S(1)}, u32[]{:S(2)}, u32[]{:S(2)}) collective-permute-start(f32[64,1024]{1,0:T(8,128)S(1)} %collective-permute-done.28.refs_0_), channel_id=1, source_target_pairs={{0,1},{1,0},{2,3},{3,2},{4,5},{5,4},{6,7},{7,6},{8,9},{9,8},{10,11... | collective-permute-start | bytes 786440 | tf_op jit(solution)/shard_map/ppermute | solution.py:720
  104.4 22.0 %collective-permute-start.27 = (f32[64,1024]{1,0:T(8,128)S(1)}, f32[64,1024]{1,0:T(8,128)S(1)}, u32[]{:S(2)}, u32[]{:S(2)}) collective-permute-start(f32[64,1024]{1,0:T(8,128)S(1)} %collective-permute-done.26.refs_0_), channel_id=1, source_target_pairs={{0,1},{1,0},{2,3},{3,2},{4,5},{5,4},{6,7},{7,6},{8,9},{9,8},{10,11... | collective-permute-start | bytes 786440 | tf_op jit(solution)/shard_map/ppermute | solution.py:720
  104.4 3.7 %collective-permute-start.35 = (f32[8,32]{1,0:T(8,128)S(1)}, f32[8,32]{1,0:T(8,128)S(1)}, u32[]{:S(2)}, u32[]{:S(2)}) collective-permute-start(f32[8,32]{1,0:T(8,128)S(1)} %fusion.14), channel_id=1, source_target_pairs={{0,4},{1,5},{2,6},{3,7},{4,0},{5,1},{6,2},{7,3},{8,12},{9,13},{10,... | collective-permute-start | bytes 3080 | tf_op jit(solution)/shard_map/ppermute | solution.py:645
  108.1 3.6 %collective-permute-start.36 = (f32[8,32]{1,0:T(8,128)S(1)}, f32[8,32]{1,0:T(8,128)S(1)}, u32[]{:S(2)}, u32[]{:S(2)}) collective-permute-start(f32[8,32]{1,0:T(8,128)S(1)} %add.99), channel_id=1, source_target_pairs={{0,8},{8,0},{16,24},{24,16},{1,9},{9,1},{17,25},{25,17},{2,10},{10... | collective-permute-start | bytes 3080 | tf_op jit(solution)/shard_map/ppermute | solution.py:645
  111.7 4.5 %collective-permute-start.37 = (f32[8,32]{1,0:T(8,128)S(1)}, f32[8,32]{1,0:T(8,128)S(1)}, u32[]{:S(2)}, u32[]{:S(2)}) collective-permute-start(f32[8,32]{1,0:T(8,128)S(1)} %add.100), channel_id=1, source_target_pairs={{0,16},{8,24},{16,0},{24,8},{1,17},{9,25},{17,1},{25,9},{2,18},{10... | collective-permute-start | bytes 3080 | tf_op jit(solution)/shard_map/ppermute | solution.py:645
